TPU v7x, 32 devices: a whole 2x2x4 slice. The times are simulated.
32 devices in a mesh: dp: 8 (over y, x, core), seq: 4 (over z).
Axes of the slice: x: 2, y: 2, z: 4, core: 2. Of those that a mesh axis runs over, the one named last changes fastest.
Arguments:
- tokens: bfloat16 [8, 1024, 768], P('dp', 'seq'), may hold values from -6 to 6
- segments: int32 [8, 1024], P('dp', 'seq'), may hold values from 0 to 7, never falling along the last dimension, each value on 1 to 256 neighbouring positions
- query_weight: bfloat16 [768, 768], P('dp', 'seq'), may hold values from -0.3125 to 0.3125
- key_weight: bfloat16 [768, 768], P('dp', 'seq'), may hold values from -0.3125 to 0.3125
- value_weight: bfloat16 [768, 768], P('dp', 'seq'), may hold values from -0.21875 to 0.21875
- output_weight: bfloat16 [768, 768], P('dp', 'seq'), may hold values from -0.875 to 0.875
- query_bias: bfloat16 [768], P('dp'), may hold values from -3 to 3
- value_bias: bfloat16 [768], P('dp'), may hold values from -3 to 3
- output_bias: bfloat16 [768], P('dp'), may hold values from -3 to 3
- first_gain: bfloat16 [768], P('dp'), may hold values from 0.5 to 1.5
- first_shift: bfloat16 [768], P('dp'), may hold values from -3 to 3
- up_weight: bfloat16 [768, 3072], P('dp', 'seq'), may hold values from -0.21875 to 0.21875
- up_bias: bfloat16 [3072], P('dp'), may hold values from -3 to 3
- down_weight: bfloat16 [3072, 768], P('seq', 'dp'), may hold values from -0.109375 to 0.109375
- down_bias: bfloat16 [768], P('dp'), may hold values from -3 to 3
- second_gain: bfloat16 [768], P('dp'), may hold values from 0.5 to 1.5
- second_shift: bfloat16 [768], P('dp'), may hold values from -3 to 3
- cotangent: bfloat16 [8, 1024, 768], P('dp', 'seq'), may hold values from -6 to 6
Outputs:
- layer_output: bfloat16 [8, 1024, 768], P('dp', 'seq')
- input_grad: float32 [8, 1024, 768], P('dp', 'seq')
- query_weight_grad: float32 [768, 768], P('dp', 'seq')
- key_weight_grad: float32 [768, 768], P('dp', 'seq')
- value_weight_grad: float32 [768, 768], P('dp', 'seq')
- output_weight_grad: float32 [768, 768], P('dp', 'seq')
- query_bias_grad: float32 [768], P('dp')
- value_bias_grad: float32 [768], P('dp')
- output_bias_grad: float32 [768], P('dp')
- first_gain_grad: float32 [768], P('dp')
- first_shift_grad: float32 [768], P('dp')
- up_weight_grad: float32 [768, 3072], P('dp', 'seq')
- up_bias_grad: float32 [3072], P('dp')
- down_weight_grad: float32 [3072, 768], P('seq', 'dp')
- down_bias_grad: float32 [768], P('dp')
- second_gain_grad: float32 [768], P('dp')
- second_shift_grad: float32 [768], P('dp')
Inputs may be any that keep to these rules, and one draw needn't show every extreme that they name: `segments`: each sequence holds 8 documents numbered from 0 in order of position; each has 1 to 256 tokens, and one has exactly that many.
All inputs are finite; a program needn't handle non-finite values.
Results may differ from a plain program's by a relative error of at most 0.017.
The roundings to bfloat16 on the way count: a program that leaves them out, or rounds other values in their place, can miss the bound.
Values may be sent and summed in bfloat16 or wider, within the bound.
No kernel may reach another device: no remote copies, remote signals or barrier semaphores. Data moves between devices by JAX's collectives and lax.ppermute only.
A program may use at most 128 MiB of HBM per device.

v0:
```python
import jax
import jax.numpy as jnp
from jax import lax
from jax.sharding import PartitionSpec as P

D = 768
HEADS = 12
HEAD_DIM = 64
FF = 3072


EPS = 1e-05
MASKED = -1e30


def norm_forward(total, gain, shift):
    center = total - jnp.mean(total, axis=-1, keepdims=True)
    scale_inv = lax.rsqrt(jnp.mean(center * center, axis=-1, keepdims=True) + EPS)
    normed = center * scale_inv
    return (normed * gain + shift, normed, scale_inv)


def norm_backward(upstream, normed, scale_inv, gain):
    grad_normed = upstream * gain
    inner = (
        grad_normed
        - jnp.mean(grad_normed, axis=-1, keepdims=True)
        - normed * jnp.mean(grad_normed * normed, axis=-1, keepdims=True)
    )
    return (inner * scale_inv, jnp.sum(upstream * normed, axis=0), jnp.sum(upstream, axis=0))


def gelu_exact(values):
    return jax.nn.gelu(values, approximate=False)


def attend_forward(queries, keys, values, docs, block_rows):
    count = queries.shape[0] // block_rows
    factor = HEAD_DIM ** (-0.5)

    def one_block(index):
        start = index * block_rows
        query_block = lax.dynamic_slice_in_dim(queries, start, block_rows, 0)
        query_docs = lax.dynamic_slice_in_dim(docs, start, block_rows, 0)
        scores = (
            jnp.einsum("qhd,khd->hqk", query_block, keys, preferred_element_type=jnp.float32)
            * factor
        )
        scores = jnp.where((query_docs[:, None] == docs[None, :])[None], scores, MASKED)
        top = jnp.max(scores, axis=-1, keepdims=True)
        expo = jnp.exp(scores - top)
        total = jnp.sum(expo, axis=-1, keepdims=True)
        probs = (expo / total).astype(jnp.bfloat16)
        context = jnp.einsum("hqk,khd->qhd", probs, values, preferred_element_type=jnp.float32)
        return (context.astype(jnp.bfloat16), (top + jnp.log(total))[..., 0])

    context, log_total = lax.map(one_block, jnp.arange(count))
    return (context.reshape(queries.shape), log_total)


def attend_backward(queries, keys, values, docs, log_total, grad_context, block_rows):
    count = queries.shape[0] // block_rows
    factor = HEAD_DIM ** (-0.5)

    def one_block(carry, index):
        grad_keys, grad_values = carry
        start = index * block_rows
        query_block = lax.dynamic_slice_in_dim(queries, start, block_rows, 0)
        query_docs = lax.dynamic_slice_in_dim(docs, start, block_rows, 0)
        grad_block = lax.dynamic_slice_in_dim(grad_context, start, block_rows, 0)
        scores = (
            jnp.einsum("qhd,khd->hqk", query_block, keys, preferred_element_type=jnp.float32)
            * factor
        )
        same = (query_docs[:, None] == docs[None, :])[None]
        probs = jnp.where(same, jnp.exp(scores - log_total[index][..., None]), 0.0)
        grad_values = grad_values + jnp.einsum(
            "hqk,qhd->khd",
            probs.astype(jnp.bfloat16),
            grad_block,
            preferred_element_type=jnp.float32,
        )
        grad_probs = jnp.einsum(
            "qhd,khd->hqk", grad_block, values, preferred_element_type=jnp.float32
        )
        inner = jnp.sum(probs * grad_probs, axis=-1, keepdims=True)
        grad_scores = (probs * (grad_probs - inner)).astype(jnp.bfloat16)
        grad_query = (
            jnp.einsum("hqk,khd->qhd", grad_scores, keys, preferred_element_type=jnp.float32)
            * factor
        ).astype(jnp.bfloat16)
        grad_keys = (
            grad_keys
            + jnp.einsum(
                "hqk,qhd->khd", grad_scores, query_block, preferred_element_type=jnp.float32
            )
            * factor
        )
        return ((grad_keys, grad_values), grad_query)

    zeros = jnp.zeros(keys.shape, jnp.float32)
    (grad_keys, grad_values), grad_queries = lax.scan(one_block, (zeros, zeros), jnp.arange(count))
    return (
        grad_queries.reshape(queries.shape),
        grad_keys.astype(jnp.bfloat16),
        grad_values.astype(jnp.bfloat16),
    )


def per_device(
    tokens,
    segments,
    query_weight,
    key_weight,
    value_weight,
    output_weight,
    query_bias,
    value_bias,
    output_bias,
    first_gain,
    first_shift,
    up_weight,
    up_bias,
    down_weight,
    down_bias,
    second_gain,
    second_shift,
    cotangent,
):
    seq_count = lax.axis_size("seq")
    heads_here = HEADS // seq_count
    width_here = heads_here * HEAD_DIM
    narrow = (
        lax.all_gather(query_weight, "seq", axis=1, tiled=True),
        lax.all_gather(key_weight, "seq", axis=1, tiled=True),
        lax.all_gather(value_weight, "seq", axis=1, tiled=True),
        lax.all_gather(output_weight, "seq", axis=1, tiled=True),
    )
    full = (
        lax.all_gather(narrow[0], "dp", axis=0, tiled=True),
        lax.all_gather(narrow[1], "dp", axis=0, tiled=True),
        lax.all_gather(narrow[2], "dp", axis=0, tiled=True),
        lax.all_gather(narrow[3], "dp", axis=0, tiled=True),
        lax.all_gather(up_weight, "dp", axis=0, tiled=True),
        lax.all_gather(down_weight, "dp", axis=1, tiled=True),
        lax.all_gather(query_bias, "dp", axis=0, tiled=True),
        lax.all_gather(value_bias, "dp", axis=0, tiled=True),
        lax.all_gather(output_bias, "dp", axis=0, tiled=True),
        lax.all_gather(first_gain, "dp", axis=0, tiled=True),
        lax.all_gather(first_shift, "dp", axis=0, tiled=True),
        lax.all_gather(up_bias, "dp", axis=0, tiled=True),
        lax.all_gather(down_bias, "dp", axis=0, tiled=True),
        lax.all_gather(second_gain, "dp", axis=0, tiled=True),
        lax.all_gather(second_shift, "dp", axis=0, tiled=True),
    )
    (
        query_full,
        key_full,
        value_full,
        output_full,
        up_full,
        down_full,
        query_shift,
        value_shift,
        output_shift,
        gain_one,
        shift_one,
        up_shift,
        down_shift,
        gain_two,
        shift_two,
    ) = full
    doc_ids = lax.all_gather(segments, "seq", axis=1, tiled=True)[0]
    rows = tokens[0]
    local_rows = rows.shape[0]
    length = doc_ids.shape[0]
    block_rows = min(512, length)

    def to_heads(values):
        return values.reshape(local_rows, seq_count, width_here)

    query = (jnp.dot(rows, query_full, preferred_element_type=jnp.float32) + query_shift).astype(
        jnp.bfloat16
    )
    key = jnp.dot(rows, key_full, preferred_element_type=jnp.float32).astype(jnp.bfloat16)
    value = (jnp.dot(rows, value_full, preferred_element_type=jnp.float32) + value_shift).astype(
        jnp.bfloat16
    )
    spread = (
        lax.all_to_all(to_heads(query), "seq", split_axis=1, concat_axis=0, tiled=True),
        lax.all_to_all(to_heads(key), "seq", split_axis=1, concat_axis=0, tiled=True),
        lax.all_to_all(to_heads(value), "seq", split_axis=1, concat_axis=0, tiled=True),
    )
    query_heads = spread[0].reshape(length, heads_here, HEAD_DIM)
    key_heads = spread[1].reshape(length, heads_here, HEAD_DIM)
    value_heads = spread[2].reshape(length, heads_here, HEAD_DIM)
    context_heads, log_total = attend_forward(
        query_heads, key_heads, value_heads, doc_ids, block_rows
    )
    context = lax.all_to_all(
        context_heads.reshape(length, 1, width_here), "seq", split_axis=0, concat_axis=1, tiled=True
    ).reshape(local_rows, D)
    attention = jnp.dot(context, output_full, preferred_element_type=jnp.float32) + output_shift
    first, normed_one, inverse_one = norm_forward(
        rows.astype(jnp.float32) + attention, gain_one, shift_one
    )
    quarter = up_full.shape[1]
    offset = lax.axis_index("seq") * quarter
    low_first = lax.all_gather(first.astype(jnp.bfloat16), "seq", axis=0, tiled=True)
    gate = jnp.dot(
        low_first, up_full, preferred_element_type=jnp.float32
    ) + lax.dynamic_slice_in_dim(up_shift, offset, quarter, 0)
    active = gelu_exact(gate).astype(jnp.bfloat16)
    partial_out = jnp.dot(active, down_full, preferred_element_type=jnp.float32)
    branch = (
        lax.psum_scatter(
            partial_out.astype(jnp.bfloat16), "seq", scatter_dimension=0, tiled=True
        ).astype(jnp.float32)
        + down_shift
    )
    second, normed_two, inverse_two = norm_forward(first + branch, gain_two, shift_two)
    layer_output = second.astype(jnp.bfloat16).reshape(1, local_rows, D)
    upstream = cotangent[0].astype(jnp.float32)
    grad_total_two, grad_gain_two, grad_shift_two = norm_backward(
        upstream, normed_two, inverse_two, gain_two
    )
    grad_branch = grad_total_two.astype(jnp.bfloat16)
    grad_down_shift = jnp.sum(grad_branch, axis=0, dtype=jnp.float32)
    branch_rows = lax.all_gather(grad_branch, "seq", axis=0, tiled=True)
    grad_down = jnp.dot(active.T, branch_rows, preferred_element_type=jnp.float32)
    grad_active = jnp.dot(branch_rows, down_full.T, preferred_element_type=jnp.float32)
    gate_pull = jax.vjp(gelu_exact, gate)[1]
    grad_gate = gate_pull(grad_active)[0].astype(jnp.bfloat16)
    grad_up_shift = lax.dynamic_update_slice_in_dim(
        jnp.zeros((FF,), jnp.float32), jnp.sum(grad_gate, axis=0, dtype=jnp.float32), offset, 0
    )
    grad_up = jnp.dot(low_first.T, grad_gate, preferred_element_type=jnp.float32)
    partial_in = jnp.dot(grad_gate, up_full.T, preferred_element_type=jnp.float32)
    grad_first = grad_total_two + lax.psum_scatter(
        partial_in, "seq", scatter_dimension=0, tiled=True
    )
    grad_total_one, grad_gain_one, grad_shift_one = norm_backward(
        grad_first, normed_one, inverse_one, gain_one
    )
    grad_attention = grad_total_one.astype(jnp.bfloat16)
    grad_output_shift = jnp.sum(grad_attention, axis=0, dtype=jnp.float32)
    grad_output = jnp.dot(context.T, grad_attention, preferred_element_type=jnp.float32)
    grad_context = jnp.dot(
        grad_attention, output_full.T, preferred_element_type=jnp.float32
    ).astype(jnp.bfloat16)
    grad_context_heads = lax.all_to_all(
        to_heads(grad_context), "seq", split_axis=1, concat_axis=0, tiled=True
    ).reshape(length, heads_here, HEAD_DIM)
    grad_query_heads, grad_key_heads, grad_value_heads = attend_backward(
        query_heads, key_heads, value_heads, doc_ids, log_total, grad_context_heads, block_rows
    )
    returned = (
        lax.all_to_all(
            grad_query_heads.reshape(length, 1, width_here),
            "seq",
            split_axis=0,
            concat_axis=1,
            tiled=True,
        ),
        lax.all_to_all(
            grad_key_heads.reshape(length, 1, width_here),
            "seq",
            split_axis=0,
            concat_axis=1,
            tiled=True,
        ),
        lax.all_to_all(
            grad_value_heads.reshape(length, 1, width_here),
            "seq",
            split_axis=0,
            concat_axis=1,
            tiled=True,
        ),
    )
    grad_query = returned[0].reshape(local_rows, D)
    grad_key = returned[1].reshape(local_rows, D)
    grad_value = returned[2].reshape(local_rows, D)
    grad_query_weight = jnp.dot(rows.T, grad_query, preferred_element_type=jnp.float32)
    grad_key_weight = jnp.dot(rows.T, grad_key, preferred_element_type=jnp.float32)
    grad_value_weight = jnp.dot(rows.T, grad_value, preferred_element_type=jnp.float32)
    grad_query_shift = jnp.sum(grad_query, axis=0, dtype=jnp.float32)
    grad_value_shift = jnp.sum(grad_value, axis=0, dtype=jnp.float32)
    input_grad = grad_total_one + jnp.dot(
        grad_query, query_full.T, preferred_element_type=jnp.float32
    )
    input_grad = input_grad + jnp.dot(grad_key, key_full.T, preferred_element_type=jnp.float32)
    input_grad = input_grad + jnp.dot(grad_value, value_full.T, preferred_element_type=jnp.float32)

    def tiled(vector):
        return jnp.broadcast_to(vector[:, None], (vector.shape[0], seq_count))

    summed = (
        lax.psum_scatter(grad_query_weight, "dp", scatter_dimension=0, tiled=True),
        lax.psum_scatter(grad_key_weight, "dp", scatter_dimension=0, tiled=True),
        lax.psum_scatter(grad_value_weight, "dp", scatter_dimension=0, tiled=True),
        lax.psum_scatter(grad_output, "dp", scatter_dimension=0, tiled=True),
        lax.psum_scatter(grad_up, "dp", scatter_dimension=0, tiled=True),
        lax.psum_scatter(grad_down, "dp", scatter_dimension=1, tiled=True),
        lax.psum_scatter(tiled(grad_query_shift), "dp", scatter_dimension=0, tiled=True),
        lax.psum_scatter(tiled(grad_value_shift), "dp", scatter_dimension=0, tiled=True),
        lax.psum_scatter(tiled(grad_output_shift), "dp", scatter_dimension=0, tiled=True),
        lax.psum_scatter(tiled(grad_gain_one), "dp", scatter_dimension=0, tiled=True),
        lax.psum_scatter(tiled(grad_shift_one), "dp", scatter_dimension=0, tiled=True),
        lax.psum_scatter(tiled(grad_up_shift), "dp", scatter_dimension=0, tiled=True),
        lax.psum_scatter(tiled(grad_down_shift), "dp", scatter_dimension=0, tiled=True),
        lax.psum_scatter(tiled(grad_gain_two), "dp", scatter_dimension=0, tiled=True),
        lax.psum_scatter(tiled(grad_shift_two), "dp", scatter_dimension=0, tiled=True),
    )
    owned = (
        lax.psum_scatter(
            summed[0].astype(jnp.bfloat16), "seq", scatter_dimension=1, tiled=True
        ).astype(jnp.float32),
        lax.psum_scatter(
            summed[1].astype(jnp.bfloat16), "seq", scatter_dimension=1, tiled=True
        ).astype(jnp.float32),
        lax.psum_scatter(
            summed[2].astype(jnp.bfloat16), "seq", scatter_dimension=1, tiled=True
        ).astype(jnp.float32),
        lax.psum_scatter(
            summed[3].astype(jnp.bfloat16), "seq", scatter_dimension=1, tiled=True
        ).astype(jnp.float32),
        lax.psum_scatter(
            summed[6].astype(jnp.bfloat16), "seq", scatter_dimension=1, tiled=True
        ).astype(jnp.float32),
        lax.psum_scatter(
            summed[7].astype(jnp.bfloat16), "seq", scatter_dimension=1, tiled=True
        ).astype(jnp.float32),
        lax.psum_scatter(
            summed[8].astype(jnp.bfloat16), "seq", scatter_dimension=1, tiled=True
        ).astype(jnp.float32),
        lax.psum_scatter(
            summed[9].astype(jnp.bfloat16), "seq", scatter_dimension=1, tiled=True
        ).astype(jnp.float32),
        lax.psum_scatter(
            summed[10].astype(jnp.bfloat16), "seq", scatter_dimension=1, tiled=True
        ).astype(jnp.float32),
        lax.psum_scatter(
            summed[11].astype(jnp.bfloat16), "seq", scatter_dimension=1, tiled=True
        ).astype(jnp.float32),
        lax.psum_scatter(
            summed[12].astype(jnp.bfloat16), "seq", scatter_dimension=1, tiled=True
        ).astype(jnp.float32),
        lax.psum_scatter(
            summed[13].astype(jnp.bfloat16), "seq", scatter_dimension=1, tiled=True
        ).astype(jnp.float32),
        lax.psum_scatter(
            summed[14].astype(jnp.bfloat16), "seq", scatter_dimension=1, tiled=True
        ).astype(jnp.float32),
    )
    matrices = (owned[0], owned[1], owned[2], owned[3], summed[4], summed[5])
    vectors = owned[4:]
    flat = tuple((item[:, 0] for item in vectors))
    return (
        layer_output,
        input_grad.reshape(1, local_rows, D),
        matrices[0],
        matrices[1],
        matrices[2],
        matrices[3],
        flat[0],
        flat[1],
        flat[2],
        flat[3],
        flat[4],
        matrices[4],
        flat[5],
        matrices[5],
        flat[6],
        flat[7],
        flat[8],
    )


def solution(mesh):
    placed = (
        P("dp", "seq", None),
        P("dp", "seq"),
        P("dp", "seq"),
        P("dp", "seq"),
        P("dp", "seq"),
        P("dp", "seq"),
        P("dp"),
        P("dp"),
        P("dp"),
        P("dp"),
        P("dp"),
        P("dp", "seq"),
        P("dp"),
        P("seq", "dp"),
        P("dp"),
        P("dp"),
        P("dp"),
        P("dp", "seq", None),
    )
    return jax.shard_map(
        per_device,
        mesh=mesh,
        in_specs=placed,
        out_specs=(
            P("dp", "seq", None),
            P("dp", "seq", None),
            P("dp", "seq"),
            P("dp", "seq"),
            P("dp", "seq"),
            P("dp", "seq"),
            P("dp"),
            P("dp"),
            P("dp"),
            P("dp"),
            P("dp"),
            P("dp", "seq"),
            P("dp"),
            P("seq", "dp"),
            P("dp"),
            P("dp"),
            P("dp"),
        ),
        check_vma=False,
    )
```

profile of v0, /device:TPU:0, one launch (start us, length us, event | category | flops | bytes accessed | tf_op | source)
XLA Modules:
  0.0 1129.0 jit_solution(14315118774349498603)
XLA Ops:
  8.3 15.5 %all_gather.67 = bf16[96,768]{0,1:T(8,128)(2,1)S(1)} all-gather(bf16[96,192]{0,1:T(8,128)(2,1)S(1)} %copy.130), channel_id=1, replica_groups=mesh['dp'=8,'seq'=4] {'seq'}, dimensions={1}, use_global_device_ids=true | all-gather | bytes 184320 | tf_op jit(solution)/shard_map/all_gather | solution.py:134
  74.5 23.0 %all-reduce.17 = (bf16[768]{0:T(1024)(128)(2,1)S(1)}, bf16[768]{0:T(1024)(128)(2,1)S(1)}, bf16[768]{0:T(1024)(128)(2,1)S(1)}, bf16[768]{0:T(1024)(128)(2,1)S(1)}...) all-reduce(bf16[768]{0:T(1024)(128)(2,1)S(1)} %dynamic-update-slice, ...), channel_id=1, replica_groups=mesh['dp'=8,'seq'=4] {'dp'}, use_global_device_ids=true, to_apply=%add | all-reduce | flops 6144 | bytes 24576
  197.4 25.4 %all-gather.18.cloned.1.call-done = bf16[1024,768]{1,0:T(8,128)(2,1)} async-done(((bf16[256,768]{1,0:T(8,128)(2,1)}), bf16[1024,768]{1,0:T(8,128)(2,1)}) %all-gather.18.cloned.1.call-update) | async-done | bytes 1572880 | tf_op jit(solution)/shard_map/all_gather | solution.py:209
  252.6 34.8 %reduce-scatter.48.cloned.1.call-done = bf16[256,768]{1,0:T(8,128)(2,1)} async-done(((bf16[1024,768]{1,0:T(8,128)(2,1)}), bf16[256,768]{1,0:T(8,128)(2,1)}) %reduce-scatter.48.cloned.1.call-update) | async-done | bytes 393232 | tf_op jit(solution)/shard_map/reduce_scatter | solution.py:216
  291.7 36.2 %all-gather.24.cloned.1.call-done = bf16[1024,768]{1,0:T(8,128)(2,1)} async-done(((bf16[256,768]{1,0:T(8,128)(2,1)}), bf16[1024,768]{1,0:T(8,128)(2,1)}) %all-gather.24.cloned.1.call-update) | async-done | bytes 1572880 | tf_op jit(solution)/shard_map/all_gather | solution.py:229
  340.0 58.0 %reduce-scatter.50.cloned.1.call-done = f32[256,768]{1,0:T(8,128)} async-done(((f32[1024,768]{1,0:T(8,128)}), f32[256,768]{1,0:T(8,128)}) %reduce-scatter.50.cloned.1.call-update) | async-done | bytes 786448 | tf_op jit(solution)/shard_map/reduce_scatter | solution.py:239
  424.9 27.3 %while.28 = (s32[]{:T(128)}, f32[1024,3,64]{0,2,1:T(8,128)S(1)}, f32[1024,3,64]{0,2,1:T(8,128)}, bf16[2,512,3,64]{1,3,2,0:T(8,128)(2,1)}, s32[2]{0:T(128)S(1)}, ...) while((s32[]{:T(128)}, f32[1024,3,64]{0,2,1:T(8,128)S(1)}, ...), condition=%wide.region_16.17_spmd.clone, body=%wide.region_14.16_spmd.clone.sunk | while | flops 1031928320 | bytes 65659312 | solution.py:102
  455.1 14.3 %all_to_all.120 = bf16[4,2,24576]{2,1,0:T(2,128)(2,1)} all-to-all(bf16[4,2,24576]{2,1,0:T(2,128)(2,1)S(1)} %reshape.354), channel_id=1, replica_groups=mesh['dp'=8,'seq'=4] {'seq'}, dimensions={0} | all-to-all | bytes 786432 | tf_op jit(solution)/shard_map/all_to_all | solution.py:272
  540.4 26.9 %reduce-scatter.66.cloned.1.call-done = f32[96,768]{1,0:T(8,128)} async-done(((f32[768,768]{1,0:T(8,128)}), f32[96,768]{1,0:T(8,128)}) %reduce-scatter.66.cloned.1.call-update) | async-done | bytes 294928
  569.1 44.2 %reduce-scatter.64.cloned.1.call-done = f32[96,768]{1,0:T(8,128)} async-done(((f32[768,768]{1,0:T(8,128)}), f32[96,768]{1,0:T(8,128)}) %reduce-scatter.64.cloned.1.call-update) | async-done | bytes 294928
  625.2 24.9 %reduce-scatter.88.cloned.1.call-done = f32[96,4]{1,0:T(8,128)} async-done(((f32[768,4]{1,0:T(8,128)}), f32[96,4]{1,0:T(8,128)}) %reduce-scatter.88.cloned.1.call-update) | async-done | bytes 1552
  651.0 35.9 %reduce-scatter.86.cloned.1.call-done = f32[96,4]{1,0:T(8,128)} async-done(((f32[768,4]{1,0:T(8,128)}), f32[96,4]{1,0:T(8,128)}) %reduce-scatter.86.cloned.1.call-update) | async-done | bytes 1552
  687.8 35.9 %reduce-scatter.84.cloned.1.call-done = f32[96,4]{1,0:T(8,128)} async-done(((f32[768,4]{1,0:T(8,128)}), f32[96,4]{1,0:T(8,128)}) %reduce-scatter.84.cloned.1.call-update) | async-done | bytes 1552
  724.6 40.8 %reduce-scatter.82.cloned.1.call-done = f32[384,4]{1,0:T(8,128)} async-done(((f32[3072,4]{1,0:T(8,128)}), f32[384,4]{1,0:T(8,128)}) %reduce-scatter.82.cloned.1.call-update) | async-done | bytes 6160
  766.4 35.9 %reduce-scatter.76.cloned.1.call-done = f32[96,4]{1,0:T(8,128)} async-done(((f32[768,4]{1,0:T(8,128)}), f32[96,4]{1,0:T(8,128)}) %reduce-scatter.76.cloned.1.call-update) | async-done | bytes 1552
  803.1 35.9 %reduce-scatter.78.cloned.1.call-done = f32[96,4]{1,0:T(8,128)} async-done(((f32[768,4]{1,0:T(8,128)}), f32[96,4]{1,0:T(8,128)}) %reduce-scatter.78.cloned.1.call-update) | async-done | bytes 1552
  839.9 36.1 %reduce-scatter.80.cloned.1.call-done = f32[96,4]{1,0:T(8,128)} async-done(((f32[768,4]{1,0:T(8,128)}), f32[96,4]{1,0:T(8,128)}) %reduce-scatter.80.cloned.1.call-update) | async-done | bytes 1552
  880.7 32.2 %reduce-scatter.74.cloned.1.call-done = f32[96,4]{1,0:T(8,128)} async-done(((f32[768,4]{1,0:T(8,128)}), f32[96,4]{1,0:T(8,128)}) %reduce-scatter.74.cloned.1.call-update) | async-done | bytes 1552
  913.7 36.1 %reduce-scatter.72.cloned.1.call-done = f32[96,4]{1,0:T(8,128)} async-done(((f32[768,4]{1,0:T(8,128)}), f32[96,4]{1,0:T(8,128)}) %reduce-scatter.72.cloned.1.call-update) | async-done | bytes 1552
  950.7 18.9 %all-reduce.18 = (bf16[96,4]{0,1:T(4,128)(2,1)S(1)}, bf16[96,4]{0,1:T(4,128)(2,1)S(1)}, bf16[96,4]{0,1:T(4,128)(2,1)S(1)}, bf16[96,4]{0,1:T(4,128)(2,1)S(1)}, bf...) all-reduce(bf16[96,4]{0,1:T(4,128)(2,1)S(1)} %copy.174, ...), channel_id=13, replica_groups=mesh['dp'=8,'seq'=4] {'seq'}, use_global_device_ids=true, to_apply=%region_27.28.clone | all-reduce | flops 4608 | bytes 18432
  992.8 18.2 %reduce-scatter.54.cloned.1.call-done = bf16[96,192]{0,1:T(8,128)(2,1)} async-done(((bf16[96,768]{0,1:T(8,128)(2,1)}), bf16[96,192]{0,1:T(8,128)(2,1)}) %reduce-scatter.54.cloned.1.call-update) | async-done | bytes 36880 | tf_op jit(solution)/shard_map/reduce_scatter | solution.py:318
  1012.6 18.3 %reduce-scatter.52.cloned.1.call-done = bf16[96,192]{0,1:T(8,128)(2,1)} async-done(((bf16[96,768]{0,1:T(8,128)(2,1)}), bf16[96,192]{0,1:T(8,128)(2,1)}) %reduce-scatter.52.cloned.1.call-update) | async-done | bytes 36880 | tf_op jit(solution)/shard_map/reduce_scatter | solution.py:315
  1032.3 43.1 %reduce-scatter.62.cloned.1.call-done = f32[768,96]{0,1:T(8,128)} async-done(((f32[768,768]{0,1:T(8,128)}), f32[768,96]{0,1:T(8,128)}) %reduce-scatter.62.cloned.1.call-update) | async-done | bytes 294928 | tf_op jit(solution)/shard_map/reduce_scatter | solution.py:303
  1075.5 46.8 %reduce-scatter.60.cloned.1.call-done = f32[96,768]{1,0:T(8,128)} async-done(((f32[768,768]{1,0:T(8,128)}), f32[96,768]{1,0:T(8,128)}) %reduce-scatter.60.cloned.1.call-update) | async-done | bytes 294928 | tf_op jit(solution)/shard_map/reduce_scatter | solution.py:302
  (396 shorter events, 383.4 us)
Async XLA Ops:
  7.3 90.2 %all-gather.10.cloned.1.call-start = ((), (), s32[]{:S(2)}) async-start(), calls=%async_computation.29 | async-start | bytes 1327104 | tf_op jit(solution)/shard_map/all_gather | solution.py:140
  24.6 80.5 %all-gather.14.cloned.1.call-start = ((), (), s32[]{:S(2)}) async-start(), calls=%async_computation.31 | async-start | bytes 1327104 | tf_op jit(solution)/shard_map/all_gather | solution.py:142
  55.9 123.1 %all-gather.16.cloned.1.call-start = ((), (), s32[]{:S(2)}) async-start(), calls=%async_computation.32 | async-start | bytes 1327104 | tf_op jit(solution)/shard_map/all_gather | solution.py:143
  182.9 104.5 %reduce-scatter.48.cloned.1.call-start = ((), (), s32[]{:S(2)}) async-start(), calls=%async_computation.36 | async-start | bytes 1966080 | tf_op jit(solution)/shard_map/reduce_scatter | solution.py:216
  291.7 106.3 %reduce-scatter.50.cloned.1.call-start = ((), (), s32[]{:S(2)}) async-start(), calls=%async_computation.38 | async-start | bytes 3932160 | tf_op jit(solution)/shard_map/reduce_scatter | solution.py:239
  407.9 128.7 %reduce-scatter.58.cloned.1.call-start = ((), (), s32[]{:S(2)}) async-start(), calls=%async_computation.42 | async-start | bytes 2654208 | tf_op jit(solution)/shard_map/reduce_scatter | solution.py:301
  410.8 127.7 %reduce-scatter.68.cloned.1.call-start = ((), (), s32[]{:S(2)}) async-start(), calls=%async_computation.47 | async-start | bytes 2654208
  479.8 87.5 %reduce-scatter.66.cloned.1.call-start = ((), (), s32[]{:S(2)}) async-start(), calls=%async_computation.46 | async-start | bytes 2654208
  502.8 110.6 %reduce-scatter.64.cloned.1.call-start = ((), (), s32[]{:S(2)}) async-start(), calls=%async_computation.45 | async-start | bytes 2654208
  525.4 124.7 %reduce-scatter.88.cloned.1.call-start = ((), (), s32[]{:S(2)}) async-start(), calls=%async_computation.57 | async-start | bytes 442368
  526.5 160.4 %reduce-scatter.86.cloned.1.call-start = ((), (), s32[]{:S(2)}) async-start(), calls=%async_computation.56 | async-start | bytes 442368
  527.5 196.2 %reduce-scatter.84.cloned.1.call-start = ((), (), s32[]{:S(2)}) async-start(), calls=%async_computation.55 | async-start | bytes 442368
  528.5 236.8 %reduce-scatter.82.cloned.1.call-start = ((), (), s32[]{:S(2)}) async-start(), calls=%async_computation.54 | async-start | bytes 1769472
  530.5 271.7 %reduce-scatter.76.cloned.1.call-start = ((), (), s32[]{:S(2)}) async-start(), calls=%async_computation.51 | async-start | bytes 442368
  531.5 307.5 %reduce-scatter.78.cloned.1.call-start = ((), (), s32[]{:S(2)}) async-start(), calls=%async_computation.52 | async-start | bytes 442368
  532.6 343.4 %reduce-scatter.80.cloned.1.call-start = ((), (), s32[]{:S(2)}) async-start(), calls=%async_computation.53 | async-start | bytes 442368
  533.5 379.3 %reduce-scatter.74.cloned.1.call-start = ((), (), s32[]{:S(2)}) async-start(), calls=%async_computation.50 | async-start | bytes 442368
  535.1 414.7 %reduce-scatter.72.cloned.1.call-start = ((), (), s32[]{:S(2)}) async-start(), calls=%async_computation.49 | async-start | bytes 442368
  536.5 443.5 %reduce-scatter.70.cloned.1.call-start = ((), (), s32[]{:S(2)}) async-start(), calls=%async_computation.48 | async-start | bytes 245760
  538.4 452.8 %reduce-scatter.56.cloned.1.call-start = ((), (), s32[]{:S(2)}) async-start(), calls=%async_computation.41 | async-start | bytes 245760 | tf_op jit(solution)/shard_map/reduce_scatter | solution.py:321
  540.3 470.7 %reduce-scatter.54.cloned.1.call-start = ((), (), s32[]{:S(2)}) async-start(), calls=%async_computation.40 | async-start | bytes 245760 | tf_op jit(solution)/shard_map/reduce_scatter | solution.py:318
  569.1 461.7 %reduce-scatter.52.cloned.1.call-start = ((), (), s32[]{:S(2)}) async-start(), calls=%async_computation.39 | async-start | bytes 245760 | tf_op jit(solution)/shard_map/reduce_scatter | solution.py:315
  615.2 460.3 %reduce-scatter.62.cloned.1.call-start = ((), (), s32[]{:S(2)}) async-start(), calls=%async_computation.44 | async-start | bytes 2654208 | tf_op jit(solution)/shard_map/reduce_scatter | solution.py:303
  620.1 502.2 %reduce-scatter.60.cloned.1.call-start = ((), (), s32[]{:S(2)}) async-start(), calls=%async_computation.43 | async-start | bytes 2654208 | tf_op jit(solution)/shard_map/reduce_scatter | solution.py:302
  (61 other events, 1645.1 us)
Sparse Core Ops, SparseCore 0:
  24.7 25.3 all-gather.9
  52.6 24.0 all-gather.13
  79.2 24.1 all-gather.11
  105.1 24.0 all-gather.15
  132.2 28.4 all-gather.19
  182.3 40.3 all-gather.17
  252.1 35.2 reduce-scatter.47
  291.8 36.0 all-gather.23
  338.9 59.0 reduce-scatter.49
  412.1 43.8 reduce-scatter.57
  479.9 41.4 reduce-scatter.67
  524.8 42.4 reduce-scatter.65
  570.8 42.4 reduce-scatter.63
  616.2 33.8 reduce-scatter.87
  653.1 33.8 reduce-scatter.85
  689.8 33.8 reduce-scatter.83
  726.8 38.4 reduce-scatter.81
  768.4 33.8 reduce-scatter.75
  805.2 33.7 reduce-scatter.77
  842.1 33.8 reduce-scatter.79
  879.0 33.8 reduce-scatter.73
  915.9 33.8 reduce-scatter.71
  1034.7 40.7 reduce-scatter.61
  1079.8 42.4 reduce-scatter.59
  (5 shorter events, 94.7 us)
where the time goes:
time: 1140 us; the launch traced here: 1130 us
  waiting for transfers between devices  720 us (63%)
  blocking collectives  167 us (15%)
  local copies, waits for them, and re-layouts  84.7 us (7%)
  matrix products  75.6 us (7%)
  other arithmetic  38 us (3%)
  starting transfers between devices  20.9 us (2%)
  between operations  16 us (1%)
    unnamed x42, waiting for transfers between devices  386 us
    reduce_scatter x1, waiting for transfers between devices, per_device(): lax.psum_scatter(partial_in, 'seq', scatter_dimension=0, tiled=True)  58 us
    unnamed x138, local copies, waits for them, and re-layouts  47.2 us
    reduce_scatter x1, waiting for transfers between devices, per_device(): lax.psum_scatter(grad_up, 'dp', scatter_dimension=0, tiled=True)  46.8 us
    reduce_scatter x1, waiting for transfers between devices, per_device(): lax.psum_scatter(grad_down, 'dp', scatter_dimension=1, tiled=True)  43.1 us
    unnamed x2, blocking collectives  41.9 us
    all_gather x1, waiting for transfers between devices, per_device(): branch_rows = lax.all_gather(grad_branch, 'seq', axis=0, tiled=True)  36.2 us
    reduce_scatter x1, waiting for transfers between devices, per_device(): lax.psum_scatter(partial_out.astype(jnp.bfloat16), 'seq', scatter_dimensi...  34.8 us
  transfers between devices with their start and end apart: 34, of which 25 were waited for; matrix products, arithmetic and copies ran while one was open for 15% of the time, Pallas kernels for 0%

commit v1 on v0

v1 whole, which is shorter than its diff:
```python
import jax
import jax.numpy as jnp
from jax import lax
from jax.experimental import pallas as pl
from jax.experimental.pallas import tpu as pltpu
from jax.sharding import PartitionSpec as P

D = 768
HEADS = 12
HEAD_DIM = 64
FF = 3072
EPS = 1e-05
MASKED = 1e30
PAIR = 2 * HEAD_DIM
QUARTER = D // 4
HALF = D // 2
HID = FF // 4
VECS = 8
BF = jnp.bfloat16
F32 = jnp.float32
ROOT_HALF = 0.7071067811865476
ROOT_TWO_PI = 0.3989422804014327


def dot(a, b):
    return lax.dot_general(a, b, (((1,), (0,)), ((), ())), preferred_element_type=F32)


def dot_nt(a, b):
    return lax.dot_general(a, b, (((1,), (1,)), ((), ())), preferred_element_type=F32)


def dot_tn(a, b):
    return lax.dot_general(a, b, (((0,), (0,)), ((), ())), preferred_element_type=F32)


def swap(value, axis, mask):
    count = lax.axis_size(axis)
    return lax.ppermute(value, axis, [(k, k ^ mask) for k in range(count)])


def whole(shape):
    return pl.BlockSpec(shape, lambda *_: (0,) * len(shape))


def params():
    return pltpu.CompilerParams(vmem_limit_bytes=60 * 1024 * 1024)


def call(body, scalars, operands, in_specs, outs, out_specs, grid, scratch=(), flops=0):
    spec = pltpu.PrefetchScalarGridSpec(
        num_scalar_prefetch=1,
        grid=grid,
        in_specs=in_specs,
        out_specs=out_specs,
        scratch_shapes=list(scratch),
    )
    moved = sum(o.size * o.dtype.itemsize for o in list(operands) + list(outs))
    return pl.pallas_call(
        body,
        out_shape=outs,
        grid_spec=spec,
        compiler_params=params(),
        cost_estimate=pl.CostEstimate(flops=flops, transcendentals=0, bytes_accessed=moved),
    )(scalars, *operands)


def struct(shape, dtype):
    return jax.ShapeDtypeStruct(shape, dtype)


def gather_pieces(piece):
    count = lax.axis_size("dp")
    if piece.shape[0] % 16 or count & (count - 1):
        return [lax.all_gather(piece, "dp", axis=0, tiled=True)]
    chip = {0: piece}
    for j in range(count - 2, 0, -2):
        chip[j] = swap(piece, "dp", j)
    pieces = []
    for j in range(0, count, 2):
        pieces += [chip[j], swap(chip[j], "dp", 1)]
    return pieces


def place(target, refs, base, source_cols, target_cols):
    rows = refs[0].shape[0]
    for j, ref in enumerate(refs):
        start = 0 if len(refs) == 1 else pl.multiple_of((base ^ j) * rows, 16)
        target[pl.ds(start, rows), target_cols] = ref[:, source_cols]


def split_rows(result, base, keep, send):
    count, rows = 2 * keep.shape[0], keep.shape[1]
    for j in range(count):
        block = result[pl.ds(pl.multiple_of((base ^ j) * rows, 16), rows), :].astype(BF)
        if j % 2:
            send[j // 2] = block
        else:
            keep[j // 2] = block


def qkv_attend(scalars, own, partner, halo_near, halo_far, own_docs, bias, pieces, rows):
    count = len(pieces)
    base = 3 * rows

    def body(sc, own_ref, partner_ref, near_ref, far_ref, docs_ref, bias_ref, *refs):
        weight_refs, refs = refs[:count], refs[count:]
        q_ref, k_ref, v_ref, ctx_ref, x_ref, w_ref, hot_ref, mask_ref = refs
        step = pl.program_id(0)

        @pl.when(step == 0)
        def _():
            near = sc[0]
            own_at = pl.multiple_of(near * rows, rows)
            partner_at = pl.multiple_of((1 - near) * rows, rows)
            number = lax.broadcasted_iota(jnp.int32, (16, rows), 0).astype(F32)

            def mark(line, at):
                hit = jnp.broadcast_to(line, (16, rows)) == number
                hot_ref[:, pl.ds(at, rows)] = jnp.where(hit, 1.0, 0.0).astype(BF)

            x_ref[pl.ds(own_at, rows), :] = own_ref[...]
            x_ref[pl.ds(partner_at, rows), :] = partner_ref[:rows, :]
            mark(docs_ref[...], own_at)
            mark(partner_ref[rows : rows + 1, :rows].astype(F32), partner_at)

            def halo(ref):
                x_ref[2 * rows :, :] = ref[:rows, :]
                mark(ref[rows : rows + 1, :rows].astype(F32), 2 * rows)

            pl.when(near == 1)(lambda: halo(near_ref))
            pl.when(near == 0)(lambda: halo(far_ref))
            place(w_ref, weight_refs, sc[1], slice(None), slice(None))
            hot = hot_ref[...]
            mask_ref[...] = (dot_tn(hot[:, : 2 * rows], hot) - 1.0) * MASKED

        at = pl.multiple_of(step * 3 * PAIR, PAIR)
        both = (dot(x_ref[...], w_ref[:, pl.ds(at, 3 * PAIR)]) + bias_ref[...]).astype(BF)
        query, key, value = both[:, :PAIR], both[:, PAIR : 2 * PAIR], both[:, 2 * PAIR :]
        q_ref[...] = query
        k_ref[...] = key
        v_ref[...] = value
        lane = lax.broadcasted_iota(jnp.int32, (1, PAIR), 1)
        for start, reach in ((0, 2 * rows), (rows, 3 * rows)):
            total = jnp.zeros((rows, PAIR), F32)
            for head in range(2):
                part = jnp.where((lane // HEAD_DIM) == head, 1.0, 0.0)
                mine = (query[start : start + rows].astype(F32) * (part * HEAD_DIM**-0.5)).astype(BF)
                scores = dot_nt(mine, key[:reach]) + mask_ref[start : start + rows, :reach]
                expo = jnp.exp(scores - jnp.max(scores, axis=-1, keepdims=True))
                probs = expo * (1.0 / jnp.sum(expo, axis=-1, keepdims=True))
                total = total + dot(probs.astype(BF), value[:reach]) * part
            ctx_ref[start : start + rows, :] = total.astype(BF)

    column = lambda height: pl.BlockSpec((height, PAIR), lambda p, _: (0, p))
    operands = [own, partner, halo_near, halo_far, own_docs, bias] + pieces
    in_specs = [whole(o.shape) for o in operands]
    in_specs[5] = pl.BlockSpec((1, 3 * PAIR), lambda p, _: (0, p))
    outs = [
        struct((base, HALF), BF),
        struct((base, HALF), BF),
        struct((base, HALF), BF),
        struct((2 * rows, HALF), BF),
        struct((base, D), BF),
        struct((D, 3 * HALF), BF),
        struct((16, base), BF),
    ]
    out_specs = [column(base)] * 3 + [column(2 * rows)] + [whole(o.shape) for o in outs[4:]]
    return call(
        body,
        scalars,
        operands,
        in_specs,
        outs,
        out_specs,
        (HALF // PAIR,),
        [pltpu.VMEM((2 * rows, base), F32)],
        flops=2 * base * D * 3 * HALF,
    )


def feed_forward(scalars, ctx_mine, ctx_partner, x, vecs, up_bias, pieces, rows):
    count = len(pieces)

    def body(sc, mine_ref, partner_ref, x_ref, vec_ref, bias_ref, *refs):
        weight_refs, refs = refs[:count], refs[count:]
        (up_ref, down_ref, out_ref, norm_ref, inv_ref, first_ref, gate_ref, active_ref, part_ref) = refs[:9]
        full_ref, other_ref = refs[9:]

        @pl.when(pl.program_id(0) == 0)
        def _():
            place(up_ref, weight_refs, sc[1], slice(0, HID), slice(0, HID))
            place(down_ref, weight_refs, sc[1], slice(HID, 2 * HID), slice(0, HID))
            place(up_ref, weight_refs, sc[1], slice(2 * HID, 3 * HID), slice(HID, 2 * HID))
            place(down_ref, weight_refs, sc[1], slice(3 * HID, 4 * HID), slice(HID, 2 * HID))
            place(full_ref, weight_refs, sc[1], slice(4 * HID, 4 * HID + D), slice(None))
            for ref, flip in ((out_ref, 0), (other_ref, 1)):
                for k in range(2):
                    at = pl.multiple_of((sc[2] ^ flip ^ (2 * k)) * QUARTER, 16)
                    ref[k * QUARTER : (k + 1) * QUARTER, :] = full_ref[pl.ds(at, QUARTER), :]

        attention = dot(mine_ref[...], out_ref[...]) + dot(partner_ref[...], other_ref[...])
        total = x_ref[...].astype(F32) + (attention + vec_ref[2:3, :])
        center = total - jnp.mean(total, axis=-1, keepdims=True)
        inverse = lax.rsqrt(jnp.mean(center * center, axis=-1, keepdims=True) + EPS)
        normed = center * inverse
        norm_ref[...] = normed
        inv_ref[...] = jnp.broadcast_to(inverse, (rows, 128))
        first = (normed * vec_ref[3:4, :] + vec_ref[4:5, :]).astype(BF)
        first_ref[...] = first
        gate = dot(first, up_ref[...]) + bias_ref[...]
        gate_ref[...] = gate
        active = (gate * (1.0 + lax.erf(gate * ROOT_HALF)) * 0.5).astype(BF)
        active_ref[...] = active
        part_ref[...] = dot_nt(active, down_ref[...]).astype(BF)

    block = lambda width: pl.BlockSpec((rows, width), lambda r, _: (r, 0))
    operands = [ctx_mine, ctx_partner, x, vecs, up_bias] + pieces
    in_specs = [block(HALF), block(HALF), block(D)] + [whole(o.shape) for o in operands[3:]]
    outs = [
        struct((D, 2 * HID), BF),
        struct((D, 2 * HID), BF),
        struct((HALF, D), BF),
        struct((2 * rows, D), F32),
        struct((2 * rows, 128), F32),
        struct((2 * rows, D), BF),
        struct((2 * rows, 2 * HID), F32),
        struct((2 * rows, 2 * HID), BF),
        struct((2 * rows, D), BF),
    ]
    out_specs = [whole(o.shape) for o in outs[:3]] + [block(o.shape[1]) for o in outs[3:]]
    return call(
        body,
        scalars,
        operands,
        in_specs,
        outs,
        out_specs,
        (2,),
        [pltpu.VMEM((D, D), BF), pltpu.VMEM((HALF, D), BF)],
        flops=2 * 2 * rows * D * (D + 4 * HID),
    )


def gelu_slope(scalars, gate):
    rows = gate.shape[0] // 4

    def body(_, gate_ref, slope_ref):
        gate_here = gate_ref[...]
        bell = jnp.exp(gate_here * gate_here * -0.5) * ROOT_TWO_PI
        slope_ref[...] = 0.5 * (1.0 + lax.erf(gate_here * ROOT_HALF)) + gate_here * bell

    spec = pl.BlockSpec((rows, gate.shape[1]), lambda r, _: (r, 0))
    return call(body, scalars, [gate], [spec], [struct(gate.shape, F32)], [spec], (4,))[0]


def second_norm(scalars, part, received, normed, slope, cot_own, cot_partner, vecs, up, down, rows):
    def body(
        sc, part_ref, recv_ref, norm_ref, slope_ref, own_ref, partner_ref, vec_ref, up_ref, down_ref, *refs
    ):
        (out_ref, total_grad_ref, branch_grad_ref, gate_grad_ref, first_part_ref, sums_ref, bias_ref) = refs
        step = pl.program_id(0)
        mine = step == sc[0]

        @pl.when(step == 0)
        def _():
            sums_ref[...] = jnp.zeros_like(sums_ref)
            bias_ref[...] = jnp.zeros_like(bias_ref)

        first = norm_ref[...] * vec_ref[3:4, :] + vec_ref[4:5, :]
        branch = part_ref[...].astype(F32) + recv_ref[...].astype(F32) + vec_ref[5:6, :]
        total = first + branch
        center = total - jnp.mean(total, axis=-1, keepdims=True)
        inverse = lax.rsqrt(jnp.mean(center * center, axis=-1, keepdims=True) + EPS)
        here = center * inverse
        upstream = jnp.where(mine, own_ref[...].astype(F32), partner_ref[...].astype(F32))
        scaled = upstream * vec_ref[6:7, :]
        inner = (
            scaled
            - jnp.mean(scaled, axis=-1, keepdims=True)
            - here * jnp.mean(scaled * here, axis=-1, keepdims=True)
        )
        total_grad = inner * inverse
        total_grad_ref[...] = total_grad
        branch_grad = total_grad.astype(BF)
        branch_grad_ref[...] = branch_grad

        @pl.when(mine)
        def _():
            out_ref[...] = (here * vec_ref[6:7, :] + vec_ref[7:8, :]).astype(BF)
            sums_ref[0:1, :] += jnp.sum(upstream * here, axis=0, keepdims=True)
            sums_ref[1:2, :] += jnp.sum(upstream, axis=0, keepdims=True)
            sums_ref[2:3, :] += jnp.sum(branch_grad.astype(F32), axis=0, keepdims=True)

        gate_grad = (dot(branch_grad, down_ref[...]) * slope_ref[...]).astype(BF)
        gate_grad_ref[...] = gate_grad
        bias_ref[0:1, :] += jnp.sum(gate_grad.astype(F32), axis=0, keepdims=True)
        first_part_ref[...] = dot_nt(gate_grad, up_ref[...]).astype(BF)

    block = lambda width: pl.BlockSpec((rows, width), lambda r, _: (r, 0))
    operands = [part, received, normed, slope, cot_own, cot_partner, vecs, up, down]
    in_specs = [block(D), block(D), block(D), block(2 * HID)] + [whole(o.shape) for o in operands[4:]]
    outs = [
        struct((rows, D), BF),
        struct((2 * rows, D), F32),
        struct((2 * rows, D), BF),
        struct((2 * rows, 2 * HID), BF),
        struct((2 * rows, D), BF),
        struct((8, D), F32),
        struct((8, 2 * HID), F32),
    ]
    out_specs = [
        whole((rows, D)),
        block(D),
        block(D),
        block(2 * HID),
        block(D),
        whole((8, D)),
        whole((8, 2 * HID)),
    ]
    return call(
        body, scalars, operands, in_specs, outs, out_specs, (2,), flops=2 * 2 * rows * D * 4 * HID
    )


def split_outs(count, width):
    return [struct((count // 2, D // count, width), BF)] * 2


def can_split(count):
    return (D // count) % 16 == 0 and count & (count - 1) == 0


def feed_forward_grads(scalars, first, gate_grad, branch_grad, active, count):
    tall = first.shape[0]

    def body(sc, first_ref, gate_ref, branch_ref, active_ref, *refs):
        result_ref = refs[-1]
        step = pl.program_id(0)

        @pl.when(step % 2 == 0)
        def _():
            result_ref[...] = dot_tn(first_ref[...], gate_ref[...])

        @pl.when(step % 2 == 1)
        def _():
            result_ref[...] = dot_tn(branch_ref[...], active_ref[...])

        if len(refs) == 2:
            refs[0][...] = result_ref[...]
        else:
            split_rows(result_ref, sc[1], refs[0], refs[1])

    half = pl.BlockSpec((tall, HID), lambda c, _: (0, c // 2))
    if can_split(count):
        outs = split_outs(count, 4 * HID)
        out_specs = [pl.BlockSpec((count // 2, D // count, HID), lambda c, _: (0, 0, c))] * 2
    else:
        outs = [struct((D, 4 * HID), F32)]
        out_specs = [pl.BlockSpec((D, HID), lambda c, _: (0, c))]
    return call(
        body,
        scalars,
        [first, gate_grad, branch_grad, active],
        [whole(first.shape), half, whole(branch_grad.shape), half],
        outs,
        out_specs,
        (4,),
        [pltpu.VMEM((D, HID), F32)],
        flops=2 * tall * D * 4 * HID,
    )


def first_norm(scalars, part, received, total_grad, normed, inverse, vecs, out_weight, rows):
    def body(sc, part_ref, recv_ref, grad_ref, norm_ref, inv_ref, vec_ref, weight_ref, *refs):
        own_ref, attention_ref, context_ref, send_ref, sums_ref = refs
        step = pl.program_id(0)
        mine = step == sc[0]

        @pl.when(step == 0)
        def _():
            sums_ref[...] = jnp.zeros_like(sums_ref)

        upstream = grad_ref[...] + part_ref[...].astype(F32) + recv_ref[...].astype(F32)
        here = norm_ref[...]
        scaled = upstream * vec_ref[3:4, :]
        inner = (
            scaled
            - jnp.mean(scaled, axis=-1, keepdims=True)
            - here * jnp.mean(scaled * here, axis=-1, keepdims=True)
        )
        total = inner * inv_ref[:, :1]
        attention = total.astype(BF)
        attention_ref[...] = attention

        @pl.when(mine)
        def _():
            own_ref[...] = total
            sums_ref[0:1, :] += jnp.sum(upstream * here, axis=0, keepdims=True)
            sums_ref[1:2, :] += jnp.sum(upstream, axis=0, keepdims=True)
            sums_ref[2:3, :] += jnp.sum(attention.astype(F32), axis=0, keepdims=True)

        context = dot_nt(attention, weight_ref[...]).astype(BF)
        context_ref[...] = context

        @pl.when(step == 1)
        def _():
            turned = jnp.concatenate([weight_ref[QUARTER:, :], weight_ref[:QUARTER, :]], axis=0)
            send_ref[...] = dot_nt(attention, turned).astype(BF)

    block = lambda width: pl.BlockSpec((rows, width), lambda r, _: (r, 0))
    operands = [part, received, total_grad, normed, inverse, vecs, out_weight]
    in_specs = [block(D)] * 4 + [block(128), whole(vecs.shape), whole(out_weight.shape)]
    outs = [
        struct((rows, D), F32),
        struct((2 * rows, D), BF),
        struct((2 * rows, HALF), BF),
        struct((rows, HALF), BF),
        struct((8, D), F32),
    ]
    out_specs = [whole((rows, D)), block(D), block(HALF), whole((rows, HALF)), whole((8, D))]
    return call(body, scalars, operands, in_specs, outs, out_specs, (2,), flops=2 * 2 * rows * D * HALF)


def output_grads(scalars, ctx_mine, ctx_partner, attention, count):
    tall = attention.shape[0]

    def body(sc, mine_ref, partner_ref, grad_ref, *refs):
        result_ref = refs[-1]
        for ref, flip in ((mine_ref, 0), (partner_ref, 1)):
            part = dot_tn(ref[...], grad_ref[...])
            for k in range(2):
                at = pl.multiple_of((sc[2] ^ flip ^ (2 * k)) * QUARTER, 16)
                result_ref[pl.ds(at, QUARTER), :] = part[k * QUARTER : (k + 1) * QUARTER, :]
        if len(refs) == 2:
            refs[0][...] = result_ref[...]
        else:
            split_rows(result_ref, sc[1], refs[0], refs[1])

    outs = split_outs(count, D) if can_split(count) else [struct((D, D), F32)]
    operands = [ctx_mine, ctx_partner, attention]
    return call(
        body,
        scalars,
        operands,
        [whole(o.shape) for o in operands],
        outs,
        [whole(o.shape) for o in outs],
        (1,),
        [pltpu.VMEM((D, D), F32)],
        flops=2 * tall * D * D,
    )


def attend_backward(scalars, query, key, value, grad_pair, grad_halo, hot, weight, rows):
    base = 3 * rows
    steps = HALF // PAIR

    def body(sc, q_ref, k_ref, v_ref, pair_ref, halo_ref, hot_ref, w_ref, *refs):
        out_ref, keep_ref, send_ref, mask_ref, key_ref, value_ref, acc_ref = refs
        step = pl.program_id(0)

        @pl.when(step == 0)
        def _():
            mask_ref[...] = (dot_tn(hot_ref[...], hot_ref[...]) - 1.0) * MASKED

        key_ref[...] = jnp.zeros_like(key_ref)
        value_ref[...] = jnp.zeros_like(value_ref)
        lane = lax.broadcasted_iota(jnp.int32, (1, PAIR), 1)
        query_grads = [jnp.zeros((PAIR, rows), F32), jnp.zeros((PAIR, rows), F32)]
        for head in range(2):
            part = jnp.where((lane // HEAD_DIM) == head, 1.0, 0.0)
            key_turned = (k_ref[...].astype(F32) * part).T.astype(BF)
            for index, (low, high) in enumerate(((0, 2 * rows), (0, base), (rows, base))):
                start = index * rows
                mine = (q_ref[start : start + rows].astype(F32) * (part * HEAD_DIM**-0.5)).astype(BF)
                grads = halo_ref[...] if index == 2 else pair_ref[start : start + rows]
                grads = (grads.astype(F32) * part).astype(BF)
                scores = dot_nt(k_ref[low:high], mine) + mask_ref[low:high, start : start + rows]
                expo = jnp.exp(scores - jnp.max(scores, axis=0, keepdims=True))
                probs = expo * (1.0 / jnp.sum(expo, axis=0, keepdims=True))
                pulled = dot_nt(v_ref[low:high], grads)
                inner = jnp.sum(probs * pulled, axis=0, keepdims=True)
                score_grads = (probs * (pulled - inner)).astype(BF)
                top = min(high, 2 * rows)
                span = top - low
                value_ref[low:top, :] += dot(probs[:span].astype(BF), grads)
                key_ref[low:top, :] += dot(score_grads[:span], mine)
                if index < 2:
                    query_grads[index] = query_grads[index] + dot(key_turned[:, low:high], score_grads)
        for index in range(2):
            turned = (query_grads[index] * HEAD_DIM**-0.5).T.astype(BF)
            out_ref[index * rows : (index + 1) * rows, :PAIR] = turned
        out_ref[:, PAIR : 2 * PAIR] = key_ref[...].astype(BF)
        out_ref[:, 2 * PAIR :] = value_ref[...].astype(BF)
        product = dot_nt(out_ref[...], w_ref[...])

        @pl.when(step == 0)
        def _():
            acc_ref[...] = product

        @pl.when(step > 0)
        def _():
            acc_ref[...] += product

        @pl.when(step == steps - 1)
        def _():
            near = sc[0]
            keep_ref[...] = acc_ref[pl.ds(pl.multiple_of(near * rows, rows), rows), :]
            other = acc_ref[pl.ds(pl.multiple_of((1 - near) * rows, rows), rows), :]
            send_ref[...] = other.astype(BF)

    column = lambda height: pl.BlockSpec((height, PAIR), lambda p, _: (0, p))
    operands = [query, key, value, grad_pair, grad_halo, hot, weight]
    in_specs = [column(base)] * 3 + [column(2 * rows), column(rows), whole(hot.shape)]
    in_specs += [pl.BlockSpec((D, 3 * PAIR), lambda p, _: (0, p))]
    outs = [struct((2 * rows, 3 * HALF), BF), struct((rows, D), F32), struct((rows, D), BF)]
    out_specs = [
        pl.BlockSpec((2 * rows, 3 * PAIR), lambda p, _: (0, p)),
        whole((rows, D)),
        whole((rows, D)),
    ]
    scratch = [
        pltpu.VMEM((base, base), F32),
        pltpu.VMEM((2 * rows, PAIR), F32),
        pltpu.VMEM((2 * rows, PAIR), F32),
        pltpu.VMEM((2 * rows, D), F32),
    ]
    return call(
        body,
        scalars,
        operands,
        in_specs,
        outs,
        out_specs,
        (steps,),
        scratch,
        flops=2 * HALF * base * base * 5 + 2 * 2 * rows * D * 3 * HALF,
    )


def projection_grads(scalars, x, grads, count, rows):
    tall = 2 * rows

    def body(sc, x_ref, grad_ref, *refs):
        result_ref = refs[-1]
        result_ref[...] = dot_tn(x_ref[...], grad_ref[...])
        refs[-2][...] = jnp.broadcast_to(
            jnp.sum(grad_ref[...].astype(F32), axis=0, keepdims=True), (8, 3 * PAIR)
        )
        if len(refs) == 3:
            refs[0][...] = result_ref[...]
        else:
            split_rows(result_ref, sc[1], refs[0], refs[1])

    if can_split(count):
        outs = split_outs(count, 3 * HALF)
        out_specs = [pl.BlockSpec((count // 2, D // count, 3 * PAIR), lambda p, _: (0, 0, p))] * 2
    else:
        outs = [struct((D, 3 * HALF), F32)]
        out_specs = [pl.BlockSpec((D, 3 * PAIR), lambda p, _: (0, p))]
    outs = outs + [struct((8, 3 * HALF), F32)]
    out_specs = out_specs + [pl.BlockSpec((8, 3 * PAIR), lambda p, _: (0, p))]
    return call(
        body,
        scalars,
        [x, grads],
        [pl.BlockSpec((tall, D), lambda p, _: (0, 0)), pl.BlockSpec((tall, 3 * PAIR), lambda p, _: (0, p))],
        outs,
        out_specs,
        (HALF // PAIR,),
        [pltpu.VMEM((D, 3 * PAIR), F32)],
        flops=2 * tall * D * 3 * HALF,
    )


def combine(scalars, keep, received):
    count, rows, width = keep.shape
    chunk = width // 3

    def body(_, keep_ref, recv_ref, *refs):
        for k in range(count):
            total = keep_ref[k].astype(F32) + recv_ref[k].astype(F32)
            refs[k][...] = total.astype(refs[k].dtype)

    block = pl.BlockSpec((count, rows, chunk), lambda c, _: (0, 0, c))
    outs = [struct((rows, width), F32)] + [struct((rows, width), BF)] * (count - 1)
    spec = pl.BlockSpec((rows, chunk), lambda c, _: (0, c))
    return call(body, scalars, [keep, received], [block, block], outs, [spec] * count, (3,))


def reduce_pieces(scalars, parts):
    if len(parts) == 1:
        return lax.psum_scatter(parts[0], "dp", scatter_dimension=0, tiled=True)
    keep, send = parts
    sums = combine(scalars, keep, swap(send, "dp", 1))
    total = sums[0]
    for k in range(len(sums) - 1, 0, -1):
        total = total + swap(sums[k], "dp", 2 * k).astype(F32)
    return total


def per_device(
    tokens,
    segments,
    query_weight,
    key_weight,
    value_weight,
    output_weight,
    query_bias,
    value_bias,
    output_bias,
    first_gain,
    first_shift,
    up_weight,
    up_bias,
    down_weight,
    down_bias,
    second_gain,
    second_shift,
    cotangent,
):
    seq_count = lax.axis_size("seq")
    count = lax.axis_size("dp")
    place_z = lax.axis_index("seq")
    place_dp = lax.axis_index("dp")
    assert seq_count == 4
    rows = tokens.shape[1]
    piece_rows = query_weight.shape[0]
    near = ((place_z == 1) | (place_z == 2)).astype(jnp.int32)
    scalars = jnp.stack([near, place_dp, place_z]).astype(jnp.int32)

    narrow = jnp.concatenate([query_weight, key_weight, value_weight, output_weight], axis=1)
    wide = jnp.concatenate([up_weight, down_weight.T], axis=1)
    narrow_far = swap(narrow, "seq", 2)
    own = tokens[0]
    own_docs = segments.astype(F32)
    marks = jnp.pad(segments.astype(BF), ((0, 15), (0, D - rows)))
    labelled = jnp.concatenate([own, marks], axis=0)
    partner = swap(labelled, "seq", 1)
    halo_near = lax.ppermute(labelled, "seq", [(1, 2), (2, 1)])
    halo_far = lax.ppermute(labelled, "seq", [(1, 3), (2, 0)])
    wide_far = swap(wide, "seq", 2)
    cot_own = cotangent[0]
    cot_partner = swap(cot_own, "seq", 1)

    vectors = jnp.concatenate(
        [
            query_bias,
            value_bias,
            output_bias,
            first_gain,
            first_shift,
            down_bias,
            second_gain,
            second_shift,
            up_bias,
        ]
    )
    spread = lax.all_to_all(
        jnp.broadcast_to(vectors[None], (count, vectors.shape[0])), "dp", 0, 0, tiled=True
    )
    main = spread[:, : VECS * piece_rows].astype(F32)
    main = main.reshape(count, VECS, piece_rows).transpose(1, 0, 2).reshape(VECS, D)
    hidden_bias = spread[:, VECS * piece_rows :].astype(F32).reshape(4, HID)

    def mine_of(table):
        first_half = lax.dynamic_index_in_dim(table, place_z, 0)
        return jnp.concatenate([first_half, lax.dynamic_index_in_dim(table, place_z ^ 2, 0)], axis=1)

    up_bias_here = mine_of(hidden_bias)
    query_bias_here = mine_of(main[0].reshape(4, QUARTER))
    value_bias_here = mine_of(main[1].reshape(4, QUARTER))
    bias = jnp.concatenate([query_bias_here, jnp.zeros((1, HALF), F32), value_bias_here], axis=0)
    bias = bias.reshape(3, 3, PAIR).transpose(1, 0, 2).reshape(1, 3 * HALF)

    columns = jnp.stack(
        [
            jnp.concatenate(
                [narrow[:, k * QUARTER : (k + 1) * QUARTER], narrow_far[:, k * QUARTER : (k + 1) * QUARTER]],
                axis=1,
            )
            for k in range(3)
        ],
        axis=1,
    )
    columns = columns.reshape(piece_rows, 3, 3, PAIR).transpose(0, 2, 1, 3).reshape(piece_rows, 3 * HALF)
    projection_pieces = gather_pieces(columns)
    out_half = jnp.stack([narrow[:, 3 * QUARTER :], narrow_far[:, 3 * QUARTER :]])
    out_far = swap(out_half, "seq", 1)
    out_all = jnp.concatenate([out_half, out_far], axis=0)
    order = jnp.arange(4) ^ place_z
    slot = jnp.array([0, 2, 1, 3])[order]
    out_piece = jnp.take(out_all, slot, axis=0).transpose(1, 0, 2).reshape(piece_rows, D)
    feed_pieces = gather_pieces(jnp.concatenate([wide, wide_far, out_piece], axis=1))

    query, key, value, ctx_mine, x, weight, hot = qkv_attend(
        scalars, own, partner, halo_near, halo_far, own_docs, bias, projection_pieces, rows
    )
    ctx_partner = swap(ctx_mine, "seq", 1)
    up, down, out_mine, normed, inverse, first, gate, active, part = feed_forward(
        scalars, ctx_mine, ctx_partner, x, main, up_bias_here, feed_pieces, rows
    )
    part_far = swap(part, "seq", 1)
    slope = gelu_slope(scalars, gate)
    layer_output, total_grad, branch_grad, gate_grad, first_part, sums_two, hidden_sums = second_norm(
        scalars, part, part_far, normed, slope, cot_own, cot_partner, main, up, down, rows
    )
    first_part_far = swap(first_part, "seq", 1)
    feed_parts = feed_forward_grads(scalars, first, gate_grad, branch_grad, active, count)
    own_grad, attention_grad, ctx_grad, halo_send, sums_one = first_norm(
        scalars, first_part, first_part_far, total_grad, normed, inverse, main, out_mine, rows
    )
    halo_grad = swap(halo_send, "seq", 2)
    out_parts = output_grads(scalars, ctx_mine, ctx_partner, attention_grad, count)
    feed_total = reduce_pieces(scalars, feed_parts)
    feed_far = swap(feed_total[:, 2 * HID :].astype(BF), "seq", 2).astype(F32)
    feed_mine = feed_total[:, : 2 * HID] + feed_far
    out_total = reduce_pieces(scalars, out_parts).reshape(piece_rows, 4, QUARTER)
    out_mine_grad = lax.dynamic_index_in_dim(out_total, place_z, 1, keepdims=False)
    out_send = lax.dynamic_index_in_dim(out_total, place_z ^ 2, 1, keepdims=False).astype(BF)
    out_grad = out_mine_grad + swap(out_send, "seq", 2).astype(F32)

    grads, input_keep, input_send = attend_backward(
        scalars, query, key, value, ctx_grad, halo_grad, hot, weight, rows
    )
    input_grad = own_grad + input_keep + swap(input_send, "seq", 1).astype(F32)
    *projection_parts, projection_sums = projection_grads(scalars, x, grads, count, rows)
    projection_total = reduce_pieces(scalars, projection_parts)
    projection_total = projection_total.reshape(piece_rows, 3, 3, PAIR).transpose(0, 2, 1, 3)
    projection_total = projection_total.reshape(piece_rows, 3, HALF)
    projection_far = swap(projection_total[:, :, QUARTER:].astype(BF), "seq", 2).astype(F32)
    projection_mine = projection_total[:, :, :QUARTER] + projection_far

    bias_sums = projection_sums[0].reshape(3, 3, PAIR).transpose(1, 0, 2).reshape(3, 2, QUARTER)

    def spread_out(table, width):
        slots = jnp.arange(4)[:, None]
        wide_table = jnp.where(slots == place_z, table[0][None], 0.0)
        wide_table = jnp.where(slots == (place_z ^ 2), table[1][None], wide_table)
        return wide_table.reshape(4 * width)

    stacked = jnp.stack(
        [
            spread_out(bias_sums[0], QUARTER),
            spread_out(bias_sums[2], QUARTER),
            sums_one[2],
            sums_one[0],
            sums_one[1],
            sums_two[2],
            sums_two[0],
            sums_two[1],
        ]
    )
    stacked = stacked.reshape(VECS, count, piece_rows).transpose(1, 0, 2).reshape(count, VECS * piece_rows)
    hidden = spread_out(hidden_sums[0].reshape(2, HID), HID).reshape(count, FF // count)
    small = jnp.concatenate([stacked, hidden], axis=1)
    small = jnp.broadcast_to(small[:, None], (count, 4, small.shape[1])).reshape(count * 4, -1)
    small = jnp.sum(lax.all_to_all(small, ("dp", "seq"), 0, 0, tiled=True), axis=0)
    vec = [small[k * piece_rows : (k + 1) * piece_rows] for k in range(VECS)]
    return (
        layer_output[None],
        input_grad[None],
        projection_mine[:, 0],
        projection_mine[:, 1],
        projection_mine[:, 2],
        out_grad,
        vec[0],
        vec[1],
        vec[2],
        vec[3],
        vec[4],
        feed_mine[:, :HID],
        small[VECS * piece_rows :],
        feed_mine[:, HID:].T,
        vec[5],
        vec[6],
        vec[7],
    )


def solution(mesh):
    placed = (
        P("dp", "seq", None),
        P("dp", "seq"),
        P("dp", "seq"),
        P("dp", "seq"),
        P("dp", "seq"),
        P("dp", "seq"),
        P("dp"),
        P("dp"),
        P("dp"),
        P("dp"),
        P("dp"),
        P("dp", "seq"),
        P("dp"),
        P("seq", "dp"),
        P("dp"),
        P("dp"),
        P("dp"),
        P("dp", "seq", None),
    )
    return jax.shard_map(
        per_device,
        mesh=mesh,
        in_specs=placed,
        out_specs=(
            P("dp", "seq", None),
            P("dp", "seq", None),
            P("dp", "seq"),
            P("dp", "seq"),
            P("dp", "seq"),
            P("dp", "seq"),
            P("dp"),
            P("dp"),
            P("dp"),
            P("dp"),
            P("dp"),
            P("dp", "seq"),
            P("dp"),
            P("seq", "dp"),
            P("dp"),
            P("dp"),
            P("dp"),
        ),
        check_vma=False,
    )
```

time: 1140 us -> 310 us (0.27)
  waiting for transfers between devices: 720 us -> 129 us
  blocking collectives: 167 us -> 0 us
  Pallas kernels: 0 us -> 94.2 us
  matrix products: 75.6 us -> 0 us
  local copies, waits for them, and re-layouts: 84.7 us -> 20.5 us
  starting transfers between devices: 20.9 us -> 50.6 us
  other arithmetic: 38 us -> 13 us
  between operations: 16 us -> 1.5 us
    unnamed x42 -> x0, waiting for transfers between devices: 386 us -> none
    reduce_scatter x8 -> x0, waiting for transfers between devices: 229 us -> none  [the longest x1 58 us: per_device(): lax.psum_scatter(partial_in, 'seq', scatter_dimension=0, tiled=True)]
    ppermute x0 -> x41, waiting for transfers between devices: none -> 102 us  [the longest x39 102 us: swap(): return lax.ppermute(value, axis, [(k, k ^ mask) for k in range(count)])]
    pallas_call x0 -> x12, Pallas kernels: none -> 94.2 us  [call(): pl.pallas_call(body, out_shape=outs, grid_spec=spec, compiler_params=para...]
    all_gather x6 -> x0, blocking collectives: 82.9 us -> none  [the longest x1 15.5 us: per_device(): lax.all_gather(query_weight, 'seq', axis=1, tiled=True)]
    dot_general x32 -> x0, matrix products: 75.6 us -> none  [the longest x1 11.1 us: per_device(): jnp.dot(low_first, up_full, preferred_element_type=jnp.float32)]
    all_gather x8 -> x0, waiting for transfers between devices: 75.3 us -> none  [the longest x1 36.2 us: per_device(): branch_rows = lax.all_gather(grad_branch, 'seq', axis=0, tiled=True)]
    ppermute x0 -> x41, starting transfers between devices: none -> 43.2 us  [the longest x39 41 us: swap(): return lax.ppermute(value, axis, [(k, k ^ mask) for k in range(count)])]
  transfers between devices with their start and end apart: 34 -> 43, of which waited for: 25 -> 18; matrix products, arithmetic and copies ran while one was open for 15% -> 8% of each run, Pallas kernels for 0% -> 24%
where the time goes in v1:
time: 310 us; the launch traced here: 309 us
  waiting for transfers between devices  129 us (42%)
  Pallas kernels  94.2 us (30%)
  starting transfers between devices  50.6 us (16%)
  local copies, waits for them, and re-layouts  20.5 us (7%)
  other arithmetic  13 us (4%)
    ppermute x39, waiting for transfers between devices, swap(): return lax.ppermute(value, axis, [(k, k ^ mask) for k in range(count)])  102 us
    pallas_call x12, Pallas kernels, call(): pl.pallas_call(body, out_shape=outs, grid_spec=spec, compiler_params=para...  94.2 us
    ppermute x39, starting transfers between devices, swap(): return lax.ppermute(value, axis, [(k, k ^ mask) for k in range(count)])  41 us
    all_to_all x1, waiting for transfers between devices, per_device(): lax.all_to_all(jnp.broadcast_to(vectors[None], (count, vectors.shape[0]))...  19.8 us
    all_to_all x1, waiting for transfers between devices, per_device(): lax.all_to_all(small, ('dp', 'seq'), 0, 0, tiled=True)  6.98 us
  transfers between devices with their start and end apart: 43, of which 18 were waited for; matrix products, arithmetic and copies ran while one was open for 8% of the time, Pallas kernels for 24%

profile of v1, /device:TPU:0, one launch (start us, length us, event | category | flops | bytes accessed | tf_op | source)
XLA Modules:
  0.0 308.6 jit_solution(1662447975477226240)
XLA Ops:
  1.7 4.1 %collective-permute-start.3 = (bf16[96,768]{1,0:T(8,128)(2,1)S(1)}, bf16[96,768]{1,0:T(8,128)(2,1)S(1)}, u32[]{:S(2)}, u32[]{:S(2)}) collective-permute-start(bf16[96,768]{1,0:T(8,128)(2,1)S(1)} %pad_maximum_fusion.3), channel_id=1, source_target_pairs={{0,2},{1,3},{2,0},{3,1},{4,6},{5,7},{6,4},{7,5},{8,10},{9,11},{10,... | collective-permute-start | bytes 442376 | tf_op jit(solution)/shard_map/ppermute | solution.py:39
  11.3 8.7 %collective-permute-done.3 = bf16[96,768]{1,0:T(8,128)(2,1)S(1)} collective-permute-done((bf16[96,768]{1,0:T(8,128)(2,1)S(1)}, bf16[96,768]{1,0:T(8,128)(2,1)S(1)}, u32[]{:S(2)}, u32[]{:S(2)}) %collective-permute-start.3) | collective-permute-done | bytes 147488 | tf_op jit(solution)/shard_map/ppermute | solution.py:39
  24.7 11.8 %collective-permute-done.13 = bf16[2,96,192]{2,1,0:T(8,128)(2,1)S(1)} collective-permute-done((bf16[2,96,192]{2,1,0:T(8,128)(2,1)S(1)}, bf16[2,96,192]{2,1,0:T(8,128)(2,1)S(1)}, u32[]{:S(2)}, u32[]{:S(2)}) %collective-permute-start.13) | collective-permute-done | bytes 73760 | tf_op jit(solution)/shard_map/ppermute | solution.py:39
  56.9 19.8 %all-to-all-done = bf16[8,2,576]{2,1,0:T(2,128)(2,1)S(1)} async-done(((bf16[8,2,576]{2,1,0:T(2,128)(2,1)}), bf16[8,2,576]{2,1,0:T(2,128)(2,1)S(1)}, u32[]{:S(2)}, u32[]{:S(2)}) %all-to-all-start) | async-done | bytes 18464 | tf_op jit(solution)/shard_map/all_to_all | solution.py:660
  81.8 12.7 %shard_map.314 = (bf16[768,384]{1,0:T(8,128)(2,1)}, bf16[768,384]{1,0:T(8,128)(2,1)}, bf16[768,384]{1,0:T(8,128)(2,1)}, bf16[512,384]{1,0:T(8,128)(2,1)}, bf16[7...) custom-call(s32[3]{0:T(128)} %pad_add_fusion.sc._, bf16[256,768]{1,0:T(8,128)(2,1)} %bitcast.61, ...), custom_call_target="tpu_custom_call" | custom-call | flops 1358954496 | bytes 8558080 | tf_op jit(solution)/shard_map/pallas_call | solution.py:59
  96.0 10.1 %collective-permute-done.11.partner_ref = bf16[512,384]{1,0:T(8,128)(2,1)} collective-permute-done((bf16[512,384]{1,0:T(8,128)(2,1)}, bf16[512,384]{1,0:T(8,128)(2,1)}, u32[]{:S(2)}, u32[]{:S(2)}) %collective-permute-start.11) | collective-permute-done | bytes 393248 | tf_op jit(solution)/shard_map/ppermute | solution.py:39
  107.0 11.2 %shard_map.315 = (bf16[768,1536]{1,0:T(8,128)(2,1)}, bf16[768,1536]{1,0:T(8,128)(2,1)}, bf16[384,768]{1,0:T(8,128)(2,1)}, f32[512,768]{1,0:T(8,128)}, f32[512,12...) custom-call(s32[3]{0:T(128)} %pad_add_fusion.sc._, ...), custom_call_target="tpu_custom_call" | custom-call | flops 3019898880 | bytes 21329920 | tf_op jit(solution)/shard_map/pallas_call | solution.py:59
  120.3 5.4 %shard_map.316.slope_ref = f32[512,1536]{1,0:T(8,128)} custom-call(s32[3]{0:T(128)} %pad_add_fusion.sc._, f32[512,1536]{1,0:T(8,128)} %get-tuple-element.71.gate_ref), custom_call_target="tpu_custom_call" | custom-call | bytes 6291456 | tf_op jit(solution)/shard_map/pallas_call | solution.py:59
  125.7 20.0 %collective-permute-done.22.partner_ref = bf16[256,768]{1,0:T(8,128)(2,1)S(1)} collective-permute-done((bf16[256,768]{1,0:T(8,128)(2,1)S(1)}, bf16[256,768]{1,0:T(8,128)(2,1)S(1)}, u32[]{:S(2)}, u32[]{:S(2)}) %collective-permute-start.22) | collective-permute-done | bytes 393248 | tf_op jit(solution)/shard_map/ppermute | solution.py:39
  146.7 9.9 %shard_map.317 = (bf16[256,768]{1,0:T(8,128)(2,1)}, f32[512,768]{1,0:T(8,128)}, bf16[512,768]{1,0:T(8,128)(2,1)}, bf16[512,1536]{1,0:T(8,128)(2,1)}, bf16[512,76...) custom-call(s32[3]{0:T(128)} %pad_add_fusion.sc._, bf16[512,768]{1,0:T(8,128)(2,1)} %get-tuple-element.69.part_ref, ...), custom_call_target="tpu_custom_call" | custom-call | flops 2415919104 | bytes 17006592 | tf_op jit(solution)/shard_map/pallas_call | solution.py:59
  158.5 8.4 %shard_map.324 = (bf16[4,96,3072]{2,1,0:T(8,128)(2,1)}, bf16[4,96,3072]{2,1,0:T(8,128)(2,1)}) custom-call(s32[3]{0:T(128)} %pad_add_fusion.sc._, bf16[512,768]{1,0:T(8,128)(2,1)} %get-tuple-element.107.first_ref, bf16[512,1536]{1,0:T(8,128)(2,1)} %get-tuple-element.108.gate_ref, bf16[512,768]{1,0:T(8,128)(2,1)} %get-tuple-element.109.branch_ref, ...), custom_call_target="tpu_custom_call" | custom-call | flops 2415919104 | bytes 9437184 | tf_op jit(solution)/shard_map/pallas_call | solution.py:59
  166.9 7.8 %collective-permute-done.23.recv_ref = bf16[512,768]{1,0:T(8,128)(2,1)S(1)} collective-permute-done((bf16[512,768]{1,0:T(8,128)(2,1)}, bf16[512,768]{1,0:T(8,128)(2,1)S(1)}, u32[]{:S(2)}, u32[]{:S(2)}) %collective-permute-start.23) | collective-permute-done | bytes 786464 | tf_op jit(solution)/shard_map/ppermute | solution.py:39
  175.6 6.4 %shard_map.318 = (f32[256,768]{1,0:T(8,128)}, bf16[512,768]{1,0:T(8,128)(2,1)}, bf16[512,384]{1,0:T(8,128)(2,1)}, bf16[256,384]{1,0:T(8,128)(2,1)}, f32[8,768]{1,0:T(8,128)}) custom-call(s32[3]{0:T(128)} %pad_add_fusion.sc._, bf16[512,768]{1,0:T(8,128)(2,1)} %get-tuple-element.75.part_ref, bf16[512,768]{1,0:T(8,128)(2,1)} %copy-done.4, ...), custom_call_target="tpu_custom_call" | custom-call | flops 301989888 | bytes 7782400 | tf_op jit(solution)/shard_map/pallas_call | solution.py:59
  187.7 3.9 %shard_map.322 = (bf16[4,96,768]{2,1,0:T(8,128)(2,1)}, bf16[4,96,768]{2,1,0:T(8,128)(2,1)}) custom-call(s32[3]{0:T(128)} %pad_add_fusion.sc._, bf16[512,384]{1,0:T(8,128)(2,1)} %get-tuple-element.67.mine_ref, bf16[512,384]{1,0:T(8,128)(2,1)} %collective-permute-done.11.partner_ref, bf16[512,768]{1,0:T(8,128)(2,1)} %get-tuple-element.96.grad_ref), custom_call_target="tpu_custom_call" | custom-call | flops 603979776 | bytes 2752512 | tf_op jit(solution)/shard_map/pallas_call | solution.py:59
  193.1 17.7 %shard_map.319 = (bf16[512,1152]{1,0:T(8,128)(2,1)}, f32[256,768]{1,0:T(8,128)}, bf16[256,768]{1,0:T(8,128)(2,1)}) custom-call(s32[3]{0:T(128)} %pad_add_fusion.sc._, bf16[768,384]{1,0:T(8,128)(2,1)} %get-tuple-element.80.q_ref, bf16[768,384]{1,0:T(8,128)(2,1)} %get-tuple-element.81.k_ref, bf16[768,384]{1,0:T(8,128)(2,1)} %get-tuple-element.82.v_ref, ...), custom_call_target="tpu_custom_call" | custom-call | flops 3170893824 | bytes 6512640 | tf_op jit(solution)/shard_map/pallas_call | solution.py:59
  210.8 5.3 %shard_map.320 = (bf16[4,96,1152]{2,1,0:T(8,128)(2,1)}, bf16[4,96,1152]{2,1,0:T(8,128)(2,1)}, f32[8,1152]{1,0:T(8,128)}) custom-call(s32[3]{0:T(128)} %pad_add_fusion.sc._, bf16[768,768]{1,0:T(8,128)(2,1)} %get-tuple-element.68.x_ref, bf16[512,1152]{1,0:T(8,128)(2,1)} %get-tuple-element.89.grad_ref), custom_call_target="tpu_custom_call" | custom-call | flops 905969664 | bytes 4165632 | tf_op jit(solution)/shard_map/pallas_call | solution.py:59
  218.7 4.1 %all-to-all-start.1 = ((f32[32,1,1152]{2,1,0:T(1,128)}), f32[32,1,1152]{2,1,0:T(1,128)S(1)}, u32[]{:S(2)}, u32[]{:S(2)}) async-start(f32[32,1,1152]{2,1,0:T(1,128)} %all_to_all.14), calls=%async_computation.1 | async-start | bytes 294912 | tf_op jit(solution)/shard_map/all_to_all | solution.py:759
  224.6 7.0 %all-to-all-done.1 = f32[32,1,1152]{2,1,0:T(1,128)S(1)} async-done(((f32[32,1,1152]{2,1,0:T(1,128)}), f32[32,1,1152]{2,1,0:T(1,128)S(1)}, u32[]{:S(2)}, u32[]{:S(2)}) %all-to-all-start.1) | async-done | bytes 147488 | tf_op jit(solution)/shard_map/all_to_all | solution.py:759
  232.9 3.7 %shard_map.323 = (f32[96,768]{1,0:T(8,128)}, bf16[96,768]{1,0:T(8,128)(2,1)}, bf16[96,768]{1,0:T(8,128)(2,1)}, bf16[96,768]{1,0:T(8,128)(2,1)}) custom-call(s32[3]{0:T(128)} %pad_add_fusion.sc._, bf16[4,96,768]{2,1,0:T(8,128)(2,1)} %get-tuple-element.97.keep_ref, bf16[4,96,768]{2,1,0:T(8,128)(2,1)} %collective-permute-done.31.recv_ref), custom_call_target="tpu_custom_call" | custom-call | bytes 1916928 | tf_op jit(solution)/shard_map/pallas_call | solution.py:59
  245.9 3.9 %shard_map.321 = (f32[96,1152]{1,0:T(8,128)}, bf16[96,1152]{1,0:T(8,128)(2,1)}, bf16[96,1152]{1,0:T(8,128)(2,1)}, bf16[96,1152]{1,0:T(8,128)(2,1)}) custom-call(s32[3]{0:T(128)} %pad_add_fusion.sc._, bf16[4,96,1152]{2,1,0:T(8,128)(2,1)} %get-tuple-element.90.keep_ref, bf16[4,96,1152]{2,1,0:T(8,128)(2,1)} %collective-permute-done.26.recv_ref), custom_call_target="tpu_custom_call" | custom-call | bytes 2875392 | tf_op jit(solution)/shard_map/pallas_call | solution.py:59
  256.5 5.5 %shard_map.325 = (f32[96,3072]{1,0:T(8,128)}, bf16[96,3072]{1,0:T(8,128)(2,1)}, bf16[96,3072]{1,0:T(8,128)(2,1)}, bf16[96,3072]{1,0:T(8,128)(2,1)}) custom-call(s32[3]{0:T(128)} %pad_add_fusion.sc._, bf16[4,96,3072]{2,1,0:T(8,128)(2,1)} %get-tuple-element.111.keep_ref, bf16[4,96,3072]{2,1,0:T(8,128)(2,1)} %copy-done.1), custom_call_target="tpu_custom_call" | custom-call | bytes 7667712 | tf_op jit(solution)/shard_map/pallas_call | solution.py:59
  269.4 10.0 %collective-permute-done.37 = bf16[96,3072]{1,0:T(8,128)(2,1)S(1)} collective-permute-done((bf16[96,3072]{1,0:T(8,128)(2,1)}, bf16[96,3072]{1,0:T(8,128)(2,1)S(1)}, u32[]{:S(2)}, u32[]{:S(2)}) %collective-permute-start.37) | collective-permute-done | bytes 589856 | tf_op jit(solution)/shard_map/ppermute | solution.py:39
  279.4 10.6 %collective-permute-done.38 = bf16[96,3072]{1,0:T(8,128)(2,1)} collective-permute-done((bf16[96,3072]{1,0:T(8,128)(2,1)}, bf16[96,3072]{1,0:T(8,128)(2,1)}, u32[]{:S(2)}, u32[]{:S(2)}) %collective-permute-start.38) | collective-permute-done | bytes 589856 | tf_op jit(solution)/shard_map/ppermute | solution.py:39
  293.3 14.4 %collective-permute-done.40 = bf16[96,1536]{1,0:T(8,128)(2,1)S(1)} collective-permute-done((bf16[96,1536]{1,0:T(8,128)(2,1)S(1)}, bf16[96,1536]{1,0:T(8,128)(2,1)S(1)}, u32[]{:S(2)}, u32[]{:S(2)}) %collective-permute-start.40) | collective-permute-done | bytes 294944 | tf_op jit(solution)/shard_map/ppermute | solution.py:39
  (261 shorter events, 84.7 us)
Async XLA Ops:
  1.7 18.3 %collective-permute-start.3 = (bf16[96,768]{1,0:T(8,128)(2,1)S(1)}, bf16[96,768]{1,0:T(8,128)(2,1)S(1)}, u32[]{:S(2)}, u32[]{:S(2)}) collective-permute-start(bf16[96,768]{1,0:T(8,128)(2,1)S(1)} %pad_maximum_fusion.3), channel_id=1, source_target_pairs={{0,2},{1,3},{2,0},{3,1},{4,6},{5,7},{6,4},{7,5},{8,10},{9,11},{10,... | collective-permute-start | bytes 442376 | tf_op jit(solution)/shard_map/ppermute | solution.py:39
  6.8 32.4 %collective-permute-start.12 = (bf16[96,1536]{1,0:T(8,128)(2,1)S(1)}, bf16[96,1536]{1,0:T(8,128)(2,1)S(1)}, u32[]{:S(2)}, u32[]{:S(2)}) collective-permute-start(bf16[96,1536]{1,0:T(8,128)(2,1)S(1)} %pad_maximum_fusion.1), channel_id=1, source_target_pairs={{0,2},{1,3},{2,0},{3,1},{4,6},{5,7},{6,4},{7,5},{8,10},{9,11},{10,... | collective-permute-start | bytes 884744 | tf_op jit(solution)/shard_map/ppermute | solution.py:39
  9.3 43.6 %collective-permute-start.2 = (bf16[272,768]{1,0:T(8,128)(2,1)S(1)}, bf16[272,768]{1,0:T(8,128)(2,1)}, u32[]{:S(2)}, u32[]{:S(2)}) collective-permute-start(bf16[272,768]{1,0:T(8,128)(2,1)S(1)} %fusion.1), channel_id=1, source_target_pairs={{1,3},{2,0},{5,7},{6,4},{9,11},{10,8},{13,15},{14,12},{17,19},{18,... | collective-permute-start | bytes 1253384 | tf_op jit(solution)/shard_map/ppermute | solution.py:642
  21.4 18.0 %collective-permute-start.9 = (bf16[96,1152]{1,0:T(8,128)(2,1)S(1)}, bf16[96,1152]{1,0:T(8,128)(2,1)S(1)}, u32[]{:S(2)}, u32[]{:S(2)}) collective-permute-start(bf16[96,1152]{1,0:T(8,128)(2,1)S(1)} %reshape.325.refs_0_), channel_id=1, source_target_pairs={{0,24},{4,28},{8,16},{12,20},{16,8},{20,12},{24,0},{28,4},{1,25},{... | collective-permute-start | bytes 663560 | tf_op jit(solution)/shard_map/ppermute | solution.py:39
  39.4 39.9 %collective-permute-start.19 = (bf16[96,3840]{1,0:T(8,128)(2,1)S(1)}, bf16[96,3840]{1,0:T(8,128)(2,1)S(1)}, u32[]{:S(2)}, u32[]{:S(2)}) collective-permute-start(bf16[96,3840]{1,0:T(8,128)(2,1)S(1)} %pad_maximum_fusion.refs_0_), channel_id=1, source_target_pairs={{0,24},{4,28},{8,16},{12,20},{16,8},{20,12},{24,0},{28,4},{1,25},{... | collective-permute-start | bytes 2211848 | tf_op jit(solution)/shard_map/ppermute | solution.py:39
  41.0 38.7 %collective-permute-start.17 = (bf16[96,3840]{1,0:T(8,128)(2,1)S(1)}, bf16[96,3840]{1,0:T(8,128)(2,1)S(1)}, u32[]{:S(2)}, u32[]{:S(2)}) collective-permute-start(bf16[96,3840]{1,0:T(8,128)(2,1)S(1)} %pad_maximum_fusion.refs_0_), channel_id=1, source_target_pairs={{0,16},{4,20},{8,24},{12,28},{16,0},{20,4},{24,8},{28,12},{1,17},{... | collective-permute-start | bytes 2211848 | tf_op jit(solution)/shard_map/ppermute | solution.py:39
  44.2 35.7 %collective-permute-start.15 = (bf16[96,3840]{1,0:T(8,128)(2,1)S(1)}, bf16[96,3840]{1,0:T(8,128)(2,1)}, u32[]{:S(2)}, u32[]{:S(2)}) collective-permute-start(bf16[96,3840]{1,0:T(8,128)(2,1)S(1)} %pad_maximum_fusion.refs_0_), channel_id=1, source_target_pairs={{0,8},{4,12},{8,0},{12,4},{16,24},{20,28},{24,16},{28,20},{1,9},{5... | collective-permute-start | bytes 2211848 | tf_op jit(solution)/shard_map/ppermute | solution.py:39
  48.6 28.1 %all-to-all-start = ((bf16[8,2,576]{2,1,0:T(2,128)(2,1)}), bf16[8,2,576]{2,1,0:T(2,128)(2,1)S(1)}, u32[]{:S(2)}, u32[]{:S(2)}) async-start(bf16[8,2,576]{2,1,0:T(2,128)(2,1)} %reshape.395), calls=%async_computation | async-start | bytes 40960 | tf_op jit(solution)/shard_map/all_to_all | solution.py:660
  52.0 25.2 %collective-permute-start.1 = (bf16[272,768]{1,0:T(8,128)(2,1)S(1)}, bf16[272,768]{1,0:T(8,128)(2,1)S(1)}, u32[]{:S(2)}, u32[]{:S(2)}) collective-permute-start(bf16[272,768]{1,0:T(8,128)(2,1)S(1)} %fusion.1), channel_id=1, source_target_pairs={{1,2},{2,1},{5,6},{6,5},{9,10},{10,9},{13,14},{14,13},{17,18},{18,... | collective-permute-start | bytes 1253384 | tf_op jit(solution)/shard_map/ppermute | solution.py:641
  52.9 24.3 %collective-permute-start = (bf16[272,768]{1,0:T(8,128)(2,1)S(1)}, bf16[272,768]{1,0:T(8,128)(2,1)}, u32[]{:S(2)}, u32[]{:S(2)}) collective-permute-start(bf16[272,768]{1,0:T(8,128)(2,1)S(1)} %fusion.1), channel_id=1, source_target_pairs={{0,1},{1,0},{2,3},{3,2},{4,5},{5,4},{6,7},{7,6},{8,9},{9,8},{10,11... | collective-permute-start | bytes 1253384 | tf_op jit(solution)/shard_map/ppermute | solution.py:39
  78.6 27.5 %collective-permute-start.14 = (bf16[96,3840]{1,0:T(8,128)(2,1)S(1)}, bf16[96,3840]{1,0:T(8,128)(2,1)S(1)}, u32[]{:S(2)}, u32[]{:S(2)}) collective-permute-start(bf16[96,3840]{1,0:T(8,128)(2,1)S(1)} %pad_maximum_fusion.refs_0_), channel_id=1, source_target_pairs={{0,4},{4,0},{8,12},{12,8},{16,20},{20,16},{24,28},{28,24},{1,5},{5... | collective-permute-start | bytes 2211848 | tf_op jit(solution)/shard_map/ppermute | solution.py:39
  79.4 26.8 %collective-permute-start.20 = (bf16[96,3840]{1,0:T(8,128)(2,1)S(1)}, bf16[96,3840]{1,0:T(8,128)(2,1)}, u32[]{:S(2)}, u32[]{:S(2)}) collective-permute-start(bf16[96,3840]{1,0:T(8,128)(2,1)S(1)} %collective-permute-done.19.refs_6_), channel_id=1, source_target_pairs={{0,4},{4,0},{8,12},{12,8},{16,20},{20,16},{24,28},{28,24},{1,5},{5... | collective-permute-start | bytes 2211848 | tf_op jit(solution)/shard_map/ppermute | solution.py:39
  79.7 26.5 %collective-permute-start.18 = (bf16[96,3840]{1,0:T(8,128)(2,1)S(1)}, bf16[96,3840]{1,0:T(8,128)(2,1)}, u32[]{:S(2)}, u32[]{:S(2)}) collective-permute-start(bf16[96,3840]{1,0:T(8,128)(2,1)S(1)} %collective-permute-done.17.refs_4_), channel_id=1, source_target_pairs={{0,4},{4,0},{8,12},{12,8},{16,20},{20,16},{24,28},{28,24},{1,5},{5... | collective-permute-start | bytes 2211848 | tf_op jit(solution)/shard_map/ppermute | solution.py:39
  79.9 26.3 %collective-permute-start.16 = (bf16[96,3840]{1,0:T(8,128)(2,1)}, bf16[96,3840]{1,0:T(8,128)(2,1)}, u32[]{:S(2)}, u32[]{:S(2)}) collective-permute-start(bf16[96,3840]{1,0:T(8,128)(2,1)} %collective-permute-done.15.refs_2_), channel_id=1, source_target_pairs={{0,4},{4,0},{8,12},{12,8},{16,20},{20,16},{24,28},{28,24},{1,5},{5... | collective-permute-start | bytes 2211848 | tf_op jit(solution)/shard_map/ppermute | solution.py:39
  118.2 27.5 %collective-permute-start.21 = (bf16[512,768]{1,0:T(8,128)(2,1)}, bf16[512,768]{1,0:T(8,128)(2,1)S(1)}, u32[]{:S(2)}, u32[]{:S(2)}) collective-permute-start(bf16[512,768]{1,0:T(8,128)(2,1)} %get-tuple-element.69.part_ref), channel_id=1, source_target_pairs={{0,1},{1,0},{2,3},{3,2},{4,5},{5,4},{6,7},{7,6},{8,9},{9,8},{10,11... | collective-permute-start | bytes 2359304 | tf_op jit(solution)/shard_map/ppermute | solution.py:39
  118.6 27.1 %collective-permute-start.22 = (bf16[256,768]{1,0:T(8,128)(2,1)S(1)}, bf16[256,768]{1,0:T(8,128)(2,1)S(1)}, u32[]{:S(2)}, u32[]{:S(2)}) collective-permute-start(bf16[256,768]{1,0:T(8,128)(2,1)S(1)} %bitcast.63), channel_id=1, source_target_pairs={{0,1},{1,0},{2,3},{3,2},{4,5},{5,4},{6,7},{7,6},{8,9},{9,8},{10,11... | collective-permute-start | bytes 1179656 | tf_op jit(solution)/shard_map/ppermute | solution.py:39
  156.6 18.1 %collective-permute-start.23 = (bf16[512,768]{1,0:T(8,128)(2,1)}, bf16[512,768]{1,0:T(8,128)(2,1)S(1)}, u32[]{:S(2)}, u32[]{:S(2)}) collective-permute-start(bf16[512,768]{1,0:T(8,128)(2,1)} %get-tuple-element.75.part_ref), channel_id=1, source_target_pairs={{0,1},{1,0},{2,3},{3,2},{4,5},{5,4},{6,7},{7,6},{8,9},{9,8},{10,11... | collective-permute-start | bytes 2359304 | tf_op jit(solution)/shard_map/ppermute | solution.py:39
  166.9 88.2 %collective-permute-start.36 = (bf16[4,96,3072]{2,1,0:T(8,128)(2,1)}, bf16[4,96,3072]{2,1,0:T(8,128)(2,1)S(1)}, u32[]{:S(2)}, u32[]{:S(2)}) collective-permute-start(bf16[4,96,3072]{2,1,0:T(8,128)(2,1)} %get-tuple-element.112), channel_id=1, source_target_pairs={{0,4},{4,0},{8,12},{12,8},{16,20},{20,16},{24,28},{28,24},{1,5},{5... | collective-permute-start | bytes 7077896 | tf_op jit(solution)/shard_map/ppermute | solution.py:39
  191.7 41.2 %collective-permute-start.31 = (bf16[4,96,768]{2,1,0:T(8,128)(2,1)}, bf16[4,96,768]{2,1,0:T(8,128)(2,1)}, u32[]{:S(2)}, u32[]{:S(2)}) collective-permute-start(bf16[4,96,768]{2,1,0:T(8,128)(2,1)} %get-tuple-element.98), channel_id=1, source_target_pairs={{0,4},{4,0},{8,12},{12,8},{16,20},{20,16},{24,28},{28,24},{1,5},{5... | collective-permute-start | bytes 1769480 | tf_op jit(solution)/shard_map/ppermute | solution.py:39
  224.6 21.2 %collective-permute-start.26 = (bf16[4,96,1152]{2,1,0:T(8,128)(2,1)}, bf16[4,96,1152]{2,1,0:T(8,128)(2,1)}, u32[]{:S(2)}, u32[]{:S(2)}) collective-permute-start(bf16[4,96,1152]{2,1,0:T(8,128)(2,1)} %get-tuple-element.91), channel_id=1, source_target_pairs={{0,4},{4,0},{8,12},{12,8},{16,20},{20,16},{24,28},{28,24},{1,5},{5... | collective-permute-start | bytes 2654216 | tf_op jit(solution)/shard_map/ppermute | solution.py:39
  262.0 17.4 %collective-permute-start.37 = (bf16[96,3072]{1,0:T(8,128)(2,1)}, bf16[96,3072]{1,0:T(8,128)(2,1)S(1)}, u32[]{:S(2)}, u32[]{:S(2)}) collective-permute-start(bf16[96,3072]{1,0:T(8,128)(2,1)} %get-tuple-element.114), channel_id=1, source_target_pairs={{0,24},{4,28},{8,16},{12,20},{16,8},{20,12},{24,0},{28,4},{1,25},{... | collective-permute-start | bytes 1769480 | tf_op jit(solution)/shard_map/ppermute | solution.py:39
  263.2 26.8 %collective-permute-start.38 = (bf16[96,3072]{1,0:T(8,128)(2,1)}, bf16[96,3072]{1,0:T(8,128)(2,1)}, u32[]{:S(2)}, u32[]{:S(2)}) collective-permute-start(bf16[96,3072]{1,0:T(8,128)(2,1)} %get-tuple-element.115), channel_id=1, source_target_pairs={{0,16},{4,20},{8,24},{12,28},{16,0},{20,4},{24,8},{28,12},{1,17},{... | collective-permute-start | bytes 1769480 | tf_op jit(solution)/shard_map/ppermute | solution.py:39
  264.3 25.7 %collective-permute-start.39 = (bf16[96,3072]{1,0:T(8,128)(2,1)}, bf16[96,3072]{1,0:T(8,128)(2,1)}, u32[]{:S(2)}, u32[]{:S(2)}) collective-permute-start(bf16[96,3072]{1,0:T(8,128)(2,1)} %get-tuple-element.116), channel_id=1, source_target_pairs={{0,8},{4,12},{8,0},{12,4},{16,24},{20,28},{24,16},{28,20},{1,9},{5... | collective-permute-start | bytes 1769480 | tf_op jit(solution)/shard_map/ppermute | solution.py:39
  267.9 24.6 %collective-permute-start.30 = (bf16[96,3,192]{2,0,1:T(8,128)(2,1)S(1)}, bf16[96,3,192]{2,0,1:T(8,128)(2,1)S(1)}, u32[]{:S(2)}, u32[]{:S(2)}) collective-permute-start(bf16[96,3,192]{2,0,1:T(8,128)(2,1)S(1)} %slice.232), channel_id=1, source_target_pairs={{0,2},{1,3},{2,0},{3,1},{4,6},{5,7},{6,4},{7,5},{8,10},{9,11},{10,... | collective-permute-start | bytes 331784 | tf_op jit(solution)/shard_map/ppermute | solution.py:39
  (55 other events, 621.8 us)

commit v2 on v1

v2 whole, which is shorter than its diff:
```python
import jax
import jax.numpy as jnp
from jax import lax
from jax.experimental import pallas as pl
from jax.experimental.pallas import tpu as pltpu
from jax.sharding import PartitionSpec as P

D = 768
HEADS = 12
HEAD_DIM = 64
FF = 3072
EPS = 1e-05
MASKED = 1e30
PAIR = 2 * HEAD_DIM
QUARTER = D // 4
HALF = D // 2
HID = FF // 4
VECS = 8
GROUPS = 8
BLOCK = D // GROUPS
LABELS = 16
BF = jnp.bfloat16
F32 = jnp.float32
ROOT_HALF = 0.7071067811865476
ROOT_TWO_PI = 0.3989422804014327


def dot(a, b):
    return lax.dot_general(a, b, (((1,), (0,)), ((), ())), preferred_element_type=F32)


def dot_nt(a, b):
    return lax.dot_general(a, b, (((1,), (1,)), ((), ())), preferred_element_type=F32)


def dot_tn(a, b):
    return lax.dot_general(a, b, (((0,), (0,)), ((), ())), preferred_element_type=F32)


def swap(value, axis, mask):
    count = lax.axis_size(axis)
    return lax.ppermute(value, axis, [(k, k ^ mask) for k in range(count)])


def together(*values):
    return lax.optimization_barrier(values)


def whole(shape):
    return pl.BlockSpec(shape, lambda *_: (0,) * len(shape))


def params():
    return pltpu.CompilerParams(vmem_limit_bytes=22 * 1024 * 1024)


def call(name, body, scalars, operands, in_specs, outs, out_specs, grid, scratch=(), micros=1):
    spec = pltpu.PrefetchScalarGridSpec(
        num_scalar_prefetch=1,
        grid=grid,
        in_specs=in_specs,
        out_specs=out_specs,
        scratch_shapes=list(scratch),
    )
    return pl.pallas_call(
        body,
        out_shape=outs,
        grid_spec=spec,
        compiler_params=params(),
        cost_estimate=pl.CostEstimate(
            flops=int(micros * 1.0e7), transcendentals=0, bytes_accessed=1024
        ),
        name=name,
    )(scalars, *operands)


def struct(shape, dtype):
    return jax.ShapeDtypeStruct(shape, dtype)


def chip_pieces(piece):
    return [piece] + [swap(piece, "dp", j) for j in range(2, GROUPS, 2)]


def core_pieces(chip):
    pieces = []
    for piece in chip:
        pieces += [piece, swap(piece, "dp", 1)]
    return pieces


def gather_rows(piece):
    full = lax.all_gather(piece, "dp", axis=0, tiled=True)
    return list(full.reshape(GROUPS, D // GROUPS, piece.shape[1]))


def place(target, refs, base, source_cols, target_cols):
    for j, ref in enumerate(refs):
        start = pl.multiple_of((base ^ j) * BLOCK, 16)
        target[pl.ds(start, BLOCK), target_cols] = ref[:BLOCK, source_cols]


def split_rows(result, base, keep, send):
    for j in range(GROUPS):
        block = result[pl.ds(pl.multiple_of((base ^ j) * BLOCK, 16), BLOCK), :].astype(BF)
        if j % 2:
            send[j // 2] = block
        else:
            keep[j // 2] = block


def simple(name, body, scalars, operands, outs, micros=1):
    return call(
        name,
        body,
        scalars,
        operands,
        [whole(o.shape) for o in operands],
        outs,
        [whole(o.shape) for o in outs],
        (1,),
        micros=micros,
    )


def label_rows(scalars, tokens, segments):
    rows = tokens.shape[0]

    def body(_, token_ref, segment_ref, out_ref, docs_ref):
        docs = segment_ref[...].astype(F32)
        docs_ref[...] = docs
        out_ref[:rows, :] = token_ref[...]
        out_ref[rows:, :] = jnp.zeros((LABELS, D), BF)
        out_ref[rows:, :rows] = jnp.broadcast_to(docs, (LABELS, rows)).astype(BF)

    outs = [struct((rows + LABELS, D), BF), struct((1, rows), F32)]
    return simple("label_rows", body, scalars, [tokens, segments], outs)


def pack_narrow(scalars, tables):
    rows = tables[0].shape[0]

    def body(_, *refs):
        joined = jnp.concatenate([ref[...].astype(F32) for ref in refs[:-1]], axis=1)
        refs[-1][...] = joined.astype(BF)

    return simple("pack_narrow", body, scalars, tables, [struct((rows, 3 * QUARTER), BF)])[0]


def pack_wide(scalars, up, down, output, output_side):
    rows = up.shape[0]

    def body(_, up_ref, down_ref, out_ref, side_ref, wide_ref):
        wide_ref[:, :HID] = up_ref[...]
        wide_ref[:, HID : 2 * HID] = down_ref[...]
        sides = [out_ref[...].astype(F32), side_ref[...].astype(F32)]
        wide_ref[:, 2 * HID :] = jnp.concatenate(sides, axis=1).astype(BF)

    out = struct((rows, 2 * HID + HALF), BF)
    return simple("pack_wide", body, scalars, [up, down, output, output_side], [out])[0]


def pack_columns(scalars, narrow, narrow_far, lines, tall):
    rows = narrow.shape[0]

    def body(_, near_ref, far_ref, *refs):
        out_ref = refs[-1]
        for kind in range(3):
            part = slice(kind * QUARTER, (kind + 1) * QUARTER)
            both = [near_ref[:, part].astype(F32), far_ref[:, part].astype(F32)]
            both = jnp.concatenate(both, axis=1).astype(BF)
            for p in range(3):
                at = (3 * p + kind) * PAIR
                out_ref[:rows, at : at + PAIR] = both[:, p * PAIR : (p + 1) * PAIR]
        if lines:
            table = jnp.concatenate(
                [ref[...].astype(F32) for ref in refs[:VECS]] + [jnp.zeros((LABELS - VECS, BLOCK), F32)],
                axis=0,
            )
            out_ref[rows:, :] = jnp.zeros((LABELS, 3 * HALF), BF)
            out_ref[rows:, :BLOCK] = table.astype(BF)
            line = jnp.broadcast_to(refs[VECS][...].astype(F32), (LABELS, FF // GROUPS))
            out_ref[rows:, D:] = line.astype(BF)

    out = struct((rows + (LABELS if lines else 0), 3 * HALF), BF)
    operands = [narrow, narrow_far] + (lines + [tall] if lines else [])
    return simple("pack_columns", body, scalars, operands, [out])[0]


def pack_feed(scalars, wide, wide_far):
    rows = wide.shape[0]

    def body(sc, wide_ref, far_ref, out_ref):
        out_ref[:, : 2 * HID] = wide_ref[:, : 2 * HID]
        out_ref[:, 2 * HID : 4 * HID] = far_ref[:, : 2 * HID]
        total = jnp.zeros((rows, D), F32)
        for k in range(4):
            ref = (wide_ref, far_ref)[k // 2]
            at = 2 * HID + (k % 2) * QUARTER
            part = ref[:, at : at + QUARTER].astype(F32)
            part = jnp.concatenate([part, jnp.zeros((rows, D - QUARTER), F32)], axis=1)
            total = total + pltpu.roll(part, (sc[2] ^ k) * QUARTER, 1)
        out_ref[:, 4 * HID :] = total.astype(BF)

    out = struct((rows, 4 * HID + D), BF)
    return simple("pack_feed", body, scalars, [wide, wide_far], [out])[0]


def qkv_attend(scalars, own, partner, halo_near, halo_far, own_docs, pieces, rows):
    count = len(pieces)
    base = 3 * rows

    def body(sc, own_ref, partner_ref, near_ref, far_ref, docs_ref, *refs):
        weight_refs, refs = refs[:count], refs[count:]
        q_ref, k_ref, v_ref, ctx_far_ref, ctx_near_ref, x_ref, w_ref, hot_ref, vec_ref, hidden_ref, mask_ref, bias_ref = refs
        step = pl.program_id(0)

        @pl.when(step == 0)
        def _():
            near = sc[0]
            own_at = pl.multiple_of(near * rows, rows)
            partner_at = pl.multiple_of((1 - near) * rows, rows)
            number = lax.broadcasted_iota(jnp.int32, (16, rows), 0).astype(F32)

            def mark(line, at):
                hit = jnp.broadcast_to(line, (16, rows)) == number
                hot_ref[:, pl.ds(at, rows)] = jnp.where(hit, 1.0, 0.0).astype(BF)

            x_ref[pl.ds(own_at, rows), :] = own_ref[...]
            x_ref[pl.ds(partner_at, rows), :] = partner_ref[:rows, :]
            mark(docs_ref[...], own_at)
            mark(partner_ref[rows : rows + 1, :rows].astype(F32), partner_at)

            def halo(ref):
                x_ref[2 * rows :, :] = ref[:rows, :]
                mark(ref[rows : rows + 1, :rows].astype(F32), 2 * rows)

            pl.when(near == 1)(lambda: halo(near_ref))
            pl.when(near == 0)(lambda: halo(far_ref))
            place(w_ref, weight_refs, sc[1], slice(None), slice(None))
            hot = hot_ref[...]
            mask_ref[...] = (dot_tn(hot[:, : 2 * rows], hot) - 1.0) * MASKED
            vectors = jnp.zeros((LABELS, D), F32)
            for j, ref in enumerate(weight_refs):
                block = sc[1] ^ j
                vectors = vectors + pltpu.roll(ref[BLOCK:, :D].astype(F32), block * BLOCK, 1)
                quarter = block // 2
                for k in range(2):

                    @pl.when(quarter == sc[2] ^ (2 * k))
                    def _():
                        to = pl.multiple_of((block % 2) * (HID // 2) + k * HID, 128)
                        hidden_ref[:, pl.ds(to, HID // 2)] = ref[BLOCK:, D:].astype(F32)

            vec_ref[...] = vectors[:VECS]
            lanes = lax.broadcasted_iota(jnp.int32, (VECS, HALF), 1)
            low = pltpu.roll(vectors[:VECS], D - sc[2] * QUARTER, 1)[:, :HALF]
            high = pltpu.roll(vectors[:VECS], D + QUARTER - (sc[2] ^ 2) * QUARTER, 1)[:, :HALF]
            bias_ref[...] = jnp.where(lanes < QUARTER, low, high)

        at = pl.multiple_of(step * 3 * PAIR, PAIR)
        both = dot(x_ref[...], w_ref[:, pl.ds(at, 3 * PAIR)])
        bias = bias_ref[:, pl.ds(pl.multiple_of(step * PAIR, PAIR), PAIR)]
        query = (both[:, :PAIR] + bias[0:1]).astype(BF)
        key = both[:, PAIR : 2 * PAIR].astype(BF)
        value = (both[:, 2 * PAIR :] + bias[1:2]).astype(BF)
        q_ref[...] = query
        k_ref[...] = key
        v_ref[...] = value
        lane = lax.broadcasted_iota(jnp.int32, (1, PAIR), 1)
        for ctx_ref, start, reach in ((ctx_far_ref, 0, 2 * rows), (ctx_near_ref, rows, 3 * rows)):
            total = jnp.zeros((rows, PAIR), F32)
            for head in range(2):
                part = jnp.where((lane // HEAD_DIM) == head, 1.0, 0.0)
                mine = (query[start : start + rows].astype(F32) * (part * HEAD_DIM**-0.5)).astype(BF)
                scores = dot_nt(mine, key[:reach]) + mask_ref[start : start + rows, :reach]
                expo = jnp.exp(scores - jnp.max(scores, axis=-1, keepdims=True))
                probs = expo * (1.0 / jnp.sum(expo, axis=-1, keepdims=True))
                total = total + dot(probs.astype(BF), value[:reach]) * part
            ctx_ref[...] = total.astype(BF)

    column = lambda height: pl.BlockSpec((height, PAIR), lambda p, _: (0, p))
    operands = [own, partner, halo_near, halo_far, own_docs] + pieces
    in_specs = [whole(o.shape) for o in operands]
    outs = [
        struct((base, HALF), BF),
        struct((base, HALF), BF),
        struct((base, HALF), BF),
        struct((rows, HALF), BF),
        struct((rows, HALF), BF),
        struct((base, D), BF),
        struct((D, 3 * HALF), BF),
        struct((16, base), BF),
        struct((VECS, D), F32),
        struct((LABELS, 2 * HID), F32),
    ]
    out_specs = [column(base)] * 3 + [column(rows)] * 2 + [whole(o.shape) for o in outs[5:]]
    return call(
        "qkv_attend",
        body,
        scalars,
        operands,
        in_specs,
        outs,
        out_specs,
        (HALF // PAIR,),
        [pltpu.VMEM((2 * rows, base), F32), pltpu.VMEM((VECS, HALF), F32)],
        micros=13,
    )


def feed_forward(scalars, block, ctx_mine, ctx_partner, x, vecs, up_bias, weights, rows):
    count = len(weights)
    fresh = count == GROUPS

    def body(sc, mine_ref, partner_ref, x_ref, vec_ref, bias_ref, *refs):
        weight_refs, refs = refs[:count], refs[count:]
        (norm_ref, inv_ref, first_ref, gate_ref, active_ref, part_ref), refs = refs[:6], refs[6:]
        if fresh:
            up_ref, down_ref, out_ref, other_ref, full_ref = refs
            place(up_ref, weight_refs, sc[1], slice(0, HID), slice(0, HID))
            place(down_ref, weight_refs, sc[1], slice(HID, 2 * HID), slice(0, HID))
            place(up_ref, weight_refs, sc[1], slice(2 * HID, 3 * HID), slice(HID, 2 * HID))
            place(down_ref, weight_refs, sc[1], slice(3 * HID, 4 * HID), slice(HID, 2 * HID))
            place(full_ref, weight_refs, sc[1], slice(4 * HID, 4 * HID + D), slice(None))
            for ref, flip in ((out_ref, 0), (other_ref, 1)):
                for k in range(2):
                    at = pl.multiple_of((sc[2] ^ flip ^ (2 * k)) * QUARTER, 16)
                    ref[k * QUARTER : (k + 1) * QUARTER, :] = full_ref[pl.ds(at, QUARTER), :]
        else:
            up_ref, down_ref, out_ref, other_ref = weight_refs

        attention = dot(mine_ref[...], out_ref[...]) + dot(partner_ref[...], other_ref[...])
        total = x_ref[...].astype(F32) + (attention + vec_ref[2:3, :])
        center = total - jnp.mean(total, axis=-1, keepdims=True)
        inverse = lax.rsqrt(jnp.mean(center * center, axis=-1, keepdims=True) + EPS)
        normed = center * inverse
        norm_ref[...] = normed
        inv_ref[...] = jnp.broadcast_to(inverse, (rows, 128))
        first = (normed * vec_ref[3:4, :] + vec_ref[4:5, :]).astype(BF)
        first_ref[...] = first
        gate = dot(first, up_ref[...]) + bias_ref[0:1, :]
        gate_ref[...] = gate
        active = (gate * (1.0 + lax.erf(gate * ROOT_HALF)) * 0.5).astype(BF)
        active_ref[...] = active
        part_ref[...] = dot_nt(active, down_ref[...]).astype(BF)

    operands = [ctx_mine, ctx_partner, x, vecs, up_bias, *weights]
    in_specs = [whole(o.shape) for o in operands]
    in_specs[2] = pl.BlockSpec((rows, D), lambda *_: (block, 0))
    outs = [
        struct((rows, D), F32),
        struct((rows, 128), F32),
        struct((rows, D), BF),
        struct((rows, 2 * HID), F32),
        struct((rows, 2 * HID), BF),
        struct((rows, D), BF),
    ]
    scratch = []
    if fresh:
        outs += [struct((D, 2 * HID), BF)] * 2 + [struct((HALF, D), BF)] * 2
        scratch = [pltpu.VMEM((D, D), BF)]
    results = call(
        "feed_forward",
        body,
        scalars,
        operands,
        in_specs,
        outs,
        [whole(o.shape) for o in outs],
        (1,),
        scratch,
        micros=6,
    )
    return results[:6], (results[6:] if fresh else weights)


def gelu_slope(scalars, gate):
    rows = gate.shape[0] // 2

    def body(_, gate_ref, slope_ref):
        gate_here = gate_ref[...]
        bell = jnp.exp(gate_here * gate_here * -0.5) * ROOT_TWO_PI
        slope_ref[...] = 0.5 * (1.0 + lax.erf(gate_here * ROOT_HALF)) + gate_here * bell

    spec = pl.BlockSpec((rows, gate.shape[1]), lambda r, _: (r, 0))
    return call(
        "gelu_slope", body, scalars, [gate], [spec], [struct(gate.shape, F32)], [spec], (2,), micros=3
    )[0]


def second_norm(scalars, block, part, received, normed, slope, cotangent, vecs, up, down, earlier, rows):
    def body(sc, part_ref, recv_ref, norm_ref, slope_ref, cot_ref, other_ref, vec_ref, up_ref, down_ref, *refs):
        old, refs = refs[: len(earlier)], refs[len(earlier) :]
        (total_grad_ref, branch_grad_ref, gate_grad_ref, first_part_ref, out_ref, sums_ref, bias_ref) = refs
        mine = sc[0] == block
        first = norm_ref[...] * vec_ref[3:4, :] + vec_ref[4:5, :]
        branch = part_ref[...].astype(F32) + recv_ref[...].astype(F32) + vec_ref[5:6, :]
        total = first + branch
        center = total - jnp.mean(total, axis=-1, keepdims=True)
        inverse = lax.rsqrt(jnp.mean(center * center, axis=-1, keepdims=True) + EPS)
        here = center * inverse
        upstream = jnp.where(mine, cot_ref[...].astype(F32), other_ref[...].astype(F32))
        scaled = upstream * vec_ref[6:7, :]
        inner = (
            scaled
            - jnp.mean(scaled, axis=-1, keepdims=True)
            - here * jnp.mean(scaled * here, axis=-1, keepdims=True)
        )
        total_grad = inner * inverse
        total_grad_ref[...] = total_grad
        branch_grad = total_grad.astype(BF)
        branch_grad_ref[...] = branch_grad
        gate_grad = (dot(branch_grad, down_ref[...]) * slope_ref[...]).astype(BF)
        gate_grad_ref[...] = gate_grad
        hidden = jnp.broadcast_to(jnp.sum(gate_grad.astype(F32), axis=0, keepdims=True), (8, 2 * HID))
        bias_ref[...] = hidden + old[2][...] if old else hidden
        first_part_ref[...] = dot_nt(gate_grad, up_ref[...]).astype(BF)

        @pl.when(mine)
        def _():
            out_ref[...] = (here * vec_ref[6:7, :] + vec_ref[7:8, :]).astype(BF)
            sums_ref[...] = jnp.zeros_like(sums_ref)
            sums_ref[0:1, :] = jnp.sum(upstream * here, axis=0, keepdims=True)
            sums_ref[1:2, :] = jnp.sum(upstream, axis=0, keepdims=True)
            sums_ref[2:3, :] = jnp.sum(branch_grad.astype(F32), axis=0, keepdims=True)

        if old:

            @pl.when(jnp.logical_not(mine))
            def _():
                out_ref[...] = old[0][...]
                sums_ref[...] = old[1][...]

        else:

            @pl.when(jnp.logical_not(mine))
            def _():
                out_ref[...] = jnp.zeros_like(out_ref)
                sums_ref[...] = jnp.zeros_like(sums_ref)

    operands = [part, received, normed, slope, *cotangent, vecs, up, down, *earlier]
    outs = [
        struct((rows, D), F32),
        struct((rows, D), BF),
        struct((rows, 2 * HID), BF),
        struct((rows, D), BF),
        struct((rows, D), BF),
        struct((8, D), F32),
        struct((8, 2 * HID), F32),
    ]
    results = call(
        "second_norm",
        body,
        scalars,
        operands,
        [whole(o.shape) for o in operands],
        outs,
        [whole(o.shape) for o in outs],
        (1,),
        micros=5,
    )
    return results[:4], results[4:]


def split_outs(width):
    return [struct((GROUPS // 2, BLOCK, width), BF)] * 2


def feed_forward_grads(scalars, blocks, rows):
    def body(sc, *refs):
        keep_ref, send_ref, result_ref = refs[-3:]
        step = pl.program_id(0)

        @pl.when(step % 2 == 0)
        def _():
            result_ref[...] = dot_tn(refs[0][...], refs[1][...]) + dot_tn(refs[4][...], refs[5][...])

        @pl.when(step % 2 == 1)
        def _():
            result_ref[...] = dot_tn(refs[2][...], refs[3][...]) + dot_tn(refs[6][...], refs[7][...])

        split_rows(result_ref, sc[1], keep_ref, send_ref)

    half = pl.BlockSpec((rows, HID), lambda c, _: (0, c // 2))
    outs = split_outs(4 * HID)
    out_specs = [pl.BlockSpec((GROUPS // 2, BLOCK, HID), lambda c, _: (0, 0, c))] * 2
    return call(
        "feed_forward_grads",
        body,
        scalars,
        [value for block in blocks for value in block],
        [whole((rows, D)), half] * 4,
        outs,
        out_specs,
        (4,),
        [pltpu.VMEM((D, HID), F32)],
        micros=8,
    )


def first_norm(scalars, block, part, received, total_grad, normed, inverse, vecs, out_weight, earlier, rows):
    def body(sc, part_ref, recv_ref, grad_ref, norm_ref, inv_ref, vec_ref, weight_ref, *refs):
        old, refs = refs[: len(earlier)], refs[len(earlier) :]
        attention_ref, context_ref, own_ref, sums_ref = refs[:4]
        mine = sc[0] == block
        upstream = grad_ref[...] + part_ref[...].astype(F32) + recv_ref[...].astype(F32)
        here = norm_ref[...]
        scaled = upstream * vec_ref[3:4, :]
        inner = (
            scaled
            - jnp.mean(scaled, axis=-1, keepdims=True)
            - here * jnp.mean(scaled * here, axis=-1, keepdims=True)
        )
        total = inner * inv_ref[:, :1]
        attention = total.astype(BF)
        attention_ref[...] = attention
        context_ref[...] = dot_nt(attention, weight_ref[...]).astype(BF)
        if block == 1:
            turned = jnp.concatenate([weight_ref[QUARTER:, :], weight_ref[:QUARTER, :]], axis=0)
            refs[4][...] = dot_nt(attention, turned).astype(BF)

        @pl.when(mine)
        def _():
            own_ref[...] = total
            sums_ref[...] = jnp.zeros_like(sums_ref)
            sums_ref[0:1, :] = jnp.sum(upstream * here, axis=0, keepdims=True)
            sums_ref[1:2, :] = jnp.sum(upstream, axis=0, keepdims=True)
            sums_ref[2:3, :] = jnp.sum(attention.astype(F32), axis=0, keepdims=True)

        @pl.when(jnp.logical_not(mine))
        def _():
            own_ref[...] = old[0][...] if old else jnp.zeros_like(own_ref)
            sums_ref[...] = old[1][...] if old else jnp.zeros_like(sums_ref)

    operands = [part, received, total_grad, normed, inverse, vecs, out_weight, *earlier]
    outs = [
        struct((rows, D), BF),
        struct((rows, HALF), BF),
        struct((rows, D), F32),
        struct((8, D), F32),
        struct((rows, HALF), BF),
    ][: 5 if block == 1 else 4]
    return call(
        "first_norm",
        body,
        scalars,
        operands,
        [whole(o.shape) for o in operands],
        outs,
        [whole(o.shape) for o in outs],
        (1,),
        micros=3,
    )


def halves(value):
    high = value.astype(BF).astype(F32)
    return jnp.concatenate([high, value - high], axis=1).astype(BF)


def whole_of(table):
    return table[:, :128].astype(F32) + table[:, 128:].astype(F32)


def output_grads(scalars, blocks, small, small_side):
    def body(sc, *refs):
        small_ref, side_ref, keep_ref, send_ref, result_ref = refs[-5:]
        for side in range(2):
            part = dot_tn(refs[side][...], refs[2][...]) + dot_tn(refs[3 + side][...], refs[5][...])
            for k in range(2):
                at = pl.multiple_of((sc[2] ^ side ^ (2 * k)) * QUARTER, 16)
                result_ref[pl.ds(at, QUARTER), :] = part[k * QUARTER : (k + 1) * QUARTER, :]
        for j in range(GROUPS):
            target = (keep_ref, send_ref)[j % 2]
            block = sc[1] ^ j
            rows = pl.ds(pl.multiple_of(block * BLOCK, 16), BLOCK)
            target[j // 2, :BLOCK] = result_ref[rows, :].astype(BF)
            target[j // 2, BLOCK:] = jnp.zeros((LABELS, D), BF)
            target[j // 2, BLOCK:, :256] = halves(small_ref[block] + side_ref[block])

    outs = [struct((GROUPS // 2, BLOCK + LABELS, D), BF)] * 2
    operands = [value for block in blocks for value in block] + [small, small_side]
    return call(
        "output_grads",
        body,
        scalars,
        operands,
        [whole(o.shape) for o in operands],
        outs,
        [whole(o.shape) for o in outs],
        (1,),
        [pltpu.VMEM((D, D), F32)],
        micros=4,
    )


def attend_backward(scalars, query, key, value, grad_blocks, hot, weight, rows):
    base = 3 * rows
    steps = HALF // PAIR

    def body(sc, q_ref, k_ref, v_ref, far_ref, near_ref, halo_ref, hot_ref, w_ref, *refs):
        out_ref, keep_ref, send_ref, sums_ref, mask_ref, key_ref, value_ref, acc_ref = refs
        step = pl.program_id(0)

        @pl.when(step == 0)
        def _():
            mask_ref[...] = (dot_tn(hot_ref[...], hot_ref[...]) - 1.0) * MASKED

        key_ref[...] = jnp.zeros_like(key_ref)
        value_ref[...] = jnp.zeros_like(value_ref)
        lane = lax.broadcasted_iota(jnp.int32, (1, PAIR), 1)
        query_grads = [jnp.zeros((PAIR, rows), F32), jnp.zeros((PAIR, rows), F32)]
        for head in range(2):
            part = jnp.where((lane // HEAD_DIM) == head, 1.0, 0.0)
            key_turned = (k_ref[...].astype(F32) * part).T.astype(BF)
            for index, (low, high) in enumerate(((0, 2 * rows), (0, base), (rows, base))):
                start = index * rows
                mine = (q_ref[start : start + rows].astype(F32) * (part * HEAD_DIM**-0.5)).astype(BF)
                grads = (far_ref, near_ref, halo_ref)[index][...]
                grads = (grads.astype(F32) * part).astype(BF)
                scores = dot_nt(k_ref[low:high], mine) + mask_ref[low:high, start : start + rows]
                expo = jnp.exp(scores - jnp.max(scores, axis=0, keepdims=True))
                probs = expo * (1.0 / jnp.sum(expo, axis=0, keepdims=True))
                pulled = dot_nt(v_ref[low:high], grads)
                inner = jnp.sum(probs * pulled, axis=0, keepdims=True)
                score_grads = (probs * (pulled - inner)).astype(BF)
                top = min(high, 2 * rows)
                span = top - low
                value_ref[low:top, :] += dot(probs[:span].astype(BF), grads)
                key_ref[low:top, :] += dot(score_grads[:span], mine)
                if index < 2:
                    query_grads[index] = query_grads[index] + dot(key_turned[:, low:high], score_grads)
        for index in range(2):
            turned = (query_grads[index] * HEAD_DIM**-0.5).T.astype(BF)
            out_ref[index * rows : (index + 1) * rows, :PAIR] = turned
        out_ref[:, PAIR : 2 * PAIR] = key_ref[...].astype(BF)
        out_ref[:, 2 * PAIR :] = value_ref[...].astype(BF)
        sums = jnp.sum(out_ref[...].astype(F32), axis=0, keepdims=True)
        sums_ref[...] = jnp.broadcast_to(sums, (8, 3 * PAIR))
        product = dot_nt(out_ref[...], w_ref[...])

        @pl.when(step == 0)
        def _():
            acc_ref[...] = product

        @pl.when(step > 0)
        def _():
            acc_ref[...] += product

        @pl.when(step == steps - 1)
        def _():
            near = sc[0]
            keep_ref[...] = acc_ref[pl.ds(pl.multiple_of(near * rows, rows), rows), :]
            other = acc_ref[pl.ds(pl.multiple_of((1 - near) * rows, rows), rows), :]
            send_ref[...] = other.astype(BF)

    column = lambda height: pl.BlockSpec((height, PAIR), lambda p, _: (0, p))
    operands = [query, key, value, *grad_blocks, hot, weight]
    in_specs = [column(base)] * 3 + [column(rows)] * 3 + [whole(hot.shape)]
    in_specs += [pl.BlockSpec((D, 3 * PAIR), lambda p, _: (0, p))]
    outs = [struct((2 * rows, 3 * HALF), BF), struct((rows, D), F32), struct((rows, D), BF)]
    outs += [struct((8, 3 * HALF), F32)]
    out_specs = [
        pl.BlockSpec((2 * rows, 3 * PAIR), lambda p, _: (0, p)),
        whole((rows, D)),
        whole((rows, D)),
        pl.BlockSpec((8, 3 * PAIR), lambda p, _: (0, p)),
    ]
    scratch = [
        pltpu.VMEM((base, base), F32),
        pltpu.VMEM((2 * rows, PAIR), F32),
        pltpu.VMEM((2 * rows, PAIR), F32),
        pltpu.VMEM((2 * rows, D), F32),
    ]
    return call(
        "attend_backward",
        body,
        scalars,
        operands,
        in_specs,
        outs,
        out_specs,
        (steps,),
        scratch,
        micros=18,
    )


def projection_grads(scalars, x, grads, rows):
    tall = 2 * rows

    def body(sc, x_ref, grad_ref, *refs):
        result_ref = refs[-1]
        result_ref[...] = dot_tn(x_ref[...], grad_ref[...])
        split_rows(result_ref, sc[1], refs[0], refs[1])

    outs = split_outs(3 * HALF)
    out_specs = [pl.BlockSpec((GROUPS // 2, BLOCK, 3 * PAIR), lambda p, _: (0, 0, p))] * 2
    return call(
        "projection_grads",
        body,
        scalars,
        [x, grads],
        [pl.BlockSpec((tall, D), lambda p, _: (0, 0)), pl.BlockSpec((tall, 3 * PAIR), lambda p, _: (0, p))],
        outs,
        out_specs,
        (HALF // PAIR,),
        [pltpu.VMEM((D, 3 * PAIR), F32)],
        micros=5,
    )


def combine(scalars, keep, received):
    count, rows, width = keep.shape
    chunk = width // 3

    def body(_, keep_ref, recv_ref, *refs):
        for k in range(count):
            total = keep_ref[k].astype(F32) + recv_ref[k].astype(F32)
            refs[k][...] = total.astype(refs[k].dtype)

    block = pl.BlockSpec((count, rows, chunk), lambda c, _: (0, 0, c))
    outs = [struct((rows, width), F32)] + [struct((rows, width), BF)] * (count - 1)
    spec = pl.BlockSpec((rows, chunk), lambda c, _: (0, c))
    return list(call(
        "combine",
        body, scalars, [keep, received], [block, block], outs, [spec] * count, (3,)))


def combine_both(scalars, keep, received, out_keep, out_received):
    count, rows, wide = keep.shape
    tall = rows + LABELS

    def body(_, keep_ref, recv_ref, out_keep_ref, out_recv_ref, *refs):
        for k in range(count):
            kind = refs[k].dtype
            refs[k][:rows, :wide] = (keep_ref[k].astype(F32) + recv_ref[k].astype(F32)).astype(kind)
            refs[k][rows:, :wide] = jnp.zeros((LABELS, wide), kind)
            total = out_keep_ref[k, :rows].astype(F32) + out_recv_ref[k, :rows].astype(F32)
            refs[k][:rows, wide:] = total.astype(kind)
            refs[k][rows:, wide:] = jnp.zeros((LABELS, D), kind)
            small = whole_of(out_keep_ref[k, rows:, :256]) + whole_of(out_recv_ref[k, rows:, :256])
            refs[k][rows:, wide : wide + 256] = halves(small).astype(kind)

    outs = [struct((tall, wide + D), F32)] + [struct((tall, wide + D), BF)] * (count - 1)
    return simple("combine_both", body, scalars, [keep, received, out_keep, out_received], outs, 2)


def total_feed(scalars, sums):
    rows = sums[0].shape[0]

    def body(_, *refs):
        keep_ref, send_ref = refs[-2:]
        total = refs[0][...]
        for ref in refs[1:-2]:
            total = total + ref[...].astype(F32)
        keep_ref[...] = total[:, : 2 * HID]
        send_ref[...] = total[:, 2 * HID :].astype(BF)

    outs = [struct((rows, 2 * HID), F32), struct((rows, 2 * HID), BF)]
    return simple("total_feed", body, scalars, sums, outs, 2)


def total_projection(scalars, sums, rows):
    tall = sums[0].shape[0]
    wide = 3 * HALF

    def body(sc, *refs):
        keep_ref, send_ref = refs[-2:]
        total = refs[0][:rows, :]
        for ref in refs[1:-2]:
            total = total + ref[:rows, :].astype(F32)
        near, far = [], []
        for kind in range(3):
            both = [total[:, (3 * p + kind) * PAIR : (3 * p + kind + 1) * PAIR] for p in range(3)]
            both = jnp.concatenate(both, axis=1)
            near.append(both[:, :QUARTER])
            far.append(both[:, QUARTER:])
        near.append(pltpu.roll(total[:, wide:], D - sc[2] * QUARTER, 1)[:, :QUARTER])
        far.append(pltpu.roll(total[:, wide:], D - (sc[2] ^ 2) * QUARTER, 1)[:, :QUARTER])
        keep_ref[:rows, :] = jnp.concatenate(near, axis=1)
        send_ref[:rows, :] = jnp.concatenate(far, axis=1).astype(BF)
        if tall > rows:
            small = jnp.zeros((LABELS, 128), F32)
            for ref in refs[:-2]:
                small = small + whole_of(ref[rows:, wide : wide + 256])
            keep_ref[rows:, :] = jnp.zeros((LABELS, D), F32)
            send_ref[rows:, :] = jnp.zeros((LABELS, D), BF)
            keep_ref[rows:, :128] = small
            send_ref[rows:, :256] = halves(small)

    outs = [struct((tall, D), F32), struct((tall, D), BF)]
    return simple("total_projection", body, scalars, sums, outs, 2)


def finish_feed(scalars, keep, received):
    rows = keep.shape[0]

    def body(_, keep_ref, recv_ref, up_ref, down_ref):
        up_ref[...] = keep_ref[:, :HID] + recv_ref[:, :HID].astype(F32)
        down_ref[...] = keep_ref[:, HID:] + recv_ref[:, HID:].astype(F32)

    outs = [struct((rows, HID), F32)] * 2
    return simple("finish_feed", body, scalars, [keep, received], outs)


def finish_projection(scalars, keep, received, rows):
    tall = keep.shape[0]

    def body(_, keep_ref, recv_ref, *refs):
        total = keep_ref[:rows, :] + recv_ref[:rows, :].astype(F32)
        for k in range(4):
            refs[k][...] = total[:, k * QUARTER : (k + 1) * QUARTER]
        if tall > rows:
            refs[4][...] = keep_ref[rows:, :128] + whole_of(recv_ref[rows:, :256])

    outs = [struct((rows, QUARTER), F32)] * 4 + ([struct((LABELS, 128), F32)] if tall > rows else [])
    return simple("finish_projection", body, scalars, [keep, received], outs)


def small_sums(scalars, sums_one, sums_two, sums_hidden, sums_projection):
    def body(sc, one_ref, two_ref, hidden_ref, projection_ref, out_ref, wide_ref, tall_ref):
        out_ref[...] = jnp.zeros_like(out_ref)
        lanes = lax.broadcasted_iota(jnp.int32, (1, D), 1)
        near, far = lanes < QUARTER, (lanes >= QUARTER) & (lanes < HALF)
        for row, kind in ((0, 0), (1, 2)):
            line = jnp.concatenate(
                [
                    projection_ref[0:1, (3 * p + kind) * PAIR : (3 * p + kind + 1) * PAIR]
                    for p in range(3)
                ]
                + [jnp.zeros((1, HALF), F32)],
                axis=1,
            )
            low = pltpu.roll(jnp.broadcast_to(jnp.where(near, line, 0.0), (8, D)), sc[2] * QUARTER, 1)
            high = jnp.broadcast_to(jnp.where(far, line, 0.0), (8, D))
            high = pltpu.roll(high, D - QUARTER + (sc[2] ^ 2) * QUARTER, 1)
            wide_ref[row : row + 1, :] = (low + high)[0:1]
        wide_ref[2:3, :] = one_ref[2:3, :]
        wide_ref[3:5, :] = one_ref[0:2, :]
        wide_ref[5:6, :] = two_ref[2:3, :]
        wide_ref[6:8, :] = two_ref[0:2, :]
        tall_ref[...] = jnp.zeros_like(tall_ref)
        for k in range(2):
            to = pl.multiple_of((sc[2] ^ (2 * k)) * HID, 128)
            tall_ref[0:1, pl.ds(to, HID)] = hidden_ref[0:1, k * HID : (k + 1) * HID]
        share = FF // GROUPS
        for d in range(GROUPS):
            out_ref[d, :VECS, :BLOCK] = wide_ref[:, d * BLOCK : (d + 1) * BLOCK]
            for c in range(share // 128):
                at = d * share + c * 128
                out_ref[d, VECS + c : VECS + c + 1, :] = tall_ref[0:1, at : at + 128]

    operands = [sums_one, sums_two, sums_hidden, sums_projection]
    shape = (GROUPS, LABELS, 128)
    return call(
        "small_sums",
        body,
        scalars,
        operands,
        [whole(o.shape) for o in operands],
        [struct(shape, F32)],
        [whole(shape)],
        (1,),
        [pltpu.VMEM((VECS, D), F32), pltpu.VMEM((8, FF), F32)],
    )[0]


def per_device(
    tokens,
    segments,
    query_weight,
    key_weight,
    value_weight,
    output_weight,
    query_bias,
    value_bias,
    output_bias,
    first_gain,
    first_shift,
    up_weight,
    up_bias,
    down_weight,
    down_bias,
    second_gain,
    second_shift,
    cotangent,
):
    seq_count = lax.axis_size("seq")
    count = lax.axis_size("dp")
    place_z = lax.axis_index("seq")
    assert seq_count == 4
    direct = count == GROUPS
    rows = tokens.shape[1]
    piece_rows = query_weight.shape[0]
    near = (place_z == 1) | (place_z == 2)
    base = lax.axis_index("dp") if direct else 0
    scalars = jnp.stack([near, base, place_z]).astype(jnp.int32)

    narrow = pack_narrow(scalars, [query_weight, key_weight, value_weight])
    narrow_far = swap(narrow, "seq", 2)
    output_side = swap(output_weight, "seq", 1)
    own = tokens[0]
    labelled, own_docs = label_rows(scalars, own, segments)
    wide = pack_wide(scalars, up_weight, down_weight.T, output_weight, output_side)
    wide_far = swap(wide, "seq", 2)
    partner = swap(labelled, "seq", 1)
    narrow_far, labelled = together(narrow_far, labelled)
    halo_near = lax.ppermute(labelled, "seq", [(1, 2), (2, 1)])
    halo_far = lax.ppermute(labelled, "seq", [(1, 3), (2, 0)])
    cot_own = cotangent[0]

    lines = [
        query_bias,
        value_bias,
        output_bias,
        first_gain,
        first_shift,
        down_bias,
        second_gain,
        second_shift,
    ]
    lines = [line[None] for line in lines] if direct else []
    columns = pack_columns(scalars, narrow, narrow_far, lines, up_bias[None])
    feed_piece = pack_feed(scalars, wide, wide_far)

    if direct:
        chip = chip_pieces(columns)
        projection_pieces, feed_piece = together(core_pieces(chip), feed_piece)
        feed_chip = chip_pieces(feed_piece)
    else:

        def label(table, line):
            table = jnp.pad(table, ((0, LABELS - table.shape[0]), (0, D - table.shape[1])))
            line = jnp.pad(line[None], ((0, LABELS - 1), (0, 0)))
            return jnp.concatenate([table, line], axis=1)

        vectors = jnp.stack(
            [
                query_bias,
                value_bias,
                output_bias,
                first_gain,
                first_shift,
                down_bias,
                second_gain,
                second_shift,
            ]
        )
        lines = lax.all_gather(vectors, "dp", axis=1, tiled=True).reshape(VECS, GROUPS, BLOCK)
        hidden_lines = lax.all_gather(up_bias, "dp", axis=0, tiled=True).reshape(GROUPS, -1)
        projection_pieces = [
            jnp.concatenate([block, label(lines[:, k], hidden_lines[k])], axis=0)
            for k, block in enumerate(gather_rows(columns))
        ]
        feed_chip = gather_rows(feed_piece)

    def rows_of(keep, send):
        return jnp.stack([keep, send], axis=1).reshape(GROUPS, -1, keep.shape[2]).astype(F32)

    def spread(sums):
        return [sums[0]] + [swap(sums[k], "dp", 2 * k) for k in range(1, len(sums))]

    def scattered(table):
        return [lax.psum_scatter(table, "dp", scatter_dimension=0, tiled=True)]

    query, key, value, *ctx_mine, x, weight, hot, vecs, hidden_bias = qkv_attend(
        scalars, own, partner, halo_near, halo_far, own_docs, projection_pieces, rows
    )
    ctx_mine, feed_chip[1:3], cot_own = together(ctx_mine, feed_chip[1:3], cot_own)
    ctx_partner = [None, None]
    ctx_partner[1] = swap(ctx_mine[1], "seq", 1)
    ctx_partner[0] = swap(ctx_mine[0], "seq", 1)
    ctx_partner, feed_chip = together(ctx_partner, feed_chip)
    weights = core_pieces(feed_chip) if direct else feed_chip
    cot_partner = swap(cot_own, "seq", 1)

    forward, slopes, part_far = [None, None], [None, None], [None, None]
    for block in (1, 0):
        forward[block], weights = feed_forward(
            scalars, block, ctx_mine[block], ctx_partner[block], x, vecs, hidden_bias, weights, rows
        )
        part_far[block] = swap(forward[block][5], "seq", 1)
    up, down, out_mine, _ = weights
    second, second_shared, first_part_far = [None, None], [], [None, None]
    for block in (1, 0):
        slopes[block] = gelu_slope(scalars, forward[block][3])
    for block in (1, 0):
        second[block], second_shared = second_norm(
            scalars,
            block,
            forward[block][5],
            part_far[block],
            forward[block][0],
            slopes[block],
            (cot_own, cot_partner),
            vecs,
            up,
            down,
            second_shared,
            rows,
        )
        if block == 1:
            first_part_far[block] = swap(second[block][3], "seq", 1)
    feed_parts = feed_forward_grads(
        scalars,
        [(forward[k][2], second[k][2], second[k][1], forward[k][4]) for k in range(2)],
        rows,
    )
    first_part_far[1], second, second_shared, feed_parts = together(
        first_part_far[1], second, second_shared, feed_parts
    )
    first_part_far[0] = swap(second[0][3], "seq", 1)
    layer_output, sums_two, sums_hidden = second_shared
    attention_grad, ctx_grad, first_shared = [None, None], [None, None], []

    def finish(block):
        attention_grad[block], ctx_grad[block], *shared = first_norm(
            scalars,
            block,
            second[block][3],
            first_part_far[block],
            second[block][0],
            forward[block][0],
            forward[block][1],
            vecs,
            out_mine,
            first_shared,
            rows,
        )
        return shared

    *first_shared, halo_send = finish(1)
    halo_grad = swap(halo_send, "seq", 2)
    if direct:
        feed_sums = combine(scalars, feed_parts[0], swap(feed_parts[1], "dp", 1))
        feed_sums[3], halo_grad = together(feed_sums[3], halo_grad)
        feed_sums, first_part_far[0] = together(feed_sums, first_part_far[0])
        feed_sums = spread(feed_sums)
    else:
        feed_sums = scattered(rows_of(*feed_parts).reshape(D, -1))
    own_grad, sums_one = finish(0)

    grads, input_keep, input_send, sums_projection = attend_backward(
        scalars, query, key, value, [*ctx_grad, halo_grad], hot, weight, rows
    )
    grads, sums_projection, input_send, feed_sums[1:3] = together(
        grads, sums_projection, input_send, feed_sums[1:3]
    )
    input_far = swap(input_send, "seq", 1)
    small = small_sums(scalars, sums_one, sums_two, sums_hidden, sums_projection)
    small_side = swap(small, "seq", 1)
    projection_parts = projection_grads(scalars, x, grads, rows)
    projection_parts, small_side, feed_sums = together(projection_parts, small_side, feed_sums)
    out_blocks = [(ctx_mine[k], ctx_partner[k], attention_grad[k]) for k in range(2)]
    if direct:
        projection_received = swap(projection_parts[1], "dp", 1)
        out_parts = output_grads(scalars, out_blocks, small, small_side)
        out_received = swap(out_parts[1], "dp", 1)
        feed_keep, feed_send = total_feed(scalars, feed_sums)
        feed_far = swap(feed_send, "seq", 2)
        sums = spread(
            combine_both(scalars, projection_parts[0], projection_received, out_parts[0], out_received)
        )
    else:
        out_parts = rows_of(*output_grads(scalars, out_blocks, small, small_side))
        sums = scattered(
            jnp.concatenate(
                [rows_of(*projection_parts).reshape(D, -1), out_parts[:, :BLOCK].reshape(D, -1)], axis=1
            )
        )
        feed_keep, feed_send = total_feed(scalars, feed_sums)
        feed_far = swap(feed_send, "seq", 2)
    up_grad, down_grad = finish_feed(scalars, feed_keep, feed_far)
    input_grad = own_grad + input_keep + input_far.astype(F32)
    if direct:
        sums, up_grad, input_grad = together(sums, up_grad, input_grad)
    keep, send = total_projection(scalars, sums, piece_rows)
    projections = list(finish_projection(scalars, keep, swap(send, "seq", 2), piece_rows))
    if direct:
        tile = projections.pop()
        wide_lines, tall_lines = tile[:VECS, :BLOCK], tile[VECS : VECS + 3].reshape(-1)
    else:
        tile = out_parts[:, BLOCK:, :128] + out_parts[:, BLOCK:, 128:256]
        tile = tile + swap(tile, "seq", 2)
        wide_lines = tile[:, :VECS, :BLOCK].transpose(1, 0, 2).reshape(VECS, D)
        wide_lines = lax.psum_scatter(wide_lines, "dp", scatter_dimension=1, tiled=True)
        tall_lines = lax.psum_scatter(tile[:, VECS : VECS + 3].reshape(-1), "dp", tiled=True)
    vec = [wide_lines[k] for k in range(VECS)]
    return (
        layer_output[None],
        input_grad[None],
        *projections,
        vec[0],
        vec[1],
        vec[2],
        vec[3],
        vec[4],
        up_grad,
        tall_lines,
        down_grad.T,
        vec[5],
        vec[6],
        vec[7],
    )


def solution(mesh):
    placed = (
        P("dp", "seq", None),
        P("dp", "seq"),
        P("dp", "seq"),
        P("dp", "seq"),
        P("dp", "seq"),
        P("dp", "seq"),
        P("dp"),
        P("dp"),
        P("dp"),
        P("dp"),
        P("dp"),
        P("dp", "seq"),
        P("dp"),
        P("seq", "dp"),
        P("dp"),
        P("dp"),
        P("dp"),
        P("dp", "seq", None),
    )
    return jax.shard_map(
        per_device,
        mesh=mesh,
        in_specs=placed,
        out_specs=(
            P("dp", "seq", None),
            P("dp", "seq", None),
            P("dp", "seq"),
            P("dp", "seq"),
            P("dp", "seq"),
            P("dp", "seq"),
            P("dp"),
            P("dp"),
            P("dp"),
            P("dp"),
            P("dp"),
            P("dp", "seq"),
            P("dp"),
            P("seq", "dp"),
            P("dp"),
            P("dp"),
            P("dp"),
        ),
        check_vma=False,
    )
```

time: 310 us -> 219 us (0.71)
  waiting for transfers between devices: 129 us -> 94.8 us
  Pallas kernels: 94.2 us -> 65.4 us
  other arithmetic: 13 us -> 1.09 us
  starting transfers between devices: 50.6 us -> 42.5 us
  local copies, waits for them, and re-layouts: 20.5 us -> 13.7 us
    pallas_call x12 -> x25, Pallas kernels: 94.2 us -> 65.4 us  [call(): pl.pallas_call(body, out_shape=outs, grid_spec=spec, compiler_params=para...]
    all_to_all x2 -> x0, waiting for transfers between devices: 26.8 us -> none  [the longest x1 19.8 us: per_device(): lax.all_to_all(jnp.broadcast_to(vectors[None], (count, vectors.shape[0]))...]
    ppermute x39, waiting for transfers between devices: 102 us -> 80.2 us  [swap(): return lax.ppermute(value, axis, [(k, k ^ mask) for k in range(count)])]
    ppermute x1, waiting for transfers between devices: 0.01 us -> 14.6 us  [per_device(): halo_far = lax.ppermute(labelled, 'seq', [(1, 3), (2, 0)])]
    all_to_all x2 -> x0, starting transfers between devices: 7.43 us -> none  [the longest x1 4.1 us: per_device(): lax.all_to_all(small, ('dp', 'seq'), 0, 0, tiled=True)]
    unnamed x76 -> x36, local copies, waits for them, and re-layouts: 5.91 us -> 11.9 us
    slice x12 -> x0, local copies, waits for them, and re-layouts: 5.3 us -> none  [the longest x1 0.86 us: per_device(): projection_sums[0].reshape(3, 3, PAIR).transpose(1, 0, 2)]
    concatenate x10 -> x0, other arithmetic: 3.99 us -> none  [the longest x1 1.02 us: per_device(): labelled = jnp.concatenate([own, marks], axis=0)]
  transfers between devices with their start and end apart: 43 -> 41, of which waited for: 18 -> 22; matrix products, arithmetic and copies ran while one was open for 8% -> 1% of each run, Pallas kernels for 24% -> 29%
where the time goes in v2:
time: 219 us
  waiting for transfers between devices  94.8 us (43%)
  Pallas kernels  65.4 us (30%)
  starting transfers between devices  42.5 us (19%)
  local copies, waits for them, and re-layouts  13.7 us (6%)
    ppermute x39, waiting for transfers between devices, swap(): return lax.ppermute(value, axis, [(k, k ^ mask) for k in range(count)])  80.2 us
    pallas_call x25, Pallas kernels, call(): pl.pallas_call(body, out_shape=outs, grid_spec=spec, compiler_params=para...  65.4 us
    ppermute x39, starting transfers between devices, swap(): return lax.ppermute(value, axis, [(k, k ^ mask) for k in range(count)])  40.6 us
    ppermute x1, waiting for transfers between devices, per_device(): halo_far = lax.ppermute(labelled, 'seq', [(1, 3), (2, 0)])  14.6 us
    unnamed x36, local copies, waits for them, and re-layouts  11.9 us
  transfers between devices with their start and end apart: 41, of which 22 were waited for; matrix products, arithmetic and copies ran while one was open for 1% of the time, Pallas kernels for 29%

profile of v2, /device:TPU:0, one launch (start us, length us, event | category | flops | bytes accessed | tf_op | source)
XLA Modules:
  0.0 218.6 jit_solution(12132175827087456633)
XLA Ops:
  3.8 4.1 %collective-permute-start.1 = (bf16[96,576]{1,0:T(8,128)(2,1)S(1)}, bf16[96,576]{1,0:T(8,128)(2,1)S(1)}, u32[]{:S(2)}, u32[]{:S(2)}) collective-permute-start(bf16[96,576]{1,0:T(8,128)(2,1)S(1)} %pack_narrow.1.near_ref), channel_id=1, source_target_pairs={{0,2},{1,3},{2,0},{3,1},{4,6},{5,7},{6,4},{7,5},{8,10},{9,11},{10,... | collective-permute-start | bytes 331784 | tf_op jit(solution)/shard_map/ppermute | solution.py:42
  27.1 2.8 %collective-permute-done.9.refs_6_ = bf16[112,1152]{1,0:T(8,128)(2,1)S(1)} collective-permute-done((bf16[112,1152]{1,0:T(8,128)(2,1)S(1)}, bf16[112,1152]{1,0:T(8,128)(2,1)S(1)}, u32[]{:S(2)}, u32[]{:S(2)}) %collective-permute-start.9) | collective-permute-done | bytes 258080 | tf_op jit(solution)/shard_map/ppermute | solution.py:42
  29.9 2.9 %collective-permute-done.5.refs_2_ = bf16[112,1152]{1,0:T(8,128)(2,1)S(1)} collective-permute-done((bf16[112,1152]{1,0:T(8,128)(2,1)S(1)}, bf16[112,1152]{1,0:T(8,128)(2,1)S(1)}, u32[]{:S(2)}, u32[]{:S(2)}) %collective-permute-start.5) | collective-permute-done | bytes 258080 | tf_op jit(solution)/shard_map/ppermute | solution.py:42
  33.6 10.7 %collective-permute-done.12.far_ref = bf16[96,1920]{1,0:T(8,128)(2,1)S(1)} collective-permute-done((bf16[96,1920]{1,0:T(8,128)(2,1)S(1)}, bf16[96,1920]{1,0:T(8,128)(2,1)S(1)}, u32[]{:S(2)}, u32[]{:S(2)}) %collective-permute-start.12) | collective-permute-done | bytes 368672 | tf_op jit(solution)/shard_map/ppermute | solution.py:42
  49.5 4.7 %collective-permute-done.partner_ref = bf16[272,768]{1,0:T(8,128)(2,1)S(1)} collective-permute-done((bf16[272,768]{1,0:T(8,128)(2,1)S(1)}, bf16[272,768]{1,0:T(8,128)(2,1)S(1)}, u32[]{:S(2)}, u32[]{:S(2)}) %collective-permute-start) | collective-permute-done | bytes 417824 | tf_op jit(solution)/shard_map/ppermute | solution.py:42
  55.5 14.6 %collective-permute-done.3.far_ref = bf16[272,768]{1,0:T(8,128)(2,1)S(1)} collective-permute-done((bf16[272,768]{1,0:T(8,128)(2,1)S(1)}, bf16[272,768]{1,0:T(8,128)(2,1)S(1)}, u32[]{:S(2)}, u32[]{:S(2)}) %collective-permute-start.3) | collective-permute-done | bytes 417824 | tf_op jit(solution)/shard_map/ppermute | solution.py:911
  70.1 10.5 %qkv_attend.1 = (bf16[768,384]{1,0:T(8,128)(2,1)S(1)}, bf16[768,384]{1,0:T(8,128)(2,1)S(1)}, bf16[768,384]{1,0:T(8,128)(2,1)S(1)}, bf16[256,384]{1,0:T(8,128)(2,...) custom-call(s32[3]{0:T(128)S(1)} %pad_add_fusion._.sc, ...), custom_call_target="tpu_custom_call" | custom-call | flops 130000000 | bytes 1024 | tf_op jit(solution)/shard_map/qkv_attend/pallas_call | solution.py:65
  82.8 3.6 %collective-permute-done.15.partner_ref.refs_1_ = bf16[256,384]{1,0:T(8,128)(2,1)S(1)} collective-permute-done((bf16[256,384]{1,0:T(8,128)(2,1)S(1)}, bf16[256,384]{1,0:T(8,128)(2,1)S(1)}, u32[]{:S(2)}, u32[]{:S(2)}) %collective-permute-start.15) | collective-permute-done | bytes 196640 | tf_op jit(solution)/shard_map/ppermute | solution.py:42
  93.9 3.2 %feed_forward.2 = (f32[256,768]{1,0:T(8,128)S(1)}, f32[256,128]{1,0:T(8,128)S(1)}, bf16[256,768]{1,0:T(8,128)(2,1)S(1)}, f32[256,1536]{1,0:T(8,128)S(1)}, bf16[2...) custom-call(s32[3]{0:T(128)S(1)} %pad_add_fusion._.sc, ...), custom_call_target="tpu_custom_call" | custom-call | flops 60000000 | bytes 1024 | tf_op jit(solution)/shard_map/feed_forward/pallas_call | solution.py:65
  98.2 2.9 %feed_forward.3 = (f32[256,768]{1,0:T(8,128)S(1)}, f32[256,128]{1,0:T(8,128)S(1)}, bf16[256,768]{1,0:T(8,128)(2,1)S(1)}, f32[256,1536]{1,0:T(8,128)S(1)}, bf16[2...) custom-call(s32[3]{0:T(128)S(1)} %pad_add_fusion._.sc, bf16[256,384]{1,0:T(8,128)(2,1)S(1)} %get-tuple-element.170.mine_ref.refs_0_, ...), custom_call_target="tpu_custom_call" | custom-call | flops 60000000 | bytes 1024 | tf_op jit(solution)/shard_map/feed_forward/pallas_call | solution.py:65
  103.3 6.3 %collective-permute-done.22.recv_ref = bf16[256,768]{1,0:T(8,128)(2,1)S(1)} collective-permute-done((bf16[256,768]{1,0:T(8,128)(2,1)S(1)}, bf16[256,768]{1,0:T(8,128)(2,1)S(1)}, u32[]{:S(2)}, u32[]{:S(2)}) %collective-permute-start.22) | collective-permute-done | bytes 393248 | tf_op jit(solution)/shard_map/ppermute | solution.py:42
  109.6 2.9 %second_norm.2 = (f32[256,768]{1,0:T(8,128)S(1)}, bf16[256,768]{1,0:T(8,128)(2,1)S(1)}, bf16[256,1536]{1,0:T(8,128)(2,1)S(1)}, bf16[256,768]{1,0:T(8,128)(2,1)S(...) custom-call(s32[3]{0:T(128)S(1)} %pad_add_fusion._.sc, ...), custom_call_target="tpu_custom_call" | custom-call | flops 50000000 | bytes 1024 | tf_op jit(solution)/shard_map/second_norm/pallas_call | solution.py:65
  115.1 3.0 %collective-permute-done.25.recv_ref = bf16[256,768]{1,0:T(8,128)(2,1)S(1)} collective-permute-done((bf16[256,768]{1,0:T(8,128)(2,1)S(1)}, bf16[256,768]{1,0:T(8,128)(2,1)S(1)}, u32[]{:S(2)}, u32[]{:S(2)}) %collective-permute-start.25) | collective-permute-done | bytes 393248 | tf_op jit(solution)/shard_map/ppermute | solution.py:42
  118.0 3.8 %second_norm.3 = (f32[256,768]{1,0:T(8,128)S(1)}, bf16[256,768]{1,0:T(8,128)(2,1)S(1)}, bf16[256,1536]{1,0:T(8,128)(2,1)S(1)}, bf16[256,768]{1,0:T(8,128)(2,1)S(...) custom-call(s32[3]{0:T(128)S(1)} %pad_add_fusion._.sc, ...), custom_call_target="tpu_custom_call" | custom-call | flops 50000000 | bytes 1024 | tf_op jit(solution)/shard_map/second_norm/pallas_call | solution.py:65
  121.8 5.0 %feed_forward_grads.1 = (bf16[4,96,3072]{2,1,0:T(8,128)(2,1)S(1)}, bf16[4,96,3072]{2,1,0:T(8,128)(2,1)S(1)}) custom-call(s32[3]{0:T(128)S(1)} %pad_add_fusion._.sc, bf16[256,768]{1,0:T(8,128)(2,1)S(1)} %get-tuple-element.207.refs_0_, bf16[256,1536]{1,0:T(8,128)(2,1)S(1)} %get-tuple-element.199.refs_1_, bf16[256,768]{1,0:T(8,128)(2,1)S(1)} %get-tuple-element.198.refs_2_, ...), custom_call_target="tpu_custom_call" | custom-call | flops 80000000 | bytes 1024 | tf_op jit(solution)/shard_map/feed_forward_grads/pallas_call | solution.py:65
  129.4 3.9 %collective-permute-start.27 = (bf16[256,384]{1,0:T(8,128)(2,1)S(1)}, bf16[256,384]{1,0:T(8,128)(2,1)S(1)}, u32[]{:S(2)}, u32[]{:S(2)}) collective-permute-start(bf16[256,384]{1,0:T(8,128)(2,1)S(1)} %get-tuple-element.228), channel_id=1, source_target_pairs={{0,2},{1,3},{2,0},{3,1},{4,6},{5,7},{6,4},{7,5},{8,10},{9,11},{10,... | collective-permute-start | bytes 589832 | tf_op jit(solution)/shard_map/ppermute | solution.py:42
  135.0 6.0 %collective-permute-done.27.halo_ref = bf16[256,384]{1,0:T(8,128)(2,1)S(1)} collective-permute-done((bf16[256,384]{1,0:T(8,128)(2,1)S(1)}, bf16[256,384]{1,0:T(8,128)(2,1)S(1)}, u32[]{:S(2)}, u32[]{:S(2)}) %collective-permute-start.27) | collective-permute-done | bytes 196640 | tf_op jit(solution)/shard_map/ppermute | solution.py:42
  148.0 15.8 %attend_backward.1 = (bf16[512,1152]{1,0:T(8,128)(2,1)S(1)}, f32[256,768]{1,0:T(8,128)S(1)}, bf16[256,768]{1,0:T(8,128)(2,1)S(1)}, f32[8,1152]{1,0:T(8,128)S(1)}) custom-call(s32[3]{0:T(128)S(1)} %pad_add_fusion._.sc, bf16[768,384]{1,0:T(8,128)(2,1)S(1)} %get-tuple-element.214.q_ref, bf16[768,384]{1,0:T(8,128)(2,1)S(1)} %get-tuple-element.215.k_ref, ...), custom_call_target="tpu_custom_call" | custom-call | flops 180000000 | bytes 1024 | tf_op jit(solution)/shard_map/attend_backward/pallas_call | solution.py:65
  163.9 7.0 %collective-permute-done.30.refs_2_ = bf16[96,3072]{1,0:T(8,128)(2,1)S(1)} collective-permute-done((bf16[96,3072]{1,0:T(8,128)(2,1)S(1)}, bf16[96,3072]{1,0:T(8,128)(2,1)S(1)}, u32[]{:S(2)}, u32[]{:S(2)}) %collective-permute-start.30) | collective-permute-done | bytes 589856 | tf_op jit(solution)/shard_map/ppermute | solution.py:42
  171.6 2.8 %collective-permute-start.31 = (f32[8,16,128]{2,1,0:T(8,128)S(1)}, f32[8,16,128]{2,1,0:T(8,128)S(1)}, u32[]{:S(2)}, u32[]{:S(2)}) collective-permute-start(f32[8,16,128]{2,1,0:T(8,128)S(1)} %small_sums.1.refs_6_), channel_id=1, source_target_pairs={{0,1},{1,0},{2,3},{3,2},{4,5},{5,4},{6,7},{7,6},{8,9},{9,8},{10,11... | collective-permute-start | bytes 196616 | tf_op jit(solution)/shard_map/ppermute | solution.py:42
  174.4 2.9 %projection_grads.1 = (bf16[4,96,1152]{2,1,0:T(8,128)(2,1)S(1)}, bf16[4,96,1152]{2,1,0:T(8,128)(2,1)S(1)}) custom-call(s32[3]{0:T(128)S(1)} %pad_add_fusion._.sc, bf16[768,768]{1,0:T(8,128)(2,1)S(1)} %get-tuple-element.174.x_ref, bf16[512,1152]{1,0:T(8,128)(2,1)S(1)} %get-tuple-element.245.grad_ref), custom_call_target="tpu_custom_call" | custom-call | flops 50000000 | bytes 1024 | tf_op jit(solution)/shard_map/projection_grads/pallas_call | solution.py:65
  187.6 8.0 %collective-permute-done.38.recv_ref = bf16[96,1536]{1,0:T(8,128)(2,1)S(1)} collective-permute-done((bf16[96,1536]{1,0:T(8,128)(2,1)S(1)}, bf16[96,1536]{1,0:T(8,128)(2,1)S(1)}, u32[]{:S(2)}, u32[]{:S(2)}) %collective-permute-start.38) | collective-permute-done | bytes 294944 | tf_op jit(solution)/shard_map/ppermute | solution.py:42
  198.1 5.9 %collective-permute-done.36.refs_2_ = bf16[112,1920]{1,0:T(8,128)(2,1)S(1)} collective-permute-done((bf16[112,1920]{1,0:T(8,128)(2,1)S(1)}, bf16[112,1920]{1,0:T(8,128)(2,1)S(1)}, u32[]{:S(2)}, u32[]{:S(2)}) %collective-permute-start.36) | collective-permute-done | bytes 430112 | tf_op jit(solution)/shard_map/ppermute | solution.py:42
  208.0 8.1 %collective-permute-done.40.recv_ref = bf16[112,768]{1,0:T(8,128)(2,1)S(1)} collective-permute-done((bf16[112,768]{1,0:T(8,128)(2,1)S(1)}, bf16[112,768]{1,0:T(8,128)(2,1)S(1)}, u32[]{:S(2)}, u32[]{:S(2)}) %collective-permute-start.40) | collective-permute-done | bytes 172064 | tf_op jit(solution)/shard_map/ppermute | solution.py:42
  (124 shorter events, 76.0 us)
Async XLA Ops:
  7.9 15.4 %collective-permute-start.11 = (bf16[96,192]{1,0:T(8,128)(2,1)}, bf16[96,192]{1,0:T(8,128)(2,1)S(1)}, u32[]{:S(2)}, u32[]{:S(2)}) collective-permute-start(bf16[96,192]{1,0:T(8,128)(2,1)} %out_ref.1), channel_id=1, source_target_pairs={{0,1},{1,0},{2,3},{3,2},{4,5},{5,4},{6,7},{7,6},{8,9},{9,8},{10,11... | collective-permute-start | bytes 110600 | tf_op jit(solution)/shard_map/ppermute | solution.py:42
  26.5 17.8 %collective-permute-start.12 = (bf16[96,1920]{1,0:T(8,128)(2,1)S(1)}, bf16[96,1920]{1,0:T(8,128)(2,1)S(1)}, u32[]{:S(2)}, u32[]{:S(2)}) collective-permute-start(bf16[96,1920]{1,0:T(8,128)(2,1)S(1)} %pack_wide.1.wide_ref), channel_id=1, source_target_pairs={{0,2},{1,3},{2,0},{3,1},{4,6},{5,7},{6,4},{7,5},{8,10},{9,11},{10,... | collective-permute-start | bytes 1105928 | tf_op jit(solution)/shard_map/ppermute | solution.py:42
  27.1 18.1 %collective-permute-start.4 = (bf16[112,1152]{1,0:T(8,128)(2,1)S(1)}, bf16[112,1152]{1,0:T(8,128)(2,1)S(1)}, u32[]{:S(2)}, u32[]{:S(2)}) collective-permute-start(bf16[112,1152]{1,0:T(8,128)(2,1)S(1)} %pack_columns.1.refs_0_), channel_id=1, source_target_pairs={{0,4},{4,0},{8,12},{12,8},{16,20},{20,16},{24,28},{28,24},{1,5},{5... | collective-permute-start | bytes 774152 | tf_op jit(solution)/shard_map/ppermute | solution.py:42
  29.9 15.3 %collective-permute-start.10 = (bf16[112,1152]{1,0:T(8,128)(2,1)S(1)}, bf16[112,1152]{1,0:T(8,128)(2,1)S(1)}, u32[]{:S(2)}, u32[]{:S(2)}) collective-permute-start(bf16[112,1152]{1,0:T(8,128)(2,1)S(1)} %collective-permute-done.9.refs_6_), channel_id=1, source_target_pairs={{0,4},{4,0},{8,12},{12,8},{16,20},{20,16},{24,28},{28,24},{1,5},{5... | collective-permute-start | bytes 774152 | tf_op jit(solution)/shard_map/ppermute | solution.py:42
  32.8 12.5 %collective-permute-start.6 = (bf16[112,1152]{1,0:T(8,128)(2,1)S(1)}, bf16[112,1152]{1,0:T(8,128)(2,1)S(1)}, u32[]{:S(2)}, u32[]{:S(2)}) collective-permute-start(bf16[112,1152]{1,0:T(8,128)(2,1)S(1)} %collective-permute-done.5.refs_2_), channel_id=1, source_target_pairs={{0,4},{4,0},{8,12},{12,8},{16,20},{20,16},{24,28},{28,24},{1,5},{5... | collective-permute-start | bytes 774152 | tf_op jit(solution)/shard_map/ppermute | solution.py:42
  33.6 11.6 %collective-permute-start.8 = (bf16[112,1152]{1,0:T(8,128)(2,1)S(1)}, bf16[112,1152]{1,0:T(8,128)(2,1)S(1)}, u32[]{:S(2)}, u32[]{:S(2)}) collective-permute-start(bf16[112,1152]{1,0:T(8,128)(2,1)S(1)} %collective-permute-done.7.refs_4_), channel_id=1, source_target_pairs={{0,4},{4,0},{8,12},{12,8},{16,20},{20,16},{24,28},{28,24},{1,5},{5... | collective-permute-start | bytes 774152 | tf_op jit(solution)/shard_map/ppermute | solution.py:42
  45.3 35.4 %collective-permute-start.13 = (bf16[96,3840]{1,0:T(8,128)(2,1)S(1)}, bf16[96,3840]{1,0:T(8,128)(2,1)S(1)}, u32[]{:S(2)}, u32[]{:S(2)}) collective-permute-start(bf16[96,3840]{1,0:T(8,128)(2,1)S(1)} %pack_feed.1.refs_0_), channel_id=1, source_target_pairs={{0,8},{4,12},{8,0},{12,4},{16,24},{20,28},{24,16},{28,20},{1,9},{5... | collective-permute-start | bytes 2211848 | tf_op jit(solution)/shard_map/ppermute | solution.py:42
  45.9 34.8 %collective-permute-start.14 = (bf16[96,3840]{1,0:T(8,128)(2,1)S(1)}, bf16[96,3840]{1,0:T(8,128)(2,1)S(1)}, u32[]{:S(2)}, u32[]{:S(2)}) collective-permute-start(bf16[96,3840]{1,0:T(8,128)(2,1)S(1)} %pack_feed.1.refs_0_), channel_id=1, source_target_pairs={{0,16},{4,20},{8,24},{12,28},{16,0},{20,4},{24,8},{28,12},{1,17},{... | collective-permute-start | bytes 2211848 | tf_op jit(solution)/shard_map/ppermute | solution.py:42
  47.4 35.4 %collective-permute-start.17 = (bf16[96,3840]{1,0:T(8,128)(2,1)S(1)}, bf16[96,3840]{1,0:T(8,128)(2,1)S(1)}, u32[]{:S(2)}, u32[]{:S(2)}) collective-permute-start(bf16[96,3840]{1,0:T(8,128)(2,1)S(1)} %pack_feed.1.refs_0_), channel_id=1, source_target_pairs={{0,24},{4,28},{8,16},{12,20},{16,8},{20,12},{24,0},{28,4},{1,25},{... | collective-permute-start | bytes 2211848 | tf_op jit(solution)/shard_map/ppermute | solution.py:42
  54.2 15.9 %collective-permute-start.3 = (bf16[272,768]{1,0:T(8,128)(2,1)S(1)}, bf16[272,768]{1,0:T(8,128)(2,1)S(1)}, u32[]{:S(2)}, u32[]{:S(2)}) collective-permute-start(bf16[272,768]{1,0:T(8,128)(2,1)S(1)} %get-tuple-element.155), channel_id=1, source_target_pairs={{1,3},{2,0},{5,7},{6,4},{9,11},{10,8},{13,15},{14,12},{17,19},{18,... | collective-permute-start | bytes 1253384 | tf_op jit(solution)/shard_map/ppermute | solution.py:911
  89.5 13.7 %collective-permute-start.23 = (bf16[256,768]{1,0:T(8,128)(2,1)S(1)}, bf16[256,768]{1,0:T(8,128)(2,1)S(1)}, u32[]{:S(2)}, u32[]{:S(2)}) collective-permute-start(bf16[256,768]{1,0:T(8,128)(2,1)S(1)} %bitcast.35), channel_id=1, source_target_pairs={{0,1},{1,0},{2,3},{3,2},{4,5},{5,4},{6,7},{7,6},{8,9},{9,8},{10,11... | collective-permute-start | bytes 1179656 | tf_op jit(solution)/shard_map/ppermute | solution.py:42
  97.1 12.5 %collective-permute-start.22 = (bf16[256,768]{1,0:T(8,128)(2,1)S(1)}, bf16[256,768]{1,0:T(8,128)(2,1)S(1)}, u32[]{:S(2)}, u32[]{:S(2)}) collective-permute-start(bf16[256,768]{1,0:T(8,128)(2,1)S(1)} %get-tuple-element.181.part_ref), channel_id=1, source_target_pairs={{0,1},{1,0},{2,3},{3,2},{4,5},{5,4},{6,7},{7,6},{8,9},{9,8},{10,11... | collective-permute-start | bytes 1179656 | tf_op jit(solution)/shard_map/ppermute | solution.py:42
  101.1 17.0 %collective-permute-start.25 = (bf16[256,768]{1,0:T(8,128)(2,1)S(1)}, bf16[256,768]{1,0:T(8,128)(2,1)S(1)}, u32[]{:S(2)}, u32[]{:S(2)}) collective-permute-start(bf16[256,768]{1,0:T(8,128)(2,1)S(1)} %get-tuple-element.191.part_ref), channel_id=1, source_target_pairs={{0,1},{1,0},{2,3},{3,2},{4,5},{5,4},{6,7},{7,6},{8,9},{9,8},{10,11... | collective-permute-start | bytes 1179656 | tf_op jit(solution)/shard_map/ppermute | solution.py:42
  112.6 14.3 %collective-permute-start.24 = (bf16[256,768]{1,0:T(8,128)(2,1)S(1)}, bf16[256,768]{1,0:T(8,128)(2,1)S(1)}, u32[]{:S(2)}, u32[]{:S(2)}) collective-permute-start(bf16[256,768]{1,0:T(8,128)(2,1)S(1)} %get-tuple-element.224.part_ref), channel_id=1, source_target_pairs={{0,1},{1,0},{2,3},{3,2},{4,5},{5,4},{6,7},{7,6},{8,9},{9,8},{10,11... | collective-permute-start | bytes 1179656 | tf_op jit(solution)/shard_map/ppermute | solution.py:42
  126.9 15.7 %collective-permute-start.28 = (bf16[256,768]{1,0:T(8,128)(2,1)S(1)}, bf16[256,768]{1,0:T(8,128)(2,1)S(1)}, u32[]{:S(2)}, u32[]{:S(2)}) collective-permute-start(bf16[256,768]{1,0:T(8,128)(2,1)S(1)} %get-tuple-element.217.part_ref), channel_id=1, source_target_pairs={{0,1},{1,0},{2,3},{3,2},{4,5},{5,4},{6,7},{7,6},{8,9},{9,8},{10,11... | collective-permute-start | bytes 1179656 | tf_op jit(solution)/shard_map/ppermute | solution.py:42
  129.4 11.6 %collective-permute-start.27 = (bf16[256,384]{1,0:T(8,128)(2,1)S(1)}, bf16[256,384]{1,0:T(8,128)(2,1)S(1)}, u32[]{:S(2)}, u32[]{:S(2)}) collective-permute-start(bf16[256,384]{1,0:T(8,128)(2,1)S(1)} %get-tuple-element.228), channel_id=1, source_target_pairs={{0,2},{1,3},{2,0},{3,1},{4,6},{5,7},{6,4},{7,5},{8,10},{9,11},{10,... | collective-permute-start | bytes 589832 | tf_op jit(solution)/shard_map/ppermute | solution.py:42
  142.7 21.2 %collective-permute-start.29 = (bf16[96,3072]{1,0:T(8,128)(2,1)S(1)}, bf16[96,3072]{1,0:T(8,128)(2,1)S(1)}, u32[]{:S(2)}, u32[]{:S(2)}) collective-permute-start(bf16[96,3072]{1,0:T(8,128)(2,1)S(1)} %get-tuple-element.243), channel_id=1, source_target_pairs={{0,8},{4,12},{8,0},{12,4},{16,24},{20,28},{24,16},{28,20},{1,9},{5... | collective-permute-start | bytes 1769480 | tf_op jit(solution)/shard_map/ppermute | solution.py:42
  143.6 27.3 %collective-permute-start.30 = (bf16[96,3072]{1,0:T(8,128)(2,1)S(1)}, bf16[96,3072]{1,0:T(8,128)(2,1)S(1)}, u32[]{:S(2)}, u32[]{:S(2)}) collective-permute-start(bf16[96,3072]{1,0:T(8,128)(2,1)S(1)} %get-tuple-element.244), channel_id=1, source_target_pairs={{0,16},{4,20},{8,24},{12,28},{16,0},{20,4},{24,8},{28,12},{1,17},{... | collective-permute-start | bytes 1769480 | tf_op jit(solution)/shard_map/ppermute | solution.py:42
  145.1 32.2 %collective-permute-start.32 = (bf16[96,3072]{1,0:T(8,128)(2,1)S(1)}, bf16[96,3072]{1,0:T(8,128)(2,1)S(1)}, u32[]{:S(2)}, u32[]{:S(2)}) collective-permute-start(bf16[96,3072]{1,0:T(8,128)(2,1)S(1)} %get-tuple-element.255), channel_id=1, source_target_pairs={{0,24},{4,28},{8,16},{12,20},{16,8},{20,12},{24,0},{28,4},{1,25},{... | collective-permute-start | bytes 1769480 | tf_op jit(solution)/shard_map/ppermute | solution.py:42
  179.5 17.6 %collective-permute-start.39 = (bf16[256,768]{1,0:T(8,128)(2,1)S(1)}, bf16[256,768]{1,0:T(8,128)(2,1)S(1)}, u32[]{:S(2)}, u32[]{:S(2)}) collective-permute-start(bf16[256,768]{1,0:T(8,128)(2,1)S(1)} %get-tuple-element.276), channel_id=1, source_target_pairs={{0,1},{1,0},{2,3},{3,2},{4,5},{5,4},{6,7},{7,6},{8,9},{9,8},{10,11... | collective-permute-start | bytes 1179656 | tf_op jit(solution)/shard_map/ppermute | solution.py:42
  181.5 14.1 %collective-permute-start.38 = (bf16[96,1536]{1,0:T(8,128)(2,1)S(1)}, bf16[96,1536]{1,0:T(8,128)(2,1)S(1)}, u32[]{:S(2)}, u32[]{:S(2)}) collective-permute-start(bf16[96,1536]{1,0:T(8,128)(2,1)S(1)} %get-tuple-element.272), channel_id=1, source_target_pairs={{0,2},{1,3},{2,0},{3,1},{4,6},{5,7},{6,4},{7,5},{8,10},{9,11},{10,... | collective-permute-start | bytes 884744 | tf_op jit(solution)/shard_map/ppermute | solution.py:42
  184.1 14.0 %collective-permute-start.35 = (bf16[112,1920]{1,0:T(8,128)(2,1)S(1)}, bf16[112,1920]{1,0:T(8,128)(2,1)S(1)}, u32[]{:S(2)}, u32[]{:S(2)}) collective-permute-start(bf16[112,1920]{1,0:T(8,128)(2,1)S(1)} %get-tuple-element.264), channel_id=1, source_target_pairs={{0,8},{4,12},{8,0},{12,4},{16,24},{20,28},{24,16},{28,20},{1,9},{5... | collective-permute-start | bytes 1290248 | tf_op jit(solution)/shard_map/ppermute | solution.py:42
  184.2 19.8 %collective-permute-start.36 = (bf16[112,1920]{1,0:T(8,128)(2,1)S(1)}, bf16[112,1920]{1,0:T(8,128)(2,1)S(1)}, u32[]{:S(2)}, u32[]{:S(2)}) collective-permute-start(bf16[112,1920]{1,0:T(8,128)(2,1)S(1)} %get-tuple-element.265), channel_id=1, source_target_pairs={{0,16},{4,20},{8,24},{12,28},{16,0},{20,4},{24,8},{28,12},{1,17},{... | collective-permute-start | bytes 1290248 | tf_op jit(solution)/shard_map/ppermute | solution.py:42
  186.2 19.5 %collective-permute-start.37 = (bf16[112,1920]{1,0:T(8,128)(2,1)S(1)}, bf16[112,1920]{1,0:T(8,128)(2,1)S(1)}, u32[]{:S(2)}, u32[]{:S(2)}) collective-permute-start(bf16[112,1920]{1,0:T(8,128)(2,1)S(1)} %get-tuple-element.266), channel_id=1, source_target_pairs={{0,24},{4,28},{8,16},{12,20},{16,8},{20,12},{24,0},{28,4},{1,25},{... | collective-permute-start | bytes 1290248 | tf_op jit(solution)/shard_map/ppermute | solution.py:42
  (35 other events, 207.2 us)

commit v3 on v2

--- a/solution.py
+++ b/solution.py
@@ -19,6 +19,8 @@
 GROUPS = 8
 BLOCK = D // GROUPS
 LABELS = 16
+MARKS = 48
+MICROS = 450
 BF = jnp.bfloat16
 F32 = jnp.float32
 ROOT_HALF = 0.7071067811865476
@@ -82,22 +84,16 @@
     return [piece] + [swap(piece, "dp", j) for j in range(2, GROUPS, 2)]
 
 
-def core_pieces(chip):
-    pieces = []
-    for piece in chip:
-        pieces += [piece, swap(piece, "dp", 1)]
-    return pieces
-
-
 def gather_rows(piece):
     full = lax.all_gather(piece, "dp", axis=0, tiled=True)
-    return list(full.reshape(GROUPS, D // GROUPS, piece.shape[1]))
-
-
-def place(target, refs, base, source_cols, target_cols):
-    for j, ref in enumerate(refs):
+    full = full.reshape(GROUPS, D // GROUPS, piece.shape[1])
+    return [full[0::2], full[1::2]]
+
+
+def place(target, pair, base, source_cols, target_cols):
+    for j in range(GROUPS):
         start = pl.multiple_of((base ^ j) * BLOCK, 16)
-        target[pl.ds(start, BLOCK), target_cols] = ref[:BLOCK, source_cols]
+        target[pl.ds(start, BLOCK), target_cols] = pair[j % 2][j // 2, :BLOCK, source_cols]
 
 
 def split_rows(result, base, keep, send):
@@ -123,96 +119,160 @@
     )
 
 
-def label_rows(scalars, tokens, segments):
+def pack_inputs(scalars, tables, tokens, segments, up, down, lines, tall):
     rows = tokens.shape[0]
-
-    def body(_, token_ref, segment_ref, out_ref, docs_ref):
-        docs = segment_ref[...].astype(F32)
+    height = tables[0].shape[0]
+    extra = LABELS if lines else 0
+    operands = list(tables) + [tokens, segments, up, down] + lines + ([tall] if lines else [])
+    count = len(operands)
+
+    def body(_, *refs):
+        sources, (send_ref, mine_ref, wide_ref, label_ref, docs_ref), refs = (
+            refs[:count],
+            refs[count : count + 5],
+            refs[count + 5 :],
+        )
+        copies = [pltpu.make_async_copy(a, b, refs[-1].at[k]) for k, (a, b) in enumerate(zip(sources, refs))]
+        for copy in copies:
+            copy.start()
+        for copy in copies:
+            copy.wait()
+        joined = jnp.concatenate([ref[...].astype(F32) for ref in refs[:4]], axis=1).astype(BF)
+        send_ref[...] = joined
+        mine_ref[:height, :HID] = refs[6][...]
+        mine_ref[:height, HID : 2 * HID] = refs[7][...]
+        mine_ref[:height, 2 * HID :] = joined[:, : 3 * QUARTER]
+        wide_ref[:, :HID] = refs[6][...]
+        wide_ref[:, HID:] = refs[7][...]
+        docs = refs[5][...].astype(F32)
         docs_ref[...] = docs
-        out_ref[:rows, :] = token_ref[...]
-        out_ref[rows:, :] = jnp.zeros((LABELS, D), BF)
-        out_ref[rows:, :rows] = jnp.broadcast_to(docs, (LABELS, rows)).astype(BF)
-
-    outs = [struct((rows + LABELS, D), BF), struct((1, rows), F32)]
-    return simple("label_rows", body, scalars, [tokens, segments], outs)
-
-
-def pack_narrow(scalars, tables):
-    rows = tables[0].shape[0]
+        label_ref[:rows, :] = refs[4][...]
+        label_ref[rows:, :] = jnp.zeros((MARKS, D), BF)
+        label_ref[rows:, :rows] = jnp.broadcast_to(docs, (MARKS, rows)).astype(BF)
+        if lines:
+            share = FF // GROUPS
+            table = [ref[...].astype(F32) for ref in refs[8 : 8 + VECS]]
+            table = jnp.concatenate(table, axis=0)
+            table = jnp.concatenate([table, jnp.zeros((VECS, share - BLOCK), F32)], axis=1)
+            line = jnp.broadcast_to(refs[8 + VECS][...].astype(F32), (VECS, share))
+            mine_ref[height:, :] = jnp.zeros((LABELS, 3 * QUARTER + 2 * HID), BF)
+            mine_ref[height:, 2 * HID : 2 * HID + share] = jnp.concatenate([table, line], axis=0).astype(BF)
+
+    outs = [
+        struct((height, D), BF),
+        struct((height + extra, 3 * QUARTER + 2 * HID), BF),
+        struct((height, 2 * HID), BF),
+        struct((rows + MARKS, D), BF),
+        struct((1, rows), F32),
+    ]
+    operands = [pltpu.with_memory_space_constraint(o, pltpu.MemorySpace.HBM) for o in operands]
+    return call(
+        "pack_inputs",
+        body,
+        scalars,
+        operands,
+        [pl.BlockSpec(memory_space=pltpu.MemorySpace.HBM)] * count,
+        outs,
+        [whole(o.shape) for o in outs],
+        (1,),
+        [pltpu.VMEM(o.shape, o.dtype) for o in operands] + [pltpu.SemaphoreType.DMA((count,))],
+    )
+
+
+def split_arrived(scalars, arrived, wide, side, mine):
+    rows, tall = arrived.shape[0], mine.shape[0]
+
+    def body(_, far_ref, wide_ref, side_ref, mine_ref, narrow_ref, out_ref, both_ref):
+        narrow_ref[...] = far_ref[:, : 3 * QUARTER]
+        out_ref[:, : 2 * HID] = wide_ref[...]
+        out_ref[:, 2 * HID :] = side_ref[...]
+        both_ref[:tall, :] = mine_ref[:, 2 * HID :]
+        both_ref[tall:, :] = far_ref[:, : 3 * QUARTER]
+
+    outs = [
+        struct((rows, 3 * QUARTER), BF),
+        struct((rows, 2 * HID + QUARTER), BF),
+        struct((rows + tall, 3 * QUARTER), BF),
+    ]
+    return simple("split_arrived", body, scalars, [arrived, wide, side, mine], outs)
+
+
+def stack_narrow(scalars, mine_chip, far_chip, both_far):
+    tall = mine_chip[0].shape[0]
+    rows = far_chip[0].shape[0]
 
     def body(_, *refs):
-        joined = jnp.concatenate([ref[...].astype(F32) for ref in refs[:-1]], axis=1)
-        refs[-1][...] = joined.astype(BF)
-
-    return simple("pack_narrow", body, scalars, tables, [struct((rows, 3 * QUARTER), BF)])[0]
-
-
-def pack_wide(scalars, up, down, output, output_side):
-    rows = up.shape[0]
-
-    def body(_, up_ref, down_ref, out_ref, side_ref, wide_ref):
-        wide_ref[:, :HID] = up_ref[...]
-        wide_ref[:, HID : 2 * HID] = down_ref[...]
-        sides = [out_ref[...].astype(F32), side_ref[...].astype(F32)]
-        wide_ref[:, 2 * HID :] = jnp.concatenate(sides, axis=1).astype(BF)
-
-    out = struct((rows, 2 * HID + HALF), BF)
-    return simple("pack_wide", body, scalars, [up, down, output, output_side], [out])[0]
-
-
-def pack_columns(scalars, narrow, narrow_far, lines, tall):
-    rows = narrow.shape[0]
-
-    def body(_, near_ref, far_ref, *refs):
         out_ref = refs[-1]
-        for kind in range(3):
-            part = slice(kind * QUARTER, (kind + 1) * QUARTER)
-            both = [near_ref[:, part].astype(F32), far_ref[:, part].astype(F32)]
-            both = jnp.concatenate(both, axis=1).astype(BF)
-            for p in range(3):
-                at = (3 * p + kind) * PAIR
-                out_ref[:rows, at : at + PAIR] = both[:, p * PAIR : (p + 1) * PAIR]
-        if lines:
-            table = jnp.concatenate(
-                [ref[...].astype(F32) for ref in refs[:VECS]] + [jnp.zeros((LABELS - VECS, BLOCK), F32)],
-                axis=0,
-            )
-            out_ref[rows:, :] = jnp.zeros((LABELS, 3 * HALF), BF)
-            out_ref[rows:, :BLOCK] = table.astype(BF)
-            line = jnp.broadcast_to(refs[VECS][...].astype(F32), (LABELS, FF // GROUPS))
-            out_ref[rows:, D:] = line.astype(BF)
-
-    out = struct((rows + (LABELS if lines else 0), 3 * HALF), BF)
-    operands = [narrow, narrow_far] + (lines + [tall] if lines else [])
-    return simple("pack_columns", body, scalars, operands, [out])[0]
-
-
-def pack_feed(scalars, wide, wide_far):
-    rows = wide.shape[0]
-
-    def body(sc, wide_ref, far_ref, out_ref):
-        out_ref[:, : 2 * HID] = wide_ref[:, : 2 * HID]
-        out_ref[:, 2 * HID : 4 * HID] = far_ref[:, : 2 * HID]
+        for k in range(3):
+            out_ref[k, :tall] = refs[k][:, 2 * HID :]
+            out_ref[k, tall:] = refs[3 + k][...]
+        out_ref[3] = refs[6][...]
+
+    shape = (GROUPS // 2, tall + rows, 3 * QUARTER)
+    operands = [*mine_chip, *far_chip, both_far]
+    return simple("stack_narrow", body, scalars, operands, [struct(shape, BF)])[0]
+
+
+def stack_wide(scalars, mine_chip, last, feed_chip):
+    def body(_, *refs):
+        out_ref = refs[-1]
+        for k in range(3):
+            out_ref[k, :, : 2 * HID] = refs[k][:BLOCK, : 2 * HID]
+        out_ref[3, :, : 2 * HID] = refs[3][...]
+        for k in range(4):
+            out_ref[k, :, 2 * HID :] = refs[4 + k][...]
+
+    shape = (GROUPS // 2, BLOCK, 4 * HID + D)
+    return simple("stack_wide", body, scalars, [*mine_chip, last, *feed_chip], [struct(shape, BF)])[0]
+
+
+def pack_feed(scalars, wide_far, first_send, arrived, side):
+    rows = wide_far.shape[0]
+    last = slice(3 * QUARTER, D)
+
+    def body(sc, far_ref, own_ref, arrived_ref, side_ref, out_ref):
+        out_ref[:, : 2 * HID] = far_ref[:, : 2 * HID]
         total = jnp.zeros((rows, D), F32)
-        for k in range(4):
-            ref = (wide_ref, far_ref)[k // 2]
-            at = 2 * HID + (k % 2) * QUARTER
-            part = ref[:, at : at + QUARTER].astype(F32)
-            part = jnp.concatenate([part, jnp.zeros((rows, D - QUARTER), F32)], axis=1)
+        for k, part in enumerate(
+            [own_ref[:, last], side_ref[...], arrived_ref[:, last], far_ref[:, 2 * HID :]]
+        ):
+            part = jnp.concatenate([part.astype(F32), jnp.zeros((rows, D - QUARTER), F32)], axis=1)
             total = total + pltpu.roll(part, (sc[2] ^ k) * QUARTER, 1)
-        out_ref[:, 4 * HID :] = total.astype(BF)
-
-    out = struct((rows, 4 * HID + D), BF)
-    return simple("pack_feed", body, scalars, [wide, wide_far], [out])[0]
-
-
-def qkv_attend(scalars, own, partner, halo_near, halo_far, own_docs, pieces, rows):
-    count = len(pieces)
-    base = 3 * rows
-
-    def body(sc, own_ref, partner_ref, near_ref, far_ref, docs_ref, *refs):
-        weight_refs, refs = refs[:count], refs[count:]
-        q_ref, k_ref, v_ref, ctx_far_ref, ctx_near_ref, x_ref, w_ref, hot_ref, vec_ref, hidden_ref, mask_ref, bias_ref = refs
+        out_ref[:, 2 * HID :] = total.astype(BF)
+
+    out = struct((rows, 2 * HID + D), BF)
+    return simple("pack_feed", body, scalars, [wide_far, first_send, arrived, side], [out])[0]
+
+
+def mark(docs, rows):
+    number = lax.broadcasted_iota(jnp.int32, (LABELS, rows), 0).astype(F32)
+    return jnp.where(jnp.broadcast_to(docs, (LABELS, rows)) == number, 1.0, 0.0).astype(BF)
+
+
+def attend(query, key, value, mask):
+    lane = lax.broadcasted_iota(jnp.int32, (1, PAIR), 1)
+    total = jnp.zeros(query.shape, F32)
+    for head in range(2):
+        part = jnp.where((lane // HEAD_DIM) == head, 1.0, 0.0)
+        mine = (query.astype(F32) * (part * HEAD_DIM**-0.5)).astype(BF)
+        scores = dot_nt(mine, key) + mask
+        expo = jnp.exp(scores - jnp.max(scores, axis=-1, keepdims=True))
+        probs = expo * (1.0 / jnp.sum(expo, axis=-1, keepdims=True))
+        total = total + dot(probs.astype(BF), value) * part
+    return total.astype(BF)
+
+
+def column(height):
+    return pl.BlockSpec((height, PAIR), lambda p, _: (0, p))
+
+
+def attend_pair(scalars, own, partner, own_docs, pieces, rows):
+    base = 2 * rows
+    tall = BLOCK + LABELS
+
+    def body(sc, own_ref, partner_ref, docs_ref, *refs):
+        weight_refs, refs = refs[:2], refs[2:]
+        q_ref, k_ref, v_ref, ctx_ref, x_ref, w_ref, hot_ref, vec_ref, hidden_ref, bias_ref, mask_ref = refs
         step = pl.program_id(0)
 
         @pl.when(step == 0)
@@ -220,37 +280,37 @@
             near = sc[0]
             own_at = pl.multiple_of(near * rows, rows)
             partner_at = pl.multiple_of((1 - near) * rows, rows)
-            number = lax.broadcasted_iota(jnp.int32, (16, rows), 0).astype(F32)
-
-            def mark(line, at):
-                hit = jnp.broadcast_to(line, (16, rows)) == number
-                hot_ref[:, pl.ds(at, rows)] = jnp.where(hit, 1.0, 0.0).astype(BF)
-
             x_ref[pl.ds(own_at, rows), :] = own_ref[...]
             x_ref[pl.ds(partner_at, rows), :] = partner_ref[:rows, :]
-            mark(docs_ref[...], own_at)
-            mark(partner_ref[rows : rows + 1, :rows].astype(F32), partner_at)
-
-            def halo(ref):
-                x_ref[2 * rows :, :] = ref[:rows, :]
-                mark(ref[rows : rows + 1, :rows].astype(F32), 2 * rows)
-
-            pl.when(near == 1)(lambda: halo(near_ref))
-            pl.when(near == 0)(lambda: halo(far_ref))
-            place(w_ref, weight_refs, sc[1], slice(None), slice(None))
+            hot_ref[:, pl.ds(own_at, rows)] = mark(docs_ref[...], rows)
+            docs = partner_ref[rows : rows + 1, :rows].astype(F32)
+            hot_ref[:, pl.ds(partner_at, rows)] = mark(docs, rows)
+            for j in range(GROUPS):
+                at = pl.ds(pl.multiple_of((sc[1] ^ j) * BLOCK, 16), BLOCK)
+                for kind in range(3):
+                    part = slice(kind * QUARTER, (kind + 1) * QUARTER)
+                    both = [weight_refs[j % 2][j // 2, top : top + BLOCK, part] for top in (0, tall)]
+                    both = [half.astype(F32) for half in both]
+                    both = jnp.concatenate(both, axis=1).astype(BF)
+                    for p in range(3):
+                        to = (3 * p + kind) * PAIR
+                        w_ref[at, to : to + PAIR] = both[:, p * PAIR : (p + 1) * PAIR]
             hot = hot_ref[...]
-            mask_ref[...] = (dot_tn(hot[:, : 2 * rows], hot) - 1.0) * MASKED
+            mask_ref[...] = (dot_tn(hot[:, :rows], hot) - 1.0) * MASKED
             vectors = jnp.zeros((LABELS, D), F32)
-            for j, ref in enumerate(weight_refs):
+            for j in range(GROUPS):
                 block = sc[1] ^ j
-                vectors = vectors + pltpu.roll(ref[BLOCK:, :D].astype(F32), block * BLOCK, 1)
+                line = weight_refs[j % 2][j // 2, BLOCK:tall, : FF // GROUPS].astype(F32)
+                table = jnp.where(lax.broadcasted_iota(jnp.int32, line.shape, 1) < BLOCK, line, 0.0)
+                table = jnp.concatenate([table, jnp.zeros((LABELS, D - FF // GROUPS), F32)], axis=1)
+                vectors = vectors + pltpu.roll(table, block * BLOCK, 1)
                 quarter = block // 2
                 for k in range(2):
 
                     @pl.when(quarter == sc[2] ^ (2 * k))
                     def _():
                         to = pl.multiple_of((block % 2) * (HID // 2) + k * HID, 128)
-                        hidden_ref[:, pl.ds(to, HID // 2)] = ref[BLOCK:, D:].astype(F32)
+                        hidden_ref[:, pl.ds(to, HID // 2)] = line[VECS:]
 
             vec_ref[...] = vectors[:VECS]
             lanes = lax.broadcasted_iota(jnp.int32, (VECS, HALF), 1)
@@ -267,36 +327,25 @@
         q_ref[...] = query
         k_ref[...] = key
         v_ref[...] = value
-        lane = lax.broadcasted_iota(jnp.int32, (1, PAIR), 1)
-        for ctx_ref, start, reach in ((ctx_far_ref, 0, 2 * rows), (ctx_near_ref, rows, 3 * rows)):
-            total = jnp.zeros((rows, PAIR), F32)
-            for head in range(2):
-                part = jnp.where((lane // HEAD_DIM) == head, 1.0, 0.0)
-                mine = (query[start : start + rows].astype(F32) * (part * HEAD_DIM**-0.5)).astype(BF)
-                scores = dot_nt(mine, key[:reach]) + mask_ref[start : start + rows, :reach]
-                expo = jnp.exp(scores - jnp.max(scores, axis=-1, keepdims=True))
-                probs = expo * (1.0 / jnp.sum(expo, axis=-1, keepdims=True))
-                total = total + dot(probs.astype(BF), value[:reach]) * part
-            ctx_ref[...] = total.astype(BF)
-
-    column = lambda height: pl.BlockSpec((height, PAIR), lambda p, _: (0, p))
-    operands = [own, partner, halo_near, halo_far, own_docs] + pieces
+        ctx_ref[...] = attend(query[:rows], key, value, mask_ref[...])
+
+    operands = [own, partner, own_docs, *pieces]
     in_specs = [whole(o.shape) for o in operands]
     outs = [
         struct((base, HALF), BF),
         struct((base, HALF), BF),
         struct((base, HALF), BF),
         struct((rows, HALF), BF),
-        struct((rows, HALF), BF),
         struct((base, D), BF),
         struct((D, 3 * HALF), BF),
-        struct((16, base), BF),
+        struct((LABELS, base), BF),
         struct((VECS, D), F32),
-        struct((LABELS, 2 * HID), F32),
+        struct((VECS, 2 * HID), F32),
+        struct((VECS, HALF), F32),
     ]
-    out_specs = [column(base)] * 3 + [column(rows)] * 2 + [whole(o.shape) for o in outs[5:]]
+    out_specs = [column(base)] * 3 + [column(rows)] + [whole(o.shape) for o in outs[4:]]
     return call(
-        "qkv_attend",
+        "attend_pair",
         body,
         scalars,
         operands,
@@ -304,24 +353,72 @@
         outs,
         out_specs,
         (HALF // PAIR,),
-        [pltpu.VMEM((2 * rows, base), F32), pltpu.VMEM((VECS, HALF), F32)],
-        micros=13,
+        [pltpu.VMEM((rows, base), F32)],
+        micros=8,
+    )
+
+
+def attend_halo(scalars, halo_near, halo_far, weight, bias, hot, query, key, value, rows):
+    def body(sc, near_ref, far_ref, w_ref, bias_ref, hot_ref, q_ref, k_ref, v_ref, *refs):
+        halo_refs, (ctx_ref, all_ref, x_ref, mask_ref) = refs[:3], refs[3:]
+
+        @pl.when(pl.program_id(0) == 0)
+        def _():
+            all_ref[:, : 2 * rows] = hot_ref[...]
+
+            def halo(ref):
+                x_ref[...] = ref[:rows, :]
+                all_ref[:, 2 * rows :] = mark(ref[rows : rows + 1, :rows].astype(F32), rows)
+
+            pl.when(sc[0] == 1)(lambda: halo(near_ref))
+            pl.when(sc[0] == 0)(lambda: halo(far_ref))
+            mask_ref[...] = (dot_tn(all_ref[:, rows : 2 * rows], all_ref[...]) - 1.0) * MASKED
+
+        both = dot(x_ref[...], w_ref[...])
+        parts = [
+            (both[:, :PAIR] + bias_ref[0:1, :]).astype(BF),
+            both[:, PAIR : 2 * PAIR].astype(BF),
+            (both[:, 2 * PAIR :] + bias_ref[1:2, :]).astype(BF),
+        ]
+        for ref, part in zip(halo_refs, parts):
+            ref[...] = part
+        keys = jnp.concatenate([k_ref[...], parts[1]], axis=0)
+        values = jnp.concatenate([v_ref[...], parts[2]], axis=0)
+        ctx_ref[...] = attend(q_ref[rows:, :], keys, values, mask_ref[...])
+
+    operands = [halo_near, halo_far, weight, bias, hot, query, key, value]
+    in_specs = [whole(o.shape) for o in operands]
+    in_specs[2] = pl.BlockSpec((D, 3 * PAIR), lambda p, _: (0, p))
+    in_specs[3] = column(VECS)
+    in_specs[5:] = [column(2 * rows)] * 3
+    outs = [struct((rows, HALF), BF)] * 4 + [struct((LABELS, 3 * rows), BF)]
+    return call(
+        "attend_halo",
+        body,
+        scalars,
+        operands,
+        in_specs,
+        outs,
+        [column(rows)] * 4 + [whole((LABELS, 3 * rows))],
+        (HALF // PAIR,),
+        [pltpu.VMEM((rows, D), BF), pltpu.VMEM((rows, 3 * rows), F32)],
+        micros=6,
     )
 
 
 def feed_forward(scalars, block, ctx_mine, ctx_partner, x, vecs, up_bias, weights, rows):
     count = len(weights)
-    fresh = count == GROUPS
+    fresh = len(weights[0].shape) == 3
 
     def body(sc, mine_ref, partner_ref, x_ref, vec_ref, bias_ref, *refs):
         weight_refs, refs = refs[:count], refs[count:]
         (norm_ref, inv_ref, first_ref, gate_ref, active_ref, part_ref), refs = refs[:6], refs[6:]
         if fresh:
             up_ref, down_ref, out_ref, other_ref, full_ref = refs
-            place(up_ref, weight_refs, sc[1], slice(0, HID), slice(0, HID))
-            place(down_ref, weight_refs, sc[1], slice(HID, 2 * HID), slice(0, HID))
-            place(up_ref, weight_refs, sc[1], slice(2 * HID, 3 * HID), slice(HID, 2 * HID))
-            place(down_ref, weight_refs, sc[1], slice(3 * HID, 4 * HID), slice(HID, 2 * HID))
+            for k in range(2):
+                at, to = 2 * k * HID, slice(k * HID, (k + 1) * HID)
+                place(up_ref, weight_refs, sc[1], slice(at, at + HID), to)
+                place(down_ref, weight_refs, sc[1], slice(at + HID, at + 2 * HID), to)
             place(full_ref, weight_refs, sc[1], slice(4 * HID, 4 * HID + D), slice(None))
             for ref, flip in ((out_ref, 0), (other_ref, 1)):
                 for k in range(2):
@@ -595,12 +692,17 @@
     )
 
 
-def attend_backward(scalars, query, key, value, grad_blocks, hot, weight, rows):
+def attend_backward(scalars, pair, halo, grad_blocks, hot, weight, rows):
     base = 3 * rows
     steps = HALF // PAIR
 
-    def body(sc, q_ref, k_ref, v_ref, far_ref, near_ref, halo_ref, hot_ref, w_ref, *refs):
-        out_ref, keep_ref, send_ref, sums_ref, mask_ref, key_ref, value_ref, acc_ref = refs
+    def body(sc, *refs):
+        pair_refs, halo_refs, refs = refs[:3], refs[3:6], refs[6:]
+        far_ref, near_ref, halo_ref, hot_ref, w_ref, *refs = refs
+        out_ref, keep_ref, send_ref, sums_ref, mask_ref, key_ref, value_ref, acc_ref, q_ref, k_ref, v_ref = refs
+        for target, first_part, last_part in zip((q_ref, k_ref, v_ref), pair_refs, halo_refs):
+            target[: 2 * rows, :] = first_part[...]
+            target[2 * rows :, :] = last_part[...]
         step = pl.program_id(0)
 
         @pl.when(step == 0)
@@ -655,9 +757,8 @@
             other = acc_ref[pl.ds(pl.multiple_of((1 - near) * rows, rows), rows), :]
             send_ref[...] = other.astype(BF)
 
-    column = lambda height: pl.BlockSpec((height, PAIR), lambda p, _: (0, p))
-    operands = [query, key, value, *grad_blocks, hot, weight]
-    in_specs = [column(base)] * 3 + [column(rows)] * 3 + [whole(hot.shape)]
+    operands = [*pair, *halo, *grad_blocks, hot, weight]
+    in_specs = [column(2 * rows)] * 3 + [column(rows)] * 6 + [whole(hot.shape)]
     in_specs += [pl.BlockSpec((D, 3 * PAIR), lambda p, _: (0, p))]
     outs = [struct((2 * rows, 3 * HALF), BF), struct((rows, D), F32), struct((rows, D), BF)]
     outs += [struct((8, 3 * HALF), F32)]
@@ -672,7 +773,7 @@
         pltpu.VMEM((2 * rows, PAIR), F32),
         pltpu.VMEM((2 * rows, PAIR), F32),
         pltpu.VMEM((2 * rows, D), F32),
-    ]
+    ] + [pltpu.VMEM((base, PAIR), BF)] * 3
     return call(
         "attend_backward",
         body,
@@ -683,7 +784,7 @@
         out_specs,
         (steps,),
         scratch,
-        micros=18,
+        micros=MICROS,
     )
 
 
@@ -898,19 +999,8 @@
     base = lax.axis_index("dp") if direct else 0
     scalars = jnp.stack([near, base, place_z]).astype(jnp.int32)
 
-    narrow = pack_narrow(scalars, [query_weight, key_weight, value_weight])
-    narrow_far = swap(narrow, "seq", 2)
-    output_side = swap(output_weight, "seq", 1)
     own = tokens[0]
-    labelled, own_docs = label_rows(scalars, own, segments)
-    wide = pack_wide(scalars, up_weight, down_weight.T, output_weight, output_side)
-    wide_far = swap(wide, "seq", 2)
-    partner = swap(labelled, "seq", 1)
-    narrow_far, labelled = together(narrow_far, labelled)
-    halo_near = lax.ppermute(labelled, "seq", [(1, 2), (2, 1)])
-    halo_far = lax.ppermute(labelled, "seq", [(1, 3), (2, 0)])
     cot_own = cotangent[0]
-
     lines = [
         query_bias,
         value_bias,
@@ -922,20 +1012,46 @@
         second_shift,
     ]
     lines = [line[None] for line in lines] if direct else []
-    columns = pack_columns(scalars, narrow, narrow_far, lines, up_bias[None])
-    feed_piece = pack_feed(scalars, wide, wide_far)
-
+    first_send, mine, wide, labelled, own_docs = pack_inputs(
+        scalars,
+        [query_weight, key_weight, value_weight, output_weight],
+        own,
+        segments,
+        up_weight,
+        down_weight.T,
+        lines,
+        up_bias[None],
+    )
+    arrived = swap(first_send, "seq", 2)
+    side = swap(output_weight, "seq", 1)
     if direct:
-        chip = chip_pieces(columns)
-        projection_pieces, feed_piece = together(core_pieces(chip), feed_piece)
-        feed_chip = chip_pieces(feed_piece)
+        mine_chip = [mine, swap(mine, "dp", 2), swap(mine, "dp", 4)]
+        labelled, side, mine_chip, arrived = together(labelled, side, mine_chip, arrived)
     else:
-
-        def label(table, line):
-            table = jnp.pad(table, ((0, LABELS - table.shape[0]), (0, D - table.shape[1])))
-            line = jnp.pad(line[None], ((0, LABELS - 1), (0, 0)))
-            return jnp.concatenate([table, line], axis=1)
-
+        arrived, labelled, side = together(arrived, labelled, side)
+    narrow_far, wide_send, both = split_arrived(scalars, arrived, wide, side, mine)
+    wide_far = swap(wide_send, "seq", 2)
+    if direct:
+        far_chip = [narrow_far, swap(narrow_far, "dp", 2), swap(narrow_far, "dp", 4)]
+        both_far = swap(both, "dp", 6)
+        mine_chip, labelled, cot_own, wide, far_chip, both_far, wide_far = together(
+            mine_chip, labelled, cot_own, wide, far_chip, both_far, wide_far
+        )
+        stacked = stack_narrow(scalars, mine_chip, far_chip, both_far)
+        pieces = [stacked, swap(stacked, "dp", 1)]
+    partner = swap(labelled, "seq", 1)
+    halo_near = lax.ppermute(labelled, "seq", [(1, 2), (2, 1)])
+    if direct:
+        feed_piece = pack_feed(scalars, wide_far, first_send, arrived, side)
+        feed_chip = [feed_piece, swap(feed_piece, "dp", 2), swap(feed_piece, "dp", 4)]
+        wide, pieces, partner, feed_chip, halo_near = together(
+            wide, pieces, partner, feed_chip, halo_near
+        )
+        feed_chip = feed_chip + [swap(feed_chip[0], "dp", 6)]
+        wide_last = swap(wide, "dp", 6)
+    halo_far = lax.ppermute(halo_near, "seq", [(1, 0), (2, 3)])
+    if not direct:
+        share = FF // GROUPS
         vectors = jnp.stack(
             [
                 query_bias,
@@ -949,12 +1065,20 @@
             ]
         )
         lines = lax.all_gather(vectors, "dp", axis=1, tiled=True).reshape(VECS, GROUPS, BLOCK)
-        hidden_lines = lax.all_gather(up_bias, "dp", axis=0, tiled=True).reshape(GROUPS, -1)
-        projection_pieces = [
-            jnp.concatenate([block, label(lines[:, k], hidden_lines[k])], axis=0)
-            for k, block in enumerate(gather_rows(columns))
+        lines = jnp.pad(lines, ((0, 0), (0, 0), (0, share - BLOCK)))
+        tall = lax.all_gather(up_bias, "dp", axis=0, tiled=True).reshape(1, GROUPS, share)
+        lines = jnp.concatenate([lines, jnp.broadcast_to(tall, (VECS, GROUPS, share))], axis=0)
+        lines = jnp.pad(lines, ((0, 0), (0, 0), (0, 3 * QUARTER - share)))
+        lines = lines.transpose(1, 0, 2)
+        gathered = gather_rows(mine)
+        pieces = [
+            jnp.concatenate([half[:, :, 2 * HID :], lines[k::2], far], axis=1)
+            for k, (half, far) in enumerate(zip(gathered, gather_rows(narrow_far)))
         ]
-        feed_chip = gather_rows(feed_piece)
+        feed = gather_rows(pack_feed(scalars, wide_far, first_send, arrived, side))
+        weights = [
+            jnp.concatenate([half[:, :, : 2 * HID], far], axis=2) for half, far in zip(gathered, feed)
+        ]
 
     def rows_of(keep, send):
         return jnp.stack([keep, send], axis=1).reshape(GROUPS, -1, keep.shape[2]).astype(F32)
@@ -965,15 +1089,21 @@
     def scattered(table):
         return [lax.psum_scatter(table, "dp", scatter_dimension=0, tiled=True)]
 
-    query, key, value, *ctx_mine, x, weight, hot, vecs, hidden_bias = qkv_attend(
-        scalars, own, partner, halo_near, halo_far, own_docs, projection_pieces, rows
-    )
-    ctx_mine, feed_chip[1:3], cot_own = together(ctx_mine, feed_chip[1:3], cot_own)
-    ctx_partner = [None, None]
+    *pair, ctx_far, x, weight, hot, vecs, hidden_bias, bias = attend_pair(
+        scalars, own, partner, own_docs, pieces, rows
+    )
+    if direct:
+        pair, ctx_far, cot_own, halo_far = together(pair, ctx_far, cot_own, halo_far)
+    *halo, ctx_near, hot = attend_halo(scalars, halo_near, halo_far, weight, bias, hot, *pair, rows)
+    ctx_mine = [ctx_far, ctx_near]
+    ctx_partner = [swap(ctx_far, "seq", 1), None]
+    if direct:
+        ctx_mine[1], ctx_partner[0], wide_last, feed_chip = together(
+            ctx_mine[1], ctx_partner[0], wide_last, feed_chip
+        )
+        stacked = stack_wide(scalars, mine_chip, wide_last, feed_chip)
+        weights = [stacked, swap(stacked, "dp", 1)]
     ctx_partner[1] = swap(ctx_mine[1], "seq", 1)
-    ctx_partner[0] = swap(ctx_mine[0], "seq", 1)
-    ctx_partner, feed_chip = together(ctx_partner, feed_chip)
-    weights = core_pieces(feed_chip) if direct else feed_chip
     cot_partner = swap(cot_own, "seq", 1)
 
     forward, slopes, part_far = [None, None], [None, None], [None, None]
@@ -1035,18 +1165,13 @@
     halo_grad = swap(halo_send, "seq", 2)
     if direct:
         feed_sums = combine(scalars, feed_parts[0], swap(feed_parts[1], "dp", 1))
-        feed_sums[3], halo_grad = together(feed_sums[3], halo_grad)
-        feed_sums, first_part_far[0] = together(feed_sums, first_part_far[0])
         feed_sums = spread(feed_sums)
     else:
         feed_sums = scattered(rows_of(*feed_parts).reshape(D, -1))
     own_grad, sums_one = finish(0)
 
     grads, input_keep, input_send, sums_projection = attend_backward(
-        scalars, query, key, value, [*ctx_grad, halo_grad], hot, weight, rows
-    )
-    grads, sums_projection, input_send, feed_sums[1:3] = together(
-        grads, sums_projection, input_send, feed_sums[1:3]
+        scalars, pair, halo, [*ctx_grad, halo_grad], hot, weight, rows
     )
     input_far = swap(input_send, "seq", 1)
     small = small_sums(scalars, sums_one, sums_two, sums_hidden, sums_projection)

time: 219 us -> 197 us (0.90)
  waiting for transfers between devices: 94.8 us -> 76.1 us
  local copies, waits for them, and re-layouts: 13.7 us -> 2.38 us
  starting transfers between devices: 42.5 us -> 47 us
  Pallas kernels: 65.4 us -> 69.3 us
    ppermute x1, waiting for transfers between devices: 14.6 us -> 2.54 us  [per_device(): halo_far = lax.ppermute(halo_near, 'seq', [(1, 0), (2, 3)])]
    unnamed x36 -> x4, local copies, waits for them, and re-layouts: 11.9 us -> 0.01 us
    ppermute x39 -> x36, waiting for transfers between devices: 80.2 us -> 73.5 us  [swap(): return lax.ppermute(value, axis, [(k, k ^ mask) for k in range(count)])]
    ppermute x39 -> x36, starting transfers between devices: 40.6 us -> 45 us  [swap(): return lax.ppermute(value, axis, [(k, k ^ mask) for k in range(count)])]
    pallas_call x25 -> x26, Pallas kernels: 65.4 us -> 69.3 us  [call(): pl.pallas_call(body, out_shape=outs, grid_spec=spec, compiler_params=para...]
  transfers between devices with their start and end apart: 41 -> 38, of which waited for: 22 -> 19; matrix products, arithmetic and copies ran while one was open for 1% -> 1% of each run, Pallas kernels for 29% -> 32%
where the time goes in v3:
time: 197 us
  waiting for transfers between devices  76.1 us (39%)
  Pallas kernels  69.3 us (35%)
  starting transfers between devices  47 us (24%)
  local copies, waits for them, and re-layouts  2.38 us (1%)
    ppermute x36, waiting for transfers between devices, swap(): return lax.ppermute(value, axis, [(k, k ^ mask) for k in range(count)])  73.5 us
    pallas_call x26, Pallas kernels, call(): pl.pallas_call(body, out_shape=outs, grid_spec=spec, compiler_params=para...  69.3 us
    ppermute x36, starting transfers between devices, swap(): return lax.ppermute(value, axis, [(k, k ^ mask) for k in range(count)])  45 us
  transfers between devices with their start and end apart: 38, of which 19 were waited for; matrix products, arithmetic and copies ran while one was open for 1% of the time, Pallas kernels for 32%

profile of v3, /device:TPU:0, one launch (start us, length us, event | category | flops | bytes accessed | tf_op | source)
XLA Modules:
  0.0 196.8 jit_solution(9758438353953451884)
XLA Ops:
  4.1 3.0 %collective-permute-start.1 = (bf16[112,2112]{1,0:T(8,128)(2,1)S(1)}, bf16[112,2112]{1,0:T(8,128)(2,1)S(1)}, u32[]{:S(2)}, u32[]{:S(2)}) collective-permute-start(bf16[112,2112]{1,0:T(8,128)(2,1)S(1)} %get-tuple-element.183.mine_ref.refs_0_), channel_id=1, source_target_pairs={{0,8},{4,12},{8,0},{12,4},{16,24},{20,28},{24,16},{28,20},{1,9},{5... | collective-permute-start | bytes 1419272 | tf_op jit(solution)/shard_map/ppermute | solution.py:44
  8.6 2.6 %collective-permute-start.3 = (bf16[96,768]{1,0:T(8,128)(2,1)S(1)}, bf16[96,768]{1,0:T(8,128)(2,1)S(1)}, u32[]{:S(2)}, u32[]{:S(2)}) collective-permute-start(bf16[96,768]{1,0:T(8,128)(2,1)S(1)} %get-tuple-element.171.own_ref), channel_id=1, source_target_pairs={{0,2},{1,3},{2,0},{3,1},{4,6},{5,7},{6,4},{7,5},{8,10},{9,11},{10,... | collective-permute-start | bytes 442376 | tf_op jit(solution)/shard_map/ppermute | solution.py:44
  12.7 2.7 %collective-permute-done.side_ref = bf16[96,192]{1,0:T(8,128)(2,1)S(1)} collective-permute-done((bf16[96,192]{1,0:T(8,128)(2,1)}, bf16[96,192]{1,0:T(8,128)(2,1)S(1)}, u32[]{:S(2)}, u32[]{:S(2)}) %collective-permute-start) | collective-permute-done | bytes 36896 | tf_op jit(solution)/shard_map/ppermute | solution.py:44
  20.3 2.7 %collective-permute-start.7 = (bf16[96,1728]{1,0:T(8,128)(2,1)S(1)}, bf16[96,1728]{1,0:T(8,128)(2,1)S(1)}, u32[]{:S(2)}, u32[]{:S(2)}) collective-permute-start(bf16[96,1728]{1,0:T(8,128)(2,1)S(1)} %get-tuple-element.181), channel_id=1, source_target_pairs={{0,2},{1,3},{2,0},{3,1},{4,6},{5,7},{6,4},{7,5},{8,10},{9,11},{10,... | collective-permute-start | bytes 995336 | tf_op jit(solution)/shard_map/ppermute | solution.py:44
  26.4 6.8 %collective-permute-done.4.refs_4_ = bf16[96,576]{1,0:T(8,128)(2,1)S(1)} collective-permute-done((bf16[96,576]{1,0:T(8,128)(2,1)S(1)}, bf16[96,576]{1,0:T(8,128)(2,1)S(1)}, u32[]{:S(2)}, u32[]{:S(2)}) %collective-permute-start.4) | collective-permute-done | bytes 110624 | tf_op jit(solution)/shard_map/ppermute | solution.py:44
  33.2 4.0 %collective-permute-done.7.far_ref = bf16[96,1728]{1,0:T(8,128)(2,1)S(1)} collective-permute-done((bf16[96,1728]{1,0:T(8,128)(2,1)S(1)}, bf16[96,1728]{1,0:T(8,128)(2,1)S(1)}, u32[]{:S(2)}, u32[]{:S(2)}) %collective-permute-start.7) | collective-permute-done | bytes 331808 | tf_op jit(solution)/shard_map/ppermute | solution.py:44
  43.6 10.2 %collective-permute-done.10.refs_5_ = bf16[96,2304]{1,0:T(8,128)(2,1)S(1)} collective-permute-done((bf16[96,2304]{1,0:T(8,128)(2,1)S(1)}, bf16[96,2304]{1,0:T(8,128)(2,1)S(1)}, u32[]{:S(2)}, u32[]{:S(2)}) %collective-permute-start.10) | collective-permute-done | bytes 442400 | tf_op jit(solution)/shard_map/ppermute | solution.py:44
  55.4 2.4 %collective-permute-start.16 = (bf16[96,2304]{1,0:T(8,128)(2,1)S(1)}, bf16[96,2304]{1,0:T(8,128)(2,1)S(1)}, u32[]{:S(2)}, u32[]{:S(2)}) collective-permute-start(bf16[96,2304]{1,0:T(8,128)(2,1)S(1)} %pack_feed.1.refs_4_), channel_id=1, source_target_pairs={{0,24},{4,28},{8,16},{12,20},{16,8},{20,12},{24,0},{28,4},{1,25},{... | collective-permute-start | bytes 1327112 | tf_op jit(solution)/shard_map/ppermute | solution.py:44
  58.4 6.7 %attend_pair.1 = (bf16[512,384]{1,0:T(8,128)(2,1)S(1)}, bf16[512,384]{1,0:T(8,128)(2,1)S(1)}, bf16[512,384]{1,0:T(8,128)(2,1)S(1)}, bf16[256,384]{1,0:T(8,128)(2...) custom-call(s32[3]{0:T(128)S(1)} %pad_add_fusion._.sc, ...), custom_call_target="tpu_custom_call" | custom-call | flops 80000000 | bytes 1024 | tf_op jit(solution)/shard_map/attend_pair/pallas_call | solution.py:67
  65.1 2.5 %collective-permute-done.13.far_ref = bf16[304,768]{1,0:T(8,128)(2,1)S(1)} collective-permute-done((bf16[304,768]{1,0:T(8,128)(2,1)S(1)}, bf16[304,768]{1,0:T(8,128)(2,1)S(1)}, u32[]{:S(2)}, u32[]{:S(2)}) %collective-permute-start.13) | collective-permute-done | bytes 466976 | tf_op jit(solution)/shard_map/ppermute | solution.py:1052
  67.9 6.1 %attend_halo.1 = (bf16[256,384]{1,0:T(8,128)(2,1)S(1)}, bf16[256,384]{1,0:T(8,128)(2,1)S(1)}, bf16[256,384]{1,0:T(8,128)(2,1)S(1)}, bf16[256,384]{1,0:T(8,128)(2,1)S(1)}, bf16[16,768]{1,0:T(8,128)(2,1)S(1)}) custom-call(s32[3]{0:T(128)S(1)} %pad_add_fusion._.sc, bf16[304,768]{1,0:T(8,128)(2,1)S(1)} %collective-permute-done.12.near_ref, ...), custom_call_target="tpu_custom_call" | custom-call | flops 60000000 | bytes 1024 | tf_op jit(solution)/shard_map/attend_halo/pallas_call | solution.py:67
  77.2 5.6 %collective-permute-done.17.partner_ref.refs_4_ = bf16[256,384]{1,0:T(8,128)(2,1)S(1)} collective-permute-done((bf16[256,384]{1,0:T(8,128)(2,1)S(1)}, bf16[256,384]{1,0:T(8,128)(2,1)S(1)}, u32[]{:S(2)}, u32[]{:S(2)}) %collective-permute-start.17) | collective-permute-done | bytes 196640 | tf_op jit(solution)/shard_map/ppermute | solution.py:44
  82.9 3.2 %feed_forward.2 = (f32[256,768]{1,0:T(8,128)S(1)}, f32[256,128]{1,0:T(8,128)S(1)}, bf16[256,768]{1,0:T(8,128)(2,1)S(1)}, f32[256,1536]{1,0:T(8,128)S(1)}, bf16[2...) custom-call(s32[3]{0:T(128)S(1)} %pad_add_fusion._.sc, ...), custom_call_target="tpu_custom_call" | custom-call | flops 60000000 | bytes 1024 | tf_op jit(solution)/shard_map/feed_forward/pallas_call | solution.py:67
  88.1 2.9 %feed_forward.3 = (f32[256,768]{1,0:T(8,128)S(1)}, f32[256,128]{1,0:T(8,128)S(1)}, bf16[256,768]{1,0:T(8,128)(2,1)S(1)}, f32[256,1536]{1,0:T(8,128)S(1)}, bf16[2...) custom-call(s32[3]{0:T(128)S(1)} %pad_add_fusion._.sc, bf16[256,384]{1,0:T(8,128)(2,1)S(1)} %get-tuple-element.210.mine_ref.refs_0_, ...), custom_call_target="tpu_custom_call" | custom-call | flops 60000000 | bytes 1024 | tf_op jit(solution)/shard_map/feed_forward/pallas_call | solution.py:67
  92.3 7.5 %collective-permute-done.19.recv_ref = bf16[256,768]{1,0:T(8,128)(2,1)S(1)} collective-permute-done((bf16[256,768]{1,0:T(8,128)(2,1)S(1)}, bf16[256,768]{1,0:T(8,128)(2,1)S(1)}, u32[]{:S(2)}, u32[]{:S(2)}) %collective-permute-start.19) | collective-permute-done | bytes 393248 | tf_op jit(solution)/shard_map/ppermute | solution.py:44
  99.7 2.9 %second_norm.2 = (f32[256,768]{1,0:T(8,128)S(1)}, bf16[256,768]{1,0:T(8,128)(2,1)S(1)}, bf16[256,1536]{1,0:T(8,128)(2,1)S(1)}, bf16[256,768]{1,0:T(8,128)(2,1)S(...) custom-call(s32[3]{0:T(128)S(1)} %pad_add_fusion._.sc, ...), custom_call_target="tpu_custom_call" | custom-call | flops 50000000 | bytes 1024 | tf_op jit(solution)/shard_map/second_norm/pallas_call | solution.py:67
  108.2 3.8 %second_norm.3 = (f32[256,768]{1,0:T(8,128)S(1)}, bf16[256,768]{1,0:T(8,128)(2,1)S(1)}, bf16[256,1536]{1,0:T(8,128)(2,1)S(1)}, bf16[256,768]{1,0:T(8,128)(2,1)S(...) custom-call(s32[3]{0:T(128)S(1)} %pad_add_fusion._.sc, ...), custom_call_target="tpu_custom_call" | custom-call | flops 50000000 | bytes 1024 | tf_op jit(solution)/shard_map/second_norm/pallas_call | solution.py:67
  111.9 5.0 %feed_forward_grads.1 = (bf16[4,96,3072]{2,1,0:T(8,128)(2,1)S(1)}, bf16[4,96,3072]{2,1,0:T(8,128)(2,1)S(1)}) custom-call(s32[3]{0:T(128)S(1)} %pad_add_fusion._.sc, bf16[256,768]{1,0:T(8,128)(2,1)S(1)} %get-tuple-element.250.refs_0_, bf16[256,1536]{1,0:T(8,128)(2,1)S(1)} %get-tuple-element.242.refs_1_, bf16[256,768]{1,0:T(8,128)(2,1)S(1)} %get-tuple-element.241.refs_2_, ...), custom_call_target="tpu_custom_call" | custom-call | flops 80000000 | bytes 1024 | tf_op jit(solution)/shard_map/feed_forward_grads/pallas_call | solution.py:67
  127.1 5.7 %collective-permute-done.23.recv_ref = bf16[256,768]{1,0:T(8,128)(2,1)S(1)} collective-permute-done((bf16[256,768]{1,0:T(8,128)(2,1)S(1)}, bf16[256,768]{1,0:T(8,128)(2,1)S(1)}, u32[]{:S(2)}, u32[]{:S(2)}) %collective-permute-start.23) | collective-permute-done | bytes 393248 | tf_op jit(solution)/shard_map/ppermute | solution.py:44
  134.6 16.0 %attend_backward.1 = (bf16[512,1152]{1,0:T(8,128)(2,1)S(1)}, f32[256,768]{1,0:T(8,128)S(1)}, bf16[256,768]{1,0:T(8,128)(2,1)S(1)}, f32[8,1152]{1,0:T(8,128)S(1)}) custom-call(s32[3]{0:T(128)S(1)} %pad_add_fusion._.sc, bf16[512,384]{1,0:T(8,128)(2,1)S(1)} %get-tuple-element.206.q_ref.refs_0_, bf16[512,384]{1,0:T(8,128)(2,1)S(1)} %get-tuple-element.207.k_ref.refs_1_, ...), custom_call_target="tpu_custom_call" | custom-call | flops 4499999744 | bytes 1024 | tf_op jit(solution)/shard_map/attend_backward/pallas_call | solution.py:67
  152.0 2.9 %projection_grads.1 = (bf16[4,96,1152]{2,1,0:T(8,128)(2,1)S(1)}, bf16[4,96,1152]{2,1,0:T(8,128)(2,1)S(1)}) custom-call(s32[3]{0:T(128)S(1)} %pad_add_fusion._.sc, bf16[512,768]{1,0:T(8,128)(2,1)S(1)} %get-tuple-element.216.x_ref, bf16[512,1152]{1,0:T(8,128)(2,1)S(1)} %get-tuple-element.273.grad_ref), custom_call_target="tpu_custom_call" | custom-call | flops 50000000 | bytes 1024 | tf_op jit(solution)/shard_map/projection_grads/pallas_call | solution.py:67
  166.5 4.5 %collective-permute-done.36 = bf16[256,768]{1,0:T(8,128)(2,1)S(1)} collective-permute-done((bf16[256,768]{1,0:T(8,128)(2,1)S(1)}, bf16[256,768]{1,0:T(8,128)(2,1)S(1)}, u32[]{:S(2)}, u32[]{:S(2)}) %collective-permute-start.36) | collective-permute-done | bytes 393248 | tf_op jit(solution)/shard_map/ppermute | solution.py:44
  172.0 8.5 %collective-permute-done.35.recv_ref = bf16[96,1536]{1,0:T(8,128)(2,1)S(1)} collective-permute-done((bf16[96,1536]{1,0:T(8,128)(2,1)S(1)}, bf16[96,1536]{1,0:T(8,128)(2,1)S(1)}, u32[]{:S(2)}, u32[]{:S(2)}) %collective-permute-start.35) | collective-permute-done | bytes 294944 | tf_op jit(solution)/shard_map/ppermute | solution.py:44
  185.6 8.7 %collective-permute-done.37.recv_ref = bf16[112,768]{1,0:T(8,128)(2,1)S(1)} collective-permute-done((bf16[112,768]{1,0:T(8,128)(2,1)S(1)}, bf16[112,768]{1,0:T(8,128)(2,1)S(1)}, u32[]{:S(2)}, u32[]{:S(2)}) %collective-permute-start.37) | collective-permute-done | bytes 172064 | tf_op jit(solution)/shard_map/ppermute | solution.py:44
  (87 shorter events, 69.0 us)
Async XLA Ops:
  4.1 14.1 %collective-permute-start.1 = (bf16[112,2112]{1,0:T(8,128)(2,1)S(1)}, bf16[112,2112]{1,0:T(8,128)(2,1)S(1)}, u32[]{:S(2)}, u32[]{:S(2)}) collective-permute-start(bf16[112,2112]{1,0:T(8,128)(2,1)S(1)} %get-tuple-element.183.mine_ref.refs_0_), channel_id=1, source_target_pairs={{0,8},{4,12},{8,0},{12,4},{16,24},{20,28},{24,16},{28,20},{1,9},{5... | collective-permute-start | bytes 1419272 | tf_op jit(solution)/shard_map/ppermute | solution.py:44
  7.1 12.6 %collective-permute-start.2 = (bf16[112,2112]{1,0:T(8,128)(2,1)S(1)}, bf16[112,2112]{1,0:T(8,128)(2,1)S(1)}, u32[]{:S(2)}, u32[]{:S(2)}) collective-permute-start(bf16[112,2112]{1,0:T(8,128)(2,1)S(1)} %get-tuple-element.183.mine_ref.refs_0_), channel_id=1, source_target_pairs={{0,16},{4,20},{8,24},{12,28},{16,0},{20,4},{24,8},{28,12},{1,17},{... | collective-permute-start | bytes 1419272 | tf_op jit(solution)/shard_map/ppermute | solution.py:44
  20.3 16.9 %collective-permute-start.7 = (bf16[96,1728]{1,0:T(8,128)(2,1)S(1)}, bf16[96,1728]{1,0:T(8,128)(2,1)S(1)}, u32[]{:S(2)}, u32[]{:S(2)}) collective-permute-start(bf16[96,1728]{1,0:T(8,128)(2,1)S(1)} %get-tuple-element.181), channel_id=1, source_target_pairs={{0,2},{1,3},{2,0},{3,1},{4,6},{5,7},{6,4},{7,5},{8,10},{9,11},{10,... | collective-permute-start | bytes 995336 | tf_op jit(solution)/shard_map/ppermute | solution.py:44
  37.8 16.3 %collective-permute-start.8 = (bf16[4,208,576]{2,1,0:T(8,128)(2,1)S(1)}, bf16[4,208,576]{2,1,0:T(8,128)(2,1)S(1)}, u32[]{:S(2)}, u32[]{:S(2)}) collective-permute-start(bf16[4,208,576]{2,1,0:T(8,128)(2,1)S(1)} %stack_narrow.1.refs_0_), channel_id=1, source_target_pairs={{0,4},{4,0},{8,12},{12,8},{16,20},{20,16},{24,28},{28,24},{1,5},{5... | collective-permute-start | bytes 2875400 | tf_op jit(solution)/shard_map/ppermute | solution.py:44
  37.9 16.2 %collective-permute-start.12 = (bf16[304,768]{1,0:T(8,128)(2,1)S(1)}, bf16[304,768]{1,0:T(8,128)(2,1)S(1)}, u32[]{:S(2)}, u32[]{:S(2)}) collective-permute-start(bf16[304,768]{1,0:T(8,128)(2,1)S(1)} %get-tuple-element.190), channel_id=1, source_target_pairs={{1,2},{2,1},{5,6},{6,5},{9,10},{10,9},{13,14},{14,13},{17,18},{18,... | collective-permute-start | bytes 1400840 | tf_op jit(solution)/shard_map/ppermute | solution.py:1043
  38.6 15.5 %collective-permute-start.9 = (bf16[304,768]{1,0:T(8,128)(2,1)S(1)}, bf16[304,768]{1,0:T(8,128)(2,1)S(1)}, u32[]{:S(2)}, u32[]{:S(2)}) collective-permute-start(bf16[304,768]{1,0:T(8,128)(2,1)S(1)} %get-tuple-element.190), channel_id=1, source_target_pairs={{0,1},{1,0},{2,3},{3,2},{4,5},{5,4},{6,7},{7,6},{8,9},{9,8},{10,11... | collective-permute-start | bytes 1400840 | tf_op jit(solution)/shard_map/ppermute | solution.py:44
  41.4 12.3 %collective-permute-start.10 = (bf16[96,2304]{1,0:T(8,128)(2,1)S(1)}, bf16[96,2304]{1,0:T(8,128)(2,1)S(1)}, u32[]{:S(2)}, u32[]{:S(2)}) collective-permute-start(bf16[96,2304]{1,0:T(8,128)(2,1)S(1)} %pack_feed.1.refs_4_), channel_id=1, source_target_pairs={{0,8},{4,12},{8,0},{12,4},{16,24},{20,28},{24,16},{28,20},{1,9},{5... | collective-permute-start | bytes 1327112 | tf_op jit(solution)/shard_map/ppermute | solution.py:44
  54.1 13.6 %collective-permute-start.13 = (bf16[304,768]{1,0:T(8,128)(2,1)S(1)}, bf16[304,768]{1,0:T(8,128)(2,1)S(1)}, u32[]{:S(2)}, u32[]{:S(2)}) collective-permute-start(bf16[304,768]{1,0:T(8,128)(2,1)S(1)} %collective-permute-done.12.near_ref), channel_id=1, source_target_pairs={{1,0},{2,3},{5,4},{6,7},{9,8},{10,11},{13,12},{14,15},{17,16},{18,... | collective-permute-start | bytes 1400840 | tf_op jit(solution)/shard_map/ppermute | solution.py:1052
  55.4 18.6 %collective-permute-start.16 = (bf16[96,2304]{1,0:T(8,128)(2,1)S(1)}, bf16[96,2304]{1,0:T(8,128)(2,1)S(1)}, u32[]{:S(2)}, u32[]{:S(2)}) collective-permute-start(bf16[96,2304]{1,0:T(8,128)(2,1)S(1)} %pack_feed.1.refs_4_), channel_id=1, source_target_pairs={{0,24},{4,28},{8,16},{12,20},{16,8},{20,12},{24,0},{28,4},{1,25},{... | collective-permute-start | bytes 1327112 | tf_op jit(solution)/shard_map/ppermute | solution.py:44
  57.9 16.1 %collective-permute-start.15 = (bf16[96,1536]{1,0:T(8,128)(2,1)S(1)}, bf16[96,1536]{1,0:T(8,128)(2,1)S(1)}, u32[]{:S(2)}, u32[]{:S(2)}) collective-permute-start(bf16[96,1536]{1,0:T(8,128)(2,1)S(1)} %get-tuple-element.211.wide_ref), channel_id=1, source_target_pairs={{0,24},{4,28},{8,16},{12,20},{16,8},{20,12},{24,0},{28,4},{1,25},{... | collective-permute-start | bytes 884744 | tf_op jit(solution)/shard_map/ppermute | solution.py:44
  77.1 15.1 %collective-permute-start.20 = (bf16[256,768]{1,0:T(8,128)(2,1)S(1)}, bf16[256,768]{1,0:T(8,128)(2,1)S(1)}, u32[]{:S(2)}, u32[]{:S(2)}) collective-permute-start(bf16[256,768]{1,0:T(8,128)(2,1)S(1)} %bitcast.35), channel_id=1, source_target_pairs={{0,1},{1,0},{2,3},{3,2},{4,5},{5,4},{6,7},{7,6},{8,9},{9,8},{10,11... | collective-permute-start | bytes 1179656 | tf_op jit(solution)/shard_map/ppermute | solution.py:44
  86.1 13.7 %collective-permute-start.19 = (bf16[256,768]{1,0:T(8,128)(2,1)S(1)}, bf16[256,768]{1,0:T(8,128)(2,1)S(1)}, u32[]{:S(2)}, u32[]{:S(2)}) collective-permute-start(bf16[256,768]{1,0:T(8,128)(2,1)S(1)} %get-tuple-element.224.part_ref), channel_id=1, source_target_pairs={{0,1},{1,0},{2,3},{3,2},{4,5},{5,4},{6,7},{7,6},{8,9},{9,8},{10,11... | collective-permute-start | bytes 1179656 | tf_op jit(solution)/shard_map/ppermute | solution.py:44
  91.0 17.2 %collective-permute-start.22 = (bf16[256,768]{1,0:T(8,128)(2,1)S(1)}, bf16[256,768]{1,0:T(8,128)(2,1)S(1)}, u32[]{:S(2)}, u32[]{:S(2)}) collective-permute-start(bf16[256,768]{1,0:T(8,128)(2,1)S(1)} %get-tuple-element.234.part_ref), channel_id=1, source_target_pairs={{0,1},{1,0},{2,3},{3,2},{4,5},{5,4},{6,7},{7,6},{8,9},{9,8},{10,11... | collective-permute-start | bytes 1179656 | tf_op jit(solution)/shard_map/ppermute | solution.py:44
  102.7 14.3 %collective-permute-start.21 = (bf16[256,768]{1,0:T(8,128)(2,1)S(1)}, bf16[256,768]{1,0:T(8,128)(2,1)S(1)}, u32[]{:S(2)}, u32[]{:S(2)}) collective-permute-start(bf16[256,768]{1,0:T(8,128)(2,1)S(1)} %get-tuple-element.263.part_ref), channel_id=1, source_target_pairs={{0,1},{1,0},{2,3},{3,2},{4,5},{5,4},{6,7},{7,6},{8,9},{9,8},{10,11... | collective-permute-start | bytes 1179656 | tf_op jit(solution)/shard_map/ppermute | solution.py:44
  117.0 15.7 %collective-permute-start.23 = (bf16[256,768]{1,0:T(8,128)(2,1)S(1)}, bf16[256,768]{1,0:T(8,128)(2,1)S(1)}, u32[]{:S(2)}, u32[]{:S(2)}) collective-permute-start(bf16[256,768]{1,0:T(8,128)(2,1)S(1)} %get-tuple-element.260.part_ref), channel_id=1, source_target_pairs={{0,1},{1,0},{2,3},{3,2},{4,5},{5,4},{6,7},{7,6},{8,9},{9,8},{10,11... | collective-permute-start | bytes 1179656 | tf_op jit(solution)/shard_map/ppermute | solution.py:44
  120.4 14.2 %collective-permute-start.24 = (bf16[256,384]{1,0:T(8,128)(2,1)S(1)}, bf16[256,384]{1,0:T(8,128)(2,1)S(1)}, u32[]{:S(2)}, u32[]{:S(2)}) collective-permute-start(bf16[256,384]{1,0:T(8,128)(2,1)S(1)} %get-tuple-element.271), channel_id=1, source_target_pairs={{0,2},{1,3},{2,0},{3,1},{4,6},{5,7},{6,4},{7,5},{8,10},{9,11},{10,... | collective-permute-start | bytes 589832 | tf_op jit(solution)/shard_map/ppermute | solution.py:44
  123.6 32.0 %collective-permute-start.27 = (bf16[96,3072]{1,0:T(8,128)(2,1)S(1)}, bf16[96,3072]{1,0:T(8,128)(2,1)S(1)}, u32[]{:S(2)}, u32[]{:S(2)}) collective-permute-start(bf16[96,3072]{1,0:T(8,128)(2,1)S(1)} %get-tuple-element.283), channel_id=1, source_target_pairs={{0,8},{4,12},{8,0},{12,4},{16,24},{20,28},{24,16},{28,20},{1,9},{5... | collective-permute-start | bytes 1769480 | tf_op jit(solution)/shard_map/ppermute | solution.py:44
  125.0 30.5 %collective-permute-start.28 = (bf16[96,3072]{1,0:T(8,128)(2,1)S(1)}, bf16[96,3072]{1,0:T(8,128)(2,1)S(1)}, u32[]{:S(2)}, u32[]{:S(2)}) collective-permute-start(bf16[96,3072]{1,0:T(8,128)(2,1)S(1)} %get-tuple-element.284), channel_id=1, source_target_pairs={{0,16},{4,20},{8,24},{12,28},{16,0},{20,4},{24,8},{28,12},{1,17},{... | collective-permute-start | bytes 1769480 | tf_op jit(solution)/shard_map/ppermute | solution.py:44
  126.6 29.0 %collective-permute-start.29 = (bf16[96,3072]{1,0:T(8,128)(2,1)S(1)}, bf16[96,3072]{1,0:T(8,128)(2,1)S(1)}, u32[]{:S(2)}, u32[]{:S(2)}) collective-permute-start(bf16[96,3072]{1,0:T(8,128)(2,1)S(1)} %get-tuple-element.285), channel_id=1, source_target_pairs={{0,24},{4,28},{8,16},{12,20},{16,8},{20,12},{24,0},{28,4},{1,25},{... | collective-permute-start | bytes 1769480 | tf_op jit(solution)/shard_map/ppermute | solution.py:44
  157.8 13.2 %collective-permute-start.36 = (bf16[256,768]{1,0:T(8,128)(2,1)S(1)}, bf16[256,768]{1,0:T(8,128)(2,1)S(1)}, u32[]{:S(2)}, u32[]{:S(2)}) collective-permute-start(bf16[256,768]{1,0:T(8,128)(2,1)S(1)} %get-tuple-element.306), channel_id=1, source_target_pairs={{0,1},{1,0},{2,3},{3,2},{4,5},{5,4},{6,7},{7,6},{8,9},{9,8},{10,11... | collective-permute-start | bytes 1179656 | tf_op jit(solution)/shard_map/ppermute | solution.py:44
  160.4 21.5 %collective-permute-start.32 = (bf16[112,1920]{1,0:T(8,128)(2,1)S(1)}, bf16[112,1920]{1,0:T(8,128)(2,1)S(1)}, u32[]{:S(2)}, u32[]{:S(2)}) collective-permute-start(bf16[112,1920]{1,0:T(8,128)(2,1)S(1)} %get-tuple-element.294), channel_id=1, source_target_pairs={{0,8},{4,12},{8,0},{12,4},{16,24},{20,28},{24,16},{28,20},{1,9},{5... | collective-permute-start | bytes 1290248 | tf_op jit(solution)/shard_map/ppermute | solution.py:44
  161.9 21.1 %collective-permute-start.33 = (bf16[112,1920]{1,0:T(8,128)(2,1)S(1)}, bf16[112,1920]{1,0:T(8,128)(2,1)S(1)}, u32[]{:S(2)}, u32[]{:S(2)}) collective-permute-start(bf16[112,1920]{1,0:T(8,128)(2,1)S(1)} %get-tuple-element.295), channel_id=1, source_target_pairs={{0,16},{4,20},{8,24},{12,28},{16,0},{20,4},{24,8},{28,12},{1,17},{... | collective-permute-start | bytes 1290248 | tf_op jit(solution)/shard_map/ppermute | solution.py:44
  163.4 19.6 %collective-permute-start.34 = (bf16[112,1920]{1,0:T(8,128)(2,1)S(1)}, bf16[112,1920]{1,0:T(8,128)(2,1)S(1)}, u32[]{:S(2)}, u32[]{:S(2)}) collective-permute-start(bf16[112,1920]{1,0:T(8,128)(2,1)S(1)} %get-tuple-element.296), channel_id=1, source_target_pairs={{0,24},{4,28},{8,16},{12,20},{16,8},{20,12},{24,0},{28,4},{1,25},{... | collective-permute-start | bytes 1290248 | tf_op jit(solution)/shard_map/ppermute | solution.py:44
  164.8 15.8 %collective-permute-start.35 = (bf16[96,1536]{1,0:T(8,128)(2,1)S(1)}, bf16[96,1536]{1,0:T(8,128)(2,1)S(1)}, u32[]{:S(2)}, u32[]{:S(2)}) collective-permute-start(bf16[96,1536]{1,0:T(8,128)(2,1)S(1)} %get-tuple-element.302), channel_id=1, source_target_pairs={{0,2},{1,3},{2,0},{3,1},{4,6},{5,7},{6,4},{7,5},{8,10},{9,11},{10,... | collective-permute-start | bytes 884744 | tf_op jit(solution)/shard_map/ppermute | solution.py:44
  (16 other events, 124.5 us)

commit v4 on v3

--- a/solution.py
+++ b/solution.py
@@ -249,17 +249,29 @@
     return jnp.where(jnp.broadcast_to(docs, (LABELS, rows)) == number, 1.0, 0.0).astype(BF)
 
 
-def attend(query, key, value, mask):
+def attend(query, key, value, mask, log_ref, step):
     lane = lax.broadcasted_iota(jnp.int32, (1, PAIR), 1)
     total = jnp.zeros(query.shape, F32)
+    scaled = jnp.zeros(query.shape, F32)
+    logs = jnp.zeros(query.shape, F32)
+    value = jnp.concatenate([value, jnp.ones(value.shape, BF)], axis=1)
     for head in range(2):
         part = jnp.where((lane // HEAD_DIM) == head, 1.0, 0.0)
         mine = (query.astype(F32) * (part * HEAD_DIM**-0.5)).astype(BF)
         scores = dot_nt(mine, key) + mask
-        expo = jnp.exp(scores - jnp.max(scores, axis=-1, keepdims=True))
-        probs = expo * (1.0 / jnp.sum(expo, axis=-1, keepdims=True))
-        total = total + dot(probs.astype(BF), value) * part
-    return total.astype(BF)
+        top = jnp.max(scores, axis=-1, keepdims=True)
+        expo = jnp.exp(scores - top)
+        whole_sum = jnp.sum(expo, axis=-1, keepdims=True)
+        probs = expo * (1.0 / whole_sum)
+        rounded = probs.astype(BF)
+        context = dot(rounded, value)
+        total = total + context[:, :PAIR] * part
+        scaled = scaled + context[:, :PAIR] * part / context[:, PAIR:]
+        logs = jnp.where(lane == head, top + jnp.log(whole_sum), logs)
+    turned = logs.T
+    for head in range(2):
+        log_ref[pl.ds(2 * step + head, 1), :] = turned[head : head + 1, :]
+    return total.astype(BF), scaled
 
 
 def column(height):
@@ -272,7 +284,8 @@
 
     def body(sc, own_ref, partner_ref, docs_ref, *refs):
         weight_refs, refs = refs[:2], refs[2:]
-        q_ref, k_ref, v_ref, ctx_ref, x_ref, w_ref, hot_ref, vec_ref, hidden_ref, bias_ref, mask_ref = refs
+        q_ref, k_ref, v_ref, ctx_ref, x_ref, w_ref, hot_ref, vec_ref, hidden_ref, bias_ref, log_ref, *refs = refs
+        scaled_ref, mask_ref = refs
         step = pl.program_id(0)
 
         @pl.when(step == 0)
@@ -317,6 +330,7 @@
             low = pltpu.roll(vectors[:VECS], D - sc[2] * QUARTER, 1)[:, :HALF]
             high = pltpu.roll(vectors[:VECS], D + QUARTER - (sc[2] ^ 2) * QUARTER, 1)[:, :HALF]
             bias_ref[...] = jnp.where(lanes < QUARTER, low, high)
+            log_ref[...] = jnp.zeros_like(log_ref)
 
         at = pl.multiple_of(step * 3 * PAIR, PAIR)
         both = dot(x_ref[...], w_ref[:, pl.ds(at, 3 * PAIR)])
@@ -327,7 +341,7 @@
         q_ref[...] = query
         k_ref[...] = key
         v_ref[...] = value
-        ctx_ref[...] = attend(query[:rows], key, value, mask_ref[...])
+        ctx_ref[...], scaled_ref[...] = attend(query[:rows], key, value, mask_ref[...], log_ref, step)
 
     operands = [own, partner, own_docs, *pieces]
     in_specs = [whole(o.shape) for o in operands]
@@ -342,8 +356,10 @@
         struct((VECS, D), F32),
         struct((VECS, 2 * HID), F32),
         struct((VECS, HALF), F32),
+        struct((VECS, rows), F32),
+        struct((rows, HALF), F32),
     ]
-    out_specs = [column(base)] * 3 + [column(rows)] + [whole(o.shape) for o in outs[4:]]
+    out_specs = [column(base)] * 3 + [column(rows)] + [whole(o.shape) for o in outs[4:-1]] + [column(rows)]
     return call(
         "attend_pair",
         body,
@@ -360,7 +376,7 @@
 
 def attend_halo(scalars, halo_near, halo_far, weight, bias, hot, query, key, value, rows):
     def body(sc, near_ref, far_ref, w_ref, bias_ref, hot_ref, q_ref, k_ref, v_ref, *refs):
-        halo_refs, (ctx_ref, all_ref, x_ref, mask_ref) = refs[:3], refs[3:]
+        halo_refs, (ctx_ref, scaled_ref, all_ref, log_ref, x_ref, mask_ref) = refs[:3], refs[3:]
 
         @pl.when(pl.program_id(0) == 0)
         def _():
@@ -373,6 +389,7 @@
             pl.when(sc[0] == 1)(lambda: halo(near_ref))
             pl.when(sc[0] == 0)(lambda: halo(far_ref))
             mask_ref[...] = (dot_tn(all_ref[:, rows : 2 * rows], all_ref[...]) - 1.0) * MASKED
+            log_ref[...] = jnp.zeros_like(log_ref)
 
         both = dot(x_ref[...], w_ref[...])
         parts = [
@@ -384,14 +401,17 @@
             ref[...] = part
         keys = jnp.concatenate([k_ref[...], parts[1]], axis=0)
         values = jnp.concatenate([v_ref[...], parts[2]], axis=0)
-        ctx_ref[...] = attend(q_ref[rows:, :], keys, values, mask_ref[...])
+        ctx_ref[...], scaled_ref[...] = attend(
+            q_ref[rows:, :], keys, values, mask_ref[...], log_ref, pl.program_id(0)
+        )
 
     operands = [halo_near, halo_far, weight, bias, hot, query, key, value]
     in_specs = [whole(o.shape) for o in operands]
     in_specs[2] = pl.BlockSpec((D, 3 * PAIR), lambda p, _: (0, p))
     in_specs[3] = column(VECS)
     in_specs[5:] = [column(2 * rows)] * 3
-    outs = [struct((rows, HALF), BF)] * 4 + [struct((LABELS, 3 * rows), BF)]
+    outs = [struct((rows, HALF), BF)] * 4 + [struct((rows, HALF), F32)]
+    outs += [struct((LABELS, 3 * rows), BF), struct((VECS, rows), F32)]
     return call(
         "attend_halo",
         body,
@@ -399,7 +419,7 @@
         operands,
         in_specs,
         outs,
-        [column(rows)] * 4 + [whole((LABELS, 3 * rows))],
+        [column(rows)] * 5 + [whole((LABELS, 3 * rows)), whole((VECS, rows))],
         (HALF // PAIR,),
         [pltpu.VMEM((rows, D), BF), pltpu.VMEM((rows, 3 * rows), F32)],
         micros=6,
@@ -596,10 +616,12 @@
     )
 
 
-def first_norm(scalars, block, part, received, total_grad, normed, inverse, vecs, out_weight, earlier, rows):
-    def body(sc, part_ref, recv_ref, grad_ref, norm_ref, inv_ref, vec_ref, weight_ref, *refs):
+def first_norm(
+    scalars, block, part, received, total_grad, normed, inverse, vecs, out_weight, ctx, logs, earlier, rows
+):
+    def body(sc, part_ref, recv_ref, grad_ref, norm_ref, inv_ref, vec_ref, weight_ref, ctx_ref, log_ref, *refs):
         old, refs = refs[: len(earlier)], refs[len(earlier) :]
-        attention_ref, context_ref, own_ref, sums_ref = refs[:4]
+        attention_ref, context_ref, inner_ref, own_ref, sums_ref = refs[:5]
         mine = sc[0] == block
         upstream = grad_ref[...] + part_ref[...].astype(F32) + recv_ref[...].astype(F32)
         here = norm_ref[...]
@@ -612,10 +634,29 @@
         total = inner * inv_ref[:, :1]
         attention = total.astype(BF)
         attention_ref[...] = attention
-        context_ref[...] = dot_nt(attention, weight_ref[...]).astype(BF)
+        context = dot_nt(attention, weight_ref[...]).astype(BF)
+        context_ref[...] = context
+        lane = lax.broadcasted_iota(jnp.int32, (VECS, HALF), 1) // HEAD_DIM
+        picks = jnp.where(lane == lax.broadcasted_iota(jnp.int32, (VECS, HALF), 0), 1.0, 0.0)
+        inner = lax.dot_general(
+            picks,
+            context.astype(F32) * ctx_ref[...],
+            (((1,), (1,)), ((), ())),
+            precision=lax.Precision.HIGHEST,
+            preferred_element_type=F32,
+        )
+        inner_ref[...] = inner
         if block == 1:
+            send_ref = refs[5]
             turned = jnp.concatenate([weight_ref[QUARTER:, :], weight_ref[:QUARTER, :]], axis=0)
-            refs[4][...] = dot_nt(attention, turned).astype(BF)
+            send_ref[:rows, :] = dot_nt(attention, turned).astype(BF)
+            rest = jnp.concatenate([log_ref[...], inner], axis=0)
+            send_ref[rows:, :] = jnp.zeros((3 * LABELS, HALF), BF)
+            for k in range(3):
+                at = rows + k * LABELS
+                piece = rest.astype(BF)
+                send_ref[at : at + LABELS, :rows] = piece
+                rest = rest - piece.astype(F32)
 
         @pl.when(mine)
         def _():
@@ -630,14 +671,15 @@
             own_ref[...] = old[0][...] if old else jnp.zeros_like(own_ref)
             sums_ref[...] = old[1][...] if old else jnp.zeros_like(sums_ref)
 
-    operands = [part, received, total_grad, normed, inverse, vecs, out_weight, *earlier]
+    operands = [part, received, total_grad, normed, inverse, vecs, out_weight, ctx, logs, *earlier]
     outs = [
         struct((rows, D), BF),
         struct((rows, HALF), BF),
+        struct((VECS, rows), F32),
         struct((rows, D), F32),
         struct((8, D), F32),
-        struct((rows, HALF), BF),
-    ][: 5 if block == 1 else 4]
+        struct((rows + 3 * LABELS, HALF), BF),
+    ][: 6 if block == 1 else 5]
     return call(
         "first_norm",
         body,
@@ -692,14 +734,15 @@
     )
 
 
-def attend_backward(scalars, pair, halo, grad_blocks, hot, weight, rows):
+def attend_backward(scalars, pair, halo, grad_blocks, logs, inners, hot, weight, rows):
     base = 3 * rows
     steps = HALF // PAIR
 
     def body(sc, *refs):
         pair_refs, halo_refs, refs = refs[:3], refs[3:6], refs[6:]
-        far_ref, near_ref, halo_ref, hot_ref, w_ref, *refs = refs
-        out_ref, keep_ref, send_ref, sums_ref, mask_ref, key_ref, value_ref, acc_ref, q_ref, k_ref, v_ref = refs
+        far_ref, near_ref, halo_ref, stats_ref, *refs = refs
+        log_refs, inner_refs, (hot_ref, w_ref, *refs) = refs[:2], refs[2:4], refs[4:]
+        out_ref, keep_ref, send_ref, sums_ref, mask_ref, key_ref, value_ref, acc_ref, q_ref, k_ref, v_ref, line_ref = refs
         for target, first_part, last_part in zip((q_ref, k_ref, v_ref), pair_refs, halo_refs):
             target[: 2 * rows, :] = first_part[...]
             target[2 * rows :, :] = last_part[...]
@@ -708,6 +751,11 @@
         @pl.when(step == 0)
         def _():
             mask_ref[...] = (dot_tn(hot_ref[...], hot_ref[...]) - 1.0) * MASKED
+            lines = jnp.zeros((LABELS, rows), F32)
+            for k in range(3):
+                at = rows + k * LABELS
+                lines = lines + stats_ref[at : at + LABELS, :rows].astype(F32)
+            line_ref[...] = lines
 
         key_ref[...] = jnp.zeros_like(key_ref)
         value_ref[...] = jnp.zeros_like(value_ref)
@@ -716,16 +764,19 @@
         for head in range(2):
             part = jnp.where((lane // HEAD_DIM) == head, 1.0, 0.0)
             key_turned = (k_ref[...].astype(F32) * part).T.astype(BF)
-            for index, (low, high) in enumerate(((0, 2 * rows), (0, base), (rows, base))):
+            line = 2 * step + head
+            other = lax.rem(line + 3, 6)
+            lines = [(log_refs[k][pl.ds(line, 1), :], inner_refs[k][pl.ds(line, 1), :]) for k in range(2)]
+            lines += [(line_ref[pl.ds(other, 1), :], line_ref[pl.ds(other + VECS, 1), :])]
+            for index, (low, high) in enumerate(((0, 2 * rows), (0, base), (rows, 2 * rows))):
                 start = index * rows
                 mine = (q_ref[start : start + rows].astype(F32) * (part * HEAD_DIM**-0.5)).astype(BF)
-                grads = (far_ref, near_ref, halo_ref)[index][...]
+                grads = (far_ref, near_ref, halo_ref)[index][:rows, :]
                 grads = (grads.astype(F32) * part).astype(BF)
                 scores = dot_nt(k_ref[low:high], mine) + mask_ref[low:high, start : start + rows]
-                expo = jnp.exp(scores - jnp.max(scores, axis=0, keepdims=True))
-                probs = expo * (1.0 / jnp.sum(expo, axis=0, keepdims=True))
+                log_total, inner = lines[index]
+                probs = jnp.exp(scores - log_total)
                 pulled = dot_nt(v_ref[low:high], grads)
-                inner = jnp.sum(probs * pulled, axis=0, keepdims=True)
                 score_grads = (probs * (pulled - inner)).astype(BF)
                 top = min(high, 2 * rows)
                 span = top - low
@@ -757,8 +808,10 @@
             other = acc_ref[pl.ds(pl.multiple_of((1 - near) * rows, rows), rows), :]
             send_ref[...] = other.astype(BF)
 
-    operands = [*pair, *halo, *grad_blocks, hot, weight]
-    in_specs = [column(2 * rows)] * 3 + [column(rows)] * 6 + [whole(hot.shape)]
+    stats = grad_blocks[2]
+    operands = [*pair, *halo, *grad_blocks, stats, *logs, *inners, hot, weight]
+    in_specs = [column(2 * rows)] * 3 + [column(rows)] * 5 + [column(stats.shape[0])]
+    in_specs += [whole(o.shape) for o in operands[9:15]]
     in_specs += [pl.BlockSpec((D, 3 * PAIR), lambda p, _: (0, p))]
     outs = [struct((2 * rows, 3 * HALF), BF), struct((rows, D), F32), struct((rows, D), BF)]
     outs += [struct((8, 3 * HALF), F32)]
@@ -774,6 +827,7 @@
         pltpu.VMEM((2 * rows, PAIR), F32),
         pltpu.VMEM((2 * rows, D), F32),
     ] + [pltpu.VMEM((base, PAIR), BF)] * 3
+    scratch += [pltpu.VMEM((LABELS, rows), F32)]
     return call(
         "attend_backward",
         body,
@@ -914,9 +968,15 @@
         for k in range(4):
             refs[k][...] = total[:, k * QUARTER : (k + 1) * QUARTER]
         if tall > rows:
-            refs[4][...] = keep_ref[rows:, :128] + whole_of(recv_ref[rows:, :256])
-
-    outs = [struct((rows, QUARTER), F32)] * 4 + ([struct((LABELS, 128), F32)] if tall > rows else [])
+            small = keep_ref[rows:, :128] + whole_of(recv_ref[rows:, :256])
+            for k in range(VECS):
+                refs[4 + k][...] = small[k, :BLOCK]
+            for k in range(FF // GROUPS // 128):
+                refs[4 + VECS][k * 128 : (k + 1) * 128] = small[VECS + k]
+
+    outs = [struct((rows, QUARTER), F32)] * 4
+    if tall > rows:
+        outs += [struct((BLOCK,), F32)] * VECS + [struct((FF // GROUPS,), F32)]
     return simple("finish_projection", body, scalars, [keep, received], outs)
 
 
@@ -1089,12 +1149,12 @@
     def scattered(table):
         return [lax.psum_scatter(table, "dp", scatter_dimension=0, tiled=True)]
 
-    *pair, ctx_far, x, weight, hot, vecs, hidden_bias, bias = attend_pair(
+    *pair, ctx_far, x, weight, hot, vecs, hidden_bias, bias, log_far, scaled_far = attend_pair(
         scalars, own, partner, own_docs, pieces, rows
     )
     if direct:
         pair, ctx_far, cot_own, halo_far = together(pair, ctx_far, cot_own, halo_far)
-    *halo, ctx_near, hot = attend_halo(scalars, halo_near, halo_far, weight, bias, hot, *pair, rows)
+    *halo, ctx_near, scaled_near, hot, log_near = attend_halo(scalars, halo_near, halo_far, weight, bias, hot, *pair, rows)
     ctx_mine = [ctx_far, ctx_near]
     ctx_partner = [swap(ctx_far, "seq", 1), None]
     if direct:
@@ -1143,10 +1203,11 @@
     )
     first_part_far[0] = swap(second[0][3], "seq", 1)
     layer_output, sums_two, sums_hidden = second_shared
-    attention_grad, ctx_grad, first_shared = [None, None], [None, None], []
+    attention_grad, ctx_grad, inners, first_shared = [None, None], [None, None], [None, None], []
+    logs, scaled = [log_far, log_near], [scaled_far, scaled_near]
 
     def finish(block):
-        attention_grad[block], ctx_grad[block], *shared = first_norm(
+        attention_grad[block], ctx_grad[block], inners[block], *shared = first_norm(
             scalars,
             block,
             second[block][3],
@@ -1156,6 +1217,8 @@
             forward[block][1],
             vecs,
             out_mine,
+            scaled[block],
+            logs[block],
             first_shared,
             rows,
         )
@@ -1171,7 +1234,7 @@
     own_grad, sums_one = finish(0)
 
     grads, input_keep, input_send, sums_projection = attend_backward(
-        scalars, pair, halo, [*ctx_grad, halo_grad], hot, weight, rows
+        scalars, pair, halo, [*ctx_grad, halo_grad], logs, inners, hot, weight, rows
     )
     input_far = swap(input_send, "seq", 1)
     small = small_sums(scalars, sums_one, sums_two, sums_hidden, sums_projection)
@@ -1204,15 +1267,14 @@
     keep, send = total_projection(scalars, sums, piece_rows)
     projections = list(finish_projection(scalars, keep, swap(send, "seq", 2), piece_rows))
     if direct:
-        tile = projections.pop()
-        wide_lines, tall_lines = tile[:VECS, :BLOCK], tile[VECS : VECS + 3].reshape(-1)
+        projections, vec, tall_lines = projections[:4], projections[4:-1], projections[-1]
     else:
         tile = out_parts[:, BLOCK:, :128] + out_parts[:, BLOCK:, 128:256]
         tile = tile + swap(tile, "seq", 2)
         wide_lines = tile[:, :VECS, :BLOCK].transpose(1, 0, 2).reshape(VECS, D)
         wide_lines = lax.psum_scatter(wide_lines, "dp", scatter_dimension=1, tiled=True)
         tall_lines = lax.psum_scatter(tile[:, VECS : VECS + 3].reshape(-1), "dp", tiled=True)
-    vec = [wide_lines[k] for k in range(VECS)]
+        vec = [wide_lines[k] for k in range(VECS)]
     return (
         layer_output[None],
         input_grad[None],

time: 197 us -> 193 us (0.980)
  Pallas kernels: 69.3 us -> 64.1 us
    pallas_call x26, Pallas kernels: 69.3 us -> 64.1 us  [call(): pl.pallas_call(body, out_shape=outs, grid_spec=spec, compiler_params=para...]
  transfers between devices with their start and end apart: 38 -> 38, of which waited for: 19 -> 21; matrix products, arithmetic and copies ran while one was open for 1% -> 1% of each run, Pallas kernels for 32% -> 30%
where the time goes in v4:
time: 193 us
  waiting for transfers between devices  77.8 us (40%)
  Pallas kernels  64.1 us (33%)
  starting transfers between devices  47.8 us (25%)
    ppermute x36, waiting for transfers between devices, swap(): return lax.ppermute(value, axis, [(k, k ^ mask) for k in range(count)])  74.8 us
    pallas_call x26, Pallas kernels, call(): pl.pallas_call(body, out_shape=outs, grid_spec=spec, compiler_params=para...  64.1 us
    ppermute x36, starting transfers between devices, swap(): return lax.ppermute(value, axis, [(k, k ^ mask) for k in range(count)])  45.9 us
  transfers between devices with their start and end apart: 38, of which 21 were waited for; matrix products, arithmetic and copies ran while one was open for 1% of the time, Pallas kernels for 30%

profile of v4, /device:TPU:0, one launch (start us, length us, event | category | flops | bytes accessed | tf_op | source)
XLA Modules:
  0.0 193.1 jit_solution(7265481715967145011)
XLA Ops:
  4.1 3.0 %collective-permute-start.1 = (bf16[112,2112]{1,0:T(8,128)(2,1)S(1)}, bf16[112,2112]{1,0:T(8,128)(2,1)S(1)}, u32[]{:S(2)}, u32[]{:S(2)}) collective-permute-start(bf16[112,2112]{1,0:T(8,128)(2,1)S(1)} %get-tuple-element.197.mine_ref.refs_0_), channel_id=1, source_target_pairs={{0,8},{4,12},{8,0},{12,4},{16,24},{20,28},{24,16},{28,20},{1,9},{5... | collective-permute-start | bytes 1419272 | tf_op jit(solution)/shard_map/ppermute | solution.py:44
  8.6 2.6 %collective-permute-start.3 = (bf16[96,768]{1,0:T(8,128)(2,1)S(1)}, bf16[96,768]{1,0:T(8,128)(2,1)S(1)}, u32[]{:S(2)}, u32[]{:S(2)}) collective-permute-start(bf16[96,768]{1,0:T(8,128)(2,1)S(1)} %get-tuple-element.185.own_ref), channel_id=1, source_target_pairs={{0,2},{1,3},{2,0},{3,1},{4,6},{5,7},{6,4},{7,5},{8,10},{9,11},{10,... | collective-permute-start | bytes 442376 | tf_op jit(solution)/shard_map/ppermute | solution.py:44
  12.7 2.7 %collective-permute-done.side_ref = bf16[96,192]{1,0:T(8,128)(2,1)S(1)} collective-permute-done((bf16[96,192]{1,0:T(8,128)(2,1)}, bf16[96,192]{1,0:T(8,128)(2,1)S(1)}, u32[]{:S(2)}, u32[]{:S(2)}) %collective-permute-start) | collective-permute-done | bytes 36896 | tf_op jit(solution)/shard_map/ppermute | solution.py:44
  20.3 2.7 %collective-permute-start.7 = (bf16[96,1728]{1,0:T(8,128)(2,1)S(1)}, bf16[96,1728]{1,0:T(8,128)(2,1)S(1)}, u32[]{:S(2)}, u32[]{:S(2)}) collective-permute-start(bf16[96,1728]{1,0:T(8,128)(2,1)S(1)} %get-tuple-element.195), channel_id=1, source_target_pairs={{0,2},{1,3},{2,0},{3,1},{4,6},{5,7},{6,4},{7,5},{8,10},{9,11},{10,... | collective-permute-start | bytes 995336 | tf_op jit(solution)/shard_map/ppermute | solution.py:44
  26.4 6.8 %collective-permute-done.4.refs_4_ = bf16[96,576]{1,0:T(8,128)(2,1)S(1)} collective-permute-done((bf16[96,576]{1,0:T(8,128)(2,1)S(1)}, bf16[96,576]{1,0:T(8,128)(2,1)S(1)}, u32[]{:S(2)}, u32[]{:S(2)}) %collective-permute-start.4) | collective-permute-done | bytes 110624 | tf_op jit(solution)/shard_map/ppermute | solution.py:44
  33.2 4.0 %collective-permute-done.7.far_ref = bf16[96,1728]{1,0:T(8,128)(2,1)S(1)} collective-permute-done((bf16[96,1728]{1,0:T(8,128)(2,1)S(1)}, bf16[96,1728]{1,0:T(8,128)(2,1)S(1)}, u32[]{:S(2)}, u32[]{:S(2)}) %collective-permute-start.7) | collective-permute-done | bytes 331808 | tf_op jit(solution)/shard_map/ppermute | solution.py:44
  43.6 10.2 %collective-permute-done.10.refs_5_ = bf16[96,2304]{1,0:T(8,128)(2,1)S(1)} collective-permute-done((bf16[96,2304]{1,0:T(8,128)(2,1)S(1)}, bf16[96,2304]{1,0:T(8,128)(2,1)S(1)}, u32[]{:S(2)}, u32[]{:S(2)}) %collective-permute-start.10) | collective-permute-done | bytes 442400 | tf_op jit(solution)/shard_map/ppermute | solution.py:44
  58.4 6.3 %attend_pair.1 = (bf16[512,384]{1,0:T(8,128)(2,1)S(1)}, bf16[512,384]{1,0:T(8,128)(2,1)S(1)}, bf16[512,384]{1,0:T(8,128)(2,1)S(1)}, bf16[256,384]{1,0:T(8,128)(2...) custom-call(s32[3]{0:T(128)S(1)} %pad_add_fusion._.sc, ...), custom_call_target="tpu_custom_call" | custom-call | flops 80000000 | bytes 1024 | tf_op jit(solution)/shard_map/attend_pair/pallas_call | solution.py:67
  64.7 3.0 %collective-permute-done.13.far_ref = bf16[304,768]{1,0:T(8,128)(2,1)S(1)} collective-permute-done((bf16[304,768]{1,0:T(8,128)(2,1)S(1)}, bf16[304,768]{1,0:T(8,128)(2,1)S(1)}, u32[]{:S(2)}, u32[]{:S(2)}) %collective-permute-start.13) | collective-permute-done | bytes 466976 | tf_op jit(solution)/shard_map/ppermute | solution.py:1112
  67.7 5.5 %attend_halo.1 = (bf16[256,384]{1,0:T(8,128)(2,1)S(1)}, bf16[256,384]{1,0:T(8,128)(2,1)S(1)}, bf16[256,384]{1,0:T(8,128)(2,1)S(1)}, bf16[256,384]{1,0:T(8,128)(2...) custom-call(s32[3]{0:T(128)S(1)} %pad_add_fusion._.sc, ...), custom_call_target="tpu_custom_call" | custom-call | flops 60000000 | bytes 1024 | tf_op jit(solution)/shard_map/attend_halo/pallas_call | solution.py:67
  74.7 2.5 %collective-permute-start.17 = (bf16[256,384]{1,0:T(8,128)(2,1)S(1)}, bf16[256,384]{1,0:T(8,128)(2,1)S(1)}, u32[]{:S(2)}, u32[]{:S(2)}) collective-permute-start(bf16[256,384]{1,0:T(8,128)(2,1)S(1)} %get-tuple-element.229.mine_ref.refs_3_), channel_id=1, source_target_pairs={{0,1},{1,0},{2,3},{3,2},{4,5},{5,4},{6,7},{7,6},{8,9},{9,8},{10,11... | collective-permute-start | bytes 589832 | tf_op jit(solution)/shard_map/ppermute | solution.py:44
  77.2 5.6 %collective-permute-done.17.partner_ref.refs_4_ = bf16[256,384]{1,0:T(8,128)(2,1)S(1)} collective-permute-done((bf16[256,384]{1,0:T(8,128)(2,1)S(1)}, bf16[256,384]{1,0:T(8,128)(2,1)S(1)}, u32[]{:S(2)}, u32[]{:S(2)}) %collective-permute-start.17) | collective-permute-done | bytes 196640 | tf_op jit(solution)/shard_map/ppermute | solution.py:44
  82.9 3.2 %feed_forward.2 = (f32[256,768]{1,0:T(8,128)S(1)}, f32[256,128]{1,0:T(8,128)S(1)}, bf16[256,768]{1,0:T(8,128)(2,1)S(1)}, f32[256,1536]{1,0:T(8,128)S(1)}, bf16[2...) custom-call(s32[3]{0:T(128)S(1)} %pad_add_fusion._.sc, ...), custom_call_target="tpu_custom_call" | custom-call | flops 60000000 | bytes 1024 | tf_op jit(solution)/shard_map/feed_forward/pallas_call | solution.py:67
  88.1 2.9 %feed_forward.3 = (f32[256,768]{1,0:T(8,128)S(1)}, f32[256,128]{1,0:T(8,128)S(1)}, bf16[256,768]{1,0:T(8,128)(2,1)S(1)}, f32[256,1536]{1,0:T(8,128)S(1)}, bf16[2...) custom-call(s32[3]{0:T(128)S(1)} %pad_add_fusion._.sc, bf16[256,384]{1,0:T(8,128)(2,1)S(1)} %get-tuple-element.224.mine_ref.refs_0_, ...), custom_call_target="tpu_custom_call" | custom-call | flops 60000000 | bytes 1024 | tf_op jit(solution)/shard_map/feed_forward/pallas_call | solution.py:67
  92.3 7.4 %collective-permute-done.19.recv_ref = bf16[256,768]{1,0:T(8,128)(2,1)S(1)} collective-permute-done((bf16[256,768]{1,0:T(8,128)(2,1)S(1)}, bf16[256,768]{1,0:T(8,128)(2,1)S(1)}, u32[]{:S(2)}, u32[]{:S(2)}) %collective-permute-start.19) | collective-permute-done | bytes 393248 | tf_op jit(solution)/shard_map/ppermute | solution.py:44
  99.7 2.9 %second_norm.2 = (f32[256,768]{1,0:T(8,128)S(1)}, bf16[256,768]{1,0:T(8,128)(2,1)S(1)}, bf16[256,1536]{1,0:T(8,128)(2,1)S(1)}, bf16[256,768]{1,0:T(8,128)(2,1)S(...) custom-call(s32[3]{0:T(128)S(1)} %pad_add_fusion._.sc, ...), custom_call_target="tpu_custom_call" | custom-call | flops 50000000 | bytes 1024 | tf_op jit(solution)/shard_map/second_norm/pallas_call | solution.py:67
  108.2 3.8 %second_norm.3 = (f32[256,768]{1,0:T(8,128)S(1)}, bf16[256,768]{1,0:T(8,128)(2,1)S(1)}, bf16[256,1536]{1,0:T(8,128)(2,1)S(1)}, bf16[256,768]{1,0:T(8,128)(2,1)S(...) custom-call(s32[3]{0:T(128)S(1)} %pad_add_fusion._.sc, ...), custom_call_target="tpu_custom_call" | custom-call | flops 50000000 | bytes 1024 | tf_op jit(solution)/shard_map/second_norm/pallas_call | solution.py:67
  111.9 5.0 %feed_forward_grads.1 = (bf16[4,96,3072]{2,1,0:T(8,128)(2,1)S(1)}, bf16[4,96,3072]{2,1,0:T(8,128)(2,1)S(1)}) custom-call(s32[3]{0:T(128)S(1)} %pad_add_fusion._.sc, bf16[256,768]{1,0:T(8,128)(2,1)S(1)} %get-tuple-element.264.refs_0_, bf16[256,1536]{1,0:T(8,128)(2,1)S(1)} %get-tuple-element.256.refs_1_, bf16[256,768]{1,0:T(8,128)(2,1)S(1)} %get-tuple-element.255.refs_2_, ...), custom_call_target="tpu_custom_call" | custom-call | flops 80000000 | bytes 1024 | tf_op jit(solution)/shard_map/feed_forward_grads/pallas_call | solution.py:67
  127.6 6.0 %collective-permute-done.23.recv_ref = bf16[256,768]{1,0:T(8,128)(2,1)S(1)} collective-permute-done((bf16[256,768]{1,0:T(8,128)(2,1)S(1)}, bf16[256,768]{1,0:T(8,128)(2,1)S(1)}, u32[]{:S(2)}, u32[]{:S(2)}) %collective-permute-start.23) | collective-permute-done | bytes 393248 | tf_op jit(solution)/shard_map/ppermute | solution.py:44
  135.9 10.7 %attend_backward.1 = (bf16[512,1152]{1,0:T(8,128)(2,1)S(1)}, f32[256,768]{1,0:T(8,128)S(1)}, bf16[256,768]{1,0:T(8,128)(2,1)S(1)}, f32[8,1152]{1,0:T(8,128)S(1)}) custom-call(s32[3]{0:T(128)S(1)} %pad_add_fusion._.sc, bf16[512,384]{1,0:T(8,128)(2,1)S(1)} %get-tuple-element.220.q_ref.refs_0_, bf16[512,384]{1,0:T(8,128)(2,1)S(1)} %get-tuple-element.221.k_ref.refs_1_, ...), custom_call_target="tpu_custom_call" | custom-call | flops 4499999744 | bytes 1024 | tf_op jit(solution)/shard_map/attend_backward/pallas_call | solution.py:67
  147.6 2.9 %projection_grads.1 = (bf16[4,96,1152]{2,1,0:T(8,128)(2,1)S(1)}, bf16[4,96,1152]{2,1,0:T(8,128)(2,1)S(1)}) custom-call(s32[3]{0:T(128)S(1)} %pad_add_fusion._.sc, bf16[512,768]{1,0:T(8,128)(2,1)S(1)} %get-tuple-element.230.x_ref, bf16[512,1152]{1,0:T(8,128)(2,1)S(1)} %get-tuple-element.293.grad_ref), custom_call_target="tpu_custom_call" | custom-call | flops 50000000 | bytes 1024 | tf_op jit(solution)/shard_map/projection_grads/pallas_call | solution.py:67
  164.2 4.5 %collective-permute-done.36 = bf16[256,768]{1,0:T(8,128)(2,1)S(1)} collective-permute-done((bf16[256,768]{1,0:T(8,128)(2,1)S(1)}, bf16[256,768]{1,0:T(8,128)(2,1)S(1)}, u32[]{:S(2)}, u32[]{:S(2)}) %collective-permute-start.36) | collective-permute-done | bytes 393248 | tf_op jit(solution)/shard_map/ppermute | solution.py:44
  169.7 8.2 %collective-permute-done.35.recv_ref = bf16[96,1536]{1,0:T(8,128)(2,1)S(1)} collective-permute-done((bf16[96,1536]{1,0:T(8,128)(2,1)S(1)}, bf16[96,1536]{1,0:T(8,128)(2,1)S(1)}, u32[]{:S(2)}, u32[]{:S(2)}) %collective-permute-start.35) | collective-permute-done | bytes 294944 | tf_op jit(solution)/shard_map/ppermute | solution.py:44
  183.2 8.4 %collective-permute-done.37.recv_ref = bf16[112,768]{1,0:T(8,128)(2,1)S(1)} collective-permute-done((bf16[112,768]{1,0:T(8,128)(2,1)S(1)}, bf16[112,768]{1,0:T(8,128)(2,1)S(1)}, u32[]{:S(2)}, u32[]{:S(2)}) %collective-permute-start.37) | collective-permute-done | bytes 172064 | tf_op jit(solution)/shard_map/ppermute | solution.py:44
  (85 shorter events, 71.2 us)
Async XLA Ops:
  4.1 14.1 %collective-permute-start.1 = (bf16[112,2112]{1,0:T(8,128)(2,1)S(1)}, bf16[112,2112]{1,0:T(8,128)(2,1)S(1)}, u32[]{:S(2)}, u32[]{:S(2)}) collective-permute-start(bf16[112,2112]{1,0:T(8,128)(2,1)S(1)} %get-tuple-element.197.mine_ref.refs_0_), channel_id=1, source_target_pairs={{0,8},{4,12},{8,0},{12,4},{16,24},{20,28},{24,16},{28,20},{1,9},{5... | collective-permute-start | bytes 1419272 | tf_op jit(solution)/shard_map/ppermute | solution.py:44
  7.1 12.6 %collective-permute-start.2 = (bf16[112,2112]{1,0:T(8,128)(2,1)S(1)}, bf16[112,2112]{1,0:T(8,128)(2,1)S(1)}, u32[]{:S(2)}, u32[]{:S(2)}) collective-permute-start(bf16[112,2112]{1,0:T(8,128)(2,1)S(1)} %get-tuple-element.197.mine_ref.refs_0_), channel_id=1, source_target_pairs={{0,16},{4,20},{8,24},{12,28},{16,0},{20,4},{24,8},{28,12},{1,17},{... | collective-permute-start | bytes 1419272 | tf_op jit(solution)/shard_map/ppermute | solution.py:44
  20.3 16.9 %collective-permute-start.7 = (bf16[96,1728]{1,0:T(8,128)(2,1)S(1)}, bf16[96,1728]{1,0:T(8,128)(2,1)S(1)}, u32[]{:S(2)}, u32[]{:S(2)}) collective-permute-start(bf16[96,1728]{1,0:T(8,128)(2,1)S(1)} %get-tuple-element.195), channel_id=1, source_target_pairs={{0,2},{1,3},{2,0},{3,1},{4,6},{5,7},{6,4},{7,5},{8,10},{9,11},{10,... | collective-permute-start | bytes 995336 | tf_op jit(solution)/shard_map/ppermute | solution.py:44
  37.8 16.3 %collective-permute-start.8 = (bf16[4,208,576]{2,1,0:T(8,128)(2,1)S(1)}, bf16[4,208,576]{2,1,0:T(8,128)(2,1)S(1)}, u32[]{:S(2)}, u32[]{:S(2)}) collective-permute-start(bf16[4,208,576]{2,1,0:T(8,128)(2,1)S(1)} %stack_narrow.1.refs_0_), channel_id=1, source_target_pairs={{0,4},{4,0},{8,12},{12,8},{16,20},{20,16},{24,28},{28,24},{1,5},{5... | collective-permute-start | bytes 2875400 | tf_op jit(solution)/shard_map/ppermute | solution.py:44
  37.9 16.2 %collective-permute-start.12 = (bf16[304,768]{1,0:T(8,128)(2,1)S(1)}, bf16[304,768]{1,0:T(8,128)(2,1)S(1)}, u32[]{:S(2)}, u32[]{:S(2)}) collective-permute-start(bf16[304,768]{1,0:T(8,128)(2,1)S(1)} %get-tuple-element.204), channel_id=1, source_target_pairs={{1,2},{2,1},{5,6},{6,5},{9,10},{10,9},{13,14},{14,13},{17,18},{18,... | collective-permute-start | bytes 1400840 | tf_op jit(solution)/shard_map/ppermute | solution.py:1103
  38.6 15.5 %collective-permute-start.9 = (bf16[304,768]{1,0:T(8,128)(2,1)S(1)}, bf16[304,768]{1,0:T(8,128)(2,1)S(1)}, u32[]{:S(2)}, u32[]{:S(2)}) collective-permute-start(bf16[304,768]{1,0:T(8,128)(2,1)S(1)} %get-tuple-element.204), channel_id=1, source_target_pairs={{0,1},{1,0},{2,3},{3,2},{4,5},{5,4},{6,7},{7,6},{8,9},{9,8},{10,11... | collective-permute-start | bytes 1400840 | tf_op jit(solution)/shard_map/ppermute | solution.py:44
  41.4 12.3 %collective-permute-start.10 = (bf16[96,2304]{1,0:T(8,128)(2,1)S(1)}, bf16[96,2304]{1,0:T(8,128)(2,1)S(1)}, u32[]{:S(2)}, u32[]{:S(2)}) collective-permute-start(bf16[96,2304]{1,0:T(8,128)(2,1)S(1)} %pack_feed.1.refs_4_), channel_id=1, source_target_pairs={{0,8},{4,12},{8,0},{12,4},{16,24},{20,28},{24,16},{28,20},{1,9},{5... | collective-permute-start | bytes 1327112 | tf_op jit(solution)/shard_map/ppermute | solution.py:44
  54.1 13.6 %collective-permute-start.13 = (bf16[304,768]{1,0:T(8,128)(2,1)S(1)}, bf16[304,768]{1,0:T(8,128)(2,1)S(1)}, u32[]{:S(2)}, u32[]{:S(2)}) collective-permute-start(bf16[304,768]{1,0:T(8,128)(2,1)S(1)} %collective-permute-done.12.near_ref), channel_id=1, source_target_pairs={{1,0},{2,3},{5,4},{6,7},{9,8},{10,11},{13,12},{14,15},{17,16},{18,... | collective-permute-start | bytes 1400840 | tf_op jit(solution)/shard_map/ppermute | solution.py:1112
  55.4 18.4 %collective-permute-start.16 = (bf16[96,2304]{1,0:T(8,128)(2,1)S(1)}, bf16[96,2304]{1,0:T(8,128)(2,1)S(1)}, u32[]{:S(2)}, u32[]{:S(2)}) collective-permute-start(bf16[96,2304]{1,0:T(8,128)(2,1)S(1)} %pack_feed.1.refs_4_), channel_id=1, source_target_pairs={{0,24},{4,28},{8,16},{12,20},{16,8},{20,12},{24,0},{28,4},{1,25},{... | collective-permute-start | bytes 1327112 | tf_op jit(solution)/shard_map/ppermute | solution.py:44
  57.9 16.0 %collective-permute-start.15 = (bf16[96,1536]{1,0:T(8,128)(2,1)S(1)}, bf16[96,1536]{1,0:T(8,128)(2,1)S(1)}, u32[]{:S(2)}, u32[]{:S(2)}) collective-permute-start(bf16[96,1536]{1,0:T(8,128)(2,1)S(1)} %get-tuple-element.225.wide_ref), channel_id=1, source_target_pairs={{0,24},{4,28},{8,16},{12,20},{16,8},{20,12},{24,0},{28,4},{1,25},{... | collective-permute-start | bytes 884744 | tf_op jit(solution)/shard_map/ppermute | solution.py:44
  77.1 15.2 %collective-permute-start.20 = (bf16[256,768]{1,0:T(8,128)(2,1)S(1)}, bf16[256,768]{1,0:T(8,128)(2,1)S(1)}, u32[]{:S(2)}, u32[]{:S(2)}) collective-permute-start(bf16[256,768]{1,0:T(8,128)(2,1)S(1)} %bitcast.17), channel_id=1, source_target_pairs={{0,1},{1,0},{2,3},{3,2},{4,5},{5,4},{6,7},{7,6},{8,9},{9,8},{10,11... | collective-permute-start | bytes 1179656 | tf_op jit(solution)/shard_map/ppermute | solution.py:44
  86.1 13.7 %collective-permute-start.19 = (bf16[256,768]{1,0:T(8,128)(2,1)S(1)}, bf16[256,768]{1,0:T(8,128)(2,1)S(1)}, u32[]{:S(2)}, u32[]{:S(2)}) collective-permute-start(bf16[256,768]{1,0:T(8,128)(2,1)S(1)} %get-tuple-element.238.part_ref), channel_id=1, source_target_pairs={{0,1},{1,0},{2,3},{3,2},{4,5},{5,4},{6,7},{7,6},{8,9},{9,8},{10,11... | collective-permute-start | bytes 1179656 | tf_op jit(solution)/shard_map/ppermute | solution.py:44
  91.0 17.2 %collective-permute-start.22 = (bf16[256,768]{1,0:T(8,128)(2,1)S(1)}, bf16[256,768]{1,0:T(8,128)(2,1)S(1)}, u32[]{:S(2)}, u32[]{:S(2)}) collective-permute-start(bf16[256,768]{1,0:T(8,128)(2,1)S(1)} %get-tuple-element.248.part_ref), channel_id=1, source_target_pairs={{0,1},{1,0},{2,3},{3,2},{4,5},{5,4},{6,7},{7,6},{8,9},{9,8},{10,11... | collective-permute-start | bytes 1179656 | tf_op jit(solution)/shard_map/ppermute | solution.py:44
  102.7 14.3 %collective-permute-start.21 = (bf16[256,768]{1,0:T(8,128)(2,1)S(1)}, bf16[256,768]{1,0:T(8,128)(2,1)S(1)}, u32[]{:S(2)}, u32[]{:S(2)}) collective-permute-start(bf16[256,768]{1,0:T(8,128)(2,1)S(1)} %get-tuple-element.279.part_ref), channel_id=1, source_target_pairs={{0,1},{1,0},{2,3},{3,2},{4,5},{5,4},{6,7},{7,6},{8,9},{9,8},{10,11... | collective-permute-start | bytes 1179656 | tf_op jit(solution)/shard_map/ppermute | solution.py:44
  117.0 16.5 %collective-permute-start.23 = (bf16[256,768]{1,0:T(8,128)(2,1)S(1)}, bf16[256,768]{1,0:T(8,128)(2,1)S(1)}, u32[]{:S(2)}, u32[]{:S(2)}) collective-permute-start(bf16[256,768]{1,0:T(8,128)(2,1)S(1)} %get-tuple-element.274.part_ref), channel_id=1, source_target_pairs={{0,1},{1,0},{2,3},{3,2},{4,5},{5,4},{6,7},{7,6},{8,9},{9,8},{10,11... | collective-permute-start | bytes 1179656 | tf_op jit(solution)/shard_map/ppermute | solution.py:44
  120.9 15.0 %collective-permute-start.24 = (bf16[304,384]{1,0:T(8,128)(2,1)S(1)}, bf16[304,384]{1,0:T(8,128)(2,1)S(1)}, u32[]{:S(2)}, u32[]{:S(2)}) collective-permute-start(bf16[304,384]{1,0:T(8,128)(2,1)S(1)} %get-tuple-element.289), channel_id=1, source_target_pairs={{0,2},{1,3},{2,0},{3,1},{4,6},{5,7},{6,4},{7,5},{8,10},{9,11},{10,... | collective-permute-start | bytes 700424 | tf_op jit(solution)/shard_map/ppermute | solution.py:44
  124.0 27.7 %collective-permute-start.27 = (bf16[96,3072]{1,0:T(8,128)(2,1)S(1)}, bf16[96,3072]{1,0:T(8,128)(2,1)S(1)}, u32[]{:S(2)}, u32[]{:S(2)}) collective-permute-start(bf16[96,3072]{1,0:T(8,128)(2,1)S(1)} %get-tuple-element.303), channel_id=1, source_target_pairs={{0,8},{4,12},{8,0},{12,4},{16,24},{20,28},{24,16},{28,20},{1,9},{5... | collective-permute-start | bytes 1769480 | tf_op jit(solution)/shard_map/ppermute | solution.py:44
  125.5 27.5 %collective-permute-start.28 = (bf16[96,3072]{1,0:T(8,128)(2,1)S(1)}, bf16[96,3072]{1,0:T(8,128)(2,1)S(1)}, u32[]{:S(2)}, u32[]{:S(2)}) collective-permute-start(bf16[96,3072]{1,0:T(8,128)(2,1)S(1)} %get-tuple-element.304), channel_id=1, source_target_pairs={{0,16},{4,20},{8,24},{12,28},{16,0},{20,4},{24,8},{28,12},{1,17},{... | collective-permute-start | bytes 1769480 | tf_op jit(solution)/shard_map/ppermute | solution.py:44
  127.0 26.0 %collective-permute-start.29 = (bf16[96,3072]{1,0:T(8,128)(2,1)S(1)}, bf16[96,3072]{1,0:T(8,128)(2,1)S(1)}, u32[]{:S(2)}, u32[]{:S(2)}) collective-permute-start(bf16[96,3072]{1,0:T(8,128)(2,1)S(1)} %get-tuple-element.305), channel_id=1, source_target_pairs={{0,24},{4,28},{8,16},{12,20},{16,8},{20,12},{24,0},{28,4},{1,25},{... | collective-permute-start | bytes 1769480 | tf_op jit(solution)/shard_map/ppermute | solution.py:44
  155.1 13.6 %collective-permute-start.36 = (bf16[256,768]{1,0:T(8,128)(2,1)S(1)}, bf16[256,768]{1,0:T(8,128)(2,1)S(1)}, u32[]{:S(2)}, u32[]{:S(2)}) collective-permute-start(bf16[256,768]{1,0:T(8,128)(2,1)S(1)} %get-tuple-element.326), channel_id=1, source_target_pairs={{0,1},{1,0},{2,3},{3,2},{4,5},{5,4},{6,7},{7,6},{8,9},{9,8},{10,11... | collective-permute-start | bytes 1179656 | tf_op jit(solution)/shard_map/ppermute | solution.py:44
  157.8 21.5 %collective-permute-start.32 = (bf16[112,1920]{1,0:T(8,128)(2,1)S(1)}, bf16[112,1920]{1,0:T(8,128)(2,1)S(1)}, u32[]{:S(2)}, u32[]{:S(2)}) collective-permute-start(bf16[112,1920]{1,0:T(8,128)(2,1)S(1)} %get-tuple-element.314), channel_id=1, source_target_pairs={{0,8},{4,12},{8,0},{12,4},{16,24},{20,28},{24,16},{28,20},{1,9},{5... | collective-permute-start | bytes 1290248 | tf_op jit(solution)/shard_map/ppermute | solution.py:44
  159.1 20.2 %collective-permute-start.33 = (bf16[112,1920]{1,0:T(8,128)(2,1)S(1)}, bf16[112,1920]{1,0:T(8,128)(2,1)S(1)}, u32[]{:S(2)}, u32[]{:S(2)}) collective-permute-start(bf16[112,1920]{1,0:T(8,128)(2,1)S(1)} %get-tuple-element.315), channel_id=1, source_target_pairs={{0,16},{4,20},{8,24},{12,28},{16,0},{20,4},{24,8},{28,12},{1,17},{... | collective-permute-start | bytes 1290248 | tf_op jit(solution)/shard_map/ppermute | solution.py:44
  160.0 20.2 %collective-permute-start.34 = (bf16[112,1920]{1,0:T(8,128)(2,1)S(1)}, bf16[112,1920]{1,0:T(8,128)(2,1)S(1)}, u32[]{:S(2)}, u32[]{:S(2)}) collective-permute-start(bf16[112,1920]{1,0:T(8,128)(2,1)S(1)} %get-tuple-element.316), channel_id=1, source_target_pairs={{0,24},{4,28},{8,16},{12,20},{16,8},{20,12},{24,0},{28,4},{1,25},{... | collective-permute-start | bytes 1290248 | tf_op jit(solution)/shard_map/ppermute | solution.py:44
  162.1 15.8 %collective-permute-start.35 = (bf16[96,1536]{1,0:T(8,128)(2,1)S(1)}, bf16[96,1536]{1,0:T(8,128)(2,1)S(1)}, u32[]{:S(2)}, u32[]{:S(2)}) collective-permute-start(bf16[96,1536]{1,0:T(8,128)(2,1)S(1)} %get-tuple-element.322), channel_id=1, source_target_pairs={{0,2},{1,3},{2,0},{3,1},{4,6},{5,7},{6,4},{7,5},{8,10},{9,11},{10,... | collective-permute-start | bytes 884744 | tf_op jit(solution)/shard_map/ppermute | solution.py:44
  (16 other events, 125.4 us)

commit v5 on v4

--- a/solution.py
+++ b/solution.py
@@ -17,6 +17,7 @@
 HID = FF // 4
 VECS = 8
 GROUPS = 8
+SHARE = FF // GROUPS // 128
 BLOCK = D // GROUPS
 LABELS = 16
 MARKS = 48
@@ -122,7 +123,7 @@
 def pack_inputs(scalars, tables, tokens, segments, up, down, lines, tall):
     rows = tokens.shape[0]
     height = tables[0].shape[0]
-    extra = LABELS if lines else 0
+    skip = 2 * HID + (128 if lines else 0)
     operands = list(tables) + [tokens, segments, up, down] + lines + ([tall] if lines else [])
     count = len(operands)
 
@@ -138,10 +139,13 @@
         for copy in copies:
             copy.wait()
         joined = jnp.concatenate([ref[...].astype(F32) for ref in refs[:4]], axis=1).astype(BF)
-        send_ref[...] = joined
-        mine_ref[:height, :HID] = refs[6][...]
-        mine_ref[:height, HID : 2 * HID] = refs[7][...]
-        mine_ref[:height, 2 * HID :] = joined[:, : 3 * QUARTER]
+        send_ref[:, :D] = joined
+        send_ref[:, D : D + HID] = refs[6][...]
+        send_ref[:, D + HID :] = refs[7][...]
+        mine_ref[:, :HID] = refs[6][...]
+        mine_ref[:, HID : 2 * HID] = refs[7][...]
+        part = joined[:, : 3 * QUARTER].astype(F32)
+        mine_ref[:, skip:] = part.astype(BF)
         wide_ref[:, :HID] = refs[6][...]
         wide_ref[:, HID:] = refs[7][...]
         docs = refs[5][...].astype(F32)
@@ -150,17 +154,17 @@
         label_ref[rows:, :] = jnp.zeros((MARKS, D), BF)
         label_ref[rows:, :rows] = jnp.broadcast_to(docs, (MARKS, rows)).astype(BF)
         if lines:
-            share = FF // GROUPS
-            table = [ref[...].astype(F32) for ref in refs[8 : 8 + VECS]]
+            table = [ref[...].astype(F32)[None, :] for ref in refs[8 : 8 + VECS]]
             table = jnp.concatenate(table, axis=0)
-            table = jnp.concatenate([table, jnp.zeros((VECS, share - BLOCK), F32)], axis=1)
-            line = jnp.broadcast_to(refs[8 + VECS][...].astype(F32), (VECS, share))
-            mine_ref[height:, :] = jnp.zeros((LABELS, 3 * QUARTER + 2 * HID), BF)
-            mine_ref[height:, 2 * HID : 2 * HID + share] = jnp.concatenate([table, line], axis=0).astype(BF)
+            table = [jnp.concatenate([table, jnp.zeros((VECS, 128 - BLOCK), F32)], axis=1)]
+            line = refs[8 + VECS][...].astype(F32)[None, :]
+            table += [line[:, c * 128 : (c + 1) * 128] for c in range(SHARE)]
+            table += [jnp.zeros((height - VECS - SHARE, 128), F32)]
+            mine_ref[:, 2 * HID : skip] = jnp.concatenate(table, axis=0).astype(BF)
 
     outs = [
-        struct((height, D), BF),
-        struct((height + extra, 3 * QUARTER + 2 * HID), BF),
+        struct((height, D + 2 * HID), BF),
+        struct((height, skip + 3 * QUARTER), BF),
         struct((height, 2 * HID), BF),
         struct((rows + MARKS, D), BF),
         struct((1, rows), F32),
@@ -179,32 +183,45 @@
     )
 
 
-def split_arrived(scalars, arrived, wide, side, mine):
-    rows, tall = arrived.shape[0], mine.shape[0]
-
-    def body(_, far_ref, wide_ref, side_ref, mine_ref, narrow_ref, out_ref, both_ref):
+def split_arrived(scalars, arrived, mine, labelled):
+    rows = arrived.shape[0]
+    tall = rows + LABELS
+    skip = mine.shape[1] - 3 * QUARTER
+    direct = skip > 2 * HID
+
+    def body(_, far_ref, mine_ref, label_ref, narrow_ref, both_ref, send_ref):
         narrow_ref[...] = far_ref[:, : 3 * QUARTER]
-        out_ref[:, : 2 * HID] = wide_ref[...]
-        out_ref[:, 2 * HID :] = side_ref[...]
-        both_ref[:tall, :] = mine_ref[:, 2 * HID :]
+        both_ref[:rows, :] = mine_ref[:, skip:]
         both_ref[tall:, :] = far_ref[:, : 3 * QUARTER]
+        send_ref[...] = label_ref[...]
+        if direct:
+            both_ref[rows:tall, :] = jnp.zeros((LABELS, 3 * QUARTER), BF)
+            both_ref[rows:tall, :128] = mine_ref[:LABELS, 2 * HID : skip]
+            part = far_ref[:, 3 * QUARTER : D].astype(F32)
+            step = rows // 4
+            part = jnp.concatenate([part[k * step : (k + 1) * step] for k in range(4)], axis=1)
+            part = jnp.concatenate([part, jnp.zeros((MARKS - LABELS - step, D), F32)], axis=0)
+            send_ref[labelled.shape[0] - MARKS + LABELS :, :] = part.astype(BF)
 
     outs = [
         struct((rows, 3 * QUARTER), BF),
-        struct((rows, 2 * HID + QUARTER), BF),
         struct((rows + tall, 3 * QUARTER), BF),
+        struct(labelled.shape, BF),
     ]
-    return simple("split_arrived", body, scalars, [arrived, wide, side, mine], outs)
+    return simple("split_arrived", body, scalars, [arrived, mine, labelled], outs)
 
 
 def stack_narrow(scalars, mine_chip, far_chip, both_far):
-    tall = mine_chip[0].shape[0]
     rows = far_chip[0].shape[0]
+    tall = rows + LABELS
+    skip = mine_chip[0].shape[1] - 3 * QUARTER
 
     def body(_, *refs):
         out_ref = refs[-1]
         for k in range(3):
-            out_ref[k, :tall] = refs[k][:, 2 * HID :]
+            out_ref[k, :rows] = refs[k][:, skip:]
+            out_ref[k, rows:tall] = jnp.zeros((LABELS, 3 * QUARTER), BF)
+            out_ref[k, rows:tall, :128] = refs[k][:LABELS, 2 * HID : skip]
             out_ref[k, tall:] = refs[3 + k][...]
         out_ref[3] = refs[6][...]
 
@@ -226,22 +243,26 @@
     return simple("stack_wide", body, scalars, [*mine_chip, last, *feed_chip], [struct(shape, BF)])[0]
 
 
-def pack_feed(scalars, wide_far, first_send, arrived, side):
-    rows = wide_far.shape[0]
-    last = slice(3 * QUARTER, D)
-
-    def body(sc, far_ref, own_ref, arrived_ref, side_ref, out_ref):
-        out_ref[:, : 2 * HID] = far_ref[:, : 2 * HID]
+def pack_feed(scalars, first_send, arrived, side, last):
+    rows = arrived.shape[0]
+    columns = slice(3 * QUARTER, D)
+
+    def body(sc, own_ref, arrived_ref, side_ref, last_ref, out_ref):
+        out_ref[:, : 2 * HID] = arrived_ref[:, D:]
+        final = last_ref[...].astype(F32)
+        if last.shape[1] == D:
+            step = rows // 4
+            final = final[last.shape[0] - MARKS + LABELS :]
+            final = [final[:step, k * QUARTER : (k + 1) * QUARTER] for k in range(4)]
+            final = jnp.concatenate(final, axis=0)
         total = jnp.zeros((rows, D), F32)
-        for k, part in enumerate(
-            [own_ref[:, last], side_ref[...], arrived_ref[:, last], far_ref[:, 2 * HID :]]
-        ):
+        for k, part in enumerate([own_ref[:, columns], side_ref[...], arrived_ref[:, columns], final]):
             part = jnp.concatenate([part.astype(F32), jnp.zeros((rows, D - QUARTER), F32)], axis=1)
             total = total + pltpu.roll(part, (sc[2] ^ k) * QUARTER, 1)
         out_ref[:, 2 * HID :] = total.astype(BF)
 
     out = struct((rows, 2 * HID + D), BF)
-    return simple("pack_feed", body, scalars, [wide_far, first_send, arrived, side], [out])[0]
+    return simple("pack_feed", body, scalars, [first_send, arrived, side, last], [out])[0]
 
 
 def mark(docs, rows):
@@ -313,17 +334,19 @@
             vectors = jnp.zeros((LABELS, D), F32)
             for j in range(GROUPS):
                 block = sc[1] ^ j
-                line = weight_refs[j % 2][j // 2, BLOCK:tall, : FF // GROUPS].astype(F32)
+                line = weight_refs[j % 2][j // 2, BLOCK:tall, :128].astype(F32)
                 table = jnp.where(lax.broadcasted_iota(jnp.int32, line.shape, 1) < BLOCK, line, 0.0)
-                table = jnp.concatenate([table, jnp.zeros((LABELS, D - FF // GROUPS), F32)], axis=1)
+                table = jnp.concatenate([table, jnp.zeros((LABELS, D - 128), F32)], axis=1)
                 vectors = vectors + pltpu.roll(table, block * BLOCK, 1)
                 quarter = block // 2
                 for k in range(2):
 
                     @pl.when(quarter == sc[2] ^ (2 * k))
                     def _():
-                        to = pl.multiple_of((block % 2) * (HID // 2) + k * HID, 128)
-                        hidden_ref[:, pl.ds(to, HID // 2)] = line[VECS:]
+                        for c in range(SHARE):
+                            to = pl.multiple_of((block % 2) * (HID // 2) + k * HID + c * 128, 128)
+                            value = jnp.broadcast_to(line[VECS + c : VECS + c + 1], (VECS, 128))
+                            hidden_ref[:, pl.ds(to, 128)] = value
 
             vec_ref[...] = vectors[:VECS]
             lanes = lax.broadcasted_iota(jnp.int32, (VECS, HALF), 1)
@@ -695,11 +718,11 @@
 
 def halves(value):
     high = value.astype(BF).astype(F32)
-    return jnp.concatenate([high, value - high], axis=1).astype(BF)
+    return jnp.concatenate([high, value - high], axis=0).astype(BF)
 
 
 def whole_of(table):
-    return table[:, :128].astype(F32) + table[:, 128:].astype(F32)
+    return table[:LABELS].astype(F32) + table[LABELS : 2 * LABELS].astype(F32)
 
 
 def output_grads(scalars, blocks, small, small_side):
@@ -714,11 +737,11 @@
             target = (keep_ref, send_ref)[j % 2]
             block = sc[1] ^ j
             rows = pl.ds(pl.multiple_of(block * BLOCK, 16), BLOCK)
-            target[j // 2, :BLOCK] = result_ref[rows, :].astype(BF)
-            target[j // 2, BLOCK:] = jnp.zeros((LABELS, D), BF)
-            target[j // 2, BLOCK:, :256] = halves(small_ref[block] + side_ref[block])
-
-    outs = [struct((GROUPS // 2, BLOCK + LABELS, D), BF)] * 2
+            target[j // 2, :, :D] = result_ref[rows, :].astype(BF)
+            target[j // 2, :, D:] = jnp.zeros((BLOCK, 128), BF)
+            target[j // 2, : 2 * LABELS, D:] = halves(small_ref[block] + side_ref[block])
+
+    outs = [struct((GROUPS // 2, BLOCK, D + 128), BF)] * 2
     operands = [value for block in blocks for value in block] + [small, small_side]
     return call(
         "output_grads",
@@ -885,20 +908,19 @@
 
 def combine_both(scalars, keep, received, out_keep, out_received):
     count, rows, wide = keep.shape
-    tall = rows + LABELS
+    last = wide + D
 
     def body(_, keep_ref, recv_ref, out_keep_ref, out_recv_ref, *refs):
         for k in range(count):
             kind = refs[k].dtype
-            refs[k][:rows, :wide] = (keep_ref[k].astype(F32) + recv_ref[k].astype(F32)).astype(kind)
-            refs[k][rows:, :wide] = jnp.zeros((LABELS, wide), kind)
-            total = out_keep_ref[k, :rows].astype(F32) + out_recv_ref[k, :rows].astype(F32)
-            refs[k][:rows, wide:] = total.astype(kind)
-            refs[k][rows:, wide:] = jnp.zeros((LABELS, D), kind)
-            small = whole_of(out_keep_ref[k, rows:, :256]) + whole_of(out_recv_ref[k, rows:, :256])
-            refs[k][rows:, wide : wide + 256] = halves(small).astype(kind)
-
-    outs = [struct((tall, wide + D), F32)] + [struct((tall, wide + D), BF)] * (count - 1)
+            refs[k][:, :wide] = (keep_ref[k].astype(F32) + recv_ref[k].astype(F32)).astype(kind)
+            total = out_keep_ref[k, :, :D].astype(F32) + out_recv_ref[k, :, :D].astype(F32)
+            refs[k][:, wide:last] = total.astype(kind)
+            small = whole_of(out_keep_ref[k, :, D:]) + whole_of(out_recv_ref[k, :, D:])
+            refs[k][:, last:] = jnp.zeros((rows, 128), kind)
+            refs[k][: 2 * LABELS, last:] = halves(small).astype(kind)
+
+    outs = [struct((rows, last + 128), F32)] + [struct((rows, last + 128), BF)] * (count - 1)
     return simple("combine_both", body, scalars, [keep, received, out_keep, out_received], outs, 2)
 
 
@@ -917,15 +939,16 @@
     return simple("total_feed", body, scalars, sums, outs, 2)
 
 
-def total_projection(scalars, sums, rows):
-    tall = sums[0].shape[0]
+def total_projection(scalars, sums):
+    rows, width = sums[0].shape
     wide = 3 * HALF
+    last = wide + D
 
     def body(sc, *refs):
         keep_ref, send_ref = refs[-2:]
-        total = refs[0][:rows, :]
+        total = refs[0][:, :last]
         for ref in refs[1:-2]:
-            total = total + ref[:rows, :].astype(F32)
+            total = total + ref[:, :last].astype(F32)
         near, far = [], []
         for kind in range(3):
             both = [total[:, (3 * p + kind) * PAIR : (3 * p + kind + 1) * PAIR] for p in range(3)]
@@ -934,18 +957,19 @@
             far.append(both[:, QUARTER:])
         near.append(pltpu.roll(total[:, wide:], D - sc[2] * QUARTER, 1)[:, :QUARTER])
         far.append(pltpu.roll(total[:, wide:], D - (sc[2] ^ 2) * QUARTER, 1)[:, :QUARTER])
-        keep_ref[:rows, :] = jnp.concatenate(near, axis=1)
-        send_ref[:rows, :] = jnp.concatenate(far, axis=1).astype(BF)
-        if tall > rows:
+        keep_ref[:, :D] = jnp.concatenate(near, axis=1)
+        send_ref[:, :D] = jnp.concatenate(far, axis=1).astype(BF)
+        if width > last:
             small = jnp.zeros((LABELS, 128), F32)
             for ref in refs[:-2]:
-                small = small + whole_of(ref[rows:, wide : wide + 256])
-            keep_ref[rows:, :] = jnp.zeros((LABELS, D), F32)
-            send_ref[rows:, :] = jnp.zeros((LABELS, D), BF)
-            keep_ref[rows:, :128] = small
-            send_ref[rows:, :256] = halves(small)
-
-    outs = [struct((tall, D), F32), struct((tall, D), BF)]
+                small = small + whole_of(ref[:, last:])
+            keep_ref[:, D:] = jnp.zeros((rows, 128), F32)
+            send_ref[:, D:] = jnp.zeros((rows, 128), BF)
+            keep_ref[:LABELS, D:] = small
+            send_ref[: 2 * LABELS, D:] = halves(small)
+
+    width_out = D + width - last
+    outs = [struct((rows, width_out), F32), struct((rows, width_out), BF)]
     return simple("total_projection", body, scalars, sums, outs, 2)
 
 
@@ -960,22 +984,22 @@
     return simple("finish_feed", body, scalars, [keep, received], outs)
 
 
-def finish_projection(scalars, keep, received, rows):
-    tall = keep.shape[0]
+def finish_projection(scalars, keep, received):
+    rows, width = keep.shape
 
     def body(_, keep_ref, recv_ref, *refs):
-        total = keep_ref[:rows, :] + recv_ref[:rows, :].astype(F32)
+        total = keep_ref[:, :D] + recv_ref[:, :D].astype(F32)
         for k in range(4):
             refs[k][...] = total[:, k * QUARTER : (k + 1) * QUARTER]
-        if tall > rows:
-            small = keep_ref[rows:, :128] + whole_of(recv_ref[rows:, :256])
+        if width > D:
+            small = keep_ref[:LABELS, D:] + whole_of(recv_ref[:, D:])
             for k in range(VECS):
                 refs[4 + k][...] = small[k, :BLOCK]
-            for k in range(FF // GROUPS // 128):
+            for k in range(SHARE):
                 refs[4 + VECS][k * 128 : (k + 1) * 128] = small[VECS + k]
 
     outs = [struct((rows, QUARTER), F32)] * 4
-    if tall > rows:
+    if width > D:
         outs += [struct((BLOCK,), F32)] * VECS + [struct((FF // GROUPS,), F32)]
     return simple("finish_projection", body, scalars, [keep, received], outs)
 
@@ -1071,7 +1095,7 @@
         second_gain,
         second_shift,
     ]
-    lines = [line[None] for line in lines] if direct else []
+    lines = lines if direct else []
     first_send, mine, wide, labelled, own_docs = pack_inputs(
         scalars,
         [query_weight, key_weight, value_weight, output_weight],
@@ -1080,38 +1104,32 @@
         up_weight,
         down_weight.T,
         lines,
-        up_bias[None],
+        up_bias,
     )
     arrived = swap(first_send, "seq", 2)
     side = swap(output_weight, "seq", 1)
     if direct:
         mine_chip = [mine, swap(mine, "dp", 2), swap(mine, "dp", 4)]
-        labelled, side, mine_chip, arrived = together(labelled, side, mine_chip, arrived)
+        wide_last = swap(wide, "dp", 6)
+        labelled, side, wide_last, mine_chip, arrived = together(
+            labelled, side, wide_last, mine_chip, arrived
+        )
     else:
         arrived, labelled, side = together(arrived, labelled, side)
-    narrow_far, wide_send, both = split_arrived(scalars, arrived, wide, side, mine)
-    wide_far = swap(wide_send, "seq", 2)
+    narrow_far, both, partner_send = split_arrived(scalars, arrived, mine, labelled)
+    partner = swap(partner_send, "seq", 1)
+    halo_near = lax.ppermute(labelled, "seq", [(1, 2), (2, 1)])
     if direct:
         far_chip = [narrow_far, swap(narrow_far, "dp", 2), swap(narrow_far, "dp", 4)]
         both_far = swap(both, "dp", 6)
-        mine_chip, labelled, cot_own, wide, far_chip, both_far, wide_far = together(
-            mine_chip, labelled, cot_own, wide, far_chip, both_far, wide_far
+        mine_chip, cot_own, far_chip, both_far, partner, halo_near = together(
+            mine_chip, cot_own, far_chip, both_far, partner, halo_near
         )
         stacked = stack_narrow(scalars, mine_chip, far_chip, both_far)
         pieces = [stacked, swap(stacked, "dp", 1)]
-    partner = swap(labelled, "seq", 1)
-    halo_near = lax.ppermute(labelled, "seq", [(1, 2), (2, 1)])
-    if direct:
-        feed_piece = pack_feed(scalars, wide_far, first_send, arrived, side)
-        feed_chip = [feed_piece, swap(feed_piece, "dp", 2), swap(feed_piece, "dp", 4)]
-        wide, pieces, partner, feed_chip, halo_near = together(
-            wide, pieces, partner, feed_chip, halo_near
-        )
-        feed_chip = feed_chip + [swap(feed_chip[0], "dp", 6)]
-        wide_last = swap(wide, "dp", 6)
+        feed_chip = chip_pieces(pack_feed(scalars, first_send, arrived, side, partner))
     halo_far = lax.ppermute(halo_near, "seq", [(1, 0), (2, 3)])
     if not direct:
-        share = FF // GROUPS
         vectors = jnp.stack(
             [
                 query_bias,
@@ -1125,17 +1143,18 @@
             ]
         )
         lines = lax.all_gather(vectors, "dp", axis=1, tiled=True).reshape(VECS, GROUPS, BLOCK)
-        lines = jnp.pad(lines, ((0, 0), (0, 0), (0, share - BLOCK)))
-        tall = lax.all_gather(up_bias, "dp", axis=0, tiled=True).reshape(1, GROUPS, share)
-        lines = jnp.concatenate([lines, jnp.broadcast_to(tall, (VECS, GROUPS, share))], axis=0)
-        lines = jnp.pad(lines, ((0, 0), (0, 0), (0, 3 * QUARTER - share)))
+        lines = jnp.pad(lines, ((0, 0), (0, 0), (0, 128 - BLOCK)))
+        tall = lax.all_gather(up_bias, "dp", axis=0, tiled=True).reshape(GROUPS, SHARE, 128).transpose(1, 0, 2)
+        lines = jnp.concatenate([lines, tall], axis=0)
+        lines = jnp.pad(lines, ((0, LABELS - VECS - SHARE), (0, 0), (0, 3 * QUARTER - 128)))
         lines = lines.transpose(1, 0, 2)
         gathered = gather_rows(mine)
         pieces = [
             jnp.concatenate([half[:, :, 2 * HID :], lines[k::2], far], axis=1)
             for k, (half, far) in enumerate(zip(gathered, gather_rows(narrow_far)))
         ]
-        feed = gather_rows(pack_feed(scalars, wide_far, first_send, arrived, side))
+        last = swap(arrived[:, 3 * QUARTER : D], "seq", 1)
+        feed = gather_rows(pack_feed(scalars, first_send, arrived, side, last))
         weights = [
             jnp.concatenate([half[:, :, : 2 * HID], far], axis=2) for half, far in zip(gathered, feed)
         ]
@@ -1255,7 +1274,7 @@
         out_parts = rows_of(*output_grads(scalars, out_blocks, small, small_side))
         sums = scattered(
             jnp.concatenate(
-                [rows_of(*projection_parts).reshape(D, -1), out_parts[:, :BLOCK].reshape(D, -1)], axis=1
+                [rows_of(*projection_parts).reshape(D, -1), out_parts[:, :, :D].reshape(D, -1)], axis=1
             )
         )
         feed_keep, feed_send = total_feed(scalars, feed_sums)
@@ -1264,12 +1283,12 @@
     input_grad = own_grad + input_keep + input_far.astype(F32)
     if direct:
         sums, up_grad, input_grad = together(sums, up_grad, input_grad)
-    keep, send = total_projection(scalars, sums, piece_rows)
-    projections = list(finish_projection(scalars, keep, swap(send, "seq", 2), piece_rows))
+    keep, send = total_projection(scalars, sums)
+    projections = list(finish_projection(scalars, keep, swap(send, "seq", 2)))
     if direct:
         projections, vec, tall_lines = projections[:4], projections[4:-1], projections[-1]
     else:
-        tile = out_parts[:, BLOCK:, :128] + out_parts[:, BLOCK:, 128:256]
+        tile = out_parts[:, :LABELS, D:] + out_parts[:, LABELS : 2 * LABELS, D:]
         tile = tile + swap(tile, "seq", 2)
         wide_lines = tile[:, :VECS, :BLOCK].transpose(1, 0, 2).reshape(VECS, D)
         wide_lines = lax.psum_scatter(wide_lines, "dp", scatter_dimension=1, tiled=True)

time: 193 us -> 186 us (0.964)
  starting transfers between devices: 47.8 us -> 44.2 us
  waiting for transfers between devices: 77.8 us -> 75.3 us
    ppermute x36 -> x35, waiting for transfers between devices: 74.8 us -> 69.8 us  [swap(): return lax.ppermute(value, axis, [(k, k ^ mask) for k in range(count)])]
    ppermute x36 -> x35, starting transfers between devices: 45.9 us -> 42.2 us  [swap(): return lax.ppermute(value, axis, [(k, k ^ mask) for k in range(count)])]
    ppermute x1, waiting for transfers between devices: 3.01 us -> 5.49 us  [per_device(): halo_far = lax.ppermute(halo_near, 'seq', [(1, 0), (2, 3)])]
  transfers between devices with their start and end apart: 38 -> 37, of which waited for: 21 -> 17; matrix products, arithmetic and copies ran while one was open for 1% -> 1% of each run, Pallas kernels for 30% -> 31%
where the time goes in v5:
time: 186 us
  waiting for transfers between devices  75.3 us (40%)
  Pallas kernels  64.2 us (35%)
  starting transfers between devices  44.2 us (24%)
    ppermute x35, waiting for transfers between devices, swap(): return lax.ppermute(value, axis, [(k, k ^ mask) for k in range(count)])  69.8 us
    pallas_call x26, Pallas kernels, call(): pl.pallas_call(body, out_shape=outs, grid_spec=spec, compiler_params=para...  64.2 us
    ppermute x35, starting transfers between devices, swap(): return lax.ppermute(value, axis, [(k, k ^ mask) for k in range(count)])  42.2 us
    ppermute x1, waiting for transfers between devices, per_device(): halo_far = lax.ppermute(halo_near, 'seq', [(1, 0), (2, 3)])  5.49 us
  transfers between devices with their start and end apart: 37, of which 17 were waited for; matrix products, arithmetic and copies ran while one was open for 1% of the time, Pallas kernels for 31%

profile of v5, /device:TPU:0, one launch (start us, length us, event | category | flops | bytes accessed | tf_op | source)
XLA Modules:
  0.0 185.9 jit_solution(13402951385233307204)
XLA Ops:
  2.8 4.1 %collective-permute-start.4 = (bf16[96,2304]{1,0:T(8,128)(2,1)S(1)}, bf16[96,2304]{1,0:T(8,128)(2,1)S(1)}, u32[]{:S(2)}, u32[]{:S(2)}) collective-permute-start(bf16[96,2304]{1,0:T(8,128)(2,1)S(1)} %get-tuple-element.178.own_ref), channel_id=1, source_target_pairs={{0,2},{1,3},{2,0},{3,1},{4,6},{5,7},{6,4},{7,5},{8,10},{9,11},{10,... | collective-permute-start | bytes 1327112 | tf_op jit(solution)/shard_map/ppermute | solution.py:45
  12.0 5.6 %collective-permute-done.side_ref = bf16[96,192]{1,0:T(8,128)(2,1)S(1)} collective-permute-done((bf16[96,192]{1,0:T(8,128)(2,1)}, bf16[96,192]{1,0:T(8,128)(2,1)S(1)}, u32[]{:S(2)}, u32[]{:S(2)}) %collective-permute-start) | collective-permute-done | bytes 36896 | tf_op jit(solution)/shard_map/ppermute | solution.py:45
  17.6 8.4 %collective-permute-done.1.refs_3_ = bf16[96,1536]{1,0:T(8,128)(2,1)S(1)} collective-permute-done((bf16[96,1536]{1,0:T(8,128)(2,1)S(1)}, bf16[96,1536]{1,0:T(8,128)(2,1)S(1)}, u32[]{:S(2)}, u32[]{:S(2)}) %collective-permute-start.1) | collective-permute-done | bytes 294944 | tf_op jit(solution)/shard_map/ppermute | solution.py:45
  32.6 7.8 %collective-permute-done.5.refs_4_ = bf16[96,576]{1,0:T(8,128)(2,1)S(1)} collective-permute-done((bf16[96,576]{1,0:T(8,128)(2,1)S(1)}, bf16[96,576]{1,0:T(8,128)(2,1)S(1)}, u32[]{:S(2)}, u32[]{:S(2)}) %collective-permute-start.5) | collective-permute-done | bytes 110624 | tf_op jit(solution)/shard_map/ppermute | solution.py:45
  46.9 6.3 %attend_pair.1 = (bf16[512,384]{1,0:T(8,128)(2,1)S(1)}, bf16[512,384]{1,0:T(8,128)(2,1)S(1)}, bf16[512,384]{1,0:T(8,128)(2,1)S(1)}, bf16[256,384]{1,0:T(8,128)(2...) custom-call(s32[3]{0:T(128)S(1)} %pad_add_fusion._.sc, ...), custom_call_target="tpu_custom_call" | custom-call | flops 80000000 | bytes 1024 | tf_op jit(solution)/shard_map/attend_pair/pallas_call | solution.py:68
  53.2 5.5 %collective-permute-done.11.far_ref = bf16[304,768]{1,0:T(8,128)(2,1)S(1)} collective-permute-done((bf16[304,768]{1,0:T(8,128)(2,1)S(1)}, bf16[304,768]{1,0:T(8,128)(2,1)S(1)}, u32[]{:S(2)}, u32[]{:S(2)}) %collective-permute-start.11) | collective-permute-done | bytes 466976 | tf_op jit(solution)/shard_map/ppermute | solution.py:1131
  58.7 5.5 %attend_halo.1 = (bf16[256,384]{1,0:T(8,128)(2,1)S(1)}, bf16[256,384]{1,0:T(8,128)(2,1)S(1)}, bf16[256,384]{1,0:T(8,128)(2,1)S(1)}, bf16[256,384]{1,0:T(8,128)(2...) custom-call(s32[3]{0:T(128)S(1)} %pad_add_fusion._.sc, ...), custom_call_target="tpu_custom_call" | custom-call | flops 60000000 | bytes 1024 | tf_op jit(solution)/shard_map/attend_halo/pallas_call | solution.py:68
  64.2 2.5 %collective-permute-done.14.refs_6_ = bf16[96,2304]{1,0:T(8,128)(2,1)S(1)} collective-permute-done((bf16[96,2304]{1,0:T(8,128)(2,1)S(1)}, bf16[96,2304]{1,0:T(8,128)(2,1)S(1)}, u32[]{:S(2)}, u32[]{:S(2)}) %collective-permute-start.14) | collective-permute-done | bytes 442400 | tf_op jit(solution)/shard_map/ppermute | solution.py:45
  67.5 5.0 %collective-permute-start.16 = (bf16[256,384]{1,0:T(8,128)(2,1)S(1)}, bf16[256,384]{1,0:T(8,128)(2,1)S(1)}, u32[]{:S(2)}, u32[]{:S(2)}) collective-permute-start(bf16[256,384]{1,0:T(8,128)(2,1)S(1)} %get-tuple-element.213.mine_ref.refs_3_), channel_id=1, source_target_pairs={{0,1},{1,0},{2,3},{3,2},{4,5},{5,4},{6,7},{7,6},{8,9},{9,8},{10,11... | collective-permute-start | bytes 589832 | tf_op jit(solution)/shard_map/ppermute | solution.py:45
  72.6 5.6 %collective-permute-done.16.partner_ref.refs_4_ = bf16[256,384]{1,0:T(8,128)(2,1)S(1)} collective-permute-done((bf16[256,384]{1,0:T(8,128)(2,1)S(1)}, bf16[256,384]{1,0:T(8,128)(2,1)S(1)}, u32[]{:S(2)}, u32[]{:S(2)}) %collective-permute-start.16) | collective-permute-done | bytes 196640 | tf_op jit(solution)/shard_map/ppermute | solution.py:45
  78.2 3.2 %feed_forward.2 = (f32[256,768]{1,0:T(8,128)S(1)}, f32[256,128]{1,0:T(8,128)S(1)}, bf16[256,768]{1,0:T(8,128)(2,1)S(1)}, f32[256,1536]{1,0:T(8,128)S(1)}, bf16[2...) custom-call(s32[3]{0:T(128)S(1)} %pad_add_fusion._.sc, ...), custom_call_target="tpu_custom_call" | custom-call | flops 60000000 | bytes 1024 | tf_op jit(solution)/shard_map/feed_forward/pallas_call | solution.py:68
  83.4 2.9 %feed_forward.3 = (f32[256,768]{1,0:T(8,128)S(1)}, f32[256,128]{1,0:T(8,128)S(1)}, bf16[256,768]{1,0:T(8,128)(2,1)S(1)}, f32[256,1536]{1,0:T(8,128)S(1)}, bf16[2...) custom-call(s32[3]{0:T(128)S(1)} %pad_add_fusion._.sc, bf16[256,384]{1,0:T(8,128)(2,1)S(1)} %get-tuple-element.210.mine_ref.refs_0_, ...), custom_call_target="tpu_custom_call" | custom-call | flops 60000000 | bytes 1024 | tf_op jit(solution)/shard_map/feed_forward/pallas_call | solution.py:68
  87.6 7.4 %collective-permute-done.18.recv_ref = bf16[256,768]{1,0:T(8,128)(2,1)S(1)} collective-permute-done((bf16[256,768]{1,0:T(8,128)(2,1)S(1)}, bf16[256,768]{1,0:T(8,128)(2,1)S(1)}, u32[]{:S(2)}, u32[]{:S(2)}) %collective-permute-start.18) | collective-permute-done | bytes 393248 | tf_op jit(solution)/shard_map/ppermute | solution.py:45
  95.1 2.9 %second_norm.2 = (f32[256,768]{1,0:T(8,128)S(1)}, bf16[256,768]{1,0:T(8,128)(2,1)S(1)}, bf16[256,1536]{1,0:T(8,128)(2,1)S(1)}, bf16[256,768]{1,0:T(8,128)(2,1)S(...) custom-call(s32[3]{0:T(128)S(1)} %pad_add_fusion._.sc, ...), custom_call_target="tpu_custom_call" | custom-call | flops 50000000 | bytes 1024 | tf_op jit(solution)/shard_map/second_norm/pallas_call | solution.py:68
  98.0 2.3 %collective-permute-start.20 = (bf16[256,768]{1,0:T(8,128)(2,1)S(1)}, bf16[256,768]{1,0:T(8,128)(2,1)S(1)}, u32[]{:S(2)}, u32[]{:S(2)}) collective-permute-start(bf16[256,768]{1,0:T(8,128)(2,1)S(1)} %get-tuple-element.263.part_ref), channel_id=1, source_target_pairs={{0,1},{1,0},{2,3},{3,2},{4,5},{5,4},{6,7},{7,6},{8,9},{9,8},{10,11... | collective-permute-start | bytes 1179656 | tf_op jit(solution)/shard_map/ppermute | solution.py:45
  103.5 3.8 %second_norm.3 = (f32[256,768]{1,0:T(8,128)S(1)}, bf16[256,768]{1,0:T(8,128)(2,1)S(1)}, bf16[256,1536]{1,0:T(8,128)(2,1)S(1)}, bf16[256,768]{1,0:T(8,128)(2,1)S(...) custom-call(s32[3]{0:T(128)S(1)} %pad_add_fusion._.sc, ...), custom_call_target="tpu_custom_call" | custom-call | flops 50000000 | bytes 1024 | tf_op jit(solution)/shard_map/second_norm/pallas_call | solution.py:68
  107.3 5.0 %feed_forward_grads.1 = (bf16[4,96,3072]{2,1,0:T(8,128)(2,1)S(1)}, bf16[4,96,3072]{2,1,0:T(8,128)(2,1)S(1)}) custom-call(s32[3]{0:T(128)S(1)} %pad_add_fusion._.sc, bf16[256,768]{1,0:T(8,128)(2,1)S(1)} %get-tuple-element.248.refs_0_, bf16[256,1536]{1,0:T(8,128)(2,1)S(1)} %get-tuple-element.240.refs_1_, bf16[256,768]{1,0:T(8,128)(2,1)S(1)} %get-tuple-element.239.refs_2_, ...), custom_call_target="tpu_custom_call" | custom-call | flops 80000000 | bytes 1024 | tf_op jit(solution)/shard_map/feed_forward_grads/pallas_call | solution.py:68
  122.3 6.6 %collective-permute-done.22.recv_ref = bf16[256,768]{1,0:T(8,128)(2,1)S(1)} collective-permute-done((bf16[256,768]{1,0:T(8,128)(2,1)S(1)}, bf16[256,768]{1,0:T(8,128)(2,1)S(1)}, u32[]{:S(2)}, u32[]{:S(2)}) %collective-permute-start.22) | collective-permute-done | bytes 393248 | tf_op jit(solution)/shard_map/ppermute | solution.py:45
  128.9 2.3 %first_norm.3 = (bf16[256,768]{1,0:T(8,128)(2,1)S(1)}, bf16[256,384]{1,0:T(8,128)(2,1)S(1)}, f32[8,256]{1,0:T(8,128)S(1)}, f32[256,768]{1,0:T(8,128)S(1)}, f32[8,768]{1,0:T(8,128)S(1)}) custom-call(s32[3]{0:T(128)S(1)} %pad_add_fusion._.sc, bf16[256,768]{1,0:T(8,128)(2,1)S(1)} %get-tuple-element.258.part_ref, ...), custom_call_target="tpu_custom_call" | custom-call | flops 30000000 | bytes 1024 | tf_op jit(solution)/shard_map/first_norm/pallas_call | solution.py:68
  131.3 10.7 %attend_backward.1 = (bf16[512,1152]{1,0:T(8,128)(2,1)S(1)}, f32[256,768]{1,0:T(8,128)S(1)}, bf16[256,768]{1,0:T(8,128)(2,1)S(1)}, f32[8,1152]{1,0:T(8,128)S(1)}) custom-call(s32[3]{0:T(128)S(1)} %pad_add_fusion._.sc, bf16[512,384]{1,0:T(8,128)(2,1)S(1)} %get-tuple-element.206.q_ref.refs_0_, bf16[512,384]{1,0:T(8,128)(2,1)S(1)} %get-tuple-element.207.k_ref.refs_1_, ...), custom_call_target="tpu_custom_call" | custom-call | flops 4499999744 | bytes 1024 | tf_op jit(solution)/shard_map/attend_backward/pallas_call | solution.py:68
  142.8 2.9 %projection_grads.1 = (bf16[4,96,1152]{2,1,0:T(8,128)(2,1)S(1)}, bf16[4,96,1152]{2,1,0:T(8,128)(2,1)S(1)}) custom-call(s32[3]{0:T(128)S(1)} %pad_add_fusion._.sc, bf16[512,768]{1,0:T(8,128)(2,1)S(1)} %get-tuple-element.214.x_ref, bf16[512,1152]{1,0:T(8,128)(2,1)S(1)} %get-tuple-element.277.grad_ref), custom_call_target="tpu_custom_call" | custom-call | flops 50000000 | bytes 1024 | tf_op jit(solution)/shard_map/projection_grads/pallas_call | solution.py:68
  158.8 4.5 %collective-permute-done.35 = bf16[256,768]{1,0:T(8,128)(2,1)S(1)} collective-permute-done((bf16[256,768]{1,0:T(8,128)(2,1)S(1)}, bf16[256,768]{1,0:T(8,128)(2,1)S(1)}, u32[]{:S(2)}, u32[]{:S(2)}) %collective-permute-start.35) | collective-permute-done | bytes 393248 | tf_op jit(solution)/shard_map/ppermute | solution.py:45
  164.3 8.2 %collective-permute-done.34.recv_ref = bf16[96,1536]{1,0:T(8,128)(2,1)S(1)} collective-permute-done((bf16[96,1536]{1,0:T(8,128)(2,1)S(1)}, bf16[96,1536]{1,0:T(8,128)(2,1)S(1)}, u32[]{:S(2)}, u32[]{:S(2)}) %collective-permute-start.34) | collective-permute-done | bytes 294944 | tf_op jit(solution)/shard_map/ppermute | solution.py:45
  175.8 8.5 %collective-permute-done.36.recv_ref = bf16[96,896]{1,0:T(8,128)(2,1)S(1)} collective-permute-done((bf16[96,896]{1,0:T(8,128)(2,1)S(1)}, bf16[96,896]{1,0:T(8,128)(2,1)S(1)}, u32[]{:S(2)}, u32[]{:S(2)}) %collective-permute-start.36) | collective-permute-done | bytes 172064 | tf_op jit(solution)/shard_map/ppermute | solution.py:45
  (82 shorter events, 57.3 us)
Async XLA Ops:
  2.8 23.7 %collective-permute-start.4 = (bf16[96,2304]{1,0:T(8,128)(2,1)S(1)}, bf16[96,2304]{1,0:T(8,128)(2,1)S(1)}, u32[]{:S(2)}, u32[]{:S(2)}) collective-permute-start(bf16[96,2304]{1,0:T(8,128)(2,1)S(1)} %get-tuple-element.178.own_ref), channel_id=1, source_target_pairs={{0,2},{1,3},{2,0},{3,1},{4,6},{5,7},{6,4},{7,5},{8,10},{9,11},{10,... | collective-permute-start | bytes 1327112 | tf_op jit(solution)/shard_map/ppermute | solution.py:45
  6.9 19.0 %collective-permute-start.2 = (bf16[96,2240]{1,0:T(8,128)(2,1)S(1)}, bf16[96,2240]{1,0:T(8,128)(2,1)S(1)}, u32[]{:S(2)}, u32[]{:S(2)}) collective-permute-start(bf16[96,2240]{1,0:T(8,128)(2,1)S(1)} %get-tuple-element.190.mine_ref.refs_0_), channel_id=1, source_target_pairs={{0,8},{4,12},{8,0},{12,4},{16,24},{20,28},{24,16},{28,20},{1,9},{5... | collective-permute-start | bytes 1290248 | tf_op jit(solution)/shard_map/ppermute | solution.py:45
  8.4 17.7 %collective-permute-start.3 = (bf16[96,2240]{1,0:T(8,128)(2,1)S(1)}, bf16[96,2240]{1,0:T(8,128)(2,1)S(1)}, u32[]{:S(2)}, u32[]{:S(2)}) collective-permute-start(bf16[96,2240]{1,0:T(8,128)(2,1)S(1)} %get-tuple-element.190.mine_ref.refs_0_), channel_id=1, source_target_pairs={{0,16},{4,20},{8,24},{12,28},{16,0},{20,4},{24,8},{28,12},{1,17},{... | collective-permute-start | bytes 1290248 | tf_op jit(solution)/shard_map/ppermute | solution.py:45
  10.0 16.0 %collective-permute-start.1 = (bf16[96,1536]{1,0:T(8,128)(2,1)S(1)}, bf16[96,1536]{1,0:T(8,128)(2,1)S(1)}, u32[]{:S(2)}, u32[]{:S(2)}) collective-permute-start(bf16[96,1536]{1,0:T(8,128)(2,1)S(1)} %get-tuple-element.176), channel_id=1, source_target_pairs={{0,24},{4,28},{8,16},{12,20},{16,8},{20,12},{24,0},{28,4},{1,25},{... | collective-permute-start | bytes 884744 | tf_op jit(solution)/shard_map/ppermute | solution.py:45
  27.2 13.2 %collective-permute-start.8 = (bf16[304,768]{1,0:T(8,128)(2,1)S(1)}, bf16[304,768]{1,0:T(8,128)(2,1)S(1)}, u32[]{:S(2)}, u32[]{:S(2)}) collective-permute-start(bf16[304,768]{1,0:T(8,128)(2,1)S(1)} %get-tuple-element.186), channel_id=1, source_target_pairs={{0,1},{1,0},{2,3},{3,2},{4,5},{5,4},{6,7},{7,6},{8,9},{9,8},{10,11... | collective-permute-start | bytes 1400840 | tf_op jit(solution)/shard_map/ppermute | solution.py:45
  28.4 12.1 %collective-permute-start.9 = (bf16[304,768]{1,0:T(8,128)(2,1)S(1)}, bf16[304,768]{1,0:T(8,128)(2,1)S(1)}, u32[]{:S(2)}, u32[]{:S(2)}) collective-permute-start(bf16[304,768]{1,0:T(8,128)(2,1)S(1)} %get-tuple-element.183.label_ref), channel_id=1, source_target_pairs={{1,2},{2,1},{5,6},{6,5},{9,10},{10,9},{13,14},{14,13},{17,18},{18,... | collective-permute-start | bytes 1400840 | tf_op jit(solution)/shard_map/ppermute | solution.py:1121
  41.2 17.5 %collective-permute-start.11 = (bf16[304,768]{1,0:T(8,128)(2,1)S(1)}, bf16[304,768]{1,0:T(8,128)(2,1)S(1)}, u32[]{:S(2)}, u32[]{:S(2)}) collective-permute-start(bf16[304,768]{1,0:T(8,128)(2,1)S(1)} %collective-permute-done.9.near_ref), channel_id=1, source_target_pairs={{1,0},{2,3},{5,4},{6,7},{9,8},{10,11},{13,12},{14,15},{17,16},{18,... | collective-permute-start | bytes 1400840 | tf_op jit(solution)/shard_map/ppermute | solution.py:1131
  43.4 20.9 %collective-permute-start.13 = (bf16[96,2304]{1,0:T(8,128)(2,1)S(1)}, bf16[96,2304]{1,0:T(8,128)(2,1)S(1)}, u32[]{:S(2)}, u32[]{:S(2)}) collective-permute-start(bf16[96,2304]{1,0:T(8,128)(2,1)S(1)} %pack_feed.1.refs_4_), channel_id=1, source_target_pairs={{0,8},{4,12},{8,0},{12,4},{16,24},{20,28},{24,16},{28,20},{1,9},{5... | collective-permute-start | bytes 1327112 | tf_op jit(solution)/shard_map/ppermute | solution.py:45
  44.9 21.8 %collective-permute-start.14 = (bf16[96,2304]{1,0:T(8,128)(2,1)S(1)}, bf16[96,2304]{1,0:T(8,128)(2,1)S(1)}, u32[]{:S(2)}, u32[]{:S(2)}) collective-permute-start(bf16[96,2304]{1,0:T(8,128)(2,1)S(1)} %pack_feed.1.refs_4_), channel_id=1, source_target_pairs={{0,16},{4,20},{8,24},{12,28},{16,0},{20,4},{24,8},{28,12},{1,17},{... | collective-permute-start | bytes 1327112 | tf_op jit(solution)/shard_map/ppermute | solution.py:45
  46.3 20.4 %collective-permute-start.15 = (bf16[96,2304]{1,0:T(8,128)(2,1)S(1)}, bf16[96,2304]{1,0:T(8,128)(2,1)S(1)}, u32[]{:S(2)}, u32[]{:S(2)}) collective-permute-start(bf16[96,2304]{1,0:T(8,128)(2,1)S(1)} %pack_feed.1.refs_4_), channel_id=1, source_target_pairs={{0,24},{4,28},{8,16},{12,20},{16,8},{20,12},{24,0},{28,4},{1,25},{... | collective-permute-start | bytes 1327112 | tf_op jit(solution)/shard_map/ppermute | solution.py:45
  72.5 15.2 %collective-permute-start.19 = (bf16[256,768]{1,0:T(8,128)(2,1)S(1)}, bf16[256,768]{1,0:T(8,128)(2,1)S(1)}, u32[]{:S(2)}, u32[]{:S(2)}) collective-permute-start(bf16[256,768]{1,0:T(8,128)(2,1)S(1)} %bitcast.9), channel_id=1, source_target_pairs={{0,1},{1,0},{2,3},{3,2},{4,5},{5,4},{6,7},{7,6},{8,9},{9,8},{10,11... | collective-permute-start | bytes 1179656 | tf_op jit(solution)/shard_map/ppermute | solution.py:45
  81.4 13.7 %collective-permute-start.18 = (bf16[256,768]{1,0:T(8,128)(2,1)S(1)}, bf16[256,768]{1,0:T(8,128)(2,1)S(1)}, u32[]{:S(2)}, u32[]{:S(2)}) collective-permute-start(bf16[256,768]{1,0:T(8,128)(2,1)S(1)} %get-tuple-element.222.part_ref), channel_id=1, source_target_pairs={{0,1},{1,0},{2,3},{3,2},{4,5},{5,4},{6,7},{7,6},{8,9},{9,8},{10,11... | collective-permute-start | bytes 1179656 | tf_op jit(solution)/shard_map/ppermute | solution.py:45
  86.3 17.2 %collective-permute-start.21 = (bf16[256,768]{1,0:T(8,128)(2,1)S(1)}, bf16[256,768]{1,0:T(8,128)(2,1)S(1)}, u32[]{:S(2)}, u32[]{:S(2)}) collective-permute-start(bf16[256,768]{1,0:T(8,128)(2,1)S(1)} %get-tuple-element.232.part_ref), channel_id=1, source_target_pairs={{0,1},{1,0},{2,3},{3,2},{4,5},{5,4},{6,7},{7,6},{8,9},{9,8},{10,11... | collective-permute-start | bytes 1179656 | tf_op jit(solution)/shard_map/ppermute | solution.py:45
  98.0 14.3 %collective-permute-start.20 = (bf16[256,768]{1,0:T(8,128)(2,1)S(1)}, bf16[256,768]{1,0:T(8,128)(2,1)S(1)}, u32[]{:S(2)}, u32[]{:S(2)}) collective-permute-start(bf16[256,768]{1,0:T(8,128)(2,1)S(1)} %get-tuple-element.263.part_ref), channel_id=1, source_target_pairs={{0,1},{1,0},{2,3},{3,2},{4,5},{5,4},{6,7},{7,6},{8,9},{9,8},{10,11... | collective-permute-start | bytes 1179656 | tf_op jit(solution)/shard_map/ppermute | solution.py:45
  112.4 16.5 %collective-permute-start.22 = (bf16[256,768]{1,0:T(8,128)(2,1)S(1)}, bf16[256,768]{1,0:T(8,128)(2,1)S(1)}, u32[]{:S(2)}, u32[]{:S(2)}) collective-permute-start(bf16[256,768]{1,0:T(8,128)(2,1)S(1)} %get-tuple-element.258.part_ref), channel_id=1, source_target_pairs={{0,1},{1,0},{2,3},{3,2},{4,5},{5,4},{6,7},{7,6},{8,9},{9,8},{10,11... | collective-permute-start | bytes 1179656 | tf_op jit(solution)/shard_map/ppermute | solution.py:45
  116.3 15.0 %collective-permute-start.23 = (bf16[304,384]{1,0:T(8,128)(2,1)S(1)}, bf16[304,384]{1,0:T(8,128)(2,1)S(1)}, u32[]{:S(2)}, u32[]{:S(2)}) collective-permute-start(bf16[304,384]{1,0:T(8,128)(2,1)S(1)} %get-tuple-element.273), channel_id=1, source_target_pairs={{0,2},{1,3},{2,0},{3,1},{4,6},{5,7},{6,4},{7,5},{8,10},{9,11},{10,... | collective-permute-start | bytes 700424 | tf_op jit(solution)/shard_map/ppermute | solution.py:45
  118.8 28.2 %collective-permute-start.26 = (bf16[96,3072]{1,0:T(8,128)(2,1)S(1)}, bf16[96,3072]{1,0:T(8,128)(2,1)S(1)}, u32[]{:S(2)}, u32[]{:S(2)}) collective-permute-start(bf16[96,3072]{1,0:T(8,128)(2,1)S(1)} %get-tuple-element.287), channel_id=1, source_target_pairs={{0,8},{4,12},{8,0},{12,4},{16,24},{20,28},{24,16},{28,20},{1,9},{5... | collective-permute-start | bytes 1769480 | tf_op jit(solution)/shard_map/ppermute | solution.py:45
  120.1 26.9 %collective-permute-start.27 = (bf16[96,3072]{1,0:T(8,128)(2,1)S(1)}, bf16[96,3072]{1,0:T(8,128)(2,1)S(1)}, u32[]{:S(2)}, u32[]{:S(2)}) collective-permute-start(bf16[96,3072]{1,0:T(8,128)(2,1)S(1)} %get-tuple-element.288), channel_id=1, source_target_pairs={{0,16},{4,20},{8,24},{12,28},{16,0},{20,4},{24,8},{28,12},{1,17},{... | collective-permute-start | bytes 1769480 | tf_op jit(solution)/shard_map/ppermute | solution.py:45
  120.9 26.7 %collective-permute-start.28 = (bf16[96,3072]{1,0:T(8,128)(2,1)S(1)}, bf16[96,3072]{1,0:T(8,128)(2,1)S(1)}, u32[]{:S(2)}, u32[]{:S(2)}) collective-permute-start(bf16[96,3072]{1,0:T(8,128)(2,1)S(1)} %get-tuple-element.289), channel_id=1, source_target_pairs={{0,24},{4,28},{8,16},{12,20},{16,8},{20,12},{24,0},{28,4},{1,25},{... | collective-permute-start | bytes 1769480 | tf_op jit(solution)/shard_map/ppermute | solution.py:45
  149.7 13.6 %collective-permute-start.35 = (bf16[256,768]{1,0:T(8,128)(2,1)S(1)}, bf16[256,768]{1,0:T(8,128)(2,1)S(1)}, u32[]{:S(2)}, u32[]{:S(2)}) collective-permute-start(bf16[256,768]{1,0:T(8,128)(2,1)S(1)} %get-tuple-element.310), channel_id=1, source_target_pairs={{0,1},{1,0},{2,3},{3,2},{4,5},{5,4},{6,7},{7,6},{8,9},{9,8},{10,11... | collective-permute-start | bytes 1179656 | tf_op jit(solution)/shard_map/ppermute | solution.py:45
  152.3 21.5 %collective-permute-start.31 = (bf16[96,2048]{1,0:T(8,128)(2,1)S(1)}, bf16[96,2048]{1,0:T(8,128)(2,1)S(1)}, u32[]{:S(2)}, u32[]{:S(2)}) collective-permute-start(bf16[96,2048]{1,0:T(8,128)(2,1)S(1)} %get-tuple-element.298), channel_id=1, source_target_pairs={{0,8},{4,12},{8,0},{12,4},{16,24},{20,28},{24,16},{28,20},{1,9},{5... | collective-permute-start | bytes 1179656 | tf_op jit(solution)/shard_map/ppermute | solution.py:45
  153.2 20.6 %collective-permute-start.32 = (bf16[96,2048]{1,0:T(8,128)(2,1)S(1)}, bf16[96,2048]{1,0:T(8,128)(2,1)S(1)}, u32[]{:S(2)}, u32[]{:S(2)}) collective-permute-start(bf16[96,2048]{1,0:T(8,128)(2,1)S(1)} %get-tuple-element.299), channel_id=1, source_target_pairs={{0,16},{4,20},{8,24},{12,28},{16,0},{20,4},{24,8},{28,12},{1,17},{... | collective-permute-start | bytes 1179656 | tf_op jit(solution)/shard_map/ppermute | solution.py:45
  154.7 19.1 %collective-permute-start.33 = (bf16[96,2048]{1,0:T(8,128)(2,1)S(1)}, bf16[96,2048]{1,0:T(8,128)(2,1)S(1)}, u32[]{:S(2)}, u32[]{:S(2)}) collective-permute-start(bf16[96,2048]{1,0:T(8,128)(2,1)S(1)} %get-tuple-element.300), channel_id=1, source_target_pairs={{0,24},{4,28},{8,16},{12,20},{16,8},{20,12},{24,0},{28,4},{1,25},{... | collective-permute-start | bytes 1179656 | tf_op jit(solution)/shard_map/ppermute | solution.py:45
  156.7 15.8 %collective-permute-start.34 = (bf16[96,1536]{1,0:T(8,128)(2,1)S(1)}, bf16[96,1536]{1,0:T(8,128)(2,1)S(1)}, u32[]{:S(2)}, u32[]{:S(2)}) collective-permute-start(bf16[96,1536]{1,0:T(8,128)(2,1)S(1)} %get-tuple-element.306), channel_id=1, source_target_pairs={{0,2},{1,3},{2,0},{3,1},{4,6},{5,7},{6,4},{7,5},{8,10},{9,11},{10,... | collective-permute-start | bytes 884744 | tf_op jit(solution)/shard_map/ppermute | solution.py:45
  (15 other events, 108.6 us)

commit v6 on v5

--- a/solution.py
+++ b/solution.py
@@ -22,6 +22,7 @@
 LABELS = 16
 MARKS = 48
 MICROS = 450
+FEED_MICROS = 300
 BF = jnp.bfloat16
 F32 = jnp.float32
 ROOT_HALF = 0.7071067811865476
@@ -728,8 +729,13 @@
 def output_grads(scalars, blocks, small, small_side):
     def body(sc, *refs):
         small_ref, side_ref, keep_ref, send_ref, result_ref = refs[-5:]
+        grads = []
+        for ref in (refs[2], refs[5]):
+            turned = pltpu.roll(ref[...].astype(F32), D - sc[2] * QUARTER, 1)
+            turned = [turned[:, :QUARTER], turned[:, HALF : HALF + QUARTER]]
+            grads.append(jnp.concatenate(turned, axis=1).astype(BF))
         for side in range(2):
-            part = dot_tn(refs[side][...], refs[2][...]) + dot_tn(refs[3 + side][...], refs[5][...])
+            part = dot_tn(refs[side][...], grads[0]) + dot_tn(refs[3 + side][...], grads[1])
             for k in range(2):
                 at = pl.multiple_of((sc[2] ^ side ^ (2 * k)) * QUARTER, 16)
                 result_ref[pl.ds(at, QUARTER), :] = part[k * QUARTER : (k + 1) * QUARTER, :]
@@ -737,11 +743,11 @@
             target = (keep_ref, send_ref)[j % 2]
             block = sc[1] ^ j
             rows = pl.ds(pl.multiple_of(block * BLOCK, 16), BLOCK)
-            target[j // 2, :, :D] = result_ref[rows, :].astype(BF)
-            target[j // 2, :, D:] = jnp.zeros((BLOCK, 128), BF)
-            target[j // 2, : 2 * LABELS, D:] = halves(small_ref[block] + side_ref[block])
-
-    outs = [struct((GROUPS // 2, BLOCK, D + 128), BF)] * 2
+            target[j // 2, :, :HALF] = result_ref[rows, :].astype(BF)
+            target[j // 2, :, HALF:] = jnp.zeros((BLOCK, 128), BF)
+            target[j // 2, : 2 * LABELS, HALF:] = halves(small_ref[block] + side_ref[block])
+
+    outs = [struct((GROUPS // 2, BLOCK, HALF + 128), BF)] * 2
     operands = [value for block in blocks for value in block] + [small, small_side]
     return call(
         "output_grads",
@@ -752,7 +758,7 @@
         outs,
         [whole(o.shape) for o in outs],
         (1,),
-        [pltpu.VMEM((D, D), F32)],
+        [pltpu.VMEM((D, HALF), F32)],
         micros=4,
     )
 
@@ -908,15 +914,15 @@
 
 def combine_both(scalars, keep, received, out_keep, out_received):
     count, rows, wide = keep.shape
-    last = wide + D
+    last = wide + HALF
 
     def body(_, keep_ref, recv_ref, out_keep_ref, out_recv_ref, *refs):
         for k in range(count):
             kind = refs[k].dtype
             refs[k][:, :wide] = (keep_ref[k].astype(F32) + recv_ref[k].astype(F32)).astype(kind)
-            total = out_keep_ref[k, :, :D].astype(F32) + out_recv_ref[k, :, :D].astype(F32)
+            total = out_keep_ref[k, :, :HALF].astype(F32) + out_recv_ref[k, :, :HALF].astype(F32)
             refs[k][:, wide:last] = total.astype(kind)
-            small = whole_of(out_keep_ref[k, :, D:]) + whole_of(out_recv_ref[k, :, D:])
+            small = whole_of(out_keep_ref[k, :, HALF:]) + whole_of(out_recv_ref[k, :, HALF:])
             refs[k][:, last:] = jnp.zeros((rows, 128), kind)
             refs[k][: 2 * LABELS, last:] = halves(small).astype(kind)
 
@@ -933,18 +939,19 @@
         for ref in refs[1:-2]:
             total = total + ref[...].astype(F32)
         keep_ref[...] = total[:, : 2 * HID]
-        send_ref[...] = total[:, 2 * HID :].astype(BF)
-
-    outs = [struct((rows, 2 * HID), F32), struct((rows, 2 * HID), BF)]
+        send_ref[:, : 2 * HID] = total[:, 2 * HID :].astype(BF)
+        send_ref[:, 2 * HID :] = jnp.zeros((rows, 256), BF)
+
+    outs = [struct((rows, 2 * HID), F32), struct((rows, 2 * HID + 256), BF)]
     return simple("total_feed", body, scalars, sums, outs, 2)
 
 
 def total_projection(scalars, sums):
     rows, width = sums[0].shape
     wide = 3 * HALF
-    last = wide + D
-
-    def body(sc, *refs):
+    last = wide + HALF
+
+    def body(_, *refs):
         keep_ref, send_ref = refs[-2:]
         total = refs[0][:, :last]
         for ref in refs[1:-2]:
@@ -955,8 +962,8 @@
             both = jnp.concatenate(both, axis=1)
             near.append(both[:, :QUARTER])
             far.append(both[:, QUARTER:])
-        near.append(pltpu.roll(total[:, wide:], D - sc[2] * QUARTER, 1)[:, :QUARTER])
-        far.append(pltpu.roll(total[:, wide:], D - (sc[2] ^ 2) * QUARTER, 1)[:, :QUARTER])
+        near.append(total[:, wide : wide + QUARTER])
+        far.append(total[:, wide + QUARTER : last])
         keep_ref[:, :D] = jnp.concatenate(near, axis=1)
         send_ref[:, :D] = jnp.concatenate(far, axis=1).astype(BF)
         if width > last:
@@ -978,10 +985,10 @@
 
     def body(_, keep_ref, recv_ref, up_ref, down_ref):
         up_ref[...] = keep_ref[:, :HID] + recv_ref[:, :HID].astype(F32)
-        down_ref[...] = keep_ref[:, HID:] + recv_ref[:, HID:].astype(F32)
+        down_ref[...] = keep_ref[:, HID:] + recv_ref[:, HID : 2 * HID].astype(F32)
 
     outs = [struct((rows, HID), F32)] * 2
-    return simple("finish_feed", body, scalars, [keep, received], outs)
+    return simple("finish_feed", body, scalars, [keep, received], outs, FEED_MICROS)
 
 
 def finish_projection(scalars, keep, received):
@@ -1260,12 +1267,14 @@
     small_side = swap(small, "seq", 1)
     projection_parts = projection_grads(scalars, x, grads, rows)
     projection_parts, small_side, feed_sums = together(projection_parts, small_side, feed_sums)
+    if direct:
+        feed_keep, feed_send = total_feed(scalars, feed_sums)
+        attention_grad, feed_send = together(attention_grad, feed_send)
     out_blocks = [(ctx_mine[k], ctx_partner[k], attention_grad[k]) for k in range(2)]
     if direct:
         projection_received = swap(projection_parts[1], "dp", 1)
         out_parts = output_grads(scalars, out_blocks, small, small_side)
         out_received = swap(out_parts[1], "dp", 1)
-        feed_keep, feed_send = total_feed(scalars, feed_sums)
         feed_far = swap(feed_send, "seq", 2)
         sums = spread(
             combine_both(scalars, projection_parts[0], projection_received, out_parts[0], out_received)
@@ -1274,21 +1283,24 @@
         out_parts = rows_of(*output_grads(scalars, out_blocks, small, small_side))
         sums = scattered(
             jnp.concatenate(
-                [rows_of(*projection_parts).reshape(D, -1), out_parts[:, :, :D].reshape(D, -1)], axis=1
+                [rows_of(*projection_parts).reshape(D, -1), out_parts[:, :, :HALF].reshape(D, -1)], axis=1
             )
         )
         feed_keep, feed_send = total_feed(scalars, feed_sums)
         feed_far = swap(feed_send, "seq", 2)
+    if direct:
+        sums, feed_far, input_far = together(sums, feed_far, input_far)
+    keep, send = total_projection(scalars, sums)
+    received = swap(send, "seq", 2)
     up_grad, down_grad = finish_feed(scalars, feed_keep, feed_far)
     input_grad = own_grad + input_keep + input_far.astype(F32)
     if direct:
-        sums, up_grad, input_grad = together(sums, up_grad, input_grad)
-    keep, send = total_projection(scalars, sums)
-    projections = list(finish_projection(scalars, keep, swap(send, "seq", 2)))
+        received, up_grad, input_grad = together(received, up_grad, input_grad)
+    projections = list(finish_projection(scalars, keep, received))
     if direct:
         projections, vec, tall_lines = projections[:4], projections[4:-1], projections[-1]
     else:
-        tile = out_parts[:, :LABELS, D:] + out_parts[:, LABELS : 2 * LABELS, D:]
+        tile = out_parts[:, :LABELS, HALF:] + out_parts[:, LABELS : 2 * LABELS, HALF:]
         tile = tile + swap(tile, "seq", 2)
         wide_lines = tile[:, :VECS, :BLOCK].transpose(1, 0, 2).reshape(VECS, D)
         wide_lines = lax.psum_scatter(wide_lines, "dp", scatter_dimension=1, tiled=True)

time: 186 us -> 182 us (0.978)
  waiting for transfers between devices: 75.3 us -> 71.6 us
    ppermute x35, waiting for transfers between devices: 69.8 us -> 66.1 us  [swap(): return lax.ppermute(value, axis, [(k, k ^ mask) for k in range(count)])]
  transfers between devices with their start and end apart: 37 -> 37, of which waited for: 17 -> 16; matrix products, arithmetic and copies ran while one was open for 1% -> 1% of each run, Pallas kernels for 31% -> 32%
where the time goes in v6:
time: 182 us
  waiting for transfers between devices  71.6 us (39%)
  Pallas kernels  64.2 us (35%)
  starting transfers between devices  44.1 us (24%)
    ppermute x35, waiting for transfers between devices, swap(): return lax.ppermute(value, axis, [(k, k ^ mask) for k in range(count)])  66.1 us
    pallas_call x26, Pallas kernels, call(): pl.pallas_call(body, out_shape=outs, grid_spec=spec, compiler_params=para...  64.2 us
    ppermute x35, starting transfers between devices, swap(): return lax.ppermute(value, axis, [(k, k ^ mask) for k in range(count)])  42.1 us
    ppermute x1, waiting for transfers between devices, per_device(): halo_far = lax.ppermute(halo_near, 'seq', [(1, 0), (2, 3)])  5.49 us
  transfers between devices with their start and end apart: 37, of which 16 were waited for; matrix products, arithmetic and copies ran while one was open for 1% of the time, Pallas kernels for 32%

profile of v6, /device:TPU:0, one launch (start us, length us, event | category | flops | bytes accessed | tf_op | source)
XLA Modules:
  0.0 182.1 jit_solution(7325525065394070983)
XLA Ops:
  2.8 4.1 %collective-permute-start.4 = (bf16[96,2304]{1,0:T(8,128)(2,1)S(1)}, bf16[96,2304]{1,0:T(8,128)(2,1)S(1)}, u32[]{:S(2)}, u32[]{:S(2)}) collective-permute-start(bf16[96,2304]{1,0:T(8,128)(2,1)S(1)} %get-tuple-element.184.own_ref), channel_id=1, source_target_pairs={{0,2},{1,3},{2,0},{3,1},{4,6},{5,7},{6,4},{7,5},{8,10},{9,11},{10,... | collective-permute-start | bytes 1327112 | tf_op jit(solution)/shard_map/ppermute | solution.py:46
  12.0 5.6 %collective-permute-done.side_ref = bf16[96,192]{1,0:T(8,128)(2,1)S(1)} collective-permute-done((bf16[96,192]{1,0:T(8,128)(2,1)}, bf16[96,192]{1,0:T(8,128)(2,1)S(1)}, u32[]{:S(2)}, u32[]{:S(2)}) %collective-permute-start) | collective-permute-done | bytes 36896 | tf_op jit(solution)/shard_map/ppermute | solution.py:46
  17.6 8.4 %collective-permute-done.1.refs_3_ = bf16[96,1536]{1,0:T(8,128)(2,1)S(1)} collective-permute-done((bf16[96,1536]{1,0:T(8,128)(2,1)S(1)}, bf16[96,1536]{1,0:T(8,128)(2,1)S(1)}, u32[]{:S(2)}, u32[]{:S(2)}) %collective-permute-start.1) | collective-permute-done | bytes 294944 | tf_op jit(solution)/shard_map/ppermute | solution.py:46
  29.1 2.1 %collective-permute-start.7 = (bf16[208,576]{1,0:T(8,128)(2,1)S(1)}, bf16[208,576]{1,0:T(8,128)(2,1)S(1)}, u32[]{:S(2)}, u32[]{:S(2)}) collective-permute-start(bf16[208,576]{1,0:T(8,128)(2,1)S(1)} %get-tuple-element.191), channel_id=1, source_target_pairs={{0,24},{4,28},{8,16},{12,20},{16,8},{20,12},{24,0},{28,4},{1,25},{... | collective-permute-start | bytes 718856 | tf_op jit(solution)/shard_map/ppermute | solution.py:46
  32.6 7.8 %collective-permute-done.5.refs_4_ = bf16[96,576]{1,0:T(8,128)(2,1)S(1)} collective-permute-done((bf16[96,576]{1,0:T(8,128)(2,1)S(1)}, bf16[96,576]{1,0:T(8,128)(2,1)S(1)}, u32[]{:S(2)}, u32[]{:S(2)}) %collective-permute-start.5) | collective-permute-done | bytes 110624 | tf_op jit(solution)/shard_map/ppermute | solution.py:46
  46.9 6.3 %attend_pair.1 = (bf16[512,384]{1,0:T(8,128)(2,1)S(1)}, bf16[512,384]{1,0:T(8,128)(2,1)S(1)}, bf16[512,384]{1,0:T(8,128)(2,1)S(1)}, bf16[256,384]{1,0:T(8,128)(2...) custom-call(s32[3]{0:T(128)S(1)} %pad_add_fusion._.sc, ...), custom_call_target="tpu_custom_call" | custom-call | flops 80000000 | bytes 1024 | tf_op jit(solution)/shard_map/attend_pair/pallas_call | solution.py:69
  53.2 5.5 %collective-permute-done.11.far_ref = bf16[304,768]{1,0:T(8,128)(2,1)S(1)} collective-permute-done((bf16[304,768]{1,0:T(8,128)(2,1)S(1)}, bf16[304,768]{1,0:T(8,128)(2,1)S(1)}, u32[]{:S(2)}, u32[]{:S(2)}) %collective-permute-start.11) | collective-permute-done | bytes 466976 | tf_op jit(solution)/shard_map/ppermute | solution.py:1138
  58.7 5.5 %attend_halo.1 = (bf16[256,384]{1,0:T(8,128)(2,1)S(1)}, bf16[256,384]{1,0:T(8,128)(2,1)S(1)}, bf16[256,384]{1,0:T(8,128)(2,1)S(1)}, bf16[256,384]{1,0:T(8,128)(2...) custom-call(s32[3]{0:T(128)S(1)} %pad_add_fusion._.sc, ...), custom_call_target="tpu_custom_call" | custom-call | flops 60000000 | bytes 1024 | tf_op jit(solution)/shard_map/attend_halo/pallas_call | solution.py:69
  64.2 2.5 %collective-permute-done.14.refs_6_ = bf16[96,2304]{1,0:T(8,128)(2,1)S(1)} collective-permute-done((bf16[96,2304]{1,0:T(8,128)(2,1)S(1)}, bf16[96,2304]{1,0:T(8,128)(2,1)S(1)}, u32[]{:S(2)}, u32[]{:S(2)}) %collective-permute-start.14) | collective-permute-done | bytes 442400 | tf_op jit(solution)/shard_map/ppermute | solution.py:46
  67.5 5.0 %collective-permute-start.16 = (bf16[256,384]{1,0:T(8,128)(2,1)S(1)}, bf16[256,384]{1,0:T(8,128)(2,1)S(1)}, u32[]{:S(2)}, u32[]{:S(2)}) collective-permute-start(bf16[256,384]{1,0:T(8,128)(2,1)S(1)} %get-tuple-element.219.mine_ref.refs_3_), channel_id=1, source_target_pairs={{0,1},{1,0},{2,3},{3,2},{4,5},{5,4},{6,7},{7,6},{8,9},{9,8},{10,11... | collective-permute-start | bytes 589832 | tf_op jit(solution)/shard_map/ppermute | solution.py:46
  72.6 5.6 %collective-permute-done.16.partner_ref.refs_4_ = bf16[256,384]{1,0:T(8,128)(2,1)S(1)} collective-permute-done((bf16[256,384]{1,0:T(8,128)(2,1)S(1)}, bf16[256,384]{1,0:T(8,128)(2,1)S(1)}, u32[]{:S(2)}, u32[]{:S(2)}) %collective-permute-start.16) | collective-permute-done | bytes 196640 | tf_op jit(solution)/shard_map/ppermute | solution.py:46
  78.2 3.2 %feed_forward.2 = (f32[256,768]{1,0:T(8,128)S(1)}, f32[256,128]{1,0:T(8,128)S(1)}, bf16[256,768]{1,0:T(8,128)(2,1)S(1)}, f32[256,1536]{1,0:T(8,128)S(1)}, bf16[2...) custom-call(s32[3]{0:T(128)S(1)} %pad_add_fusion._.sc, ...), custom_call_target="tpu_custom_call" | custom-call | flops 60000000 | bytes 1024 | tf_op jit(solution)/shard_map/feed_forward/pallas_call | solution.py:69
  83.4 2.9 %feed_forward.3 = (f32[256,768]{1,0:T(8,128)S(1)}, f32[256,128]{1,0:T(8,128)S(1)}, bf16[256,768]{1,0:T(8,128)(2,1)S(1)}, f32[256,1536]{1,0:T(8,128)S(1)}, bf16[2...) custom-call(s32[3]{0:T(128)S(1)} %pad_add_fusion._.sc, bf16[256,384]{1,0:T(8,128)(2,1)S(1)} %get-tuple-element.216.mine_ref.refs_0_, ...), custom_call_target="tpu_custom_call" | custom-call | flops 60000000 | bytes 1024 | tf_op jit(solution)/shard_map/feed_forward/pallas_call | solution.py:69
  87.6 7.4 %collective-permute-done.18.recv_ref = bf16[256,768]{1,0:T(8,128)(2,1)S(1)} collective-permute-done((bf16[256,768]{1,0:T(8,128)(2,1)S(1)}, bf16[256,768]{1,0:T(8,128)(2,1)S(1)}, u32[]{:S(2)}, u32[]{:S(2)}) %collective-permute-start.18) | collective-permute-done | bytes 393248 | tf_op jit(solution)/shard_map/ppermute | solution.py:46
  95.1 2.9 %second_norm.2 = (f32[256,768]{1,0:T(8,128)S(1)}, bf16[256,768]{1,0:T(8,128)(2,1)S(1)}, bf16[256,1536]{1,0:T(8,128)(2,1)S(1)}, bf16[256,768]{1,0:T(8,128)(2,1)S(...) custom-call(s32[3]{0:T(128)S(1)} %pad_add_fusion._.sc, ...), custom_call_target="tpu_custom_call" | custom-call | flops 50000000 | bytes 1024 | tf_op jit(solution)/shard_map/second_norm/pallas_call | solution.py:69
  98.0 2.3 %collective-permute-start.20 = (bf16[256,768]{1,0:T(8,128)(2,1)S(1)}, bf16[256,768]{1,0:T(8,128)(2,1)S(1)}, u32[]{:S(2)}, u32[]{:S(2)}) collective-permute-start(bf16[256,768]{1,0:T(8,128)(2,1)S(1)} %get-tuple-element.269.part_ref), channel_id=1, source_target_pairs={{0,1},{1,0},{2,3},{3,2},{4,5},{5,4},{6,7},{7,6},{8,9},{9,8},{10,11... | collective-permute-start | bytes 1179656 | tf_op jit(solution)/shard_map/ppermute | solution.py:46
  103.5 3.8 %second_norm.3 = (f32[256,768]{1,0:T(8,128)S(1)}, bf16[256,768]{1,0:T(8,128)(2,1)S(1)}, bf16[256,1536]{1,0:T(8,128)(2,1)S(1)}, bf16[256,768]{1,0:T(8,128)(2,1)S(...) custom-call(s32[3]{0:T(128)S(1)} %pad_add_fusion._.sc, ...), custom_call_target="tpu_custom_call" | custom-call | flops 50000000 | bytes 1024 | tf_op jit(solution)/shard_map/second_norm/pallas_call | solution.py:69
  107.3 5.0 %feed_forward_grads.1 = (bf16[4,96,3072]{2,1,0:T(8,128)(2,1)S(1)}, bf16[4,96,3072]{2,1,0:T(8,128)(2,1)S(1)}) custom-call(s32[3]{0:T(128)S(1)} %pad_add_fusion._.sc, bf16[256,768]{1,0:T(8,128)(2,1)S(1)} %get-tuple-element.254.refs_0_, bf16[256,1536]{1,0:T(8,128)(2,1)S(1)} %get-tuple-element.246.refs_1_, bf16[256,768]{1,0:T(8,128)(2,1)S(1)} %get-tuple-element.245.refs_2_, ...), custom_call_target="tpu_custom_call" | custom-call | flops 80000000 | bytes 1024 | tf_op jit(solution)/shard_map/feed_forward_grads/pallas_call | solution.py:69
  122.3 6.6 %collective-permute-done.22.recv_ref = bf16[256,768]{1,0:T(8,128)(2,1)S(1)} collective-permute-done((bf16[256,768]{1,0:T(8,128)(2,1)S(1)}, bf16[256,768]{1,0:T(8,128)(2,1)S(1)}, u32[]{:S(2)}, u32[]{:S(2)}) %collective-permute-start.22) | collective-permute-done | bytes 393248 | tf_op jit(solution)/shard_map/ppermute | solution.py:46
  128.9 2.4 %first_norm.3 = (bf16[256,768]{1,0:T(8,128)(2,1)S(1)}, bf16[256,384]{1,0:T(8,128)(2,1)S(1)}, f32[8,256]{1,0:T(8,128)S(1)}, f32[256,768]{1,0:T(8,128)S(1)}, f32[8,768]{1,0:T(8,128)S(1)}) custom-call(s32[3]{0:T(128)S(1)} %pad_add_fusion._.sc, bf16[256,768]{1,0:T(8,128)(2,1)S(1)} %get-tuple-element.264.part_ref, ...), custom_call_target="tpu_custom_call" | custom-call | flops 30000000 | bytes 1024 | tf_op jit(solution)/shard_map/first_norm/pallas_call | solution.py:69
  131.3 10.7 %attend_backward.1 = (bf16[512,1152]{1,0:T(8,128)(2,1)S(1)}, f32[256,768]{1,0:T(8,128)S(1)}, bf16[256,768]{1,0:T(8,128)(2,1)S(1)}, f32[8,1152]{1,0:T(8,128)S(1)}) custom-call(s32[3]{0:T(128)S(1)} %pad_add_fusion._.sc, bf16[512,384]{1,0:T(8,128)(2,1)S(1)} %get-tuple-element.212.q_ref.refs_0_, bf16[512,384]{1,0:T(8,128)(2,1)S(1)} %get-tuple-element.213.k_ref.refs_1_, ...), custom_call_target="tpu_custom_call" | custom-call | flops 4499999744 | bytes 1024 | tf_op jit(solution)/shard_map/attend_backward/pallas_call | solution.py:69
  142.8 2.9 %projection_grads.1 = (bf16[4,96,1152]{2,1,0:T(8,128)(2,1)S(1)}, bf16[4,96,1152]{2,1,0:T(8,128)(2,1)S(1)}) custom-call(s32[3]{0:T(128)S(1)} %pad_add_fusion._.sc, bf16[512,768]{1,0:T(8,128)(2,1)S(1)} %get-tuple-element.220.x_ref, bf16[512,1152]{1,0:T(8,128)(2,1)S(1)} %get-tuple-element.283.grad_ref), custom_call_target="tpu_custom_call" | custom-call | flops 50000000 | bytes 1024 | tf_op jit(solution)/shard_map/projection_grads/pallas_call | solution.py:69
  157.6 11.5 %collective-permute-done.35 = bf16[256,768]{1,0:T(8,128)(2,1)S(1)} collective-permute-done((bf16[256,768]{1,0:T(8,128)(2,1)S(1)}, bf16[256,768]{1,0:T(8,128)(2,1)S(1)}, u32[]{:S(2)}, u32[]{:S(2)}) %collective-permute-start.35) | collective-permute-done | bytes 393248 | tf_op jit(solution)/shard_map/ppermute | solution.py:46
  175.8 4.8 %collective-permute-done.36.recv_ref = bf16[96,896]{1,0:T(8,128)(2,1)S(1)} collective-permute-done((bf16[96,896]{1,0:T(8,128)(2,1)S(1)}, bf16[96,896]{1,0:T(8,128)(2,1)S(1)}, u32[]{:S(2)}, u32[]{:S(2)}) %collective-permute-start.36) | collective-permute-done | bytes 172064 | tf_op jit(solution)/shard_map/ppermute | solution.py:46
  (82 shorter events, 56.2 us)
Async XLA Ops:
  2.8 23.7 %collective-permute-start.4 = (bf16[96,2304]{1,0:T(8,128)(2,1)S(1)}, bf16[96,2304]{1,0:T(8,128)(2,1)S(1)}, u32[]{:S(2)}, u32[]{:S(2)}) collective-permute-start(bf16[96,2304]{1,0:T(8,128)(2,1)S(1)} %get-tuple-element.184.own_ref), channel_id=1, source_target_pairs={{0,2},{1,3},{2,0},{3,1},{4,6},{5,7},{6,4},{7,5},{8,10},{9,11},{10,... | collective-permute-start | bytes 1327112 | tf_op jit(solution)/shard_map/ppermute | solution.py:46
  6.9 19.0 %collective-permute-start.2 = (bf16[96,2240]{1,0:T(8,128)(2,1)S(1)}, bf16[96,2240]{1,0:T(8,128)(2,1)S(1)}, u32[]{:S(2)}, u32[]{:S(2)}) collective-permute-start(bf16[96,2240]{1,0:T(8,128)(2,1)S(1)} %get-tuple-element.196.mine_ref.refs_0_), channel_id=1, source_target_pairs={{0,8},{4,12},{8,0},{12,4},{16,24},{20,28},{24,16},{28,20},{1,9},{5... | collective-permute-start | bytes 1290248 | tf_op jit(solution)/shard_map/ppermute | solution.py:46
  8.4 17.7 %collective-permute-start.3 = (bf16[96,2240]{1,0:T(8,128)(2,1)S(1)}, bf16[96,2240]{1,0:T(8,128)(2,1)S(1)}, u32[]{:S(2)}, u32[]{:S(2)}) collective-permute-start(bf16[96,2240]{1,0:T(8,128)(2,1)S(1)} %get-tuple-element.196.mine_ref.refs_0_), channel_id=1, source_target_pairs={{0,16},{4,20},{8,24},{12,28},{16,0},{20,4},{24,8},{28,12},{1,17},{... | collective-permute-start | bytes 1290248 | tf_op jit(solution)/shard_map/ppermute | solution.py:46
  10.0 16.0 %collective-permute-start.1 = (bf16[96,1536]{1,0:T(8,128)(2,1)S(1)}, bf16[96,1536]{1,0:T(8,128)(2,1)S(1)}, u32[]{:S(2)}, u32[]{:S(2)}) collective-permute-start(bf16[96,1536]{1,0:T(8,128)(2,1)S(1)} %get-tuple-element.182), channel_id=1, source_target_pairs={{0,24},{4,28},{8,16},{12,20},{16,8},{20,12},{24,0},{28,4},{1,25},{... | collective-permute-start | bytes 884744 | tf_op jit(solution)/shard_map/ppermute | solution.py:46
  27.2 13.2 %collective-permute-start.8 = (bf16[304,768]{1,0:T(8,128)(2,1)S(1)}, bf16[304,768]{1,0:T(8,128)(2,1)S(1)}, u32[]{:S(2)}, u32[]{:S(2)}) collective-permute-start(bf16[304,768]{1,0:T(8,128)(2,1)S(1)} %get-tuple-element.192), channel_id=1, source_target_pairs={{0,1},{1,0},{2,3},{3,2},{4,5},{5,4},{6,7},{7,6},{8,9},{9,8},{10,11... | collective-permute-start | bytes 1400840 | tf_op jit(solution)/shard_map/ppermute | solution.py:46
  28.4 12.1 %collective-permute-start.9 = (bf16[304,768]{1,0:T(8,128)(2,1)S(1)}, bf16[304,768]{1,0:T(8,128)(2,1)S(1)}, u32[]{:S(2)}, u32[]{:S(2)}) collective-permute-start(bf16[304,768]{1,0:T(8,128)(2,1)S(1)} %get-tuple-element.189.label_ref), channel_id=1, source_target_pairs={{1,2},{2,1},{5,6},{6,5},{9,10},{10,9},{13,14},{14,13},{17,18},{18,... | collective-permute-start | bytes 1400840 | tf_op jit(solution)/shard_map/ppermute | solution.py:1128
  41.2 17.5 %collective-permute-start.11 = (bf16[304,768]{1,0:T(8,128)(2,1)S(1)}, bf16[304,768]{1,0:T(8,128)(2,1)S(1)}, u32[]{:S(2)}, u32[]{:S(2)}) collective-permute-start(bf16[304,768]{1,0:T(8,128)(2,1)S(1)} %collective-permute-done.9.near_ref), channel_id=1, source_target_pairs={{1,0},{2,3},{5,4},{6,7},{9,8},{10,11},{13,12},{14,15},{17,16},{18,... | collective-permute-start | bytes 1400840 | tf_op jit(solution)/shard_map/ppermute | solution.py:1138
  43.4 20.9 %collective-permute-start.13 = (bf16[96,2304]{1,0:T(8,128)(2,1)S(1)}, bf16[96,2304]{1,0:T(8,128)(2,1)S(1)}, u32[]{:S(2)}, u32[]{:S(2)}) collective-permute-start(bf16[96,2304]{1,0:T(8,128)(2,1)S(1)} %pack_feed.1.refs_4_), channel_id=1, source_target_pairs={{0,8},{4,12},{8,0},{12,4},{16,24},{20,28},{24,16},{28,20},{1,9},{5... | collective-permute-start | bytes 1327112 | tf_op jit(solution)/shard_map/ppermute | solution.py:46
  44.9 21.8 %collective-permute-start.14 = (bf16[96,2304]{1,0:T(8,128)(2,1)S(1)}, bf16[96,2304]{1,0:T(8,128)(2,1)S(1)}, u32[]{:S(2)}, u32[]{:S(2)}) collective-permute-start(bf16[96,2304]{1,0:T(8,128)(2,1)S(1)} %pack_feed.1.refs_4_), channel_id=1, source_target_pairs={{0,16},{4,20},{8,24},{12,28},{16,0},{20,4},{24,8},{28,12},{1,17},{... | collective-permute-start | bytes 1327112 | tf_op jit(solution)/shard_map/ppermute | solution.py:46
  46.3 20.4 %collective-permute-start.15 = (bf16[96,2304]{1,0:T(8,128)(2,1)S(1)}, bf16[96,2304]{1,0:T(8,128)(2,1)S(1)}, u32[]{:S(2)}, u32[]{:S(2)}) collective-permute-start(bf16[96,2304]{1,0:T(8,128)(2,1)S(1)} %pack_feed.1.refs_4_), channel_id=1, source_target_pairs={{0,24},{4,28},{8,16},{12,20},{16,8},{20,12},{24,0},{28,4},{1,25},{... | collective-permute-start | bytes 1327112 | tf_op jit(solution)/shard_map/ppermute | solution.py:46
  72.5 15.2 %collective-permute-start.19 = (bf16[256,768]{1,0:T(8,128)(2,1)S(1)}, bf16[256,768]{1,0:T(8,128)(2,1)S(1)}, u32[]{:S(2)}, u32[]{:S(2)}) collective-permute-start(bf16[256,768]{1,0:T(8,128)(2,1)S(1)} %bitcast.9), channel_id=1, source_target_pairs={{0,1},{1,0},{2,3},{3,2},{4,5},{5,4},{6,7},{7,6},{8,9},{9,8},{10,11... | collective-permute-start | bytes 1179656 | tf_op jit(solution)/shard_map/ppermute | solution.py:46
  81.4 13.7 %collective-permute-start.18 = (bf16[256,768]{1,0:T(8,128)(2,1)S(1)}, bf16[256,768]{1,0:T(8,128)(2,1)S(1)}, u32[]{:S(2)}, u32[]{:S(2)}) collective-permute-start(bf16[256,768]{1,0:T(8,128)(2,1)S(1)} %get-tuple-element.228.part_ref), channel_id=1, source_target_pairs={{0,1},{1,0},{2,3},{3,2},{4,5},{5,4},{6,7},{7,6},{8,9},{9,8},{10,11... | collective-permute-start | bytes 1179656 | tf_op jit(solution)/shard_map/ppermute | solution.py:46
  86.3 17.2 %collective-permute-start.21 = (bf16[256,768]{1,0:T(8,128)(2,1)S(1)}, bf16[256,768]{1,0:T(8,128)(2,1)S(1)}, u32[]{:S(2)}, u32[]{:S(2)}) collective-permute-start(bf16[256,768]{1,0:T(8,128)(2,1)S(1)} %get-tuple-element.238.part_ref), channel_id=1, source_target_pairs={{0,1},{1,0},{2,3},{3,2},{4,5},{5,4},{6,7},{7,6},{8,9},{9,8},{10,11... | collective-permute-start | bytes 1179656 | tf_op jit(solution)/shard_map/ppermute | solution.py:46
  98.0 14.3 %collective-permute-start.20 = (bf16[256,768]{1,0:T(8,128)(2,1)S(1)}, bf16[256,768]{1,0:T(8,128)(2,1)S(1)}, u32[]{:S(2)}, u32[]{:S(2)}) collective-permute-start(bf16[256,768]{1,0:T(8,128)(2,1)S(1)} %get-tuple-element.269.part_ref), channel_id=1, source_target_pairs={{0,1},{1,0},{2,3},{3,2},{4,5},{5,4},{6,7},{7,6},{8,9},{9,8},{10,11... | collective-permute-start | bytes 1179656 | tf_op jit(solution)/shard_map/ppermute | solution.py:46
  112.4 16.5 %collective-permute-start.22 = (bf16[256,768]{1,0:T(8,128)(2,1)S(1)}, bf16[256,768]{1,0:T(8,128)(2,1)S(1)}, u32[]{:S(2)}, u32[]{:S(2)}) collective-permute-start(bf16[256,768]{1,0:T(8,128)(2,1)S(1)} %get-tuple-element.264.part_ref), channel_id=1, source_target_pairs={{0,1},{1,0},{2,3},{3,2},{4,5},{5,4},{6,7},{7,6},{8,9},{9,8},{10,11... | collective-permute-start | bytes 1179656 | tf_op jit(solution)/shard_map/ppermute | solution.py:46
  116.3 15.0 %collective-permute-start.23 = (bf16[304,384]{1,0:T(8,128)(2,1)S(1)}, bf16[304,384]{1,0:T(8,128)(2,1)S(1)}, u32[]{:S(2)}, u32[]{:S(2)}) collective-permute-start(bf16[304,384]{1,0:T(8,128)(2,1)S(1)} %get-tuple-element.279), channel_id=1, source_target_pairs={{0,2},{1,3},{2,0},{3,1},{4,6},{5,7},{6,4},{7,5},{8,10},{9,11},{10,... | collective-permute-start | bytes 700424 | tf_op jit(solution)/shard_map/ppermute | solution.py:46
  118.8 28.2 %collective-permute-start.26 = (bf16[96,3072]{1,0:T(8,128)(2,1)S(1)}, bf16[96,3072]{1,0:T(8,128)(2,1)S(1)}, u32[]{:S(2)}, u32[]{:S(2)}) collective-permute-start(bf16[96,3072]{1,0:T(8,128)(2,1)S(1)} %get-tuple-element.293), channel_id=1, source_target_pairs={{0,8},{4,12},{8,0},{12,4},{16,24},{20,28},{24,16},{28,20},{1,9},{5... | collective-permute-start | bytes 1769480 | tf_op jit(solution)/shard_map/ppermute | solution.py:46
  120.1 27.0 %collective-permute-start.27 = (bf16[96,3072]{1,0:T(8,128)(2,1)S(1)}, bf16[96,3072]{1,0:T(8,128)(2,1)S(1)}, u32[]{:S(2)}, u32[]{:S(2)}) collective-permute-start(bf16[96,3072]{1,0:T(8,128)(2,1)S(1)} %get-tuple-element.294), channel_id=1, source_target_pairs={{0,16},{4,20},{8,24},{12,28},{16,0},{20,4},{24,8},{28,12},{1,17},{... | collective-permute-start | bytes 1769480 | tf_op jit(solution)/shard_map/ppermute | solution.py:46
  120.9 26.7 %collective-permute-start.28 = (bf16[96,3072]{1,0:T(8,128)(2,1)S(1)}, bf16[96,3072]{1,0:T(8,128)(2,1)S(1)}, u32[]{:S(2)}, u32[]{:S(2)}) collective-permute-start(bf16[96,3072]{1,0:T(8,128)(2,1)S(1)} %get-tuple-element.295), channel_id=1, source_target_pairs={{0,24},{4,28},{8,16},{12,20},{16,8},{20,12},{24,0},{28,4},{1,25},{... | collective-permute-start | bytes 1769480 | tf_op jit(solution)/shard_map/ppermute | solution.py:46
  150.7 18.5 %collective-permute-start.35 = (bf16[256,768]{1,0:T(8,128)(2,1)S(1)}, bf16[256,768]{1,0:T(8,128)(2,1)S(1)}, u32[]{:S(2)}, u32[]{:S(2)}) collective-permute-start(bf16[256,768]{1,0:T(8,128)(2,1)S(1)} %get-tuple-element.315), channel_id=1, source_target_pairs={{0,1},{1,0},{2,3},{3,2},{4,5},{5,4},{6,7},{7,6},{8,9},{9,8},{10,11... | collective-permute-start | bytes 1179656 | tf_op jit(solution)/shard_map/ppermute | solution.py:46
  152.3 16.9 %collective-permute-start.34 = (bf16[96,1792]{1,0:T(8,128)(2,1)S(1)}, bf16[96,1792]{1,0:T(8,128)(2,1)S(1)}, u32[]{:S(2)}, u32[]{:S(2)}) collective-permute-start(bf16[96,1792]{1,0:T(8,128)(2,1)S(1)} %get-tuple-element.314), channel_id=1, source_target_pairs={{0,2},{1,3},{2,0},{3,1},{4,6},{5,7},{6,4},{7,5},{8,10},{9,11},{10,... | collective-permute-start | bytes 1032200 | tf_op jit(solution)/shard_map/ppermute | solution.py:46
  154.0 15.1 %collective-permute-start.31 = (bf16[96,1664]{1,0:T(8,128)(2,1)S(1)}, bf16[96,1664]{1,0:T(8,128)(2,1)S(1)}, u32[]{:S(2)}, u32[]{:S(2)}) collective-permute-start(bf16[96,1664]{1,0:T(8,128)(2,1)S(1)} %get-tuple-element.311), channel_id=1, source_target_pairs={{0,8},{4,12},{8,0},{12,4},{16,24},{20,28},{24,16},{28,20},{1,9},{5... | collective-permute-start | bytes 958472 | tf_op jit(solution)/shard_map/ppermute | solution.py:46
  155.0 15.5 %collective-permute-start.32 = (bf16[96,1664]{1,0:T(8,128)(2,1)S(1)}, bf16[96,1664]{1,0:T(8,128)(2,1)S(1)}, u32[]{:S(2)}, u32[]{:S(2)}) collective-permute-start(bf16[96,1664]{1,0:T(8,128)(2,1)S(1)} %get-tuple-element.312), channel_id=1, source_target_pairs={{0,16},{4,20},{8,24},{12,28},{16,0},{20,4},{24,8},{28,12},{1,17},{... | collective-permute-start | bytes 958472 | tf_op jit(solution)/shard_map/ppermute | solution.py:46
  156.4 14.1 %collective-permute-start.33 = (bf16[96,1664]{1,0:T(8,128)(2,1)S(1)}, bf16[96,1664]{1,0:T(8,128)(2,1)S(1)}, u32[]{:S(2)}, u32[]{:S(2)}) collective-permute-start(bf16[96,1664]{1,0:T(8,128)(2,1)S(1)} %get-tuple-element.313), channel_id=1, source_target_pairs={{0,24},{4,28},{8,16},{12,20},{16,8},{20,12},{24,0},{28,4},{1,25},{... | collective-permute-start | bytes 958472 | tf_op jit(solution)/shard_map/ppermute | solution.py:46
  (15 other events, 110.8 us)

commit v7 on v6

--- a/solution.py
+++ b/solution.py
@@ -76,6 +76,10 @@
         ),
         name=name,
     )(scalars, *operands)
+
+
+def turn(quarters):
+    return lax.rem(quarters + 4, 4) * QUARTER
 
 
 def struct(shape, dtype):
@@ -351,8 +355,8 @@
 
             vec_ref[...] = vectors[:VECS]
             lanes = lax.broadcasted_iota(jnp.int32, (VECS, HALF), 1)
-            low = pltpu.roll(vectors[:VECS], D - sc[2] * QUARTER, 1)[:, :HALF]
-            high = pltpu.roll(vectors[:VECS], D + QUARTER - (sc[2] ^ 2) * QUARTER, 1)[:, :HALF]
+            low = pltpu.roll(vectors[:VECS], turn(-sc[2]), 1)[:, :HALF]
+            high = pltpu.roll(vectors[:VECS], turn(1 - (sc[2] ^ 2)), 1)[:, :HALF]
             bias_ref[...] = jnp.where(lanes < QUARTER, low, high)
             log_ref[...] = jnp.zeros_like(log_ref)
 
@@ -731,7 +735,7 @@
         small_ref, side_ref, keep_ref, send_ref, result_ref = refs[-5:]
         grads = []
         for ref in (refs[2], refs[5]):
-            turned = pltpu.roll(ref[...].astype(F32), D - sc[2] * QUARTER, 1)
+            turned = pltpu.roll(ref[...].astype(F32), turn(-sc[2]), 1)
             turned = [turned[:, :QUARTER], turned[:, HALF : HALF + QUARTER]]
             grads.append(jnp.concatenate(turned, axis=1).astype(BF))
         for side in range(2):
@@ -1027,7 +1031,7 @@
             )
             low = pltpu.roll(jnp.broadcast_to(jnp.where(near, line, 0.0), (8, D)), sc[2] * QUARTER, 1)
             high = jnp.broadcast_to(jnp.where(far, line, 0.0), (8, D))
-            high = pltpu.roll(high, D - QUARTER + (sc[2] ^ 2) * QUARTER, 1)
+            high = pltpu.roll(high, turn((sc[2] ^ 2) - 1), 1)
             wide_ref[row : row + 1, :] = (low + high)[0:1]
         wide_ref[2:3, :] = one_ref[2:3, :]
         wide_ref[3:5, :] = one_ref[0:2, :]

time: 182 us -> 182 us (level)
  no operation moved by 1% of the time
where the time goes in v7:
time: 182 us
  waiting for transfers between devices  71.7 us (39%)
  Pallas kernels  64.2 us (35%)
  starting transfers between devices  44 us (24%)
    ppermute x35, waiting for transfers between devices, swap(): return lax.ppermute(value, axis, [(k, k ^ mask) for k in range(count)])  66.2 us
    pallas_call x26, Pallas kernels, call(): pl.pallas_call(body, out_shape=outs, grid_spec=spec, compiler_params=para...  64.2 us
    ppermute x35, starting transfers between devices, swap(): return lax.ppermute(value, axis, [(k, k ^ mask) for k in range(count)])  42.1 us
    ppermute x1, waiting for transfers between devices, per_device(): halo_far = lax.ppermute(halo_near, 'seq', [(1, 0), (2, 3)])  5.49 us
  transfers between devices with their start and end apart: 37, of which 16 were waited for; matrix products, arithmetic and copies ran while one was open for 1% of the time, Pallas kernels for 32%

profile of v7, /device:TPU:0, one launch (start us, length us, event | category | flops | bytes accessed | tf_op | source)
XLA Modules:
  0.0 182.1 jit_solution(12166529922947200313)
XLA Ops:
  2.8 4.1 %collective-permute-start.4 = (bf16[96,2304]{1,0:T(8,128)(2,1)S(1)}, bf16[96,2304]{1,0:T(8,128)(2,1)S(1)}, u32[]{:S(2)}, u32[]{:S(2)}) collective-permute-start(bf16[96,2304]{1,0:T(8,128)(2,1)S(1)} %get-tuple-element.184.own_ref), channel_id=1, source_target_pairs={{0,2},{1,3},{2,0},{3,1},{4,6},{5,7},{6,4},{7,5},{8,10},{9,11},{10,... | collective-permute-start | bytes 1327112 | tf_op jit(solution)/shard_map/ppermute | solution.py:46
  12.0 5.6 %collective-permute-done.side_ref = bf16[96,192]{1,0:T(8,128)(2,1)S(1)} collective-permute-done((bf16[96,192]{1,0:T(8,128)(2,1)}, bf16[96,192]{1,0:T(8,128)(2,1)S(1)}, u32[]{:S(2)}, u32[]{:S(2)}) %collective-permute-start) | collective-permute-done | bytes 36896 | tf_op jit(solution)/shard_map/ppermute | solution.py:46
  17.6 8.4 %collective-permute-done.1.refs_3_ = bf16[96,1536]{1,0:T(8,128)(2,1)S(1)} collective-permute-done((bf16[96,1536]{1,0:T(8,128)(2,1)S(1)}, bf16[96,1536]{1,0:T(8,128)(2,1)S(1)}, u32[]{:S(2)}, u32[]{:S(2)}) %collective-permute-start.1) | collective-permute-done | bytes 294944 | tf_op jit(solution)/shard_map/ppermute | solution.py:46
  29.1 2.1 %collective-permute-start.7 = (bf16[208,576]{1,0:T(8,128)(2,1)S(1)}, bf16[208,576]{1,0:T(8,128)(2,1)S(1)}, u32[]{:S(2)}, u32[]{:S(2)}) collective-permute-start(bf16[208,576]{1,0:T(8,128)(2,1)S(1)} %get-tuple-element.191), channel_id=1, source_target_pairs={{0,24},{4,28},{8,16},{12,20},{16,8},{20,12},{24,0},{28,4},{1,25},{... | collective-permute-start | bytes 718856 | tf_op jit(solution)/shard_map/ppermute | solution.py:46
  32.6 7.8 %collective-permute-done.5.refs_4_ = bf16[96,576]{1,0:T(8,128)(2,1)S(1)} collective-permute-done((bf16[96,576]{1,0:T(8,128)(2,1)S(1)}, bf16[96,576]{1,0:T(8,128)(2,1)S(1)}, u32[]{:S(2)}, u32[]{:S(2)}) %collective-permute-start.5) | collective-permute-done | bytes 110624 | tf_op jit(solution)/shard_map/ppermute | solution.py:46
  46.9 6.3 %attend_pair.1 = (bf16[512,384]{1,0:T(8,128)(2,1)S(1)}, bf16[512,384]{1,0:T(8,128)(2,1)S(1)}, bf16[512,384]{1,0:T(8,128)(2,1)S(1)}, bf16[256,384]{1,0:T(8,128)(2...) custom-call(s32[3]{0:T(128)S(1)} %pad_add_fusion._.sc, ...), custom_call_target="tpu_custom_call" | custom-call | flops 80000000 | bytes 1024 | tf_op jit(solution)/shard_map/attend_pair/pallas_call | solution.py:69
  53.2 5.5 %collective-permute-done.11.far_ref = bf16[304,768]{1,0:T(8,128)(2,1)S(1)} collective-permute-done((bf16[304,768]{1,0:T(8,128)(2,1)S(1)}, bf16[304,768]{1,0:T(8,128)(2,1)S(1)}, u32[]{:S(2)}, u32[]{:S(2)}) %collective-permute-start.11) | collective-permute-done | bytes 466976 | tf_op jit(solution)/shard_map/ppermute | solution.py:1142
  58.7 5.5 %attend_halo.1 = (bf16[256,384]{1,0:T(8,128)(2,1)S(1)}, bf16[256,384]{1,0:T(8,128)(2,1)S(1)}, bf16[256,384]{1,0:T(8,128)(2,1)S(1)}, bf16[256,384]{1,0:T(8,128)(2...) custom-call(s32[3]{0:T(128)S(1)} %pad_add_fusion._.sc, ...), custom_call_target="tpu_custom_call" | custom-call | flops 60000000 | bytes 1024 | tf_op jit(solution)/shard_map/attend_halo/pallas_call | solution.py:69
  64.2 2.5 %collective-permute-done.14.refs_6_ = bf16[96,2304]{1,0:T(8,128)(2,1)S(1)} collective-permute-done((bf16[96,2304]{1,0:T(8,128)(2,1)S(1)}, bf16[96,2304]{1,0:T(8,128)(2,1)S(1)}, u32[]{:S(2)}, u32[]{:S(2)}) %collective-permute-start.14) | collective-permute-done | bytes 442400 | tf_op jit(solution)/shard_map/ppermute | solution.py:46
  67.5 5.0 %collective-permute-start.16 = (bf16[256,384]{1,0:T(8,128)(2,1)S(1)}, bf16[256,384]{1,0:T(8,128)(2,1)S(1)}, u32[]{:S(2)}, u32[]{:S(2)}) collective-permute-start(bf16[256,384]{1,0:T(8,128)(2,1)S(1)} %get-tuple-element.219.mine_ref.refs_3_), channel_id=1, source_target_pairs={{0,1},{1,0},{2,3},{3,2},{4,5},{5,4},{6,7},{7,6},{8,9},{9,8},{10,11... | collective-permute-start | bytes 589832 | tf_op jit(solution)/shard_map/ppermute | solution.py:46
  72.6 5.6 %collective-permute-done.16.partner_ref.refs_4_ = bf16[256,384]{1,0:T(8,128)(2,1)S(1)} collective-permute-done((bf16[256,384]{1,0:T(8,128)(2,1)S(1)}, bf16[256,384]{1,0:T(8,128)(2,1)S(1)}, u32[]{:S(2)}, u32[]{:S(2)}) %collective-permute-start.16) | collective-permute-done | bytes 196640 | tf_op jit(solution)/shard_map/ppermute | solution.py:46
  78.2 3.2 %feed_forward.2 = (f32[256,768]{1,0:T(8,128)S(1)}, f32[256,128]{1,0:T(8,128)S(1)}, bf16[256,768]{1,0:T(8,128)(2,1)S(1)}, f32[256,1536]{1,0:T(8,128)S(1)}, bf16[2...) custom-call(s32[3]{0:T(128)S(1)} %pad_add_fusion._.sc, ...), custom_call_target="tpu_custom_call" | custom-call | flops 60000000 | bytes 1024 | tf_op jit(solution)/shard_map/feed_forward/pallas_call | solution.py:69
  83.4 2.9 %feed_forward.3 = (f32[256,768]{1,0:T(8,128)S(1)}, f32[256,128]{1,0:T(8,128)S(1)}, bf16[256,768]{1,0:T(8,128)(2,1)S(1)}, f32[256,1536]{1,0:T(8,128)S(1)}, bf16[2...) custom-call(s32[3]{0:T(128)S(1)} %pad_add_fusion._.sc, bf16[256,384]{1,0:T(8,128)(2,1)S(1)} %get-tuple-element.216.mine_ref.refs_0_, ...), custom_call_target="tpu_custom_call" | custom-call | flops 60000000 | bytes 1024 | tf_op jit(solution)/shard_map/feed_forward/pallas_call | solution.py:69
  87.6 7.4 %collective-permute-done.18.recv_ref = bf16[256,768]{1,0:T(8,128)(2,1)S(1)} collective-permute-done((bf16[256,768]{1,0:T(8,128)(2,1)S(1)}, bf16[256,768]{1,0:T(8,128)(2,1)S(1)}, u32[]{:S(2)}, u32[]{:S(2)}) %collective-permute-start.18) | collective-permute-done | bytes 393248 | tf_op jit(solution)/shard_map/ppermute | solution.py:46
  95.1 2.9 %second_norm.2 = (f32[256,768]{1,0:T(8,128)S(1)}, bf16[256,768]{1,0:T(8,128)(2,1)S(1)}, bf16[256,1536]{1,0:T(8,128)(2,1)S(1)}, bf16[256,768]{1,0:T(8,128)(2,1)S(...) custom-call(s32[3]{0:T(128)S(1)} %pad_add_fusion._.sc, ...), custom_call_target="tpu_custom_call" | custom-call | flops 50000000 | bytes 1024 | tf_op jit(solution)/shard_map/second_norm/pallas_call | solution.py:69
  98.0 2.3 %collective-permute-start.20 = (bf16[256,768]{1,0:T(8,128)(2,1)S(1)}, bf16[256,768]{1,0:T(8,128)(2,1)S(1)}, u32[]{:S(2)}, u32[]{:S(2)}) collective-permute-start(bf16[256,768]{1,0:T(8,128)(2,1)S(1)} %get-tuple-element.269.part_ref), channel_id=1, source_target_pairs={{0,1},{1,0},{2,3},{3,2},{4,5},{5,4},{6,7},{7,6},{8,9},{9,8},{10,11... | collective-permute-start | bytes 1179656 | tf_op jit(solution)/shard_map/ppermute | solution.py:46
  103.5 3.8 %second_norm.3 = (f32[256,768]{1,0:T(8,128)S(1)}, bf16[256,768]{1,0:T(8,128)(2,1)S(1)}, bf16[256,1536]{1,0:T(8,128)(2,1)S(1)}, bf16[256,768]{1,0:T(8,128)(2,1)S(...) custom-call(s32[3]{0:T(128)S(1)} %pad_add_fusion._.sc, ...), custom_call_target="tpu_custom_call" | custom-call | flops 50000000 | bytes 1024 | tf_op jit(solution)/shard_map/second_norm/pallas_call | solution.py:69
  107.3 5.0 %feed_forward_grads.1 = (bf16[4,96,3072]{2,1,0:T(8,128)(2,1)S(1)}, bf16[4,96,3072]{2,1,0:T(8,128)(2,1)S(1)}) custom-call(s32[3]{0:T(128)S(1)} %pad_add_fusion._.sc, bf16[256,768]{1,0:T(8,128)(2,1)S(1)} %get-tuple-element.254.refs_0_, bf16[256,1536]{1,0:T(8,128)(2,1)S(1)} %get-tuple-element.246.refs_1_, bf16[256,768]{1,0:T(8,128)(2,1)S(1)} %get-tuple-element.245.refs_2_, ...), custom_call_target="tpu_custom_call" | custom-call | flops 80000000 | bytes 1024 | tf_op jit(solution)/shard_map/feed_forward_grads/pallas_call | solution.py:69
  122.3 6.6 %collective-permute-done.22.recv_ref = bf16[256,768]{1,0:T(8,128)(2,1)S(1)} collective-permute-done((bf16[256,768]{1,0:T(8,128)(2,1)S(1)}, bf16[256,768]{1,0:T(8,128)(2,1)S(1)}, u32[]{:S(2)}, u32[]{:S(2)}) %collective-permute-start.22) | collective-permute-done | bytes 393248 | tf_op jit(solution)/shard_map/ppermute | solution.py:46
  128.9 2.4 %first_norm.3 = (bf16[256,768]{1,0:T(8,128)(2,1)S(1)}, bf16[256,384]{1,0:T(8,128)(2,1)S(1)}, f32[8,256]{1,0:T(8,128)S(1)}, f32[256,768]{1,0:T(8,128)S(1)}, f32[8,768]{1,0:T(8,128)S(1)}) custom-call(s32[3]{0:T(128)S(1)} %pad_add_fusion._.sc, bf16[256,768]{1,0:T(8,128)(2,1)S(1)} %get-tuple-element.264.part_ref, ...), custom_call_target="tpu_custom_call" | custom-call | flops 30000000 | bytes 1024 | tf_op jit(solution)/shard_map/first_norm/pallas_call | solution.py:69
  131.3 10.7 %attend_backward.1 = (bf16[512,1152]{1,0:T(8,128)(2,1)S(1)}, f32[256,768]{1,0:T(8,128)S(1)}, bf16[256,768]{1,0:T(8,128)(2,1)S(1)}, f32[8,1152]{1,0:T(8,128)S(1)}) custom-call(s32[3]{0:T(128)S(1)} %pad_add_fusion._.sc, bf16[512,384]{1,0:T(8,128)(2,1)S(1)} %get-tuple-element.212.q_ref.refs_0_, bf16[512,384]{1,0:T(8,128)(2,1)S(1)} %get-tuple-element.213.k_ref.refs_1_, ...), custom_call_target="tpu_custom_call" | custom-call | flops 4499999744 | bytes 1024 | tf_op jit(solution)/shard_map/attend_backward/pallas_call | solution.py:69
  142.8 2.9 %projection_grads.1 = (bf16[4,96,1152]{2,1,0:T(8,128)(2,1)S(1)}, bf16[4,96,1152]{2,1,0:T(8,128)(2,1)S(1)}) custom-call(s32[3]{0:T(128)S(1)} %pad_add_fusion._.sc, bf16[512,768]{1,0:T(8,128)(2,1)S(1)} %get-tuple-element.220.x_ref, bf16[512,1152]{1,0:T(8,128)(2,1)S(1)} %get-tuple-element.283.grad_ref), custom_call_target="tpu_custom_call" | custom-call | flops 50000000 | bytes 1024 | tf_op jit(solution)/shard_map/projection_grads/pallas_call | solution.py:69
  157.6 11.5 %collective-permute-done.35 = bf16[256,768]{1,0:T(8,128)(2,1)S(1)} collective-permute-done((bf16[256,768]{1,0:T(8,128)(2,1)S(1)}, bf16[256,768]{1,0:T(8,128)(2,1)S(1)}, u32[]{:S(2)}, u32[]{:S(2)}) %collective-permute-start.35) | collective-permute-done | bytes 393248 | tf_op jit(solution)/shard_map/ppermute | solution.py:46
  175.8 4.8 %collective-permute-done.36.recv_ref = bf16[96,896]{1,0:T(8,128)(2,1)S(1)} collective-permute-done((bf16[96,896]{1,0:T(8,128)(2,1)S(1)}, bf16[96,896]{1,0:T(8,128)(2,1)S(1)}, u32[]{:S(2)}, u32[]{:S(2)}) %collective-permute-start.36) | collective-permute-done | bytes 172064 | tf_op jit(solution)/shard_map/ppermute | solution.py:46
  (82 shorter events, 56.2 us)
Async XLA Ops:
  2.8 23.7 %collective-permute-start.4 = (bf16[96,2304]{1,0:T(8,128)(2,1)S(1)}, bf16[96,2304]{1,0:T(8,128)(2,1)S(1)}, u32[]{:S(2)}, u32[]{:S(2)}) collective-permute-start(bf16[96,2304]{1,0:T(8,128)(2,1)S(1)} %get-tuple-element.184.own_ref), channel_id=1, source_target_pairs={{0,2},{1,3},{2,0},{3,1},{4,6},{5,7},{6,4},{7,5},{8,10},{9,11},{10,... | collective-permute-start | bytes 1327112 | tf_op jit(solution)/shard_map/ppermute | solution.py:46
  6.9 19.0 %collective-permute-start.2 = (bf16[96,2240]{1,0:T(8,128)(2,1)S(1)}, bf16[96,2240]{1,0:T(8,128)(2,1)S(1)}, u32[]{:S(2)}, u32[]{:S(2)}) collective-permute-start(bf16[96,2240]{1,0:T(8,128)(2,1)S(1)} %get-tuple-element.196.mine_ref.refs_0_), channel_id=1, source_target_pairs={{0,8},{4,12},{8,0},{12,4},{16,24},{20,28},{24,16},{28,20},{1,9},{5... | collective-permute-start | bytes 1290248 | tf_op jit(solution)/shard_map/ppermute | solution.py:46
  8.4 17.7 %collective-permute-start.3 = (bf16[96,2240]{1,0:T(8,128)(2,1)S(1)}, bf16[96,2240]{1,0:T(8,128)(2,1)S(1)}, u32[]{:S(2)}, u32[]{:S(2)}) collective-permute-start(bf16[96,2240]{1,0:T(8,128)(2,1)S(1)} %get-tuple-element.196.mine_ref.refs_0_), channel_id=1, source_target_pairs={{0,16},{4,20},{8,24},{12,28},{16,0},{20,4},{24,8},{28,12},{1,17},{... | collective-permute-start | bytes 1290248 | tf_op jit(solution)/shard_map/ppermute | solution.py:46
  10.0 16.0 %collective-permute-start.1 = (bf16[96,1536]{1,0:T(8,128)(2,1)S(1)}, bf16[96,1536]{1,0:T(8,128)(2,1)S(1)}, u32[]{:S(2)}, u32[]{:S(2)}) collective-permute-start(bf16[96,1536]{1,0:T(8,128)(2,1)S(1)} %get-tuple-element.182), channel_id=1, source_target_pairs={{0,24},{4,28},{8,16},{12,20},{16,8},{20,12},{24,0},{28,4},{1,25},{... | collective-permute-start | bytes 884744 | tf_op jit(solution)/shard_map/ppermute | solution.py:46
  27.2 13.2 %collective-permute-start.8 = (bf16[304,768]{1,0:T(8,128)(2,1)S(1)}, bf16[304,768]{1,0:T(8,128)(2,1)S(1)}, u32[]{:S(2)}, u32[]{:S(2)}) collective-permute-start(bf16[304,768]{1,0:T(8,128)(2,1)S(1)} %get-tuple-element.192), channel_id=1, source_target_pairs={{0,1},{1,0},{2,3},{3,2},{4,5},{5,4},{6,7},{7,6},{8,9},{9,8},{10,11... | collective-permute-start | bytes 1400840 | tf_op jit(solution)/shard_map/ppermute | solution.py:46
  28.4 12.1 %collective-permute-start.9 = (bf16[304,768]{1,0:T(8,128)(2,1)S(1)}, bf16[304,768]{1,0:T(8,128)(2,1)S(1)}, u32[]{:S(2)}, u32[]{:S(2)}) collective-permute-start(bf16[304,768]{1,0:T(8,128)(2,1)S(1)} %get-tuple-element.189.label_ref), channel_id=1, source_target_pairs={{1,2},{2,1},{5,6},{6,5},{9,10},{10,9},{13,14},{14,13},{17,18},{18,... | collective-permute-start | bytes 1400840 | tf_op jit(solution)/shard_map/ppermute | solution.py:1132
  41.2 17.5 %collective-permute-start.11 = (bf16[304,768]{1,0:T(8,128)(2,1)S(1)}, bf16[304,768]{1,0:T(8,128)(2,1)S(1)}, u32[]{:S(2)}, u32[]{:S(2)}) collective-permute-start(bf16[304,768]{1,0:T(8,128)(2,1)S(1)} %collective-permute-done.9.near_ref), channel_id=1, source_target_pairs={{1,0},{2,3},{5,4},{6,7},{9,8},{10,11},{13,12},{14,15},{17,16},{18,... | collective-permute-start | bytes 1400840 | tf_op jit(solution)/shard_map/ppermute | solution.py:1142
  43.4 20.9 %collective-permute-start.13 = (bf16[96,2304]{1,0:T(8,128)(2,1)S(1)}, bf16[96,2304]{1,0:T(8,128)(2,1)S(1)}, u32[]{:S(2)}, u32[]{:S(2)}) collective-permute-start(bf16[96,2304]{1,0:T(8,128)(2,1)S(1)} %pack_feed.1.refs_4_), channel_id=1, source_target_pairs={{0,8},{4,12},{8,0},{12,4},{16,24},{20,28},{24,16},{28,20},{1,9},{5... | collective-permute-start | bytes 1327112 | tf_op jit(solution)/shard_map/ppermute | solution.py:46
  44.9 21.8 %collective-permute-start.14 = (bf16[96,2304]{1,0:T(8,128)(2,1)S(1)}, bf16[96,2304]{1,0:T(8,128)(2,1)S(1)}, u32[]{:S(2)}, u32[]{:S(2)}) collective-permute-start(bf16[96,2304]{1,0:T(8,128)(2,1)S(1)} %pack_feed.1.refs_4_), channel_id=1, source_target_pairs={{0,16},{4,20},{8,24},{12,28},{16,0},{20,4},{24,8},{28,12},{1,17},{... | collective-permute-start | bytes 1327112 | tf_op jit(solution)/shard_map/ppermute | solution.py:46
  46.3 20.4 %collective-permute-start.15 = (bf16[96,2304]{1,0:T(8,128)(2,1)S(1)}, bf16[96,2304]{1,0:T(8,128)(2,1)S(1)}, u32[]{:S(2)}, u32[]{:S(2)}) collective-permute-start(bf16[96,2304]{1,0:T(8,128)(2,1)S(1)} %pack_feed.1.refs_4_), channel_id=1, source_target_pairs={{0,24},{4,28},{8,16},{12,20},{16,8},{20,12},{24,0},{28,4},{1,25},{... | collective-permute-start | bytes 1327112 | tf_op jit(solution)/shard_map/ppermute | solution.py:46
  72.5 15.2 %collective-permute-start.19 = (bf16[256,768]{1,0:T(8,128)(2,1)S(1)}, bf16[256,768]{1,0:T(8,128)(2,1)S(1)}, u32[]{:S(2)}, u32[]{:S(2)}) collective-permute-start(bf16[256,768]{1,0:T(8,128)(2,1)S(1)} %bitcast.9), channel_id=1, source_target_pairs={{0,1},{1,0},{2,3},{3,2},{4,5},{5,4},{6,7},{7,6},{8,9},{9,8},{10,11... | collective-permute-start | bytes 1179656 | tf_op jit(solution)/shard_map/ppermute | solution.py:46
  81.4 13.7 %collective-permute-start.18 = (bf16[256,768]{1,0:T(8,128)(2,1)S(1)}, bf16[256,768]{1,0:T(8,128)(2,1)S(1)}, u32[]{:S(2)}, u32[]{:S(2)}) collective-permute-start(bf16[256,768]{1,0:T(8,128)(2,1)S(1)} %get-tuple-element.228.part_ref), channel_id=1, source_target_pairs={{0,1},{1,0},{2,3},{3,2},{4,5},{5,4},{6,7},{7,6},{8,9},{9,8},{10,11... | collective-permute-start | bytes 1179656 | tf_op jit(solution)/shard_map/ppermute | solution.py:46
  86.3 17.2 %collective-permute-start.21 = (bf16[256,768]{1,0:T(8,128)(2,1)S(1)}, bf16[256,768]{1,0:T(8,128)(2,1)S(1)}, u32[]{:S(2)}, u32[]{:S(2)}) collective-permute-start(bf16[256,768]{1,0:T(8,128)(2,1)S(1)} %get-tuple-element.238.part_ref), channel_id=1, source_target_pairs={{0,1},{1,0},{2,3},{3,2},{4,5},{5,4},{6,7},{7,6},{8,9},{9,8},{10,11... | collective-permute-start | bytes 1179656 | tf_op jit(solution)/shard_map/ppermute | solution.py:46
  98.0 14.3 %collective-permute-start.20 = (bf16[256,768]{1,0:T(8,128)(2,1)S(1)}, bf16[256,768]{1,0:T(8,128)(2,1)S(1)}, u32[]{:S(2)}, u32[]{:S(2)}) collective-permute-start(bf16[256,768]{1,0:T(8,128)(2,1)S(1)} %get-tuple-element.269.part_ref), channel_id=1, source_target_pairs={{0,1},{1,0},{2,3},{3,2},{4,5},{5,4},{6,7},{7,6},{8,9},{9,8},{10,11... | collective-permute-start | bytes 1179656 | tf_op jit(solution)/shard_map/ppermute | solution.py:46
  112.4 16.5 %collective-permute-start.22 = (bf16[256,768]{1,0:T(8,128)(2,1)S(1)}, bf16[256,768]{1,0:T(8,128)(2,1)S(1)}, u32[]{:S(2)}, u32[]{:S(2)}) collective-permute-start(bf16[256,768]{1,0:T(8,128)(2,1)S(1)} %get-tuple-element.264.part_ref), channel_id=1, source_target_pairs={{0,1},{1,0},{2,3},{3,2},{4,5},{5,4},{6,7},{7,6},{8,9},{9,8},{10,11... | collective-permute-start | bytes 1179656 | tf_op jit(solution)/shard_map/ppermute | solution.py:46
  116.3 15.0 %collective-permute-start.23 = (bf16[304,384]{1,0:T(8,128)(2,1)S(1)}, bf16[304,384]{1,0:T(8,128)(2,1)S(1)}, u32[]{:S(2)}, u32[]{:S(2)}) collective-permute-start(bf16[304,384]{1,0:T(8,128)(2,1)S(1)} %get-tuple-element.279), channel_id=1, source_target_pairs={{0,2},{1,3},{2,0},{3,1},{4,6},{5,7},{6,4},{7,5},{8,10},{9,11},{10,... | collective-permute-start | bytes 700424 | tf_op jit(solution)/shard_map/ppermute | solution.py:46
  118.8 28.2 %collective-permute-start.26 = (bf16[96,3072]{1,0:T(8,128)(2,1)S(1)}, bf16[96,3072]{1,0:T(8,128)(2,1)S(1)}, u32[]{:S(2)}, u32[]{:S(2)}) collective-permute-start(bf16[96,3072]{1,0:T(8,128)(2,1)S(1)} %get-tuple-element.293), channel_id=1, source_target_pairs={{0,8},{4,12},{8,0},{12,4},{16,24},{20,28},{24,16},{28,20},{1,9},{5... | collective-permute-start | bytes 1769480 | tf_op jit(solution)/shard_map/ppermute | solution.py:46
  120.1 27.0 %collective-permute-start.27 = (bf16[96,3072]{1,0:T(8,128)(2,1)S(1)}, bf16[96,3072]{1,0:T(8,128)(2,1)S(1)}, u32[]{:S(2)}, u32[]{:S(2)}) collective-permute-start(bf16[96,3072]{1,0:T(8,128)(2,1)S(1)} %get-tuple-element.294), channel_id=1, source_target_pairs={{0,16},{4,20},{8,24},{12,28},{16,0},{20,4},{24,8},{28,12},{1,17},{... | collective-permute-start | bytes 1769480 | tf_op jit(solution)/shard_map/ppermute | solution.py:46
  120.9 26.7 %collective-permute-start.28 = (bf16[96,3072]{1,0:T(8,128)(2,1)S(1)}, bf16[96,3072]{1,0:T(8,128)(2,1)S(1)}, u32[]{:S(2)}, u32[]{:S(2)}) collective-permute-start(bf16[96,3072]{1,0:T(8,128)(2,1)S(1)} %get-tuple-element.295), channel_id=1, source_target_pairs={{0,24},{4,28},{8,16},{12,20},{16,8},{20,12},{24,0},{28,4},{1,25},{... | collective-permute-start | bytes 1769480 | tf_op jit(solution)/shard_map/ppermute | solution.py:46
  150.7 18.5 %collective-permute-start.35 = (bf16[256,768]{1,0:T(8,128)(2,1)S(1)}, bf16[256,768]{1,0:T(8,128)(2,1)S(1)}, u32[]{:S(2)}, u32[]{:S(2)}) collective-permute-start(bf16[256,768]{1,0:T(8,128)(2,1)S(1)} %get-tuple-element.315), channel_id=1, source_target_pairs={{0,1},{1,0},{2,3},{3,2},{4,5},{5,4},{6,7},{7,6},{8,9},{9,8},{10,11... | collective-permute-start | bytes 1179656 | tf_op jit(solution)/shard_map/ppermute | solution.py:46
  152.3 16.9 %collective-permute-start.34 = (bf16[96,1792]{1,0:T(8,128)(2,1)S(1)}, bf16[96,1792]{1,0:T(8,128)(2,1)S(1)}, u32[]{:S(2)}, u32[]{:S(2)}) collective-permute-start(bf16[96,1792]{1,0:T(8,128)(2,1)S(1)} %get-tuple-element.314), channel_id=1, source_target_pairs={{0,2},{1,3},{2,0},{3,1},{4,6},{5,7},{6,4},{7,5},{8,10},{9,11},{10,... | collective-permute-start | bytes 1032200 | tf_op jit(solution)/shard_map/ppermute | solution.py:46
  154.0 15.1 %collective-permute-start.31 = (bf16[96,1664]{1,0:T(8,128)(2,1)S(1)}, bf16[96,1664]{1,0:T(8,128)(2,1)S(1)}, u32[]{:S(2)}, u32[]{:S(2)}) collective-permute-start(bf16[96,1664]{1,0:T(8,128)(2,1)S(1)} %get-tuple-element.311), channel_id=1, source_target_pairs={{0,8},{4,12},{8,0},{12,4},{16,24},{20,28},{24,16},{28,20},{1,9},{5... | collective-permute-start | bytes 958472 | tf_op jit(solution)/shard_map/ppermute | solution.py:46
  155.0 15.5 %collective-permute-start.32 = (bf16[96,1664]{1,0:T(8,128)(2,1)S(1)}, bf16[96,1664]{1,0:T(8,128)(2,1)S(1)}, u32[]{:S(2)}, u32[]{:S(2)}) collective-permute-start(bf16[96,1664]{1,0:T(8,128)(2,1)S(1)} %get-tuple-element.312), channel_id=1, source_target_pairs={{0,16},{4,20},{8,24},{12,28},{16,0},{20,4},{24,8},{28,12},{1,17},{... | collective-permute-start | bytes 958472 | tf_op jit(solution)/shard_map/ppermute | solution.py:46
  156.4 14.1 %collective-permute-start.33 = (bf16[96,1664]{1,0:T(8,128)(2,1)S(1)}, bf16[96,1664]{1,0:T(8,128)(2,1)S(1)}, u32[]{:S(2)}, u32[]{:S(2)}) collective-permute-start(bf16[96,1664]{1,0:T(8,128)(2,1)S(1)} %get-tuple-element.313), channel_id=1, source_target_pairs={{0,24},{4,28},{8,16},{12,20},{16,8},{20,12},{24,0},{28,4},{1,25},{... | collective-permute-start | bytes 958472 | tf_op jit(solution)/shard_map/ppermute | solution.py:46
  (15 other events, 110.8 us)

commit v8 on v7

--- a/solution.py
+++ b/solution.py
@@ -666,13 +666,12 @@
         context_ref[...] = context
         lane = lax.broadcasted_iota(jnp.int32, (VECS, HALF), 1) // HEAD_DIM
         picks = jnp.where(lane == lax.broadcasted_iota(jnp.int32, (VECS, HALF), 0), 1.0, 0.0)
-        inner = lax.dot_general(
-            picks,
-            context.astype(F32) * ctx_ref[...],
-            (((1,), (1,)), ((), ())),
-            precision=lax.Precision.HIGHEST,
-            preferred_element_type=F32,
-        )
+        products = context.astype(F32) * ctx_ref[...]
+        inner = jnp.zeros((VECS, rows), F32)
+        for _ in range(3):
+            piece = products.astype(BF)
+            inner = inner + dot_nt(picks.astype(BF), piece)
+            products = products - piece.astype(F32)
         inner_ref[...] = inner
         if block == 1:
             send_ref = refs[5]

time: 182 us -> 182 us (level)
  transfers between devices with their start and end apart: 37 -> 37, of which waited for: 16 -> 17; matrix products, arithmetic and copies ran while one was open for 1% -> 1% of each run, Pallas kernels for 32% -> 32%
where the time goes in v8:
time: 182 us
  waiting for transfers between devices  71.8 us (39%)
  Pallas kernels  63.7 us (35%)
  starting transfers between devices  44.2 us (24%)
    ppermute x35, waiting for transfers between devices, swap(): return lax.ppermute(value, axis, [(k, k ^ mask) for k in range(count)])  66.3 us
    pallas_call x26, Pallas kernels, call(): pl.pallas_call(body, out_shape=outs, grid_spec=spec, compiler_params=para...  63.7 us
    ppermute x35, starting transfers between devices, swap(): return lax.ppermute(value, axis, [(k, k ^ mask) for k in range(count)])  42.2 us
    ppermute x1, waiting for transfers between devices, per_device(): halo_far = lax.ppermute(halo_near, 'seq', [(1, 0), (2, 3)])  5.49 us
  transfers between devices with their start and end apart: 37, of which 17 were waited for; matrix products, arithmetic and copies ran while one was open for 1% of the time, Pallas kernels for 32%

profile of v8, /device:TPU:0, one launch (start us, length us, event | category | flops | bytes accessed | tf_op | source)
XLA Modules:
  0.0 181.9 jit_solution(5250069703804243715)
XLA Ops:
  2.8 4.1 %collective-permute-start.4 = (bf16[96,2304]{1,0:T(8,128)(2,1)S(1)}, bf16[96,2304]{1,0:T(8,128)(2,1)S(1)}, u32[]{:S(2)}, u32[]{:S(2)}) collective-permute-start(bf16[96,2304]{1,0:T(8,128)(2,1)S(1)} %get-tuple-element.184.own_ref), channel_id=1, source_target_pairs={{0,2},{1,3},{2,0},{3,1},{4,6},{5,7},{6,4},{7,5},{8,10},{9,11},{10,... | collective-permute-start | bytes 1327112 | tf_op jit(solution)/shard_map/ppermute | solution.py:46
  12.0 5.6 %collective-permute-done.side_ref = bf16[96,192]{1,0:T(8,128)(2,1)S(1)} collective-permute-done((bf16[96,192]{1,0:T(8,128)(2,1)}, bf16[96,192]{1,0:T(8,128)(2,1)S(1)}, u32[]{:S(2)}, u32[]{:S(2)}) %collective-permute-start) | collective-permute-done | bytes 36896 | tf_op jit(solution)/shard_map/ppermute | solution.py:46
  17.6 8.4 %collective-permute-done.1.refs_3_ = bf16[96,1536]{1,0:T(8,128)(2,1)S(1)} collective-permute-done((bf16[96,1536]{1,0:T(8,128)(2,1)S(1)}, bf16[96,1536]{1,0:T(8,128)(2,1)S(1)}, u32[]{:S(2)}, u32[]{:S(2)}) %collective-permute-start.1) | collective-permute-done | bytes 294944 | tf_op jit(solution)/shard_map/ppermute | solution.py:46
  32.6 7.8 %collective-permute-done.5.refs_4_ = bf16[96,576]{1,0:T(8,128)(2,1)S(1)} collective-permute-done((bf16[96,576]{1,0:T(8,128)(2,1)S(1)}, bf16[96,576]{1,0:T(8,128)(2,1)S(1)}, u32[]{:S(2)}, u32[]{:S(2)}) %collective-permute-start.5) | collective-permute-done | bytes 110624 | tf_op jit(solution)/shard_map/ppermute | solution.py:46
  46.9 6.3 %attend_pair.1 = (bf16[512,384]{1,0:T(8,128)(2,1)S(1)}, bf16[512,384]{1,0:T(8,128)(2,1)S(1)}, bf16[512,384]{1,0:T(8,128)(2,1)S(1)}, bf16[256,384]{1,0:T(8,128)(2...) custom-call(s32[3]{0:T(128)S(1)} %pad_add_fusion._.sc, ...), custom_call_target="tpu_custom_call" | custom-call | flops 80000000 | bytes 1024 | tf_op jit(solution)/shard_map/attend_pair/pallas_call | solution.py:69
  53.2 5.5 %collective-permute-done.11.far_ref = bf16[304,768]{1,0:T(8,128)(2,1)S(1)} collective-permute-done((bf16[304,768]{1,0:T(8,128)(2,1)S(1)}, bf16[304,768]{1,0:T(8,128)(2,1)S(1)}, u32[]{:S(2)}, u32[]{:S(2)}) %collective-permute-start.11) | collective-permute-done | bytes 466976 | tf_op jit(solution)/shard_map/ppermute | solution.py:1141
  58.7 5.5 %attend_halo.1 = (bf16[256,384]{1,0:T(8,128)(2,1)S(1)}, bf16[256,384]{1,0:T(8,128)(2,1)S(1)}, bf16[256,384]{1,0:T(8,128)(2,1)S(1)}, bf16[256,384]{1,0:T(8,128)(2...) custom-call(s32[3]{0:T(128)S(1)} %pad_add_fusion._.sc, ...), custom_call_target="tpu_custom_call" | custom-call | flops 60000000 | bytes 1024 | tf_op jit(solution)/shard_map/attend_halo/pallas_call | solution.py:69
  64.2 2.5 %collective-permute-done.14.refs_6_ = bf16[96,2304]{1,0:T(8,128)(2,1)S(1)} collective-permute-done((bf16[96,2304]{1,0:T(8,128)(2,1)S(1)}, bf16[96,2304]{1,0:T(8,128)(2,1)S(1)}, u32[]{:S(2)}, u32[]{:S(2)}) %collective-permute-start.14) | collective-permute-done | bytes 442400 | tf_op jit(solution)/shard_map/ppermute | solution.py:46
  67.5 5.0 %collective-permute-start.16 = (bf16[256,384]{1,0:T(8,128)(2,1)S(1)}, bf16[256,384]{1,0:T(8,128)(2,1)S(1)}, u32[]{:S(2)}, u32[]{:S(2)}) collective-permute-start(bf16[256,384]{1,0:T(8,128)(2,1)S(1)} %get-tuple-element.219.mine_ref.refs_3_), channel_id=1, source_target_pairs={{0,1},{1,0},{2,3},{3,2},{4,5},{5,4},{6,7},{7,6},{8,9},{9,8},{10,11... | collective-permute-start | bytes 589832 | tf_op jit(solution)/shard_map/ppermute | solution.py:46
  72.6 5.6 %collective-permute-done.16.partner_ref.refs_4_ = bf16[256,384]{1,0:T(8,128)(2,1)S(1)} collective-permute-done((bf16[256,384]{1,0:T(8,128)(2,1)S(1)}, bf16[256,384]{1,0:T(8,128)(2,1)S(1)}, u32[]{:S(2)}, u32[]{:S(2)}) %collective-permute-start.16) | collective-permute-done | bytes 196640 | tf_op jit(solution)/shard_map/ppermute | solution.py:46
  78.2 3.2 %feed_forward.2 = (f32[256,768]{1,0:T(8,128)S(1)}, f32[256,128]{1,0:T(8,128)S(1)}, bf16[256,768]{1,0:T(8,128)(2,1)S(1)}, f32[256,1536]{1,0:T(8,128)S(1)}, bf16[2...) custom-call(s32[3]{0:T(128)S(1)} %pad_add_fusion._.sc, ...), custom_call_target="tpu_custom_call" | custom-call | flops 60000000 | bytes 1024 | tf_op jit(solution)/shard_map/feed_forward/pallas_call | solution.py:69
  83.4 2.9 %feed_forward.3 = (f32[256,768]{1,0:T(8,128)S(1)}, f32[256,128]{1,0:T(8,128)S(1)}, bf16[256,768]{1,0:T(8,128)(2,1)S(1)}, f32[256,1536]{1,0:T(8,128)S(1)}, bf16[2...) custom-call(s32[3]{0:T(128)S(1)} %pad_add_fusion._.sc, bf16[256,384]{1,0:T(8,128)(2,1)S(1)} %get-tuple-element.216.mine_ref.refs_0_, ...), custom_call_target="tpu_custom_call" | custom-call | flops 60000000 | bytes 1024 | tf_op jit(solution)/shard_map/feed_forward/pallas_call | solution.py:69
  87.6 7.4 %collective-permute-done.18.recv_ref = bf16[256,768]{1,0:T(8,128)(2,1)S(1)} collective-permute-done((bf16[256,768]{1,0:T(8,128)(2,1)S(1)}, bf16[256,768]{1,0:T(8,128)(2,1)S(1)}, u32[]{:S(2)}, u32[]{:S(2)}) %collective-permute-start.18) | collective-permute-done | bytes 393248 | tf_op jit(solution)/shard_map/ppermute | solution.py:46
  95.1 2.9 %second_norm.2 = (f32[256,768]{1,0:T(8,128)S(1)}, bf16[256,768]{1,0:T(8,128)(2,1)S(1)}, bf16[256,1536]{1,0:T(8,128)(2,1)S(1)}, bf16[256,768]{1,0:T(8,128)(2,1)S(...) custom-call(s32[3]{0:T(128)S(1)} %pad_add_fusion._.sc, ...), custom_call_target="tpu_custom_call" | custom-call | flops 50000000 | bytes 1024 | tf_op jit(solution)/shard_map/second_norm/pallas_call | solution.py:69
  98.0 2.3 %collective-permute-start.20 = (bf16[256,768]{1,0:T(8,128)(2,1)S(1)}, bf16[256,768]{1,0:T(8,128)(2,1)S(1)}, u32[]{:S(2)}, u32[]{:S(2)}) collective-permute-start(bf16[256,768]{1,0:T(8,128)(2,1)S(1)} %get-tuple-element.269.part_ref), channel_id=1, source_target_pairs={{0,1},{1,0},{2,3},{3,2},{4,5},{5,4},{6,7},{7,6},{8,9},{9,8},{10,11... | collective-permute-start | bytes 1179656 | tf_op jit(solution)/shard_map/ppermute | solution.py:46
  103.5 3.8 %second_norm.3 = (f32[256,768]{1,0:T(8,128)S(1)}, bf16[256,768]{1,0:T(8,128)(2,1)S(1)}, bf16[256,1536]{1,0:T(8,128)(2,1)S(1)}, bf16[256,768]{1,0:T(8,128)(2,1)S(...) custom-call(s32[3]{0:T(128)S(1)} %pad_add_fusion._.sc, ...), custom_call_target="tpu_custom_call" | custom-call | flops 50000000 | bytes 1024 | tf_op jit(solution)/shard_map/second_norm/pallas_call | solution.py:69
  107.3 5.0 %feed_forward_grads.1 = (bf16[4,96,3072]{2,1,0:T(8,128)(2,1)S(1)}, bf16[4,96,3072]{2,1,0:T(8,128)(2,1)S(1)}) custom-call(s32[3]{0:T(128)S(1)} %pad_add_fusion._.sc, bf16[256,768]{1,0:T(8,128)(2,1)S(1)} %get-tuple-element.254.refs_0_, bf16[256,1536]{1,0:T(8,128)(2,1)S(1)} %get-tuple-element.246.refs_1_, bf16[256,768]{1,0:T(8,128)(2,1)S(1)} %get-tuple-element.245.refs_2_, ...), custom_call_target="tpu_custom_call" | custom-call | flops 80000000 | bytes 1024 | tf_op jit(solution)/shard_map/feed_forward_grads/pallas_call | solution.py:69
  122.1 6.8 %collective-permute-done.22.recv_ref = bf16[256,768]{1,0:T(8,128)(2,1)S(1)} collective-permute-done((bf16[256,768]{1,0:T(8,128)(2,1)S(1)}, bf16[256,768]{1,0:T(8,128)(2,1)S(1)}, u32[]{:S(2)}, u32[]{:S(2)}) %collective-permute-start.22) | collective-permute-done | bytes 393248 | tf_op jit(solution)/shard_map/ppermute | solution.py:46
  128.9 2.1 %first_norm.3 = (bf16[256,768]{1,0:T(8,128)(2,1)S(1)}, bf16[256,384]{1,0:T(8,128)(2,1)S(1)}, f32[8,256]{1,0:T(8,128)S(1)}, f32[256,768]{1,0:T(8,128)S(1)}, f32[8,768]{1,0:T(8,128)S(1)}) custom-call(s32[3]{0:T(128)S(1)} %pad_add_fusion._.sc, bf16[256,768]{1,0:T(8,128)(2,1)S(1)} %get-tuple-element.264.part_ref, ...), custom_call_target="tpu_custom_call" | custom-call | flops 30000000 | bytes 1024 | tf_op jit(solution)/shard_map/first_norm/pallas_call | solution.py:69
  131.1 10.7 %attend_backward.1 = (bf16[512,1152]{1,0:T(8,128)(2,1)S(1)}, f32[256,768]{1,0:T(8,128)S(1)}, bf16[256,768]{1,0:T(8,128)(2,1)S(1)}, f32[8,1152]{1,0:T(8,128)S(1)}) custom-call(s32[3]{0:T(128)S(1)} %pad_add_fusion._.sc, bf16[512,384]{1,0:T(8,128)(2,1)S(1)} %get-tuple-element.212.q_ref.refs_0_, bf16[512,384]{1,0:T(8,128)(2,1)S(1)} %get-tuple-element.213.k_ref.refs_1_, ...), custom_call_target="tpu_custom_call" | custom-call | flops 4499999744 | bytes 1024 | tf_op jit(solution)/shard_map/attend_backward/pallas_call | solution.py:69
  142.6 2.9 %projection_grads.1 = (bf16[4,96,1152]{2,1,0:T(8,128)(2,1)S(1)}, bf16[4,96,1152]{2,1,0:T(8,128)(2,1)S(1)}) custom-call(s32[3]{0:T(128)S(1)} %pad_add_fusion._.sc, bf16[512,768]{1,0:T(8,128)(2,1)S(1)} %get-tuple-element.220.x_ref, bf16[512,1152]{1,0:T(8,128)(2,1)S(1)} %get-tuple-element.283.grad_ref), custom_call_target="tpu_custom_call" | custom-call | flops 50000000 | bytes 1024 | tf_op jit(solution)/shard_map/projection_grads/pallas_call | solution.py:69
  157.4 11.7 %collective-permute-done.35 = bf16[256,768]{1,0:T(8,128)(2,1)S(1)} collective-permute-done((bf16[256,768]{1,0:T(8,128)(2,1)S(1)}, bf16[256,768]{1,0:T(8,128)(2,1)S(1)}, u32[]{:S(2)}, u32[]{:S(2)}) %collective-permute-start.35) | collective-permute-done | bytes 393248 | tf_op jit(solution)/shard_map/ppermute | solution.py:46
  171.0 2.4 %collective-permute-start.36 = (bf16[96,896]{1,0:T(8,128)(2,1)S(1)}, bf16[96,896]{1,0:T(8,128)(2,1)S(1)}, u32[]{:S(2)}, u32[]{:S(2)}) collective-permute-start(bf16[96,896]{1,0:T(8,128)(2,1)S(1)} %get-tuple-element.320), channel_id=1, source_target_pairs={{0,2},{1,3},{2,0},{3,1},{4,6},{5,7},{6,4},{7,5},{8,10},{9,11},{10,... | collective-permute-start | bytes 516104 | tf_op jit(solution)/shard_map/ppermute | solution.py:46
  175.8 4.6 %collective-permute-done.36.recv_ref = bf16[96,896]{1,0:T(8,128)(2,1)S(1)} collective-permute-done((bf16[96,896]{1,0:T(8,128)(2,1)S(1)}, bf16[96,896]{1,0:T(8,128)(2,1)S(1)}, u32[]{:S(2)}, u32[]{:S(2)}) %collective-permute-start.36) | collective-permute-done | bytes 172064 | tf_op jit(solution)/shard_map/ppermute | solution.py:46
  (82 shorter events, 55.9 us)
Async XLA Ops:
  2.8 23.7 %collective-permute-start.4 = (bf16[96,2304]{1,0:T(8,128)(2,1)S(1)}, bf16[96,2304]{1,0:T(8,128)(2,1)S(1)}, u32[]{:S(2)}, u32[]{:S(2)}) collective-permute-start(bf16[96,2304]{1,0:T(8,128)(2,1)S(1)} %get-tuple-element.184.own_ref), channel_id=1, source_target_pairs={{0,2},{1,3},{2,0},{3,1},{4,6},{5,7},{6,4},{7,5},{8,10},{9,11},{10,... | collective-permute-start | bytes 1327112 | tf_op jit(solution)/shard_map/ppermute | solution.py:46
  6.9 19.0 %collective-permute-start.2 = (bf16[96,2240]{1,0:T(8,128)(2,1)S(1)}, bf16[96,2240]{1,0:T(8,128)(2,1)S(1)}, u32[]{:S(2)}, u32[]{:S(2)}) collective-permute-start(bf16[96,2240]{1,0:T(8,128)(2,1)S(1)} %get-tuple-element.196.mine_ref.refs_0_), channel_id=1, source_target_pairs={{0,8},{4,12},{8,0},{12,4},{16,24},{20,28},{24,16},{28,20},{1,9},{5... | collective-permute-start | bytes 1290248 | tf_op jit(solution)/shard_map/ppermute | solution.py:46
  8.4 17.7 %collective-permute-start.3 = (bf16[96,2240]{1,0:T(8,128)(2,1)S(1)}, bf16[96,2240]{1,0:T(8,128)(2,1)S(1)}, u32[]{:S(2)}, u32[]{:S(2)}) collective-permute-start(bf16[96,2240]{1,0:T(8,128)(2,1)S(1)} %get-tuple-element.196.mine_ref.refs_0_), channel_id=1, source_target_pairs={{0,16},{4,20},{8,24},{12,28},{16,0},{20,4},{24,8},{28,12},{1,17},{... | collective-permute-start | bytes 1290248 | tf_op jit(solution)/shard_map/ppermute | solution.py:46
  10.0 16.0 %collective-permute-start.1 = (bf16[96,1536]{1,0:T(8,128)(2,1)S(1)}, bf16[96,1536]{1,0:T(8,128)(2,1)S(1)}, u32[]{:S(2)}, u32[]{:S(2)}) collective-permute-start(bf16[96,1536]{1,0:T(8,128)(2,1)S(1)} %get-tuple-element.182), channel_id=1, source_target_pairs={{0,24},{4,28},{8,16},{12,20},{16,8},{20,12},{24,0},{28,4},{1,25},{... | collective-permute-start | bytes 884744 | tf_op jit(solution)/shard_map/ppermute | solution.py:46
  27.2 13.2 %collective-permute-start.8 = (bf16[304,768]{1,0:T(8,128)(2,1)S(1)}, bf16[304,768]{1,0:T(8,128)(2,1)S(1)}, u32[]{:S(2)}, u32[]{:S(2)}) collective-permute-start(bf16[304,768]{1,0:T(8,128)(2,1)S(1)} %get-tuple-element.192), channel_id=1, source_target_pairs={{0,1},{1,0},{2,3},{3,2},{4,5},{5,4},{6,7},{7,6},{8,9},{9,8},{10,11... | collective-permute-start | bytes 1400840 | tf_op jit(solution)/shard_map/ppermute | solution.py:46
  28.4 12.1 %collective-permute-start.9 = (bf16[304,768]{1,0:T(8,128)(2,1)S(1)}, bf16[304,768]{1,0:T(8,128)(2,1)S(1)}, u32[]{:S(2)}, u32[]{:S(2)}) collective-permute-start(bf16[304,768]{1,0:T(8,128)(2,1)S(1)} %get-tuple-element.189.label_ref), channel_id=1, source_target_pairs={{1,2},{2,1},{5,6},{6,5},{9,10},{10,9},{13,14},{14,13},{17,18},{18,... | collective-permute-start | bytes 1400840 | tf_op jit(solution)/shard_map/ppermute | solution.py:1131
  41.2 17.5 %collective-permute-start.11 = (bf16[304,768]{1,0:T(8,128)(2,1)S(1)}, bf16[304,768]{1,0:T(8,128)(2,1)S(1)}, u32[]{:S(2)}, u32[]{:S(2)}) collective-permute-start(bf16[304,768]{1,0:T(8,128)(2,1)S(1)} %collective-permute-done.9.near_ref), channel_id=1, source_target_pairs={{1,0},{2,3},{5,4},{6,7},{9,8},{10,11},{13,12},{14,15},{17,16},{18,... | collective-permute-start | bytes 1400840 | tf_op jit(solution)/shard_map/ppermute | solution.py:1141
  43.4 20.9 %collective-permute-start.13 = (bf16[96,2304]{1,0:T(8,128)(2,1)S(1)}, bf16[96,2304]{1,0:T(8,128)(2,1)S(1)}, u32[]{:S(2)}, u32[]{:S(2)}) collective-permute-start(bf16[96,2304]{1,0:T(8,128)(2,1)S(1)} %pack_feed.1.refs_4_), channel_id=1, source_target_pairs={{0,8},{4,12},{8,0},{12,4},{16,24},{20,28},{24,16},{28,20},{1,9},{5... | collective-permute-start | bytes 1327112 | tf_op jit(solution)/shard_map/ppermute | solution.py:46
  44.9 21.8 %collective-permute-start.14 = (bf16[96,2304]{1,0:T(8,128)(2,1)S(1)}, bf16[96,2304]{1,0:T(8,128)(2,1)S(1)}, u32[]{:S(2)}, u32[]{:S(2)}) collective-permute-start(bf16[96,2304]{1,0:T(8,128)(2,1)S(1)} %pack_feed.1.refs_4_), channel_id=1, source_target_pairs={{0,16},{4,20},{8,24},{12,28},{16,0},{20,4},{24,8},{28,12},{1,17},{... | collective-permute-start | bytes 1327112 | tf_op jit(solution)/shard_map/ppermute | solution.py:46
  46.3 20.4 %collective-permute-start.15 = (bf16[96,2304]{1,0:T(8,128)(2,1)S(1)}, bf16[96,2304]{1,0:T(8,128)(2,1)S(1)}, u32[]{:S(2)}, u32[]{:S(2)}) collective-permute-start(bf16[96,2304]{1,0:T(8,128)(2,1)S(1)} %pack_feed.1.refs_4_), channel_id=1, source_target_pairs={{0,24},{4,28},{8,16},{12,20},{16,8},{20,12},{24,0},{28,4},{1,25},{... | collective-permute-start | bytes 1327112 | tf_op jit(solution)/shard_map/ppermute | solution.py:46
  72.5 15.2 %collective-permute-start.19 = (bf16[256,768]{1,0:T(8,128)(2,1)S(1)}, bf16[256,768]{1,0:T(8,128)(2,1)S(1)}, u32[]{:S(2)}, u32[]{:S(2)}) collective-permute-start(bf16[256,768]{1,0:T(8,128)(2,1)S(1)} %bitcast.9), channel_id=1, source_target_pairs={{0,1},{1,0},{2,3},{3,2},{4,5},{5,4},{6,7},{7,6},{8,9},{9,8},{10,11... | collective-permute-start | bytes 1179656 | tf_op jit(solution)/shard_map/ppermute | solution.py:46
  81.4 13.7 %collective-permute-start.18 = (bf16[256,768]{1,0:T(8,128)(2,1)S(1)}, bf16[256,768]{1,0:T(8,128)(2,1)S(1)}, u32[]{:S(2)}, u32[]{:S(2)}) collective-permute-start(bf16[256,768]{1,0:T(8,128)(2,1)S(1)} %get-tuple-element.228.part_ref), channel_id=1, source_target_pairs={{0,1},{1,0},{2,3},{3,2},{4,5},{5,4},{6,7},{7,6},{8,9},{9,8},{10,11... | collective-permute-start | bytes 1179656 | tf_op jit(solution)/shard_map/ppermute | solution.py:46
  86.3 17.2 %collective-permute-start.21 = (bf16[256,768]{1,0:T(8,128)(2,1)S(1)}, bf16[256,768]{1,0:T(8,128)(2,1)S(1)}, u32[]{:S(2)}, u32[]{:S(2)}) collective-permute-start(bf16[256,768]{1,0:T(8,128)(2,1)S(1)} %get-tuple-element.238.part_ref), channel_id=1, source_target_pairs={{0,1},{1,0},{2,3},{3,2},{4,5},{5,4},{6,7},{7,6},{8,9},{9,8},{10,11... | collective-permute-start | bytes 1179656 | tf_op jit(solution)/shard_map/ppermute | solution.py:46
  98.0 14.3 %collective-permute-start.20 = (bf16[256,768]{1,0:T(8,128)(2,1)S(1)}, bf16[256,768]{1,0:T(8,128)(2,1)S(1)}, u32[]{:S(2)}, u32[]{:S(2)}) collective-permute-start(bf16[256,768]{1,0:T(8,128)(2,1)S(1)} %get-tuple-element.269.part_ref), channel_id=1, source_target_pairs={{0,1},{1,0},{2,3},{3,2},{4,5},{5,4},{6,7},{7,6},{8,9},{9,8},{10,11... | collective-permute-start | bytes 1179656 | tf_op jit(solution)/shard_map/ppermute | solution.py:46
  112.4 16.5 %collective-permute-start.22 = (bf16[256,768]{1,0:T(8,128)(2,1)S(1)}, bf16[256,768]{1,0:T(8,128)(2,1)S(1)}, u32[]{:S(2)}, u32[]{:S(2)}) collective-permute-start(bf16[256,768]{1,0:T(8,128)(2,1)S(1)} %get-tuple-element.264.part_ref), channel_id=1, source_target_pairs={{0,1},{1,0},{2,3},{3,2},{4,5},{5,4},{6,7},{7,6},{8,9},{9,8},{10,11... | collective-permute-start | bytes 1179656 | tf_op jit(solution)/shard_map/ppermute | solution.py:46
  116.0 15.1 %collective-permute-start.23 = (bf16[304,384]{1,0:T(8,128)(2,1)S(1)}, bf16[304,384]{1,0:T(8,128)(2,1)S(1)}, u32[]{:S(2)}, u32[]{:S(2)}) collective-permute-start(bf16[304,384]{1,0:T(8,128)(2,1)S(1)} %get-tuple-element.279), channel_id=1, source_target_pairs={{0,2},{1,3},{2,0},{3,1},{4,6},{5,7},{6,4},{7,5},{8,10},{9,11},{10,... | collective-permute-start | bytes 700424 | tf_op jit(solution)/shard_map/ppermute | solution.py:46
  118.6 28.3 %collective-permute-start.26 = (bf16[96,3072]{1,0:T(8,128)(2,1)S(1)}, bf16[96,3072]{1,0:T(8,128)(2,1)S(1)}, u32[]{:S(2)}, u32[]{:S(2)}) collective-permute-start(bf16[96,3072]{1,0:T(8,128)(2,1)S(1)} %get-tuple-element.293), channel_id=1, source_target_pairs={{0,8},{4,12},{8,0},{12,4},{16,24},{20,28},{24,16},{28,20},{1,9},{5... | collective-permute-start | bytes 1769480 | tf_op jit(solution)/shard_map/ppermute | solution.py:46
  119.8 27.0 %collective-permute-start.27 = (bf16[96,3072]{1,0:T(8,128)(2,1)S(1)}, bf16[96,3072]{1,0:T(8,128)(2,1)S(1)}, u32[]{:S(2)}, u32[]{:S(2)}) collective-permute-start(bf16[96,3072]{1,0:T(8,128)(2,1)S(1)} %get-tuple-element.294), channel_id=1, source_target_pairs={{0,16},{4,20},{8,24},{12,28},{16,0},{20,4},{24,8},{28,12},{1,17},{... | collective-permute-start | bytes 1769480 | tf_op jit(solution)/shard_map/ppermute | solution.py:46
  120.6 26.9 %collective-permute-start.28 = (bf16[96,3072]{1,0:T(8,128)(2,1)S(1)}, bf16[96,3072]{1,0:T(8,128)(2,1)S(1)}, u32[]{:S(2)}, u32[]{:S(2)}) collective-permute-start(bf16[96,3072]{1,0:T(8,128)(2,1)S(1)} %get-tuple-element.295), channel_id=1, source_target_pairs={{0,24},{4,28},{8,16},{12,20},{16,8},{20,12},{24,0},{28,4},{1,25},{... | collective-permute-start | bytes 1769480 | tf_op jit(solution)/shard_map/ppermute | solution.py:46
  150.6 18.5 %collective-permute-start.35 = (bf16[256,768]{1,0:T(8,128)(2,1)S(1)}, bf16[256,768]{1,0:T(8,128)(2,1)S(1)}, u32[]{:S(2)}, u32[]{:S(2)}) collective-permute-start(bf16[256,768]{1,0:T(8,128)(2,1)S(1)} %get-tuple-element.315), channel_id=1, source_target_pairs={{0,1},{1,0},{2,3},{3,2},{4,5},{5,4},{6,7},{7,6},{8,9},{9,8},{10,11... | collective-permute-start | bytes 1179656 | tf_op jit(solution)/shard_map/ppermute | solution.py:46
  152.3 16.8 %collective-permute-start.34 = (bf16[96,1792]{1,0:T(8,128)(2,1)S(1)}, bf16[96,1792]{1,0:T(8,128)(2,1)S(1)}, u32[]{:S(2)}, u32[]{:S(2)}) collective-permute-start(bf16[96,1792]{1,0:T(8,128)(2,1)S(1)} %get-tuple-element.314), channel_id=1, source_target_pairs={{0,2},{1,3},{2,0},{3,1},{4,6},{5,7},{6,4},{7,5},{8,10},{9,11},{10,... | collective-permute-start | bytes 1032200 | tf_op jit(solution)/shard_map/ppermute | solution.py:46
  153.8 15.2 %collective-permute-start.31 = (bf16[96,1664]{1,0:T(8,128)(2,1)S(1)}, bf16[96,1664]{1,0:T(8,128)(2,1)S(1)}, u32[]{:S(2)}, u32[]{:S(2)}) collective-permute-start(bf16[96,1664]{1,0:T(8,128)(2,1)S(1)} %get-tuple-element.311), channel_id=1, source_target_pairs={{0,8},{4,12},{8,0},{12,4},{16,24},{20,28},{24,16},{28,20},{1,9},{5... | collective-permute-start | bytes 958472 | tf_op jit(solution)/shard_map/ppermute | solution.py:46
  154.7 15.5 %collective-permute-start.32 = (bf16[96,1664]{1,0:T(8,128)(2,1)S(1)}, bf16[96,1664]{1,0:T(8,128)(2,1)S(1)}, u32[]{:S(2)}, u32[]{:S(2)}) collective-permute-start(bf16[96,1664]{1,0:T(8,128)(2,1)S(1)} %get-tuple-element.312), channel_id=1, source_target_pairs={{0,16},{4,20},{8,24},{12,28},{16,0},{20,4},{24,8},{28,12},{1,17},{... | collective-permute-start | bytes 958472 | tf_op jit(solution)/shard_map/ppermute | solution.py:46
  156.2 14.1 %collective-permute-start.33 = (bf16[96,1664]{1,0:T(8,128)(2,1)S(1)}, bf16[96,1664]{1,0:T(8,128)(2,1)S(1)}, u32[]{:S(2)}, u32[]{:S(2)}) collective-permute-start(bf16[96,1664]{1,0:T(8,128)(2,1)S(1)} %get-tuple-element.313), channel_id=1, source_target_pairs={{0,24},{4,28},{8,16},{12,20},{16,8},{20,12},{24,0},{28,4},{1,25},{... | collective-permute-start | bytes 958472 | tf_op jit(solution)/shard_map/ppermute | solution.py:46
  (15 other events, 110.4 us)

commit v9 on v8

--- a/solution.py
+++ b/solution.py
@@ -156,8 +156,8 @@
         docs = refs[5][...].astype(F32)
         docs_ref[...] = docs
         label_ref[:rows, :] = refs[4][...]
-        label_ref[rows:, :] = jnp.zeros((MARKS, D), BF)
-        label_ref[rows:, :rows] = jnp.broadcast_to(docs, (MARKS, rows)).astype(BF)
+        label_ref[rows:, :] = jnp.zeros((LABELS, D), BF)
+        label_ref[rows:, :rows] = jnp.broadcast_to(docs, (LABELS, rows)).astype(BF)
         if lines:
             table = [ref[...].astype(F32)[None, :] for ref in refs[8 : 8 + VECS]]
             table = jnp.concatenate(table, axis=0)
@@ -171,7 +171,7 @@
         struct((height, D + 2 * HID), BF),
         struct((height, skip + 3 * QUARTER), BF),
         struct((height, 2 * HID), BF),
-        struct((rows + MARKS, D), BF),
+        struct((rows + LABELS, D), BF),
         struct((1, rows), F32),
     ]
     operands = [pltpu.with_memory_space_constraint(o, pltpu.MemorySpace.HBM) for o in operands]
@@ -193,12 +193,13 @@
     tall = rows + LABELS
     skip = mine.shape[1] - 3 * QUARTER
     direct = skip > 2 * HID
+    known = labelled.shape[0]
 
     def body(_, far_ref, mine_ref, label_ref, narrow_ref, both_ref, send_ref):
         narrow_ref[...] = far_ref[:, : 3 * QUARTER]
         both_ref[:rows, :] = mine_ref[:, skip:]
         both_ref[tall:, :] = far_ref[:, : 3 * QUARTER]
-        send_ref[...] = label_ref[...]
+        send_ref[:known, :] = label_ref[...]
         if direct:
             both_ref[rows:tall, :] = jnp.zeros((LABELS, 3 * QUARTER), BF)
             both_ref[rows:tall, :128] = mine_ref[:LABELS, 2 * HID : skip]
@@ -206,12 +207,12 @@
             step = rows // 4
             part = jnp.concatenate([part[k * step : (k + 1) * step] for k in range(4)], axis=1)
             part = jnp.concatenate([part, jnp.zeros((MARKS - LABELS - step, D), F32)], axis=0)
-            send_ref[labelled.shape[0] - MARKS + LABELS :, :] = part.astype(BF)
+            send_ref[known:, :] = part.astype(BF)
 
     outs = [
         struct((rows, 3 * QUARTER), BF),
         struct((rows + tall, 3 * QUARTER), BF),
-        struct(labelled.shape, BF),
+        struct((known + (MARKS - LABELS if direct else 0), D), BF),
     ]
     return simple("split_arrived", body, scalars, [arrived, mine, labelled], outs)
 

time: 182 us -> 182 us (level)
  no operation moved by 1% of the time
where the time goes in v9:
time: 182 us
  waiting for transfers between devices  71.8 us (39%)
  Pallas kernels  63.7 us (35%)
  starting transfers between devices  44.1 us (24%)
    ppermute x35, waiting for transfers between devices, swap(): return lax.ppermute(value, axis, [(k, k ^ mask) for k in range(count)])  67.3 us
    pallas_call x26, Pallas kernels, call(): pl.pallas_call(body, out_shape=outs, grid_spec=spec, compiler_params=para...  63.7 us
    ppermute x35, starting transfers between devices, swap(): return lax.ppermute(value, axis, [(k, k ^ mask) for k in range(count)])  42.2 us
    ppermute x1, waiting for transfers between devices, per_device(): halo_far = lax.ppermute(halo_near, 'seq', [(1, 0), (2, 3)])  4.44 us
  transfers between devices with their start and end apart: 37, of which 17 were waited for; matrix products, arithmetic and copies ran while one was open for 1% of the time, Pallas kernels for 32%

profile of v9, /device:TPU:0, one launch (start us, length us, event | category | flops | bytes accessed | tf_op | source)
XLA Modules:
  0.0 181.8 jit_solution(5013962771577724470)
XLA Ops:
  2.8 4.1 %collective-permute-start.4 = (bf16[96,2304]{1,0:T(8,128)(2,1)S(1)}, bf16[96,2304]{1,0:T(8,128)(2,1)S(1)}, u32[]{:S(2)}, u32[]{:S(2)}) collective-permute-start(bf16[96,2304]{1,0:T(8,128)(2,1)S(1)} %get-tuple-element.184.own_ref), channel_id=1, source_target_pairs={{0,2},{1,3},{2,0},{3,1},{4,6},{5,7},{6,4},{7,5},{8,10},{9,11},{10,... | collective-permute-start | bytes 1327112 | tf_op jit(solution)/shard_map/ppermute | solution.py:46
  12.0 5.6 %collective-permute-done.side_ref = bf16[96,192]{1,0:T(8,128)(2,1)S(1)} collective-permute-done((bf16[96,192]{1,0:T(8,128)(2,1)}, bf16[96,192]{1,0:T(8,128)(2,1)S(1)}, u32[]{:S(2)}, u32[]{:S(2)}) %collective-permute-start) | collective-permute-done | bytes 36896 | tf_op jit(solution)/shard_map/ppermute | solution.py:46
  17.6 8.4 %collective-permute-done.1.refs_3_ = bf16[96,1536]{1,0:T(8,128)(2,1)S(1)} collective-permute-done((bf16[96,1536]{1,0:T(8,128)(2,1)S(1)}, bf16[96,1536]{1,0:T(8,128)(2,1)S(1)}, u32[]{:S(2)}, u32[]{:S(2)}) %collective-permute-start.1) | collective-permute-done | bytes 294944 | tf_op jit(solution)/shard_map/ppermute | solution.py:46
  32.6 7.8 %collective-permute-done.5.refs_4_ = bf16[96,576]{1,0:T(8,128)(2,1)S(1)} collective-permute-done((bf16[96,576]{1,0:T(8,128)(2,1)S(1)}, bf16[96,576]{1,0:T(8,128)(2,1)S(1)}, u32[]{:S(2)}, u32[]{:S(2)}) %collective-permute-start.5) | collective-permute-done | bytes 110624 | tf_op jit(solution)/shard_map/ppermute | solution.py:46
  46.9 6.3 %attend_pair.1 = (bf16[512,384]{1,0:T(8,128)(2,1)S(1)}, bf16[512,384]{1,0:T(8,128)(2,1)S(1)}, bf16[512,384]{1,0:T(8,128)(2,1)S(1)}, bf16[256,384]{1,0:T(8,128)(2...) custom-call(s32[3]{0:T(128)S(1)} %pad_add_fusion._.sc, ...), custom_call_target="tpu_custom_call" | custom-call | flops 80000000 | bytes 1024 | tf_op jit(solution)/shard_map/attend_pair/pallas_call | solution.py:69
  53.2 4.4 %collective-permute-done.11.far_ref = bf16[272,768]{1,0:T(8,128)(2,1)S(1)} collective-permute-done((bf16[272,768]{1,0:T(8,128)(2,1)S(1)}, bf16[272,768]{1,0:T(8,128)(2,1)S(1)}, u32[]{:S(2)}, u32[]{:S(2)}) %collective-permute-start.11) | collective-permute-done | bytes 417824 | tf_op jit(solution)/shard_map/ppermute | solution.py:1142
  58.2 5.5 %attend_halo.1 = (bf16[256,384]{1,0:T(8,128)(2,1)S(1)}, bf16[256,384]{1,0:T(8,128)(2,1)S(1)}, bf16[256,384]{1,0:T(8,128)(2,1)S(1)}, bf16[256,384]{1,0:T(8,128)(2...) custom-call(s32[3]{0:T(128)S(1)} %pad_add_fusion._.sc, ...), custom_call_target="tpu_custom_call" | custom-call | flops 60000000 | bytes 1024 | tf_op jit(solution)/shard_map/attend_halo/pallas_call | solution.py:69
  63.7 3.0 %collective-permute-done.14.refs_6_ = bf16[96,2304]{1,0:T(8,128)(2,1)S(1)} collective-permute-done((bf16[96,2304]{1,0:T(8,128)(2,1)S(1)}, bf16[96,2304]{1,0:T(8,128)(2,1)S(1)}, u32[]{:S(2)}, u32[]{:S(2)}) %collective-permute-start.14) | collective-permute-done | bytes 442400 | tf_op jit(solution)/shard_map/ppermute | solution.py:46
  67.5 5.0 %collective-permute-start.16 = (bf16[256,384]{1,0:T(8,128)(2,1)S(1)}, bf16[256,384]{1,0:T(8,128)(2,1)S(1)}, u32[]{:S(2)}, u32[]{:S(2)}) collective-permute-start(bf16[256,384]{1,0:T(8,128)(2,1)S(1)} %get-tuple-element.219.mine_ref.refs_3_), channel_id=1, source_target_pairs={{0,1},{1,0},{2,3},{3,2},{4,5},{5,4},{6,7},{7,6},{8,9},{9,8},{10,11... | collective-permute-start | bytes 589832 | tf_op jit(solution)/shard_map/ppermute | solution.py:46
  72.6 5.6 %collective-permute-done.16.partner_ref.refs_4_ = bf16[256,384]{1,0:T(8,128)(2,1)S(1)} collective-permute-done((bf16[256,384]{1,0:T(8,128)(2,1)S(1)}, bf16[256,384]{1,0:T(8,128)(2,1)S(1)}, u32[]{:S(2)}, u32[]{:S(2)}) %collective-permute-start.16) | collective-permute-done | bytes 196640 | tf_op jit(solution)/shard_map/ppermute | solution.py:46
  78.2 3.2 %feed_forward.2 = (f32[256,768]{1,0:T(8,128)S(1)}, f32[256,128]{1,0:T(8,128)S(1)}, bf16[256,768]{1,0:T(8,128)(2,1)S(1)}, f32[256,1536]{1,0:T(8,128)S(1)}, bf16[2...) custom-call(s32[3]{0:T(128)S(1)} %pad_add_fusion._.sc, ...), custom_call_target="tpu_custom_call" | custom-call | flops 60000000 | bytes 1024 | tf_op jit(solution)/shard_map/feed_forward/pallas_call | solution.py:69
  83.4 2.9 %feed_forward.3 = (f32[256,768]{1,0:T(8,128)S(1)}, f32[256,128]{1,0:T(8,128)S(1)}, bf16[256,768]{1,0:T(8,128)(2,1)S(1)}, f32[256,1536]{1,0:T(8,128)S(1)}, bf16[2...) custom-call(s32[3]{0:T(128)S(1)} %pad_add_fusion._.sc, bf16[256,384]{1,0:T(8,128)(2,1)S(1)} %get-tuple-element.216.mine_ref.refs_0_, ...), custom_call_target="tpu_custom_call" | custom-call | flops 60000000 | bytes 1024 | tf_op jit(solution)/shard_map/feed_forward/pallas_call | solution.py:69
  87.6 7.4 %collective-permute-done.18.recv_ref = bf16[256,768]{1,0:T(8,128)(2,1)S(1)} collective-permute-done((bf16[256,768]{1,0:T(8,128)(2,1)S(1)}, bf16[256,768]{1,0:T(8,128)(2,1)S(1)}, u32[]{:S(2)}, u32[]{:S(2)}) %collective-permute-start.18) | collective-permute-done | bytes 393248 | tf_op jit(solution)/shard_map/ppermute | solution.py:46
  95.1 2.9 %second_norm.2 = (f32[256,768]{1,0:T(8,128)S(1)}, bf16[256,768]{1,0:T(8,128)(2,1)S(1)}, bf16[256,1536]{1,0:T(8,128)(2,1)S(1)}, bf16[256,768]{1,0:T(8,128)(2,1)S(...) custom-call(s32[3]{0:T(128)S(1)} %pad_add_fusion._.sc, ...), custom_call_target="tpu_custom_call" | custom-call | flops 50000000 | bytes 1024 | tf_op jit(solution)/shard_map/second_norm/pallas_call | solution.py:69
  98.0 2.3 %collective-permute-start.20 = (bf16[256,768]{1,0:T(8,128)(2,1)S(1)}, bf16[256,768]{1,0:T(8,128)(2,1)S(1)}, u32[]{:S(2)}, u32[]{:S(2)}) collective-permute-start(bf16[256,768]{1,0:T(8,128)(2,1)S(1)} %get-tuple-element.269.part_ref), channel_id=1, source_target_pairs={{0,1},{1,0},{2,3},{3,2},{4,5},{5,4},{6,7},{7,6},{8,9},{9,8},{10,11... | collective-permute-start | bytes 1179656 | tf_op jit(solution)/shard_map/ppermute | solution.py:46
  103.5 3.8 %second_norm.3 = (f32[256,768]{1,0:T(8,128)S(1)}, bf16[256,768]{1,0:T(8,128)(2,1)S(1)}, bf16[256,1536]{1,0:T(8,128)(2,1)S(1)}, bf16[256,768]{1,0:T(8,128)(2,1)S(...) custom-call(s32[3]{0:T(128)S(1)} %pad_add_fusion._.sc, ...), custom_call_target="tpu_custom_call" | custom-call | flops 50000000 | bytes 1024 | tf_op jit(solution)/shard_map/second_norm/pallas_call | solution.py:69
  107.3 5.0 %feed_forward_grads.1 = (bf16[4,96,3072]{2,1,0:T(8,128)(2,1)S(1)}, bf16[4,96,3072]{2,1,0:T(8,128)(2,1)S(1)}) custom-call(s32[3]{0:T(128)S(1)} %pad_add_fusion._.sc, bf16[256,768]{1,0:T(8,128)(2,1)S(1)} %get-tuple-element.254.refs_0_, bf16[256,1536]{1,0:T(8,128)(2,1)S(1)} %get-tuple-element.246.refs_1_, bf16[256,768]{1,0:T(8,128)(2,1)S(1)} %get-tuple-element.245.refs_2_, ...), custom_call_target="tpu_custom_call" | custom-call | flops 80000000 | bytes 1024 | tf_op jit(solution)/shard_map/feed_forward_grads/pallas_call | solution.py:69
  122.1 6.8 %collective-permute-done.22.recv_ref = bf16[256,768]{1,0:T(8,128)(2,1)S(1)} collective-permute-done((bf16[256,768]{1,0:T(8,128)(2,1)S(1)}, bf16[256,768]{1,0:T(8,128)(2,1)S(1)}, u32[]{:S(2)}, u32[]{:S(2)}) %collective-permute-start.22) | collective-permute-done | bytes 393248 | tf_op jit(solution)/shard_map/ppermute | solution.py:46
  128.9 2.1 %first_norm.3 = (bf16[256,768]{1,0:T(8,128)(2,1)S(1)}, bf16[256,384]{1,0:T(8,128)(2,1)S(1)}, f32[8,256]{1,0:T(8,128)S(1)}, f32[256,768]{1,0:T(8,128)S(1)}, f32[8,768]{1,0:T(8,128)S(1)}) custom-call(s32[3]{0:T(128)S(1)} %pad_add_fusion._.sc, bf16[256,768]{1,0:T(8,128)(2,1)S(1)} %get-tuple-element.264.part_ref, ...), custom_call_target="tpu_custom_call" | custom-call | flops 30000000 | bytes 1024 | tf_op jit(solution)/shard_map/first_norm/pallas_call | solution.py:69
  131.1 10.7 %attend_backward.1 = (bf16[512,1152]{1,0:T(8,128)(2,1)S(1)}, f32[256,768]{1,0:T(8,128)S(1)}, bf16[256,768]{1,0:T(8,128)(2,1)S(1)}, f32[8,1152]{1,0:T(8,128)S(1)}) custom-call(s32[3]{0:T(128)S(1)} %pad_add_fusion._.sc, bf16[512,384]{1,0:T(8,128)(2,1)S(1)} %get-tuple-element.212.q_ref.refs_0_, bf16[512,384]{1,0:T(8,128)(2,1)S(1)} %get-tuple-element.213.k_ref.refs_1_, ...), custom_call_target="tpu_custom_call" | custom-call | flops 4499999744 | bytes 1024 | tf_op jit(solution)/shard_map/attend_backward/pallas_call | solution.py:69
  142.6 2.9 %projection_grads.1 = (bf16[4,96,1152]{2,1,0:T(8,128)(2,1)S(1)}, bf16[4,96,1152]{2,1,0:T(8,128)(2,1)S(1)}) custom-call(s32[3]{0:T(128)S(1)} %pad_add_fusion._.sc, bf16[512,768]{1,0:T(8,128)(2,1)S(1)} %get-tuple-element.220.x_ref, bf16[512,1152]{1,0:T(8,128)(2,1)S(1)} %get-tuple-element.283.grad_ref), custom_call_target="tpu_custom_call" | custom-call | flops 50000000 | bytes 1024 | tf_op jit(solution)/shard_map/projection_grads/pallas_call | solution.py:69
  157.3 11.7 %collective-permute-done.35 = bf16[256,768]{1,0:T(8,128)(2,1)S(1)} collective-permute-done((bf16[256,768]{1,0:T(8,128)(2,1)S(1)}, bf16[256,768]{1,0:T(8,128)(2,1)S(1)}, u32[]{:S(2)}, u32[]{:S(2)}) %collective-permute-start.35) | collective-permute-done | bytes 393248 | tf_op jit(solution)/shard_map/ppermute | solution.py:46
  171.0 2.3 %collective-permute-start.36 = (bf16[96,896]{1,0:T(8,128)(2,1)S(1)}, bf16[96,896]{1,0:T(8,128)(2,1)S(1)}, u32[]{:S(2)}, u32[]{:S(2)}) collective-permute-start(bf16[96,896]{1,0:T(8,128)(2,1)S(1)} %get-tuple-element.320), channel_id=1, source_target_pairs={{0,2},{1,3},{2,0},{3,1},{4,6},{5,7},{6,4},{7,5},{8,10},{9,11},{10,... | collective-permute-start | bytes 516104 | tf_op jit(solution)/shard_map/ppermute | solution.py:46
  175.8 4.5 %collective-permute-done.36.recv_ref = bf16[96,896]{1,0:T(8,128)(2,1)S(1)} collective-permute-done((bf16[96,896]{1,0:T(8,128)(2,1)S(1)}, bf16[96,896]{1,0:T(8,128)(2,1)S(1)}, u32[]{:S(2)}, u32[]{:S(2)}) %collective-permute-start.36) | collective-permute-done | bytes 172064 | tf_op jit(solution)/shard_map/ppermute | solution.py:46
  (82 shorter events, 56.3 us)
Async XLA Ops:
  2.8 23.7 %collective-permute-start.4 = (bf16[96,2304]{1,0:T(8,128)(2,1)S(1)}, bf16[96,2304]{1,0:T(8,128)(2,1)S(1)}, u32[]{:S(2)}, u32[]{:S(2)}) collective-permute-start(bf16[96,2304]{1,0:T(8,128)(2,1)S(1)} %get-tuple-element.184.own_ref), channel_id=1, source_target_pairs={{0,2},{1,3},{2,0},{3,1},{4,6},{5,7},{6,4},{7,5},{8,10},{9,11},{10,... | collective-permute-start | bytes 1327112 | tf_op jit(solution)/shard_map/ppermute | solution.py:46
  6.9 19.0 %collective-permute-start.2 = (bf16[96,2240]{1,0:T(8,128)(2,1)S(1)}, bf16[96,2240]{1,0:T(8,128)(2,1)S(1)}, u32[]{:S(2)}, u32[]{:S(2)}) collective-permute-start(bf16[96,2240]{1,0:T(8,128)(2,1)S(1)} %get-tuple-element.196.mine_ref.refs_0_), channel_id=1, source_target_pairs={{0,8},{4,12},{8,0},{12,4},{16,24},{20,28},{24,16},{28,20},{1,9},{5... | collective-permute-start | bytes 1290248 | tf_op jit(solution)/shard_map/ppermute | solution.py:46
  8.4 17.7 %collective-permute-start.3 = (bf16[96,2240]{1,0:T(8,128)(2,1)S(1)}, bf16[96,2240]{1,0:T(8,128)(2,1)S(1)}, u32[]{:S(2)}, u32[]{:S(2)}) collective-permute-start(bf16[96,2240]{1,0:T(8,128)(2,1)S(1)} %get-tuple-element.196.mine_ref.refs_0_), channel_id=1, source_target_pairs={{0,16},{4,20},{8,24},{12,28},{16,0},{20,4},{24,8},{28,12},{1,17},{... | collective-permute-start | bytes 1290248 | tf_op jit(solution)/shard_map/ppermute | solution.py:46
  10.0 16.0 %collective-permute-start.1 = (bf16[96,1536]{1,0:T(8,128)(2,1)S(1)}, bf16[96,1536]{1,0:T(8,128)(2,1)S(1)}, u32[]{:S(2)}, u32[]{:S(2)}) collective-permute-start(bf16[96,1536]{1,0:T(8,128)(2,1)S(1)} %get-tuple-element.182), channel_id=1, source_target_pairs={{0,24},{4,28},{8,16},{12,20},{16,8},{20,12},{24,0},{28,4},{1,25},{... | collective-permute-start | bytes 884744 | tf_op jit(solution)/shard_map/ppermute | solution.py:46
  27.2 13.2 %collective-permute-start.8 = (bf16[304,768]{1,0:T(8,128)(2,1)S(1)}, bf16[304,768]{1,0:T(8,128)(2,1)S(1)}, u32[]{:S(2)}, u32[]{:S(2)}) collective-permute-start(bf16[304,768]{1,0:T(8,128)(2,1)S(1)} %get-tuple-element.192), channel_id=1, source_target_pairs={{0,1},{1,0},{2,3},{3,2},{4,5},{5,4},{6,7},{7,6},{8,9},{9,8},{10,11... | collective-permute-start | bytes 1400840 | tf_op jit(solution)/shard_map/ppermute | solution.py:46
  28.4 12.1 %collective-permute-start.9 = (bf16[272,768]{1,0:T(8,128)(2,1)S(1)}, bf16[272,768]{1,0:T(8,128)(2,1)S(1)}, u32[]{:S(2)}, u32[]{:S(2)}) collective-permute-start(bf16[272,768]{1,0:T(8,128)(2,1)S(1)} %get-tuple-element.189.label_ref), channel_id=1, source_target_pairs={{1,2},{2,1},{5,6},{6,5},{9,10},{10,9},{13,14},{14,13},{17,18},{18,... | collective-permute-start | bytes 1253384 | tf_op jit(solution)/shard_map/ppermute | solution.py:1132
  41.2 16.4 %collective-permute-start.11 = (bf16[272,768]{1,0:T(8,128)(2,1)S(1)}, bf16[272,768]{1,0:T(8,128)(2,1)S(1)}, u32[]{:S(2)}, u32[]{:S(2)}) collective-permute-start(bf16[272,768]{1,0:T(8,128)(2,1)S(1)} %collective-permute-done.9.near_ref), channel_id=1, source_target_pairs={{1,0},{2,3},{5,4},{6,7},{9,8},{10,11},{13,12},{14,15},{17,16},{18,... | collective-permute-start | bytes 1253384 | tf_op jit(solution)/shard_map/ppermute | solution.py:1142
  43.3 20.3 %collective-permute-start.13 = (bf16[96,2304]{1,0:T(8,128)(2,1)S(1)}, bf16[96,2304]{1,0:T(8,128)(2,1)S(1)}, u32[]{:S(2)}, u32[]{:S(2)}) collective-permute-start(bf16[96,2304]{1,0:T(8,128)(2,1)S(1)} %pack_feed.1.refs_4_), channel_id=1, source_target_pairs={{0,8},{4,12},{8,0},{12,4},{16,24},{20,28},{24,16},{28,20},{1,9},{5... | collective-permute-start | bytes 1327112 | tf_op jit(solution)/shard_map/ppermute | solution.py:46
  44.9 21.8 %collective-permute-start.14 = (bf16[96,2304]{1,0:T(8,128)(2,1)S(1)}, bf16[96,2304]{1,0:T(8,128)(2,1)S(1)}, u32[]{:S(2)}, u32[]{:S(2)}) collective-permute-start(bf16[96,2304]{1,0:T(8,128)(2,1)S(1)} %pack_feed.1.refs_4_), channel_id=1, source_target_pairs={{0,16},{4,20},{8,24},{12,28},{16,0},{20,4},{24,8},{28,12},{1,17},{... | collective-permute-start | bytes 1327112 | tf_op jit(solution)/shard_map/ppermute | solution.py:46
  46.3 20.4 %collective-permute-start.15 = (bf16[96,2304]{1,0:T(8,128)(2,1)S(1)}, bf16[96,2304]{1,0:T(8,128)(2,1)S(1)}, u32[]{:S(2)}, u32[]{:S(2)}) collective-permute-start(bf16[96,2304]{1,0:T(8,128)(2,1)S(1)} %pack_feed.1.refs_4_), channel_id=1, source_target_pairs={{0,24},{4,28},{8,16},{12,20},{16,8},{20,12},{24,0},{28,4},{1,25},{... | collective-permute-start | bytes 1327112 | tf_op jit(solution)/shard_map/ppermute | solution.py:46
  72.5 15.2 %collective-permute-start.19 = (bf16[256,768]{1,0:T(8,128)(2,1)S(1)}, bf16[256,768]{1,0:T(8,128)(2,1)S(1)}, u32[]{:S(2)}, u32[]{:S(2)}) collective-permute-start(bf16[256,768]{1,0:T(8,128)(2,1)S(1)} %bitcast.9), channel_id=1, source_target_pairs={{0,1},{1,0},{2,3},{3,2},{4,5},{5,4},{6,7},{7,6},{8,9},{9,8},{10,11... | collective-permute-start | bytes 1179656 | tf_op jit(solution)/shard_map/ppermute | solution.py:46
  81.4 13.7 %collective-permute-start.18 = (bf16[256,768]{1,0:T(8,128)(2,1)S(1)}, bf16[256,768]{1,0:T(8,128)(2,1)S(1)}, u32[]{:S(2)}, u32[]{:S(2)}) collective-permute-start(bf16[256,768]{1,0:T(8,128)(2,1)S(1)} %get-tuple-element.228.part_ref), channel_id=1, source_target_pairs={{0,1},{1,0},{2,3},{3,2},{4,5},{5,4},{6,7},{7,6},{8,9},{9,8},{10,11... | collective-permute-start | bytes 1179656 | tf_op jit(solution)/shard_map/ppermute | solution.py:46
  86.3 17.2 %collective-permute-start.21 = (bf16[256,768]{1,0:T(8,128)(2,1)S(1)}, bf16[256,768]{1,0:T(8,128)(2,1)S(1)}, u32[]{:S(2)}, u32[]{:S(2)}) collective-permute-start(bf16[256,768]{1,0:T(8,128)(2,1)S(1)} %get-tuple-element.238.part_ref), channel_id=1, source_target_pairs={{0,1},{1,0},{2,3},{3,2},{4,5},{5,4},{6,7},{7,6},{8,9},{9,8},{10,11... | collective-permute-start | bytes 1179656 | tf_op jit(solution)/shard_map/ppermute | solution.py:46
  98.0 14.3 %collective-permute-start.20 = (bf16[256,768]{1,0:T(8,128)(2,1)S(1)}, bf16[256,768]{1,0:T(8,128)(2,1)S(1)}, u32[]{:S(2)}, u32[]{:S(2)}) collective-permute-start(bf16[256,768]{1,0:T(8,128)(2,1)S(1)} %get-tuple-element.269.part_ref), channel_id=1, source_target_pairs={{0,1},{1,0},{2,3},{3,2},{4,5},{5,4},{6,7},{7,6},{8,9},{9,8},{10,11... | collective-permute-start | bytes 1179656 | tf_op jit(solution)/shard_map/ppermute | solution.py:46
  112.4 16.5 %collective-permute-start.22 = (bf16[256,768]{1,0:T(8,128)(2,1)S(1)}, bf16[256,768]{1,0:T(8,128)(2,1)S(1)}, u32[]{:S(2)}, u32[]{:S(2)}) collective-permute-start(bf16[256,768]{1,0:T(8,128)(2,1)S(1)} %get-tuple-element.264.part_ref), channel_id=1, source_target_pairs={{0,1},{1,0},{2,3},{3,2},{4,5},{5,4},{6,7},{7,6},{8,9},{9,8},{10,11... | collective-permute-start | bytes 1179656 | tf_op jit(solution)/shard_map/ppermute | solution.py:46
  116.0 15.1 %collective-permute-start.23 = (bf16[304,384]{1,0:T(8,128)(2,1)S(1)}, bf16[304,384]{1,0:T(8,128)(2,1)S(1)}, u32[]{:S(2)}, u32[]{:S(2)}) collective-permute-start(bf16[304,384]{1,0:T(8,128)(2,1)S(1)} %get-tuple-element.279), channel_id=1, source_target_pairs={{0,2},{1,3},{2,0},{3,1},{4,6},{5,7},{6,4},{7,5},{8,10},{9,11},{10,... | collective-permute-start | bytes 700424 | tf_op jit(solution)/shard_map/ppermute | solution.py:46
  118.6 28.3 %collective-permute-start.26 = (bf16[96,3072]{1,0:T(8,128)(2,1)S(1)}, bf16[96,3072]{1,0:T(8,128)(2,1)S(1)}, u32[]{:S(2)}, u32[]{:S(2)}) collective-permute-start(bf16[96,3072]{1,0:T(8,128)(2,1)S(1)} %get-tuple-element.293), channel_id=1, source_target_pairs={{0,8},{4,12},{8,0},{12,4},{16,24},{20,28},{24,16},{28,20},{1,9},{5... | collective-permute-start | bytes 1769480 | tf_op jit(solution)/shard_map/ppermute | solution.py:46
  119.7 27.1 %collective-permute-start.27 = (bf16[96,3072]{1,0:T(8,128)(2,1)S(1)}, bf16[96,3072]{1,0:T(8,128)(2,1)S(1)}, u32[]{:S(2)}, u32[]{:S(2)}) collective-permute-start(bf16[96,3072]{1,0:T(8,128)(2,1)S(1)} %get-tuple-element.294), channel_id=1, source_target_pairs={{0,16},{4,20},{8,24},{12,28},{16,0},{20,4},{24,8},{28,12},{1,17},{... | collective-permute-start | bytes 1769480 | tf_op jit(solution)/shard_map/ppermute | solution.py:46
  120.6 26.9 %collective-permute-start.28 = (bf16[96,3072]{1,0:T(8,128)(2,1)S(1)}, bf16[96,3072]{1,0:T(8,128)(2,1)S(1)}, u32[]{:S(2)}, u32[]{:S(2)}) collective-permute-start(bf16[96,3072]{1,0:T(8,128)(2,1)S(1)} %get-tuple-element.295), channel_id=1, source_target_pairs={{0,24},{4,28},{8,16},{12,20},{16,8},{20,12},{24,0},{28,4},{1,25},{... | collective-permute-start | bytes 1769480 | tf_op jit(solution)/shard_map/ppermute | solution.py:46
  150.6 18.5 %collective-permute-start.35 = (bf16[256,768]{1,0:T(8,128)(2,1)S(1)}, bf16[256,768]{1,0:T(8,128)(2,1)S(1)}, u32[]{:S(2)}, u32[]{:S(2)}) collective-permute-start(bf16[256,768]{1,0:T(8,128)(2,1)S(1)} %get-tuple-element.315), channel_id=1, source_target_pairs={{0,1},{1,0},{2,3},{3,2},{4,5},{5,4},{6,7},{7,6},{8,9},{9,8},{10,11... | collective-permute-start | bytes 1179656 | tf_op jit(solution)/shard_map/ppermute | solution.py:46
  152.3 16.8 %collective-permute-start.34 = (bf16[96,1792]{1,0:T(8,128)(2,1)S(1)}, bf16[96,1792]{1,0:T(8,128)(2,1)S(1)}, u32[]{:S(2)}, u32[]{:S(2)}) collective-permute-start(bf16[96,1792]{1,0:T(8,128)(2,1)S(1)} %get-tuple-element.314), channel_id=1, source_target_pairs={{0,2},{1,3},{2,0},{3,1},{4,6},{5,7},{6,4},{7,5},{8,10},{9,11},{10,... | collective-permute-start | bytes 1032200 | tf_op jit(solution)/shard_map/ppermute | solution.py:46
  153.7 15.3 %collective-permute-start.31 = (bf16[96,1664]{1,0:T(8,128)(2,1)S(1)}, bf16[96,1664]{1,0:T(8,128)(2,1)S(1)}, u32[]{:S(2)}, u32[]{:S(2)}) collective-permute-start(bf16[96,1664]{1,0:T(8,128)(2,1)S(1)} %get-tuple-element.311), channel_id=1, source_target_pairs={{0,8},{4,12},{8,0},{12,4},{16,24},{20,28},{24,16},{28,20},{1,9},{5... | collective-permute-start | bytes 958472 | tf_op jit(solution)/shard_map/ppermute | solution.py:46
  154.7 15.5 %collective-permute-start.32 = (bf16[96,1664]{1,0:T(8,128)(2,1)S(1)}, bf16[96,1664]{1,0:T(8,128)(2,1)S(1)}, u32[]{:S(2)}, u32[]{:S(2)}) collective-permute-start(bf16[96,1664]{1,0:T(8,128)(2,1)S(1)} %get-tuple-element.312), channel_id=1, source_target_pairs={{0,16},{4,20},{8,24},{12,28},{16,0},{20,4},{24,8},{28,12},{1,17},{... | collective-permute-start | bytes 958472 | tf_op jit(solution)/shard_map/ppermute | solution.py:46
  156.1 14.1 %collective-permute-start.33 = (bf16[96,1664]{1,0:T(8,128)(2,1)S(1)}, bf16[96,1664]{1,0:T(8,128)(2,1)S(1)}, u32[]{:S(2)}, u32[]{:S(2)}) collective-permute-start(bf16[96,1664]{1,0:T(8,128)(2,1)S(1)} %get-tuple-element.313), channel_id=1, source_target_pairs={{0,24},{4,28},{8,16},{12,20},{16,8},{20,12},{24,0},{28,4},{1,25},{... | collective-permute-start | bytes 958472 | tf_op jit(solution)/shard_map/ppermute | solution.py:46
  (15 other events, 111.2 us)
